TPU v7x, 32 devices: a whole 2x2x4 slice. The times are simulated.
32 devices in a mesh: fsdp: 8 (over z, x), tensor: 4 (over y, core).
Axes of the slice: x: 2, y: 2, z: 4, core: 2. Of those that a mesh axis runs over, the one named last changes fastest.
Arguments:
- layer_in: bfloat16 [4096, 512], P(('fsdp', 'tensor')), may hold values from -6 to 6
- grad_out: bfloat16 [4096, 512], P(('fsdp', 'tensor')), may hold values from -6 to 6
- ln_scale: bfloat16 [512], P('fsdp'), may hold values from 0.099609375 to 1.8984375
- ln_bias: bfloat16 [512], P('fsdp'), may hold values from -3 to 3
- decay_rate: float32 [384], P('tensor'), may hold values from 0.02 to 0.5
- lam_im: float32 [384], P('tensor'), may hold values from -20 to 20
- log_dt: float32 [384], P('tensor'), may hold values from -6.9 to -2.3
- in_re: bfloat16 [384, 512], P('tensor', 'fsdp'), may hold values from -0.25 to 0.25
- in_im: bfloat16 [384, 512], P('tensor', 'fsdp'), may hold values from -0.25 to 0.25
- out_re: bfloat16 [384, 512], P('tensor', 'fsdp'), may hold values from -0.29882812 to 0.29882812
- out_im: bfloat16 [384, 512], P('tensor', 'fsdp'), may hold values from -0.29882812 to 0.29882812
- skip: bfloat16 [512], P('fsdp'), may hold values from -3 to 3
- glu_weight: bfloat16 [512, 512], P(None, 'fsdp'), may hold values from -0.25 to 0.25
- glu_bias: bfloat16 [512], P('fsdp'), may hold values from -4 to 4
- seq_lengths: int32 [4], replicated, may hold values from 1 to 2048, 4096 in all
Outputs:
- layer_out: bfloat16 [4096, 512], P(('fsdp', 'tensor'))
- grad_in: float32 [4096, 512], P(('fsdp', 'tensor'))
- grad_ln_scale: float32 [512], replicated
- grad_ln_bias: float32 [512], replicated
- grad_decay: float32 [384], replicated
- grad_lam_im: float32 [384], replicated
- grad_log_dt: float32 [384], replicated
- grad_in_re: float32 [384, 512], P('tensor', 'fsdp')
- grad_in_im: float32 [384, 512], P('tensor', 'fsdp')
- grad_out_re: float32 [384, 512], P('tensor', 'fsdp')
- grad_out_im: float32 [384, 512], P('tensor', 'fsdp')
- grad_skip: float32 [512], replicated
- grad_glu_weight: float32 [512, 512], P('tensor', 'fsdp')
- grad_glu_bias: float32 [512], P(('tensor', 'fsdp'))
- rms: float32 [2], replicated
Inputs may be any that keep to these rules, and one draw needn't show every extreme that they name: `seq_lengths`: the lengths sum to 4096 and the largest is exactly 2048.
All inputs are finite; a program needn't handle non-finite values.
Results may differ from a plain program's by a relative error of at most 0.012.
Values may be sent and summed in bfloat16 or wider, within the bound.
No kernel may reach another device: no remote copies, remote signals or barrier semaphores. Data moves between devices by JAX's collectives and lax.ppermute only.
A program may use at most 128 MiB of HBM per device.

v0:
```python
import jax
import jax.numpy as jnp
from jax import lax
from jax.sharding import PartitionSpec as P


def entering(x, axis, combine, identity, reverse):
    length, position = (lax.axis_size(axis), lax.axis_index(axis))
    everything = jax.tree.map(lambda part: lax.all_gather(part, axis), x)
    start = jax.tree.map(
        lambda part, zero: jnp.broadcast_to(jnp.asarray(zero, part.dtype), part.shape), x, identity
    )

    def turn(k, before):
        at = length - 1 - k if reverse else k
        reached = at > position if reverse else at < position
        new = combine(before, jax.tree.map(lambda part: part[at], everything))
        return jax.tree.map(lambda a, b: jnp.where(reached, a, b), new, before)

    return lax.fori_loop(0, length, turn, start)


def complex_mul(left_re, left_im, right_re, right_im):
    return (left_re * right_re - left_im * right_im, left_re * right_im + left_im * right_re)


def combine(former, latter):
    mul_re, mul_im = complex_mul(former[0], former[1], latter[0], latter[1])
    add_re, add_im = complex_mul(latter[0], latter[1], former[2], former[3])
    return (mul_re, mul_im, add_re + latter[2], add_im + latter[3])


def discretize(decay_rate, lam_im, log_dt):
    step_size = jnp.exp(log_dt)
    lam_re = -decay_rate
    magnitude = jnp.exp(lam_re * step_size)
    phase = lam_im * step_size
    abar_re = magnitude * jnp.cos(phase)
    abar_im = magnitude * jnp.sin(phase)
    half_sin = jnp.sin(0.5 * phase)
    less_re = jnp.expm1(lam_re * step_size) * jnp.cos(phase) - 2.0 * half_sin * half_sin
    denom = lam_re * lam_re + lam_im * lam_im
    coef_re = (less_re * lam_re + abar_im * lam_im) / denom
    coef_im = (abar_im * lam_re - less_re * lam_im) / denom
    return (abar_re, abar_im, coef_re, coef_im)


def gelu_slope(values):
    return (
        0.5 * (1.0 + lax.erf(values * 0.7071067811865476))
        + values * jnp.exp(-0.5 * values * values) * 0.3989422804014327
    )


def powers(log_mag, angle, count):
    shape = (log_mag.shape[0],) + (1,) * count.ndim
    magnitude = jnp.exp(log_mag.reshape(shape) * count)
    turned = angle.reshape(shape) * count
    return (magnitude * jnp.cos(turned), magnitude * jnp.sin(turned))


def on_device(
    layer_in,
    grad_out,
    ln_scale,
    ln_bias,
    decay_rate,
    lam_im,
    log_dt,
    in_re,
    in_im,
    out_re,
    out_im,
    skip,
    glu_weight,
    glu_bias,
    seq_lengths,
):
    tensors = lax.axis_size("tensor")
    tens_pos = lax.axis_index("tensor")
    fsdp_pos = lax.axis_index("fsdp")
    width = layer_in.shape[1]
    units = width // tensors
    states = decay_rate.shape[0]
    count_all = float(layer_in.shape[0] * tensors * lax.axis_size("fsdp") * width)
    highest = lax.Precision.HIGHEST
    w_in_re, w_in_im, w_out_re, w_out_im, w_glu, gain, norm_offset, skip_all, bias_all = (
        lax.all_gather(in_re, "fsdp", axis=1, tiled=True),
        lax.all_gather(in_im, "fsdp", axis=1, tiled=True),
        lax.all_gather(out_re, "fsdp", axis=1, tiled=True),
        lax.all_gather(out_im, "fsdp", axis=1, tiled=True),
        lax.all_gather(glu_weight, "fsdp", axis=1, tiled=True),
        lax.all_gather(ln_scale, "fsdp", axis=0, tiled=True),
        lax.all_gather(ln_bias, "fsdp", axis=0, tiled=True),
        lax.all_gather(skip, "fsdp", axis=0, tiled=True),
        lax.all_gather(glu_bias, "fsdp", axis=0, tiled=True),
    )
    resid = layer_in.astype(jnp.float32)
    centered_input = resid - jnp.mean(resid, axis=1, keepdims=True)
    inverse_deviation = lax.rsqrt(
        jnp.mean(centered_input * centered_input, axis=1, keepdims=True) + 1e-05
    )
    standardized_input = centered_input * inverse_deviation
    gain_float = gain.astype(jnp.float32)
    normalized_rows = (standardized_input * gain_float + norm_offset.astype(jnp.float32)).astype(
        jnp.bfloat16
    )
    normed_all = lax.all_gather(normalized_rows, "tensor", axis=0, tiled=True)
    rows_all = normed_all.shape[0]
    abar_re, abar_im, coef_re, coef_im = discretize(decay_rate, lam_im, log_dt)
    step_size = jnp.exp(log_dt)
    log_mag = -decay_rate * step_size
    angle = lam_im * step_size
    b_cat = jnp.concatenate([w_in_re, w_in_im], axis=0)
    proj = jnp.einsum("qh,rh->qr", b_cat, normed_all, preferred_element_type=jnp.float32)
    proj_re = proj[:states]
    proj_im = proj[states:]
    drive_re = coef_re[:, None] * proj_re - coef_im[:, None] * proj_im
    drive_im = coef_re[:, None] * proj_im + coef_im[:, None] * proj_re
    offsets = jnp.cumsum(seq_lengths) - seq_lengths
    positions = fsdp_pos * rows_all + jnp.arange(rows_all, dtype=jnp.int32)
    starts = jnp.any(positions[:, None] == offsets[None, :], axis=1)
    keep = jnp.where(starts, 0.0, 1.0).astype(jnp.float32)[None, :]
    segment = jnp.cumsum(starts.astype(jnp.int32))
    block_len = min(128, rows_all)
    blocks = rows_all // block_len
    index_f = jnp.arange(block_len, dtype=jnp.float32)
    distance = index_f[:, None] - index_f[None, :]
    lower = distance >= 0.0
    kern_re, kern_im = powers(log_mag, angle, jnp.maximum(distance, 0.0))
    seg_blocks = segment.reshape(blocks, block_len)
    same = jnp.where(
        (seg_blocks[:, :, None] == seg_blocks[:, None, :]) & lower[None], 1.0, 0.0
    ).astype(jnp.float32)
    masked_re = kern_re[:, None] * same[None]
    masked_im = kern_im[:, None] * same[None]

    def within(left, right):
        return jnp.einsum("qbts,qbs->qbt", left, right, precision=highest)

    def across(left, right):
        return jnp.einsum("qbst,qbs->qbt", left, right, precision=highest)

    blk_dre = drive_re.reshape(states, blocks, block_len)
    blk_dim = drive_im.reshape(states, blocks, block_len)
    intra_re = within(masked_re, blk_dre) - within(masked_im, blk_dim)
    intra_im = within(masked_re, blk_dim) + within(masked_im, blk_dre)
    step_re, step_im = powers(log_mag, angle, index_f + 1.0)
    done_re = []
    done_im = []
    for blk in range(blocks):
        cur_re = intra_re[:, blk]
        cur_im = intra_im[:, blk]
        if blk > 0:
            linked = jnp.where(seg_blocks[blk] == seg_blocks[blk - 1, -1], 1.0, 0.0).astype(
                jnp.float32
            )[None, :]
            prior_re = done_re[-1][:, -1:]
            prior_im = done_im[-1][:, -1:]
            cur_re = cur_re + linked * (step_re * prior_re - step_im * prior_im)
            cur_im = cur_im + linked * (step_re * prior_im + step_im * prior_re)
        done_re.append(cur_re)
        done_im.append(cur_im)
    loc_re = jnp.stack(done_re, axis=1).reshape(states, rows_all)
    loc_im = jnp.stack(done_im, axis=1).reshape(states, rows_all)
    whole_f = jnp.arange(rows_all, dtype=jnp.float32)
    entry_re, entry_im = powers(log_mag, angle, whole_f + 1.0)
    open_head = jnp.where(segment == 0, 1.0, 0.0).astype(jnp.float32)[None, :]
    entry_re = entry_re * open_head
    entry_im = entry_im * open_head
    ones_vec = jnp.ones((states,), jnp.float32)
    zero_vec = jnp.zeros((states,), jnp.float32)
    carry = entering(
        (entry_re[:, -1], entry_im[:, -1], loc_re[:, -1], loc_im[:, -1]),
        "fsdp",
        combine,
        (ones_vec, zero_vec, zero_vec, zero_vec),
        False,
    )
    enter_re = carry[2][:, None]
    enter_im = carry[3][:, None]
    state_re = loc_re + entry_re * enter_re - entry_im * enter_im
    state_im = loc_im + entry_re * enter_im + entry_im * enter_re
    s_cat = jnp.concatenate([state_re, state_im], axis=0).astype(jnp.bfloat16)
    c_cat = jnp.concatenate([w_out_re, -w_out_im], axis=0)
    readout = 2.0 * jnp.einsum("qr,qh->rh", s_cat, c_cat, preferred_element_type=jnp.float32)
    readout_rows = lax.psum_scatter(readout, "tensor", scatter_dimension=0, tiled=True)
    skip_f = skip_all.astype(jnp.float32)
    normed_f = normalized_rows.astype(jnp.float32)
    mixed = readout_rows + skip_f * normed_f
    act = jax.nn.gelu(mixed, approximate=False).astype(jnp.bfloat16)
    act_all = lax.all_gather(act, "tensor", axis=0, tiled=True)
    w_own = lax.dynamic_slice_in_dim(w_glu, tens_pos * units, units, 0)
    bias_own = lax.dynamic_slice_in_dim(bias_all, tens_pos * units, units, 0).astype(jnp.float32)
    logit = jnp.einsum("rh,kh->rk", act_all, w_own, preferred_element_type=jnp.float32) + bias_own
    gate = jax.nn.sigmoid(logit)
    act_own = lax.dynamic_slice_in_dim(act_all, tens_pos * units, units, 1).astype(jnp.float32)
    branch = (act_own * gate).astype(jnp.bfloat16)
    branch_own = lax.all_to_all(branch, "tensor", split_axis=0, concat_axis=1, tiled=True).astype(
        jnp.float32
    )
    layer_out = (resid + branch_own).astype(jnp.bfloat16)
    grad_cols = lax.all_to_all(grad_out, "tensor", split_axis=1, concat_axis=0, tiled=True).astype(
        jnp.float32
    )
    dlogit = (grad_cols * act_own * gate * (1.0 - gate)).astype(jnp.bfloat16)
    d_bias = jnp.sum(dlogit.astype(jnp.float32), axis=0)
    d_glu = jnp.einsum("rk,rh->kh", dlogit, act_all, preferred_element_type=jnp.float32)
    back_all = jnp.einsum("rk,kh->rh", dlogit, w_own, preferred_element_type=jnp.float32)
    own_part = lax.dynamic_slice_in_dim(back_all, tens_pos * units, units, 1) + grad_cols * gate
    back_all = lax.dynamic_update_slice_in_dim(back_all, own_part, tens_pos * units, 1)
    d_act = lax.psum_scatter(back_all, "tensor", scatter_dimension=0, tiled=True)
    d_mixed = d_act * gelu_slope(mixed)
    d_skip = jnp.sum(d_mixed * normed_f, axis=0)
    dy_all = lax.all_gather(d_mixed.astype(jnp.bfloat16), "tensor", axis=0, tiled=True)
    d_state = 2.0 * jnp.einsum("rh,qh->qr", dy_all, c_cat, preferred_element_type=jnp.float32)
    d_c = 2.0 * jnp.einsum("qr,rh->qh", s_cat, dy_all, preferred_element_type=jnp.float32)
    blk_gre = d_state[:states].reshape(states, blocks, block_len)
    blk_gim = d_state[states:].reshape(states, blocks, block_len)
    back_re = across(masked_re, blk_gre) + across(masked_im, blk_gim)
    back_im = across(masked_re, blk_gim) - across(masked_im, blk_gre)
    next_re, next_im = powers(log_mag, angle, float(block_len) - index_f)
    later_blocks_re = [None] * blocks
    later_blocks_im = [None] * blocks
    for blk in range(blocks - 1, -1, -1):
        cur_re = back_re[:, blk]
        cur_im = back_im[:, blk]
        if blk < blocks - 1:
            linked = jnp.where(seg_blocks[blk] == seg_blocks[blk + 1, 0], 1.0, 0.0).astype(
                jnp.float32
            )[None, :]
            follow_re = later_blocks_re[blk + 1][:, :1]
            follow_im = later_blocks_im[blk + 1][:, :1]
            cur_re = cur_re + linked * (next_re * follow_re + next_im * follow_im)
            cur_im = cur_im + linked * (next_re * follow_im - next_im * follow_re)
        later_blocks_re[blk] = cur_re
        later_blocks_im[blk] = cur_im
    adj_loc_re = jnp.stack(later_blocks_re, axis=1).reshape(states, rows_all)
    adj_loc_im = jnp.stack(later_blocks_im, axis=1).reshape(states, rows_all)
    tail_re, tail_im = powers(log_mag, angle, float(rows_all - 1) - whole_f)
    open_tail = jnp.where(segment == segment[-1], 1.0, 0.0).astype(jnp.float32)[None, :]
    tail_re = tail_re * open_tail
    tail_im = tail_im * open_tail
    head_re = keep[0, 0] * abar_re
    head_im = -keep[0, 0] * abar_im
    mul_re, mul_im = complex_mul(head_re, head_im, tail_re[:, 0], -tail_im[:, 0])
    add_re, add_im = complex_mul(head_re, head_im, adj_loc_re[:, 0], adj_loc_im[:, 0])
    back_carry = entering(
        (mul_re, mul_im, add_re, add_im),
        "fsdp",
        combine,
        (ones_vec, zero_vec, zero_vec, zero_vec),
        True,
    )
    later_re = back_carry[2][:, None]
    later_im = back_carry[3][:, None]
    adj_re = adj_loc_re + tail_re * later_re + tail_im * later_im
    adj_im = adj_loc_im + tail_re * later_im - tail_im * later_re
    prev_re = jnp.concatenate([enter_re, state_re[:, :-1]], axis=1)
    prev_im = jnp.concatenate([enter_im, state_im[:, :-1]], axis=1)
    d_abar_re = jnp.sum(keep * (adj_re * prev_re + adj_im * prev_im), axis=1)
    d_abar_im = jnp.sum(keep * (adj_im * prev_re - adj_re * prev_im), axis=1)
    d_coef_re = jnp.sum(adj_re * proj_re + adj_im * proj_im, axis=1)
    d_coef_im = jnp.sum(adj_im * proj_re - adj_re * proj_im, axis=1)
    dv_re = coef_re[:, None] * adj_re + coef_im[:, None] * adj_im
    dv_im = coef_re[:, None] * adj_im - coef_im[:, None] * adj_re
    dv_cat = jnp.concatenate([dv_re, dv_im], axis=0).astype(jnp.bfloat16)
    d_b = jnp.einsum("qr,rh->qh", dv_cat, normed_all, preferred_element_type=jnp.float32)
    d_norm_all = jnp.einsum("qr,qh->rh", dv_cat, b_cat, preferred_element_type=jnp.float32)
    normalized_gradient = (
        lax.psum_scatter(
            d_norm_all.astype(jnp.bfloat16), "tensor", scatter_dimension=0, tiled=True
        ).astype(jnp.float32)
        + d_mixed * skip_f
    )
    unused, pull = jax.vjp(discretize, decay_rate, lam_im, log_dt)
    g_decay, g_lam, g_step = pull((d_abar_re, d_abar_im, d_coef_re, d_coef_im))
    standardized_gradient = normalized_gradient * gain_float
    scale_gradient = jnp.sum(normalized_gradient * standardized_input, axis=0)
    d_shift = jnp.sum(normalized_gradient, axis=0)
    grad_in = grad_out.astype(jnp.float32) + inverse_deviation * (
        standardized_gradient
        - jnp.mean(standardized_gradient, axis=1, keepdims=True)
        - standardized_input
        * jnp.mean(standardized_gradient * standardized_input, axis=1, keepdims=True)
    )
    grads_mat = (
        lax.psum_scatter(d_b[:states], "fsdp", scatter_dimension=1, tiled=True),
        lax.psum_scatter(d_b[states:], "fsdp", scatter_dimension=1, tiled=True),
        lax.psum_scatter(d_c[:states], "fsdp", scatter_dimension=1, tiled=True),
        lax.psum_scatter(-d_c[states:], "fsdp", scatter_dimension=1, tiled=True),
        lax.psum_scatter(d_glu, "fsdp", scatter_dimension=1, tiled=True),
        lax.psum_scatter(d_bias, "fsdp", scatter_dimension=0, tiled=True),
    )

    def padded(values):
        return lax.dynamic_update_slice_in_dim(
            jnp.zeros((states * tensors,), jnp.float32), values, tens_pos * states, 0
        )

    squares = jnp.stack([jnp.sum(resid * resid), jnp.sum(branch_own * branch_own)])
    grads_vec = lax.psum(
        (scale_gradient, d_shift, d_skip, padded(g_decay), padded(g_lam), padded(g_step), squares),
        ("fsdp", "tensor"),
    )
    rms = jnp.sqrt(grads_vec[6] / count_all)
    return (
        layer_out,
        grad_in,
        grads_vec[0],
        grads_vec[1],
        grads_vec[3],
        grads_vec[4],
        grads_vec[5],
        grads_mat[0],
        grads_mat[1],
        grads_mat[2],
        grads_mat[3],
        grads_vec[2],
        grads_mat[4],
        grads_mat[5],
        rms,
    )


def solution(mesh):
    placed = (
        P(("fsdp", "tensor"), None),
        P(("fsdp", "tensor"), None),
        P("fsdp"),
        P("fsdp"),
        P("tensor"),
        P("tensor"),
        P("tensor"),
        P("tensor", "fsdp"),
        P("tensor", "fsdp"),
        P("tensor", "fsdp"),
        P("tensor", "fsdp"),
        P("fsdp"),
        P(None, "fsdp"),
        P("fsdp"),
        P(),
    )
    return jax.shard_map(
        on_device,
        mesh=mesh,
        in_specs=placed,
        out_specs=(
            P(("fsdp", "tensor"), None),
            P(("fsdp", "tensor"), None),
            P(),
            P(),
            P(),
            P(),
            P(),
            P("tensor", "fsdp"),
            P("tensor", "fsdp"),
            P("tensor", "fsdp"),
            P("tensor", "fsdp"),
            P(),
            P("tensor", "fsdp"),
            P(("tensor", "fsdp")),
            P(),
        ),
        check_vma=False,
    )
```

profile of v0, /device:TPU:0, one launch (start us, length us, event | category | flops | bytes accessed | tf_op | source)
XLA Modules:
  0.0 996.6 jit_solution(12720486370407149213)
XLA Ops:
  16.4 23.7 %all-reduce.16 = (bf16[512]{0:T(512)(128)(2,1)S(1)}, bf16[512]{0:T(512)(128)(2,1)S(1)}, bf16[512]{0:T(512)(128)(2,1)}, bf16[512]{0:T(512)(128)(2,1)}) all-reduce(bf16[512]{0:T(512)(128)(2,1)S(1)} %dynamic-update-slice.1, bf16[512]{0:T(512)(128)(2,1)S(1)} %dynamic-update-slice, ...), channel_id=1, replica_groups=mesh['fsdp'=8,'tensor'=4] {'fsdp'}, use_global_device_ids=true, to_apply=%add.1 | all-reduce | flops 2048 | bytes 8192
  42.2 30.7 %all_gather.72 = bf16[96,512]{0,1:T(8,128)(2,1)S(1)} all-gather(bf16[96,64]{0,1:T(8,128)(2,1)} %param.26), channel_id=1, replica_groups=mesh['fsdp'=8,'tensor'=4] {'fsdp'}, dimensions={1}, use_global_device_ids=true | all-gather | bytes 110592 | tf_op jit(solution)/shard_map/all_gather | solution.py:88
  72.9 30.7 %all_gather.73 = bf16[96,512]{0,1:T(8,128)(2,1)S(1)} all-gather(bf16[96,64]{0,1:T(8,128)(2,1)} %param.27), channel_id=1, replica_groups=mesh['fsdp'=8,'tensor'=4] {'fsdp'}, dimensions={1}, use_global_device_ids=true | all-gather | bytes 110592 | tf_op jit(solution)/shard_map/all_gather | solution.py:89
  115.9 23.8 %fusion.44 = (f32[96,128,128]{2,1,0:T(8,128)S(1)}, f32[96,128,128]{2,1,0:T(8,128)S(1)}) fusion(f32[96]{0:T(128)S(1)} %get-tuple-element.555, f32[128,128]{1,0:T(8,128)S(1)} %fusion.115, f32[96]{0:T(128)S(1)} %get-tuple-element.553), kind=kLoop, calls=%fused_computation.62 | loop fusion | flops 6291456 | bytes 12649216 | tf_op jit(solution)/shard_map/mul | solution.py:59
  139.8 39.2 %fusion.24 = f32[96,4,1,128]{3,2,1,0:T(1,128)S(1)} fusion(f32[96,4,128,1]{2,3,1,0:T(1,128)S(1)} %bitcast.234, f32[4,128,128]{2,1,0:T(8,128)S(1)} %and_select_fusion, f32[96,128,128]{2,1,0:T(8,128)S(1)} %get-tuple-element.615), kind=kOutput, calls=%fused_computation.40 | convolution fusion | flops 81788928 | bytes 6946816 | tf_op jit(solution)/shard_map/qbts,qbs->qbt/dot_general | solution.py:139
  179.0 39.4 %fusion.18 = f32[96,4,1,128]{3,2,1,0:T(1,128)S(1)} fusion(f32[96,4,128,1]{2,3,1,0:T(1,128)S(1)} %bitcast.235, f32[96,128,128]{2,1,0:T(8,128)S(1)} %get-tuple-element.616, f32[4,128,128]{2,1,0:T(8,128)S(1)} %and_select_fusion), kind=kOutput, calls=%fused_computation.34 | convolution fusion | flops 81788928 | bytes 6946816 | tf_op jit(solution)/shard_map/qbts,qbs->qbt/dot_general | solution.py:139
  218.4 39.6 %fusion.26 = f32[96,4,1,128]{3,2,1,0:T(1,128)S(1)} fusion(f32[96,4,128,1]{2,3,1,0:T(1,128)S(1)} %bitcast.232, f32[4,128,128]{2,1,0:T(8,128)S(1)} %and_select_fusion, f32[96,128,128]{2,1,0:T(8,128)S(1)} %get-tuple-element.615), kind=kOutput, calls=%fused_computation.42 | convolution fusion | flops 81788928 | bytes 6946816 | tf_op jit(solution)/shard_map/qbts,qbs->qbt/dot_general | solution.py:139
  258.0 39.4 %fusion.16 = f32[96,4,1,128]{3,2,1,0:T(1,128)S(1)} fusion(f32[96,4,128,1]{2,3,1,0:T(1,128)S(1)} %bitcast.233, f32[96,128,128]{2,1,0:T(8,128)S(1)} %get-tuple-element.616, f32[4,128,128]{2,1,0:T(8,128)S(1)} %and_select_fusion), kind=kOutput, calls=%fused_computation.32 | convolution fusion | flops 81788928 | bytes 6946816 | tf_op jit(solution)/shard_map/qbts,qbs->qbt/dot_general | solution.py:139
  304.8 30.5 %all_gather.81 = bf16[96,512]{0,1:T(8,128)(2,1)S(1)} all-gather(bf16[96,64]{0,1:T(8,128)(2,1)S(1)} %copy-done.48), channel_id=1, replica_groups=mesh['fsdp'=8,'tensor'=4] {'fsdp'}, dimensions={1}, use_global_device_ids=true | all-gather | bytes 110592 | tf_op jit(solution)/shard_map/all_gather | solution.py:90
  335.4 30.8 %all_gather.82 = bf16[96,512]{0,1:T(8,128)(2,1)S(1)} all-gather(bf16[96,64]{0,1:T(8,128)(2,1)S(1)} %copy-done.49), channel_id=1, replica_groups=mesh['fsdp'=8,'tensor'=4] {'fsdp'}, dimensions={1}, use_global_device_ids=true | all-gather | bytes 110592 | tf_op jit(solution)/shard_map/all_gather | solution.py:91
  371.8 33.0 %all-reduce.15 = (f32[768]{0:T(1024)S(1)}, f32[768]{0:T(1024)S(1)}, f32[768]{0:T(1024)S(1)}, f32[768]{0:T(1024)S(1)}) all-reduce(f32[768]{0:T(1024)S(1)} %dynamic-update-slice.2, f32[768]{0:T(1024)S(1)} %dynamic-update-slice.3, f32[768]{0:T(1024)S(1)} %dynamic-update-slice.4, ...), channel_id=2, replica_groups=mesh['fsdp'=8,'tensor'=4] {'fsdp'}, use_global_device_ids=true, to_apply=%add.2 | all-reduce | flops 3072 | bytes 24576
  414.8 31.3 %all_gather.85 = bf16[512,512]{0,1:T(8,128)(2,1)S(1)} all-gather(bf16[512,64]{0,1:T(8,128)(2,1)S(1)} %copy-done.23), channel_id=1, replica_groups=mesh['fsdp'=8,'tensor'=4] {'fsdp'}, dimensions={1}, use_global_device_ids=true | all-gather | bytes 589824 | tf_op jit(solution)/shard_map/all_gather | solution.py:92
  464.5 15.9 %reduce-scatter.19.cloned.1.call-done = f32[128,512]{1,0:T(8,128)} async-done(((f32[512,512]{1,0:T(8,128)}), f32[128,512]{1,0:T(8,128)}) %reduce-scatter.19.cloned.1.call-update) | async-done | bytes 262160 | tf_op jit(solution)/shard_map/reduce_scatter | solution.py:212
  492.4 24.8 %fusion.12 = f32[96,4,1,128]{3,2,1,0:T(1,128)} fusion(f32[96,4,128,1]{2,3,1,0:T(1,128)} %bitcast.238, f32[96,128,128]{2,1,0:T(8,128)} %copy-done.1, f32[4,128,128]{2,1,0:T(8,128)} %copy-done.17), kind=kOutput, calls=%fused_computation.28 | convolution fusion | flops 81788928 | bytes 6946816 | tf_op jit(solution)/shard_map/qbst,qbs->qbt/dot_general | solution.py:142
  517.2 23.2 %fusion.22 = f32[96,4,1,128]{3,2,1,0:T(1,128)} fusion(f32[96,4,128,1]{2,3,1,0:T(1,128)S(1)} %bitcast.239, f32[4,128,128]{2,1,0:T(8,128)S(1)} %copy-done.18, f32[96,128,128]{2,1,0:T(8,128)S(1)} %bitcast.221), kind=kOutput, calls=%fused_computation.38 | convolution fusion | flops 81788928 | bytes 6946816 | tf_op jit(solution)/shard_map/qbst,qbs->qbt/dot_general | solution.py:142
  541.4 25.6 %fusion.20 = f32[96,4,1,128]{3,2,1,0:T(1,128)} fusion(f32[96,4,128,1]{2,3,1,0:T(1,128)S(1)} %bitcast.236, f32[4,128,128]{2,1,0:T(8,128)} %copy-done.17, f32[96,128,128]{2,1,0:T(8,128)} %copy-done.2), kind=kOutput, calls=%fused_computation.36 | convolution fusion | flops 81788928 | bytes 6946816 | tf_op jit(solution)/shard_map/qbst,qbs->qbt/dot_general | solution.py:142
  567.1 25.4 %fusion.14 = f32[96,4,1,128]{3,2,1,0:T(1,128)} fusion(f32[96,4,128,1]{2,3,1,0:T(1,128)S(1)} %bitcast.237, f32[96,128,128]{2,1,0:T(8,128)} %copy-done.1, f32[4,128,128]{2,1,0:T(8,128)S(1)} %copy-done.19), kind=kOutput, calls=%fused_computation.30 | convolution fusion | flops 81788928 | bytes 6946816 | tf_op jit(solution)/shard_map/qbst,qbs->qbt/dot_general | solution.py:142
  603.7 37.7 %all-reduce.14 = (f32[768]{0:T(1024)S(1)}, f32[768]{0:T(1024)S(1)}, f32[768]{0:T(1024)S(1)}, f32[768]{0:T(1024)S(1)}, f32[128]{0:T(128)S(1)}) all-reduce(f32[768]{0:T(1024)S(1)} %subtract_dynamic-update-slice_fusion.1, f32[768]{0:T(1024)S(1)} %add_dynamic-update-slice_fusion.1, ...), channel_id=6, replica_groups=mesh['fsdp'=8,'tensor'=4] {'fsdp'}, use_global_device_ids=true, to_apply=%add.8 | all-reduce | flops 3200 | bytes 25600
  669.4 39.6 %all-reduce.13 = (f32[512]{0:T(512)}, f32[512]{0:T(512)}, f32[384]{0:T(512)}, f32[384]{0:T(512)}, f32[384]{0:T(512)}, /*index=5*/f32[512]{0:T(512)}, f32[2]{0:T(128)S(1)}) all-reduce(f32[512]{0:T(512)S(1)} %get-tuple-element.476, f32[512]{0:T(512)S(1)} %get-tuple-element.479, ...), channel_id=1, replica_groups=mesh['fsdp'=8,'tensor'=4] {'fsdp','tensor'}, use_global_device_ids=true, to_apply=%region_16.17 | all-reduce | flops 2690 | bytes 21520 | tf_op jit(solution)/shard_map/psum | solution.py:302
  710.4 21.2 %reduce-scatter.23.cloned.1.call-done = f32[128,64]{0,1:T(8,128)} async-done(((f32[128,512]{0,1:T(8,128)}), f32[128,64]{0,1:T(8,128)}) %reduce-scatter.23.cloned.1.call-update) | async-done | bytes 32784 | tf_op jit(solution)/shard_map/reduce_scatter | solution.py:292
  731.7 64.5 %reduce-scatter.31.cloned.1.call-done = f32[64,96]{1,0:T(8,128)} async-done(((f32[512,96]{1,0:T(8,128)}), f32[64,96]{1,0:T(8,128)}) %reduce-scatter.31.cloned.1.call-update) | async-done | bytes 24592
  796.1 64.5 %reduce-scatter.27.cloned.1.call-done = f32[64,96]{1,0:T(8,128)} async-done(((f32[512,96]{1,0:T(8,128)}), f32[64,96]{1,0:T(8,128)}) %reduce-scatter.27.cloned.1.call-update) | async-done | bytes 24592
  860.6 64.5 %reduce-scatter.25.cloned.1.call-done = f32[64,96]{1,0:T(8,128)} async-done(((f32[512,96]{1,0:T(8,128)}), f32[64,96]{1,0:T(8,128)}) %reduce-scatter.25.cloned.1.call-update) | async-done | bytes 24592
  925.1 64.5 %reduce-scatter.29.cloned.1.call-done = f32[64,96]{1,0:T(8,128)} async-done(((f32[512,96]{1,0:T(8,128)}), f32[64,96]{1,0:T(8,128)}) %reduce-scatter.29.cloned.1.call-update) | async-done | bytes 24592
  (361 shorter events, 115.1 us)
Async XLA Ops:
  7.2 438.9 %reduce-scatter.17.cloned.1.call-start = ((), (), s32[]{:S(2)}) async-start(), calls=%async_computation.10 | async-start | bytes 1310720 | tf_op jit(solution)/shard_map/reduce_scatter | solution.py:187
  7.3 360.0 %copy-start.72 = (f32[128]{0:T(128)}, f32[128]{0:T(128)S(1)}, u32[]{:S(2)}) copy-start(f32[128]{0:T(128)S(1)} %get-tuple-element.653) | copy-start | bytes 1540
  7.3 132.4 %copy-start.39 = (f32[512]{0:T(512)}, f32[512]{0:T(512)S(1)}, u32[]{:S(2)}) copy-start(f32[512]{0:T(512)S(1)} %iota_add_fusion) | copy-start | bytes 6148
  9.9 129.8 %copy-start.44 = (f32[128]{0:T(128)}, f32[128]{0:T(128)S(1)}, u32[]{:S(2)}) copy-start(f32[128]{0:T(128)S(1)} %broadcast_multiply_fusion.3) | copy-start | bytes 1540
  11.0 101.1 %copy-start.55 = (f32[128]{0:T(128)}, f32[128]{0:T(128)S(1)}, u32[]{:S(2)}) copy-start(f32[128]{0:T(128)S(1)} %add_rsqrt_fusion) | copy-start | bytes 1540
  103.8 154.2 %copy-start.17 = (f32[4,128,128]{2,1,0:T(8,128)}, f32[4,128,128]{2,1,0:T(8,128)S(1)}, u32[]{:S(2)}) copy-start(f32[4,128,128]{2,1,0:T(8,128)S(1)} %and_select_fusion) | copy-start | bytes 786436
  139.8 118.2 %copy-start.1 = (f32[96,128,128]{2,1,0:T(8,128)}, f32[96,128,128]{2,1,0:T(8,128)S(1)}, u32[]{:S(2)}) copy-start(f32[96,128,128]{2,1,0:T(8,128)S(1)} %get-tuple-element.616) | copy-start | bytes 18874372
  297.4 108.5 %copy-start.40 = (f32[512]{0:T(512)S(1)}, f32[512]{0:T(512)}, u32[]{:S(2)}) copy-start(f32[512]{0:T(512)} %copy-done.39) | copy-start | bytes 6148
  297.4 108.5 %copy-start.42 = (f32[512]{0:T(512)S(1)}, f32[512]{0:T(512)}, u32[]{:S(2)}) copy-start(f32[512]{0:T(512)} %copy-done.41) | copy-start | bytes 6148
  297.4 113.2 %copy-start.15 = (bf16[128,512]{1,0:T(8,128)(2,1)S(1)}, bf16[128,512]{1,0:T(8,128)(2,1)}, u32[]{:S(2)}) copy-start(bf16[128,512]{1,0:T(8,128)(2,1)} %param.20) | copy-start | bytes 393220
  304.8 106.5 %copy-start.35 = (f32[512]{0:T(512)}, f32[512]{0:T(512)S(1)}, u32[]{:S(2)}) copy-start(f32[512]{0:T(512)S(1)} %get-tuple-element.655) | copy-start | bytes 6148
  304.8 106.5 %copy-start.37 = (f32[512]{0:T(512)}, f32[512]{0:T(512)S(1)}, u32[]{:S(2)}) copy-start(f32[512]{0:T(512)S(1)} %get-tuple-element.656) | copy-start | bytes 6148
  370.6 109.8 %copy-start.28 = (f32[512]{0:T(512)S(1)}, f32[512]{0:T(512)}, u32[]{:S(2)}) copy-start(f32[512]{0:T(512)} %copy-done.26) | copy-start | bytes 6148
  370.7 109.8 %copy-start.46 = (f32[128]{0:T(128)S(1)}, f32[128]{0:T(128)}, u32[]{:S(2)}) copy-start(f32[128]{0:T(128)} %copy-done.44) | copy-start | bytes 1540
  370.7 109.8 %copy-start.57 = (f32[128]{0:T(128)S(1)}, f32[128]{0:T(128)}, u32[]{:S(2)}) copy-start(f32[128]{0:T(128)} %copy-done.55) | copy-start | bytes 1540
  411.3 44.2 %all-to-all-start.1 = ((bf16[128,4,128]{2,0,1:T(8,128)(2,1)}), bf16[128,4,128]{2,0,1:T(8,128)(2,1)S(1)}, u32[]{:S(2)}, u32[]{:S(2)}) async-start(bf16[128,4,128]{2,0,1:T(8,128)(2,1)} %copy_bitcast_fusion), calls=%async_computation.2 | async-start | bytes 262144 | tf_op jit(solution)/shard_map/all_to_all | solution.py:203
  414.6 65.8 %reduce-scatter.19.cloned.1.call-start = ((), (), s32[]{:S(2)}) async-start(), calls=%async_computation.11 | async-start | bytes 1310720 | tf_op jit(solution)/shard_map/reduce_scatter | solution.py:212
  458.7 207.5 %reduce-scatter.21.cloned.1.call-start = ((), (), s32[]{:S(2)}) async-start(), calls=%async_computation.12 | async-start | bytes 655360 | tf_op jit(solution)/shard_map/reduce_scatter | solution.py:271
  647.7 83.9 %reduce-scatter.23.cloned.1.call-start = ((), (), s32[]{:S(2)}) async-start(), calls=%async_computation.13 | async-start | bytes 294912 | tf_op jit(solution)/shard_map/reduce_scatter | solution.py:292
  649.8 146.3 %reduce-scatter.31.cloned.1.call-start = ((), (), s32[]{:S(2)}) async-start(), calls=%async_computation.17 | async-start | bytes 294912
  651.9 208.6 %reduce-scatter.27.cloned.1.call-start = ((), (), s32[]{:S(2)}) async-start(), calls=%async_computation.15 | async-start | bytes 294912
  653.1 7.9 all-to-all-start
  656.5 268.6 %reduce-scatter.25.cloned.1.call-start = ((), (), s32[]{:S(2)}) async-start(), calls=%async_computation.14 | async-start | bytes 294912
  664.1 325.5 %reduce-scatter.29.cloned.1.call-start = ((), (), s32[]{:S(2)}) async-start(), calls=%async_computation.16 | async-start | bytes 294912
  (63 other events, 3025.0 us)
Sparse Core Ops, SparseCore 0:
  410.7 21.4 reduce-scatter.16
  458.9 21.5 reduce-scatter.18
  647.8 18.3 reduce-scatter.20
  670.4 61.2 reduce-scatter.22
  735.8 60.2 reduce-scatter.30
  800.2 60.2 reduce-scatter.26
  864.8 60.1 reduce-scatter.24
  929.3 60.2 reduce-scatter.28
where the time goes:
time: 1000 us; the launch traced here: 997 us
  blocking collectives  310 us (31%)
  waiting for transfers between devices  301 us (30%)
  matrix products  266 us (27%)
  other arithmetic  66.1 us (7%)
  local copies, waits for them, and re-layouts  27.7 us (3%)
  between operations  18.3 us (2%)
    unnamed x12, waiting for transfers between devices  258 us
    dot_general x4, matrix products, within(): return jnp.einsum('qbts,qbs->qbt', left, right, precision=highest)  158 us
    dot_general x4, matrix products, across(): return jnp.einsum('qbst,qbs->qbt', left, right, precision=highest)  99 us
    unnamed x3, blocking collectives  94.3 us
    psum x1, blocking collectives, on_device(): lax.psum((scale_gradient, d_shift, d_skip, padded(g_decay), padded(g_lam)...  39.6 us
    all_gather x1, blocking collectives, on_device(): lax.all_gather(glu_weight, 'fsdp', axis=1, tiled=True)  31.3 us
    all_gather x1, blocking collectives, on_device(): lax.all_gather(out_im, 'fsdp', axis=1, tiled=True)  30.8 us
    all_gather x1, blocking collectives, on_device(): lax.all_gather(in_im, 'fsdp', axis=1, tiled=True)  30.7 us
  transfers between devices with their start and end apart: 10, of which 8 were waited for; matrix products, arithmetic and copies ran while one was open for 2% of the time, Pallas kernels for 0%

commit v1 on v0

v1 whole, which is shorter than its diff:
```python
import functools

import jax
import jax.numpy as jnp
from jax import lax
from jax.experimental import pallas as pl
from jax.experimental.pallas import tpu as pltpu
from jax.sharding import Mesh
from jax.sharding import PartitionSpec as P

F32 = jnp.float32
BF16 = jnp.bfloat16
AXES = ("fsdp", "ty", "tc")
VM = pl.BlockSpec(memory_space=pltpu.VMEM)
SM = pl.BlockSpec(memory_space=pltpu.SMEM)

GROUPS = 8


def sds(shape, dtype=F32):
    return jax.ShapeDtypeStruct(shape, dtype)


def low_half(shape):
    return lax.broadcasted_iota(jnp.int32, shape, len(shape) - 1) < 64


def lane_iota(shape):
    return lax.broadcasted_iota(jnp.int32, shape, len(shape) - 1)


def dot(a, b, dims):
    return lax.dot_general(a, b, (dims, ((), ())), preferred_element_type=F32)


NT = ((1,), (1,))
NN = ((1,), (0,))
TN = ((0,), (0,))


def spread(x):
    lo = low_half((x.shape[0], 128))
    upper, lower = [], []
    for c in range(x.shape[1] // 128):
        xc = x[:, 128 * c : 128 * c + 128]
        turned = pltpu.roll(xc, 64, 1)
        upper += [jnp.where(lo, xc, 0.0).astype(BF16), jnp.where(lo, turned, 0.0).astype(BF16)]
        lower += [jnp.where(lo, 0.0, turned).astype(BF16), jnp.where(lo, 0.0, xc).astype(BF16)]
    return jnp.concatenate(
        [jnp.concatenate(upper, axis=1), jnp.concatenate(lower, axis=1)], axis=0
    )


def folded(pq):
    rows = pq.shape[0] // 2
    lo = low_half((rows, 128))
    out = []
    for c in range(pq.shape[1] // 256):
        p0, p1 = pq[:rows, 256 * c : 256 * c + 128], pq[:rows, 256 * c + 128 : 256 * c + 256]
        q0, q1 = pq[rows:, 256 * c : 256 * c + 128], pq[rows:, 256 * c + 128 : 256 * c + 256]
        out.append(jnp.where(lo, p0 + pltpu.roll(q0, 64, 1), pltpu.roll(p1, 64, 1) + q1))
    return jnp.concatenate(out, axis=1)


def weights(refs, start, count):
    return jnp.concatenate(
        [
            jnp.concatenate([ref[f, start : start + count, :] for ref in refs], axis=0)
            for f in range(GROUPS)
        ],
        axis=1,
    )


def feature_rows(ref, row):
    lo = low_half((8, 128))
    first, second = [], []
    for c in range(GROUPS // 2):
        a = jnp.broadcast_to(ref[2 * c, row : row + 1, :].astype(F32), (8, 128))
        b = jnp.broadcast_to(ref[2 * c + 1, row : row + 1, :].astype(F32), (8, 128))
        first.append(jnp.where(lo, a, pltpu.roll(b, 64, 1)))
        second.append(jnp.where(lo, pltpu.roll(a, 64, 1), b))
    return jnp.concatenate(first, axis=1)[:1], jnp.concatenate(second, axis=1)[:1]


def rows_to_lanes(rows):
    turned = [rows, pltpu.roll(rows, 96, 1), pltpu.roll(rows, 64, 1), pltpu.roll(rows, 32, 1)]
    lane = lane_iota((1, 128))
    return [
        jnp.where(lane < 96, rows[0:1], turned[1][1:2]),
        jnp.where(lane < 64, turned[1][1:2], turned[2][2:3]),
        jnp.where(lane < 32, turned[2][2:3], turned[3][3:4]),
    ]


def lanes_to_rows(chunks):
    wide = [jnp.broadcast_to(chunk, (8, 128)) for chunk in chunks]
    lane = lane_iota((8, 128))
    r1 = jnp.where(lane < 32, pltpu.roll(wide[0], 32, 1), pltpu.roll(wide[1], 32, 1))
    r2 = jnp.where(lane < 64, pltpu.roll(wide[1], 64, 1), pltpu.roll(wide[2], 64, 1))
    r3 = pltpu.roll(wide[2], 96, 1)
    return [jnp.where(lane < 96, r, 0.0)[:1] for r in (wide[0], r1, r2, r3)]


def cmul(a, b):
    return a[0] * b[0] - a[1] * b[1], a[0] * b[1] + a[1] * b[0]


def tensor_pos():
    return lax.axis_index("ty") * 2 + lax.axis_index("tc")


def block_pos():
    return lax.axis_index("fsdp") * 4 + tensor_pos()


def offsets_of(seq_ref):
    out, total = [], 0
    for n in range(seq_ref.shape[0]):
        out.append(total)
        total = total + seq_ref[n]
    return out


def starts_until(offsets, base, rows):
    at = lax.broadcasted_iota(jnp.int32, (rows, 128), 0) + base
    count = jnp.zeros((rows, 128), F32)
    for off in offsets:
        count = count + jnp.where((at >= off) & (off >= base), 1.0, 0.0)
    return count


def no_start(offsets, base, rows):
    hit = False
    for off in offsets:
        hit = hit | ((off >= base) & (off < base + rows))
    return jnp.where(hit, 0.0, 1.0)


def expm1(x):
    series = x * (1 + x / 2 * (1 + x / 3 * (1 + x / 4 * (1 + x / 5 * (1 + x / 6 * (1 + x / 7))))))
    return jnp.where(jnp.abs(x) < 0.25, series, jnp.exp(x) - 1.0)


def discretize(decay_rate, lam_im, log_dt):
    step_size = jnp.exp(log_dt)
    lam_re = -decay_rate
    magnitude = jnp.exp(lam_re * step_size)
    phase = lam_im * step_size
    abar_re = magnitude * jnp.cos(phase)
    abar_im = magnitude * jnp.sin(phase)
    half_sin = jnp.sin(0.5 * phase)
    less_re = expm1(lam_re * step_size) * jnp.cos(phase) - 2.0 * half_sin * half_sin
    denom = lam_re * lam_re + lam_im * lam_im
    coef_re = (less_re * lam_re + abar_im * lam_im) / denom
    coef_im = (abar_im * lam_re - less_re * lam_im) / denom
    return abar_re, abar_im, coef_re, coef_im, step_size


def pack_kernel(re_ref, im_ref, ore_ref, oim_ref, glu_ref, sc_ref, lb_ref, sk_ref, gb_ref, de_ref, la_ref, dt_ref, out_ref):
    tens = tensor_pos()
    first = pl.multiple_of(tens * 64, 64)
    pieces = [
        jnp.concatenate([re_ref[...], im_ref[...]], axis=1),
        jnp.concatenate([ore_ref[...], oim_ref[...]], axis=1),
        jnp.concatenate([glu_ref[pl.ds(first, 64), :], glu_ref[pl.ds(first + 256, 64), :]], axis=1),
    ]
    vec = [
        jnp.concatenate([sc_ref[...], lb_ref[...]], axis=1).astype(F32),
        jnp.concatenate([sk_ref[...], gb_ref[...]], axis=1).astype(F32),
    ]
    for ref in (de_ref, la_ref, dt_ref):
        value = jnp.concatenate([ref[...], jnp.zeros((1, 32), F32)], axis=1)
        for _ in range(3):
            part = value.astype(BF16).astype(F32)
            value = value - part
            vec.append(part)
    vec.append(jnp.zeros((16 - len(vec), 128), F32))
    pieces.append(jnp.concatenate(vec, axis=0).astype(BF16))
    packet = jnp.concatenate(pieces, axis=0)
    for f in range(GROUPS):
        out_ref[f] = packet


def params_of(refs, vec_row):
    lane = lane_iota((8, 128))
    out = []
    for k, safe in enumerate((1.0, 0.0, 0.0)):
        rows = []
        for ref in refs:
            part = ref[0, vec_row : vec_row + 16, :].astype(F32)
            rows.append((part[2 + 3 * k : 3 + 3 * k] + part[3 + 3 * k : 4 + 3 * k]) + part[4 + 3 * k : 5 + 3 * k])
        value = jnp.concatenate(rows + [jnp.full((4, 128), safe, F32)], axis=0)
        out.append(jnp.where(lane < 96, value, safe))
    return out


def block_of(chunks_re, chunks_im, scratch, tens):
    for half, chunks in ((0, chunks_re), (4, chunks_im)):
        for i, row in enumerate(lanes_to_rows(chunks)):
            scratch[pl.ds(half + (tens ^ i), 1), :] = row


def chunks_from(scratch, half, tens):
    rows = jnp.concatenate([scratch[pl.ds(half + (tens ^ i), 1), :] for i in range(4)] + [jnp.zeros((4, 128), F32)], axis=0)
    return rows_to_lanes(rows)


VEC = 256


def first_kernel(blocks, x_ref, seq_ref, g0, g1, g2, g3, xhat_ref, inv_ref, normed_ref, v_ref, lane_ref, row_ref, send_ref, scratch):
    refs = (g0, g1, g2, g3)
    tens = tensor_pos()
    rows = x_ref.shape[0]
    width = x_ref.shape[1]
    x = x_ref[...].astype(F32)
    centered = x - jnp.sum(x, axis=1, keepdims=True) / width
    inverse = lax.rsqrt(jnp.sum(centered * centered, axis=1, keepdims=True) / width + 1e-05)
    xhat = centered * inverse
    xhat_ref[...] = xhat
    inv_ref[...] = jnp.broadcast_to(inverse, (rows, 128))
    scale, bias = feature_rows(g0, VEC)
    normed = (xhat * scale + bias).astype(BF16)
    normed_ref[...] = normed
    v_ref[...] = dot(spread(normed.astype(F32)), weights(refs, 0, 96), NT)

    decay, lam, log_dt = params_of(refs, VEC)
    abar_re, abar_im, coef_re, coef_im, step_size = discretize(decay, lam, log_dt)
    power = (abar_re, abar_im)
    per_row = [decay, lam, step_size, abar_re, abar_im, coef_re, coef_im]
    for _ in range(7):
        power = cmul(power, power)
    for half in (0, 1):
        for i in range(4):
            scratch[pl.ds(half * 4 + (tens ^ i), 1), :] = power[half][i : i + 1]
    for k, value in enumerate(per_row):
        row_ref[k] = value
    row_ref[len(per_row)] = scratch[...]
    abar = (rows_to_lanes(abar_re), rows_to_lanes(abar_im))
    coef = (rows_to_lanes(coef_re), rows_to_lanes(coef_im))
    for k, chunks in enumerate((*abar, *coef)):
        for c in range(3):
            lane_ref[k : k + 1, 128 * c : 128 * c + 128] = chunks[c]

    offsets = offsets_of(seq_ref)
    count = starts_until(offsets, block_pos() * rows, rows)
    open_tail = jnp.where(count == count[rows - 1 : rows], 1.0, 0.0)
    last = ([], [])
    for c in range(3):
        a = (abar[0][c], abar[1][c])
        eight, tail = eighth_powers(a, 7)
        b = (coef[0][c], coef[1][c])
        acc = (jnp.zeros((8, 128), F32), jnp.zeros((8, 128), F32))
        for blk in range(rows // 8):
            here = slice(8 * blk, 8 * blk + 8)
            v = (v_ref[here, 128 * c : 128 * c + 128], v_ref[rows + 8 * blk : rows + 8 * blk + 8, 128 * c : 128 * c + 128])
            drive = cmul(b, v)
            moved = cmul(eight, acc)
            acc = (moved[0] + drive[0] * open_tail[here], moved[1] + drive[1] * open_tail[here])
        total = cmul(tail, acc)
        last[0].append(jnp.sum(total[0], axis=0, keepdims=True))
        last[1].append(jnp.sum(total[1], axis=0, keepdims=True))
    block_of(last[0], last[1], scratch, tens)
    packet = scratch[...]
    for d in range(blocks):
        send_ref[d] = packet


def eighth_powers(a, top):
    sub = lax.broadcasted_iota(jnp.int32, (8, 128), 0)
    exponent = (7 - sub) if top == 7 else sub + 1
    a = (jnp.broadcast_to(a[0], (8, 128)), jnp.broadcast_to(a[1], (8, 128)))
    tile = (jnp.ones((8, 128), F32), jnp.zeros((8, 128), F32))
    for bit in range(4):
        if bit == 3:
            eight = a
        taken = (exponent & (1 << bit)) != 0
        more = cmul(tile, a)
        tile = (jnp.where(taken, more[0], tile[0]), jnp.where(taken, more[1], tile[1]))
        a = cmul(a, a)
    return eight, tile


def scan_chunk(value, a, count, reverse):
    rows = count.shape[0]
    at = lax.broadcasted_iota(jnp.int32, (rows, 128), 0)
    step = 1
    while step < rows:
        shift = rows - step if reverse else step
        other = pltpu.roll(count, shift, 0)
        inside = (at < rows - step) if reverse else (at >= step)
        linked = inside & (other == count)
        moved = (pltpu.roll(value[0], shift, 0), pltpu.roll(value[1], shift, 0))
        more = cmul(a, moved)
        value = (value[0] + jnp.where(linked, more[0], 0.0), value[1] + jnp.where(linked, more[1], 0.0))
        a = cmul(a, a)
        step *= 2
    return value


def carried(recv_ref, row_ref, offsets, rows, reverse, scratch, tens):
    blocks = recv_ref.shape[0]
    power = row_ref[7]
    pre, pim = power[0:4], power[4:8]
    if reverse:
        pim = -pim
    place = block_pos()

    def turn(k, state):
        j = blocks - 1 - k if reverse else k
        link = no_start(offsets, j * rows, rows)
        got = recv_ref[j]
        new = cmul((pre * link, pim * link), state)
        return new[0] + got[0:4], new[1] + got[4:8]

    zero = jnp.zeros((4, 128), F32)
    out = lax.fori_loop(0, blocks - 1 - place if reverse else place, turn, (zero, zero))
    scratch[0:4, :] = out[0]
    scratch[4:8, :] = out[1]
    return chunks_from(scratch, 0, tens), chunks_from(scratch, 4, tens)


def column_sum(value):
    return jnp.sum(value, axis=0, keepdims=True)


def second_kernel(
    blocks, recv_ref, seq_ref, x_ref, up_ref, normed_ref, v_ref, lane_ref, row_ref, g0, g1, g2, g3,
    out_ref, state_ref, dstate_ref, enter_ref, dmixed_ref, part_ref, keep_ref, away_ref, send_ref,
    scratch, gate_ref, dgate_ref,
):
    refs = (g0, g1, g2, g3)
    tens = tensor_pos()
    rows, width = x_ref.shape
    offsets = offsets_of(seq_ref)
    base = block_pos() * rows
    count = starts_until(offsets, base, rows)
    for i, ref in enumerate(refs):
        for f in range(GROUPS):
            gate_ref[f, tens ^ i] = ref[f, 192:256, :]
    enter = carried(recv_ref, row_ref, offsets, rows, False, scratch, tens)
    keep_first = no_start(offsets, base, 1)
    top = lax.broadcasted_iota(jnp.int32, (rows, 128), 0) == 0
    for c in range(3):
        lanes = slice(128 * c, 128 * c + 128)
        a = (lane_ref[0:1, lanes], lane_ref[1:2, lanes])
        b = (lane_ref[2:3, lanes], lane_ref[3:4, lanes])
        drive = cmul(b, (v_ref[:rows, lanes], v_ref[rows:, lanes]))
        came = cmul((a[0] * keep_first, a[1] * keep_first), (enter[0][c], enter[1][c]))
        drive = (drive[0] + jnp.where(top, came[0], 0.0), drive[1] + jnp.where(top, came[1], 0.0))
        state = scan_chunk(drive, a, count, False)
        state_ref[:rows, lanes] = state[0]
        state_ref[rows:, lanes] = state[1]
        enter_ref[0:1, lanes] = enter[0][c]
        enter_ref[1:2, lanes] = enter[1][c]
    twice = jnp.concatenate([state_ref[:rows].astype(BF16) * 2, state_ref[rows:].astype(BF16) * -2], axis=0)
    readout = weights(refs, 96, 96)
    skip, gate_bias = feature_rows(g0, VEC + 1)
    normed = normed_ref[...].astype(F32)
    mixed = folded(dot(twice, readout, NN)) + skip * normed
    cdf = 0.5 * (1.0 + lax.erf(mixed * 0.7071067811865476))
    act = (mixed * cdf).astype(BF16).astype(F32)
    spread_act = spread(act)
    w_gate = jnp.concatenate([gate_ref[f].reshape(256, 128) for f in range(GROUPS)], axis=1)
    logit = dot(spread_act, w_gate, NT)
    logit = jnp.concatenate([logit[:rows], logit[rows:]], axis=1) + gate_bias
    gate = 1.0 / (1.0 + jnp.exp(-logit))
    branch = (act * gate).astype(BF16).astype(F32)
    x = x_ref[...].astype(F32)
    out_ref[...] = (x + branch).astype(BF16)
    up = up_ref[...].astype(F32)
    dlogit = (up * act * gate * (1.0 - gate)).astype(BF16)
    halves = jnp.concatenate([dlogit[:, :256], dlogit[:, 256:]], axis=0)
    d_act = folded(dot(halves, w_gate, NN)) + up * gate
    slope = cdf + mixed * jnp.exp(-0.5 * mixed * mixed) * 0.3989422804014327
    d_mixed = d_act * slope
    dmixed_ref[...] = d_mixed
    dlogit_f = dlogit.astype(F32)
    squares_x, squares_b = x * x, branch * branch
    part = [column_sum(d_mixed * normed), column_sum(dlogit_f), column_sum(squares_x), column_sum(squares_b)]
    for k, value in enumerate(part):
        part_ref[k : k + 1, :] = value
    spread_dy = spread(d_mixed.astype(BF16).astype(F32))
    d_state = dot(spread_dy, readout, NT)
    dstate_ref[:rows] = d_state[:rows] * 2.0
    dstate_ref[rows:] = d_state[rows:] * -2.0
    head = jnp.where(count == 0.0, 1.0, 0.0)
    first = ([], [])
    for c in range(3):
        lanes = slice(128 * c, 128 * c + 128)
        a = (lane_ref[0:1, lanes], -lane_ref[1:2, lanes])
        eight, tail = eighth_powers(a, 0)
        acc = (jnp.zeros((8, 128), F32), jnp.zeros((8, 128), F32))
        for blk in range(rows // 8 - 1, -1, -1):
            here = slice(8 * blk, 8 * blk + 8)
            moved = cmul(eight, acc)
            acc = (
                moved[0] + dstate_ref[here, lanes] * head[here],
                moved[1] + dstate_ref[rows + 8 * blk : rows + 8 * blk + 8, lanes] * head[here],
            )
        total = cmul(tail, acc)
        first[0].append(column_sum(total[0]))
        first[1].append(column_sum(total[1]))
    block_of(first[0], first[1], scratch, tens)
    packet = scratch[...]
    for d in range(blocks):
        send_ref[d] = packet
    d_c = dot(twice, spread_dy, TN).astype(BF16)
    lo = low_half((rows, 128))
    first_units, last_units = [], []
    for c in range(2):
        left = dlogit_f[:, 256 * c : 256 * c + 128]
        right = dlogit_f[:, 256 * c + 128 : 256 * c + 256]
        first_units.append(jnp.where(lo, left, pltpu.roll(right, 64, 1)))
        last_units.append(jnp.where(lo, pltpu.roll(left, 64, 1), right))
    units = jnp.concatenate([jnp.concatenate(first_units, axis=1), jnp.concatenate(last_units, axis=1)], axis=0)
    d_gate = dot(units.astype(BF16), spread_act, TN).astype(BF16)
    for k in range(4):
        for f in range(GROUPS):
            dgate_ref[k, f] = d_gate[64 * k : 64 * k + 64, 128 * f : 128 * f + 128]
    for i in range(4):
        target = away_ref if i % 2 else keep_ref
        for f in range(GROUPS):
            target[i // 2, f, 0:96, :] = d_c[96 * i : 96 * i + 96, 128 * f : 128 * f + 128]
            target[i // 2, f, 96:160, :] = dgate_ref[tens ^ i, f]


def split_rows(value):
    upper = value.astype(BF16)
    return jnp.concatenate([upper, (value - upper.astype(F32)).astype(BF16)], axis=0)


def third_kernel(
    recv_ref, seq_ref, up_ref, normed_ref, xhat_ref, inv_ref, v_ref, lane_ref, row_ref, state_ref, dstate_ref, enter_ref, dmixed_ref,
    part_ref, g0, g1, g2, g3, gin_ref, keep_ref, away_ref, vec_ref, scratch, dv_ref,
):
    refs = (g0, g1, g2, g3)
    tens = tensor_pos()
    rows, width = up_ref.shape
    offsets = offsets_of(seq_ref)
    base = block_pos() * rows
    count = starts_until(offsets, base, rows)
    later = carried(recv_ref, row_ref, offsets, rows, True, scratch, tens)
    at = lax.broadcasted_iota(jnp.int32, (rows, 128), 0)
    before = jnp.where(at == 0, 0.0, pltpu.roll(count, 1, 0))
    keep = jnp.where(count == before, 1.0, 0.0)
    sums = ([], [], [], [])
    for c in range(3):
        lanes = slice(128 * c, 128 * c + 128)
        a = (lane_ref[0:1, lanes], -lane_ref[1:2, lanes])
        bottom = at == rows - 1
        start = (
            dstate_ref[:rows, lanes] + jnp.where(bottom, later[0][c], 0.0),
            dstate_ref[rows:, lanes] + jnp.where(bottom, later[1][c], 0.0),
        )
        adj = scan_chunk(start, a, count, True)
        prev = (
            jnp.where(at == 0, enter_ref[0:1, lanes], pltpu.roll(state_ref[:rows, lanes], 1, 0)) * keep,
            jnp.where(at == 0, enter_ref[1:2, lanes], pltpu.roll(state_ref[rows:, lanes], 1, 0)) * keep,
        )
        v = (v_ref[:rows, lanes], v_ref[rows:, lanes])
        sums[0].append(column_sum(adj[0] * prev[0] + adj[1] * prev[1]))
        sums[1].append(column_sum(adj[1] * prev[0] - adj[0] * prev[1]))
        sums[2].append(column_sum(adj[0] * v[0] + adj[1] * v[1]))
        sums[3].append(column_sum(adj[1] * v[0] - adj[0] * v[1]))
        dv = cmul((lane_ref[2:3, lanes], -lane_ref[3:4, lanes]), adj)
        dv_ref[:rows, lanes] = dv[0].astype(BF16)
        dv_ref[rows:, lanes] = dv[1].astype(BF16)
    dv = dv_ref[...]
    normed = normed_ref[...].astype(F32)
    d_b = dot(dv, spread(normed), TN).astype(BF16)
    for i in range(4):
        for f in range(GROUPS):
            block = d_b[96 * i : 96 * i + 96, 128 * f : 128 * f + 128]
            if i % 2:
                away_ref[(i // 2) * GROUPS + f] = block
            else:
                keep_ref[i // 2, f] = block
    skip, unused = feature_rows(g0, VEC + 1)
    scale, unused = feature_rows(g0, VEC)
    d_normed = folded(dot(dv, weights(refs, 0, 96), NN)) + dmixed_ref[...] * skip
    xhat = xhat_ref[...]
    d_xhat = d_normed * scale
    mean = jnp.sum(d_xhat, axis=1, keepdims=True) / width
    mean_hat = jnp.sum(d_xhat * xhat, axis=1, keepdims=True) / width
    gin_ref[...] = up_ref[...].astype(F32) + inv_ref[:, 0:1] * (d_xhat - mean - xhat * mean_hat)

    vector = [column_sum(d_normed * xhat), column_sum(d_normed), part_ref[0:1, :], part_ref[1:2, :]]
    for k, value in enumerate(vector):
        for c in range(4):
            vec_ref[4 * k + c : 4 * k + c + 1, :] = value[:, 128 * c : 128 * c + 128]
    g = [jnp.concatenate(lanes_to_rows(chunks) + [jnp.zeros((4, 128), F32)], axis=0) for chunks in sums]
    decay, lam, step, abar_re, abar_im, coef_re, coef_im = (row_ref[k] for k in range(7))
    d_abar, d_coef = (g[0], g[1]), (g[2], g[3])
    denom = decay * decay + lam * lam
    numer = (step * abar_re - coef_re, step * abar_im - coef_im)
    ratio = cmul(numer, (-decay / denom, -lam / denom))
    to_lam_a = cmul((step * abar_re, -step * abar_im), d_abar)
    to_lam_c = cmul((ratio[0], -ratio[1]), d_coef)
    g_decay = -(to_lam_a[0] + to_lam_c[0])
    g_lam = to_lam_a[1] + to_lam_c[1]
    slope = cmul((-decay, lam), (abar_re, abar_im))
    g_step = (slope[0] * d_abar[0] + slope[1] * d_abar[1] + abar_re * d_coef[0] + abar_im * d_coef[1]) * step
    for k, value in enumerate((g_decay, g_lam, g_step)):
        for i in range(4):
            vec_ref[pl.ds(16 + 4 * k + (tens ^ i), 1), :] = value[i : i + 1]
    for k in range(2):
        squares = part_ref[2 + k : 3 + k, :]
        total = squares[:, 0:128]
        for c in range(1, 4):
            total = total + squares[:, 128 * c : 128 * c + 128]
        vec_ref[28 + k : 29 + k, :] = total
    vec_ref[30:32, :] = jnp.zeros((2, 128), F32)
    away_ref[2 * GROUPS, 0:64, :] = split_rows(vec_ref[...])
    away_ref[2 * GROUPS, 64:96, :] = jnp.zeros((32, 128), BF16)


def added(a, b):
    return (a.astype(F32) + b.astype(F32)).astype(BF16)


def core_cw_kernel(keep_ref, got_ref, stay_ref, away_ref):
    for f in range(GROUPS):
        stay_ref[f] = added(keep_ref[0, f], got_ref[0, f])
        away_ref[f] = added(keep_ref[1, f], got_ref[1, f])


def joined(packet):
    return packet[0:32].astype(F32) + packet[32:64].astype(F32)


def core_b_kernel(keep_ref, vec_ref, got_ref, stay_ref, total_ref, away_ref):
    for f in range(GROUPS):
        stay_ref[f] = added(keep_ref[0, f], got_ref[f])
        away_ref[f] = added(keep_ref[1, f], got_ref[GROUPS + f])
    total = vec_ref[...] + joined(got_ref[2 * GROUPS, 0:64, :])
    total_ref[...] = total
    away_ref[GROUPS, 0:64, :] = split_rows(total)
    away_ref[GROUPS, 64:96, :] = jnp.zeros((32, 128), BF16)


def last_add_kernel(cw_ref, gotcw_ref, b_ref, vec_ref, gotb_ref, out_ref):
    total = split_rows(vec_ref[...] + joined(gotb_ref[GROUPS, 0:64, :]))
    for f in range(GROUPS):
        out_ref[f, 0:96, :] = added(b_ref[f], gotb_ref[f])
        out_ref[f, 96:256, :] = added(cw_ref[f], gotcw_ref[f])
        out_ref[f, 256:320, :] = total


def finish_vectors(vec, count_all, scale_ref, bias_ref, skip_ref, gbias_ref, decay_ref, lam_ref, step_ref, rms_ref, vec_ref):
    for k, ref in enumerate((scale_ref, bias_ref, skip_ref)):
        for c in range(4):
            ref[:, 128 * c : 128 * c + 128] = vec[4 * k + c : 4 * k + c + 1]
    for k, ref in enumerate((decay_ref, lam_ref, step_ref)):
        for c, chunk in enumerate(rows_to_lanes(vec[16 + 4 * k : 20 + 4 * k])):
            ref[:, 128 * c : 128 * c + 128] = chunk
    total = jnp.sum(vec[28:30], axis=1, keepdims=True)
    lane = lane_iota((1, 2))
    rms_ref[...] = jnp.sqrt(jnp.where(lane == 0, total[0:1], total[1:2]) / count_all)


def finish_kernel(
    count_all, got_ref, dre_ref, dim_ref, ore_ref, oim_ref, glu_ref, gbias_ref,
    scale_ref, bias_ref, skip_ref, decay_ref, lam_ref, step_ref, rms_ref, vec_ref,
):
    def total(start, count):
        value = got_ref[0, start : start + count, :].astype(F32)
        for f in range(1, GROUPS):
            value = value + got_ref[f, start : start + count, :].astype(F32)
        return value

    for start, low_ref, high_ref in ((0, dre_ref, dim_ref), (96, ore_ref, oim_ref)):
        value = total(start, 96)
        low_ref[...] = value[:, 0:64]
        high_ref[...] = pltpu.roll(value, 64, 1)[:, 0:64]
    value = total(192, 64)
    glu_ref[0:64, :] = value[:, 0:64]
    glu_ref[64:128, :] = pltpu.roll(value, 64, 1)[:, 0:64]
    vec = joined(got_ref[0, 256:320, :])
    for f in range(1, GROUPS):
        vec = vec + joined(got_ref[f, 256:320, :])
    vec_ref[...] = vec
    finish_vectors(vec, count_all, scale_ref, bias_ref, skip_ref, None, decay_ref, lam_ref, step_ref, rms_ref, None)
    place = tensor_pos() * GROUPS + lax.axis_index("fsdp")
    row = jnp.broadcast_to(vec_ref[pl.ds(12 + place // 8, 1), :], (8, 128))
    gbias_ref[...] = pltpu.roll(row, 128 - 16 * (place % 8), 1)[0:1, 0:16]


def call(kernel, outs, args, scratch=(), specs=None, limit=24):
    return pl.pallas_call(
        kernel,
        out_shape=outs,
        in_specs=specs or [VM] * len(args),
        out_specs=jax.tree.map(lambda _: VM, outs),
        scratch_shapes=list(scratch),
        compiler_params=pltpu.CompilerParams(vmem_limit_bytes=limit << 20),
    )(*args)


def swap(value, axis):
    return lax.ppermute(value, axis, [(0, 1), (1, 0)])


def on_device(
    layer_in, grad_out, ln_scale, ln_bias, decay_rate, lam_im, log_dt, in_re, in_im, out_re, out_im, skip, glu_weight, glu_bias, seq_lengths
):
    rows, width = layer_in.shape
    fsdp = lax.axis_size("fsdp")
    blocks = fsdp * 4
    count_all = float(rows * blocks * width)
    fast = fsdp == GROUPS
    if fast:
        row = lambda v: v.reshape(1, -1)
        sent = call(
            pack_kernel,
            sds((GROUPS, 272, 128), BF16),
            (in_re, in_im, out_re, out_im, glu_weight, row(ln_scale), row(ln_bias), row(skip), row(glu_bias),
             row(decay_rate), row(lam_im), row(log_dt)),
        )
        g0 = lax.all_to_all(sent, "fsdp", 0, 0, tiled=True)
        g2 = swap(g0, "ty")
        g1 = swap(g0, "tc")
        g3 = swap(g2, "tc")
    else:
        g0, g1, g2, g3 = gathered(ln_scale, ln_bias, decay_rate, lam_im, log_dt, in_re, in_im, out_re, out_im, skip, glu_weight, glu_bias)

    xhat, inverse, normed, v, lane, row_prm, carry = call(
        functools.partial(first_kernel, blocks),
        (sds((rows, width)), sds((rows, 128)), sds((rows, width), BF16), sds((2 * rows, 384)), sds((8, 384)), sds((8, 8, 128)), sds((blocks, 8, 128))),
        (layer_in, seq_lengths, g0, g1, g2, g3),
        [pltpu.VMEM((8, 128), F32)],
        [VM, SM, VM, VM, VM, VM],
    )
    came = lax.all_to_all(carry, AXES, 0, 0, tiled=True)
    layer_out, state, d_state, enter, d_mixed, part, keep_cw, away_cw, carry = call(
        functools.partial(second_kernel, blocks),
        (sds((rows, width), BF16), sds((2 * rows, 384)), sds((2 * rows, 384)), sds((8, 384)), sds((rows, width)), sds((8, width)),
         sds((2, GROUPS, 160, 128), BF16), sds((2, GROUPS, 160, 128), BF16), sds((blocks, 8, 128))),
        (came, seq_lengths, layer_in, grad_out, normed, v, lane, row_prm, g0, g1, g2, g3),
        [pltpu.VMEM((8, 128), F32), pltpu.VMEM((GROUPS, 4, 64, 128), BF16), pltpu.VMEM((4, GROUPS, 64, 128), BF16)],
        [VM, SM] + [VM] * 10,
    )
    came = lax.all_to_all(carry, AXES, 0, 0, tiled=True)
    grad_in, keep_b, away_b, vec = call(
        third_kernel,
        (sds((rows, width)), sds((2, GROUPS, 96, 128), BF16), sds((2 * GROUPS + 1, 96, 128), BF16), sds((32, 128))),
        (came, seq_lengths, grad_out, normed, xhat, inverse, v, lane, row_prm, state, d_state, enter, d_mixed, part, g0, g1, g2, g3),
        [pltpu.VMEM((8, 128), F32), pltpu.VMEM((2 * rows, 384), BF16)],
        [VM, SM] + [VM] * 16,
    )
    if not fast:
        return reduced(layer_out, grad_in, keep_cw, away_cw, keep_b, away_b, vec, count_all, fsdp, width)
    got_cw = swap(away_cw, "tc")
    stay_cw, away_cw = call(
        core_cw_kernel, (sds((GROUPS, 160, 128), BF16), sds((GROUPS, 160, 128), BF16)), (keep_cw, got_cw)
    )
    got_cw = swap(away_cw, "ty")
    got_b = swap(away_b, "tc")
    stay_b, vec, away_b = call(
        core_b_kernel, (sds((GROUPS, 96, 128), BF16), sds((32, 128)), sds((GROUPS + 1, 96, 128), BF16)), (keep_b, vec, got_b)
    )
    got_b = swap(away_b, "ty")
    sent = call(last_add_kernel, sds((GROUPS, 320, 128), BF16), (stay_cw, got_cw, stay_b, vec, got_b))
    got = lax.all_to_all(sent, "fsdp", 0, 0, tiled=True)
    d_re, d_im, d_ore, d_oim, d_glu, d_gbias, d_scale, d_bias, d_skip, g_decay, g_lam, g_step, rms = call(
        functools.partial(finish_kernel, count_all),
        (*[sds((96, 64))] * 4, sds((128, 64)), sds((1, 16)), *[sds((1, 512))] * 3, *[sds((1, 384))] * 3, sds((1, 2))),
        (got,),
        [pltpu.VMEM((32, 128), F32)],
    )
    flat = lambda value: value.reshape(-1)
    return (
        layer_out, grad_in, flat(d_scale), flat(d_bias), flat(g_decay), flat(g_lam), flat(g_step), d_re, d_im, d_ore, d_oim,
        flat(d_skip), d_glu, flat(d_gbias), flat(rms),
    )


def gathered(ln_scale, ln_bias, decay_rate, lam_im, log_dt, in_re, in_im, out_re, out_im, skip, glu_weight, glu_bias):
    tens = tensor_pos()
    full = lambda value, axis: lax.all_gather(value, "fsdp", axis=axis, tiled=True)

    def pair(first, second):
        halves = jnp.stack([first.reshape(-1, GROUPS, 64), second.reshape(-1, GROUPS, 64)], axis=2)
        return halves.reshape(-1, GROUPS, 128).swapaxes(0, 1)

    gate = full(glu_weight, 1)
    units = lambda start: lax.dynamic_slice_in_dim(gate, start, 64, 0)
    vectors = [pair(full(ln_scale, 0)[None], full(ln_bias, 0)[None]), pair(full(skip, 0)[None], full(glu_bias, 0)[None])]
    for value in (decay_rate, lam_im, log_dt):
        value = jnp.pad(value, (0, 32))
        for _ in range(3):
            piece = lax.reduce_precision(value, 8, 7)
            value = value - piece
            vectors.append(jnp.broadcast_to(piece.astype(BF16)[None, None], (GROUPS, 1, 128)))
    vectors.append(jnp.zeros((GROUPS, 5, 128), BF16))
    packet = jnp.concatenate(
        [pair(full(in_re, 1), full(in_im, 1)), pair(full(out_re, 1), full(out_im, 1)), pair(units(tens * 64), units(tens * 64 + 256)), *vectors],
        axis=1,
    )
    everyone = lax.all_gather(packet, ("ty", "tc"), axis=0)
    return [lax.dynamic_index_in_dim(everyone, tens ^ i, 0, keepdims=False) for i in range(4)]


def reduced(layer_out, grad_in, keep_cw, away_cw, keep_b, away_b, vec, count_all, fsdp, width):
    tens = tensor_pos()
    blocks_b = away_b[: 2 * GROUPS].reshape(2, GROUPS, 96, 128)

    def natural(keep, away, first, second):
        four = jnp.stack([keep[0], away[0], keep[1], away[1]]).astype(F32)
        four = jnp.concatenate([lax.dynamic_index_in_dim(four, tens ^ i, 0) for i in range(4)], axis=0)
        halves = four.reshape(4, GROUPS, -1, 2, 64).transpose(3, 0, 2, 1, 4)
        halves = halves.reshape(2, 4, halves.shape[2], width)
        if not first:
            return halves.transpose(1, 0, 2, 3).reshape(-1, width)
        return halves[0].reshape(-1, width), halves[1].reshape(-1, width)

    def scattered(value):
        value = lax.psum_scatter(value, ("ty", "tc"), scatter_dimension=0, tiled=True)
        return lax.psum_scatter(value, "fsdp", scatter_dimension=1, tiled=True)

    d_re, d_im = natural(keep_b, blocks_b, True, True)
    d_ore, d_oim = natural(keep_cw[:, :, :96], away_cw[:, :, :96], True, True)
    d_glu = natural(keep_cw[:, :, 96:], away_cw[:, :, 96:], False, False)
    vec = lax.psum(vec, AXES)
    states = lambda k: vec[16 + 4 * k : 20 + 4 * k, :96].reshape(-1)
    own = width // (4 * fsdp)
    place = tens * fsdp + lax.axis_index("fsdp")
    d_gbias = lax.dynamic_slice_in_dim(vec[12:16].reshape(-1), place * own, own, 0)
    rms = jnp.sqrt(jnp.sum(vec[28:30], axis=1) / count_all)
    return (
        layer_out, grad_in, vec[0:4].reshape(-1), vec[4:8].reshape(-1), states(0), states(1), states(2), scattered(d_re), scattered(d_im),
        scattered(d_ore), scattered(d_oim), vec[8:12].reshape(-1), scattered(d_glu), d_gbias, rms,
    )


def solution(mesh):
    tensor = ("ty", "tc")
    split = Mesh(mesh.devices.reshape(mesh.shape["fsdp"], mesh.shape["tensor"] // 2, 2), AXES)
    tokens, matrix = P(AXES, None), P(tensor, "fsdp")
    return jax.shard_map(
        on_device,
        mesh=split,
        in_specs=(
            tokens, tokens, P("fsdp"), P("fsdp"), P(tensor), P(tensor), P(tensor), matrix, matrix, matrix, matrix,
            P("fsdp"), P(None, "fsdp"), P("fsdp"), P(),
        ),
        out_specs=(
            tokens, tokens, P(), P(), P(), P(), P(), matrix, matrix, matrix, matrix, P(), matrix, P((*tensor, "fsdp")), P(),
        ),
        check_vma=False,
    )
```

time: 1000 us -> 115 us (0.12)
  waiting for transfers between devices: 301 us -> 27.3 us
  matrix products: 266 us -> 0 us
  blocking collectives: 310 us -> 65.2 us
  other arithmetic: 66.1 us -> 1.79 us
  local copies, waits for them, and re-layouts: 27.7 us -> 6.07 us
  between operations: 18.3 us -> 0.84 us
  Pallas kernels: 0 us -> 10 us
    dot_general x17 -> x0, matrix products: 266 us -> none  [the longest x4 158 us: within(): return jnp.einsum('qbts,qbs->qbt', left, right, precision=highest)]
    unnamed x12 -> x0, waiting for transfers between devices: 258 us -> none
    all_gather x8 -> x0, blocking collectives: 176 us -> none  [the longest x1 31.3 us: on_device(): lax.all_gather(glu_weight, 'fsdp', axis=1, tiled=True)]
    unnamed x3 -> x0, blocking collectives: 94.3 us -> none
    all_to_all x0 -> x4, blocking collectives: none -> 65.2 us  [the longest x1 23.2 us: on_device(): g0 = lax.all_to_all(sent, 'fsdp', 0, 0, tiled=True)]
    psum x1 -> x0, blocking collectives: 39.6 us -> none  [on_device(): lax.psum((scale_gradient, d_shift, d_skip, padded(g_decay), padded(g_lam)...]
    reduce_scatter x4 -> x0, waiting for transfers between devices: 38.6 us -> none  [the longest x1 21.2 us: on_device(): lax.psum_scatter(d_glu, 'fsdp', scatter_dimension=1, tiled=True)]
    mul x6 -> x0, other arithmetic: 31 us -> none  [the longest x2 24.9 us: powers(): return (magnitude * jnp.cos(turned), magnitude * jnp.sin(turned))]
  transfers between devices with their start and end apart: 10 -> 7, of which waited for: 8 -> 4; matrix products, arithmetic and copies ran while one was open for 2% -> 0% of each run, Pallas kernels for 0% -> 3%
where the time goes in v1:
time: 115 us; the launch traced here: 114 us
  blocking collectives  65.2 us (57%)
  waiting for transfers between devices  27.3 us (24%)
  Pallas kernels  10 us (9%)
  local copies, waits for them, and re-layouts  6.07 us (5%)
  starting transfers between devices  3.09 us (3%)
  other arithmetic  1.79 us (2%)
    ppermute x7, waiting for transfers between devices, swap(): return lax.ppermute(value, axis, [(0, 1), (1, 0)])  27.3 us
    all_to_all x1, blocking collectives, on_device(): g0 = lax.all_to_all(sent, 'fsdp', 0, 0, tiled=True)  23.2 us
    all_to_all x2, blocking collectives, on_device(): came = lax.all_to_all(carry, AXES, 0, 0, tiled=True)  22 us
    all_to_all x1, blocking collectives, on_device(): got = lax.all_to_all(sent, 'fsdp', 0, 0, tiled=True)  20.1 us
    pallas_call x8, Pallas kernels, call(): pl.pallas_call(kernel, out_shape=outs, in_specs=specs or [VM] * len(args)...  10 us
    unnamed x38, local copies, waits for them, and re-layouts  6.07 us
    ppermute x7, starting transfers between devices, swap(): return lax.ppermute(value, axis, [(0, 1), (1, 0)])  3.09 us
  transfers between devices with their start and end apart: 7, of which 4 were waited for; matrix products, arithmetic and copies ran while one was open for 0% of the time, Pallas kernels for 3%

profile of v1, /device:TPU:0, one launch (start us, length us, event | category | flops | bytes accessed | tf_op | source)
XLA Modules:
  0.0 114.4 jit_solution(12177758508318022078)
XLA Ops:
  0.7 0.8 copy.30.re_ref
  1.7 0.6 copy-done.13
  3.5 23.2 %all_to_all.20.g0 = bf16[8,272,128]{2,1,0:T(8,128)(2,1)S(1)} all-to-all(bf16[8,272,128]{2,1,0:T(8,128)(2,1)S(1)} %shard_map.262), channel_id=1, replica_groups=mesh['fsdp'=8,'ty'=2,'tc'=2] {'fsdp'}, dimensions={0} | all-to-all | bytes 1114112 | tf_op jit(solution)/shard_map/all_to_all | solution.py:621
  26.7 1.5 %collective-permute-start.1 = (bf16[8,272,128]{2,1,0:T(8,128)(2,1)S(1)}, bf16[8,272,128]{2,1,0:T(8,128)(2,1)S(1)}, u32[]{:S(2)}, u32[]{:S(2)}) collective-permute-start(bf16[8,272,128]{2,1,0:T(8,128)(2,1)S(1)} %all_to_all.20.g0), channel_id=1, source_target_pairs={{0,2},{2,0},{1,3},{3,1},{4,6},{6,4},{5,7},{7,5},{8,10},{10,8},{9,1... | collective-permute-start | bytes 1671176 | tf_op jit(solution)/shard_map/ppermute | solution.py:602
  28.2 11.9 %collective-permute-done.1.g2 = bf16[8,272,128]{2,1,0:T(8,128)(2,1)S(1)} collective-permute-done((bf16[8,272,128]{2,1,0:T(8,128)(2,1)S(1)}, bf16[8,272,128]{2,1,0:T(8,128)(2,1)S(1)}, u32[]{:S(2)}, u32[]{:S(2)}) %collective-permute-start.1) | collective-permute-done | bytes 557088 | tf_op jit(solution)/shard_map/ppermute | solution.py:602
  40.1 2.0 %collective-permute-done.2.g3 = bf16[8,272,128]{2,1,0:T(8,128)(2,1)S(1)} collective-permute-done((bf16[8,272,128]{2,1,0:T(8,128)(2,1)S(1)}, bf16[8,272,128]{2,1,0:T(8,128)(2,1)S(1)}, u32[]{:S(2)}, u32[]{:S(2)}) %collective-permute-start.2) | collective-permute-done | bytes 557088 | tf_op jit(solution)/shard_map/ppermute | solution.py:602
  42.1 1.5 %shard_map.263 = (f32[128,512]{1,0:T(8,128)S(1)}, f32[128,128]{1,0:T(8,128)S(1)}, bf16[128,512]{1,0:T(8,128)(2,1)S(1)}, f32[256,384]{1,0:T(8,128)S(1)}, f32[8,38...) custom-call(bf16[128,512]{1,0:T(8,128)(2,1)S(1)} %copy-done, s32[4]{0:T(128)S(1)} %copy-done.2, ...), custom_call_target="tpu_custom_call" | custom-call | tf_op jit(solution)/shard_map/pallas_call | solution.py:591
  43.6 11.7 %all_to_all.21.recv_ref = f32[32,8,128]{2,1,0:T(8,128)S(1)} all-to-all(f32[32,8,128]{2,1,0:T(8,128)S(1)} %get-tuple-element.53), channel_id=1, replica_groups=mesh['fsdp'=8,'ty'=2,'tc'=2] {'fsdp','ty','tc'}, dimensions={0} | all-to-all | bytes 262144 | tf_op jit(solution)/shard_map/all_to_all | solution.py:635
  55.3 3.9 %shard_map.264 = (bf16[128,512]{1,0:T(8,128)(2,1)}, f32[256,384]{1,0:T(8,128)S(1)}, f32[256,384]{1,0:T(8,128)S(1)}, f32[8,384]{1,0:T(8,128)S(1)}, f32[128,512]{1...) custom-call(f32[32,8,128]{2,1,0:T(8,128)S(1)} %all_to_all.21.recv_re, ...), custom_call_target="tpu_custom_call" | custom-call | tf_op jit(solution)/shard_map/pallas_call | solution.py:591
  59.4 10.3 %all_to_all.22.recv_ref = f32[32,8,128]{2,1,0:T(8,128)S(1)} all-to-all(f32[32,8,128]{2,1,0:T(8,128)S(1)} %get-tuple-element.59), channel_id=1, replica_groups=mesh['fsdp'=8,'ty'=2,'tc'=2] {'fsdp','ty','tc'}, dimensions={0} | all-to-all | bytes 262144 | tf_op jit(solution)/shard_map/all_to_all | solution.py:644
  69.7 3.4 %shard_map.265 = (f32[128,512]{1,0:T(8,128)}, bf16[2,8,96,128]{3,2,1,0:T(8,128)(2,1)S(1)}, bf16[17,96,128]{2,1,0:T(8,128)(2,1)S(1)}, f32[32,128]{1,0:T(8,128)S(1)}) custom-call(f32[32,8,128]{2,1,0:T(8,128)S(1)} %all_to_all.22.recv_ref, s32[4]{0:T(128)S(1)} %copy-done.2, bf16[128,512]{1,0:T(8,128)(2,1)S(1)} %copy-done.1, ...), custom_call_target="tpu_custom_call" | custom-call | tf_op jit(solution)/shard_map/pallas_call | solution.py:591
  73.9 1.0 collective-permute-done.5.got_ref
  75.0 0.8 collective-permute-start.6
  75.8 12.5 %collective-permute-done.6.gotb_ref = bf16[9,96,128]{2,1,0:T(8,128)(2,1)S(1)} collective-permute-done((bf16[9,96,128]{2,1,0:T(8,128)(2,1)S(1)}, bf16[9,96,128]{2,1,0:T(8,128)(2,1)S(1)}, u32[]{:S(2)}, u32[]{:S(2)}) %collective-permute-start.6) | collective-permute-done | bytes 221216 | tf_op jit(solution)/shard_map/ppermute | solution.py:602
  88.4 20.1 %all_to_all.23.got_ref = bf16[8,320,128]{2,1,0:T(8,128)(2,1)S(1)} all-to-all(bf16[8,320,128]{2,1,0:T(8,128)(2,1)S(1)} %shard_map.268), channel_id=1, replica_groups=mesh['fsdp'=8,'ty'=2,'tc'=2] {'fsdp'}, dimensions={0} | all-to-all | bytes 1310720 | tf_op jit(solution)/shard_map/all_to_all | solution.py:665
  108.4 0.7 shard_map.269
  109.1 0.6 reduce
  109.7 0.6 reduce.1
  110.3 0.6 reduce.2
  110.9 0.7 copy.35
  111.6 0.7 copy.36
  112.3 0.7 copy.37
  113.0 0.7 copy.38
  113.7 0.7 copy.39
  (43 shorter events, 2.5 us)
Async XLA Ops:
  0.6 0.8 copy-start.11
  0.7 1.0 copy-start.12
  1.5 1.0 copy-start.10
  1.6 0.7 copy-start.13
  2.6 0.7 copy-start.6
  2.6 0.7 copy-start.7
  2.6 0.7 copy-start.8
  2.6 0.7 copy-start.9
  2.6 0.7 copy-start.3
  2.7 0.7 copy-start.4
  2.7 0.7 copy-start.5
  3.5 38.6 %copy-start = (bf16[128,512]{1,0:T(8,128)(2,1)S(1)}, bf16[128,512]{1,0:T(8,128)(2,1)}, u32[]{:S(2)}) copy-start(bf16[128,512]{1,0:T(8,128)(2,1)} %x_ref.3) | copy-start | bytes 393220
  3.5 38.6 %copy-start.2 = (s32[4]{0:T(128)S(1)}, s32[4]{0:T(128)}, u32[]{:S(2)}) copy-start(s32[4]{0:T(128)} %seq_ref.5) | copy-start | bytes 52
  26.7 13.4 %collective-permute-start.1 = (bf16[8,272,128]{2,1,0:T(8,128)(2,1)S(1)}, bf16[8,272,128]{2,1,0:T(8,128)(2,1)S(1)}, u32[]{:S(2)}, u32[]{:S(2)}) collective-permute-start(bf16[8,272,128]{2,1,0:T(8,128)(2,1)S(1)} %all_to_all.20.g0), channel_id=1, source_target_pairs={{0,2},{2,0},{1,3},{3,1},{4,6},{6,4},{5,7},{7,5},{8,10},{10,8},{9,1... | collective-permute-start | bytes 1671176 | tf_op jit(solution)/shard_map/ppermute | solution.py:602
  28.2 11.9 %collective-permute-start = (bf16[8,272,128]{2,1,0:T(8,128)(2,1)S(1)}, bf16[8,272,128]{2,1,0:T(8,128)(2,1)S(1)}, u32[]{:S(2)}, u32[]{:S(2)}) collective-permute-start(bf16[8,272,128]{2,1,0:T(8,128)(2,1)S(1)} %all_to_all.20.g0), channel_id=1, source_target_pairs={{0,1},{1,0},{2,3},{3,2},{4,5},{5,4},{6,7},{7,6},{8,9},{9,8},{10,11... | collective-permute-start | bytes 1671176 | tf_op jit(solution)/shard_map/ppermute | solution.py:602
  40.1 2.0 %collective-permute-start.2 = (bf16[8,272,128]{2,1,0:T(8,128)(2,1)S(1)}, bf16[8,272,128]{2,1,0:T(8,128)(2,1)S(1)}, u32[]{:S(2)}, u32[]{:S(2)}) collective-permute-start(bf16[8,272,128]{2,1,0:T(8,128)(2,1)S(1)} %collective-permute-done.1.g2), channel_id=1, source_target_pairs={{0,1},{1,0},{2,3},{3,2},{4,5},{5,4},{6,7},{7,6},{8,9},{9,8},{10,11... | collective-permute-start | bytes 1671176 | tf_op jit(solution)/shard_map/ppermute | solution.py:602
  43.6 11.7 %copy-start.1 = (bf16[128,512]{1,0:T(8,128)(2,1)S(1)}, bf16[128,512]{1,0:T(8,128)(2,1)}, u32[]{:S(2)}) copy-start(bf16[128,512]{1,0:T(8,128)(2,1)} %up_ref.3) | copy-start | bytes 393220
  59.2 14.2 %collective-permute-start.3 = (bf16[2,8,160,128]{3,2,1,0:T(8,128)(2,1)S(1)}, bf16[2,8,160,128]{3,2,1,0:T(8,128)(2,1)S(1)}, u32[]{:S(2)}, u32[]{:S(2)}) collective-permute-start(bf16[2,8,160,128]{3,2,1,0:T(8,128)(2,1)S(1)} %get-tuple-element.69), channel_id=1, source_target_pairs={{0,1},{1,0},{2,3},{3,2},{4,5},{5,4},{6,7},{7,6},{8,9},{9,8},{10,11... | collective-permute-start | bytes 1966088 | tf_op jit(solution)/shard_map/ppermute | solution.py:602
  73.2 1.8 %collective-permute-start.5 = (bf16[17,96,128]{2,1,0:T(8,128)(2,1)S(1)}, bf16[17,96,128]{2,1,0:T(8,128)(2,1)S(1)}, u32[]{:S(2)}, u32[]{:S(2)}) collective-permute-start(bf16[17,96,128]{2,1,0:T(8,128)(2,1)S(1)} %get-tuple-element.74), channel_id=1, source_target_pairs={{0,1},{1,0},{2,3},{3,2},{4,5},{5,4},{6,7},{7,6},{8,9},{9,8},{10,11... | collective-permute-start | bytes 1253384 | tf_op jit(solution)/shard_map/ppermute | solution.py:602
  73.5 14.7 %collective-permute-start.4 = (bf16[8,160,128]{2,1,0:T(8,128)(2,1)S(1)}, bf16[8,160,128]{2,1,0:T(8,128)(2,1)S(1)}, u32[]{:S(2)}, u32[]{:S(2)}) collective-permute-start(bf16[8,160,128]{2,1,0:T(8,128)(2,1)S(1)} %get-tuple-element.71), channel_id=1, source_target_pairs={{0,2},{2,0},{1,3},{3,1},{4,6},{6,4},{5,7},{7,5},{8,10},{10,8},{9,1... | collective-permute-start | bytes 983048 | tf_op jit(solution)/shard_map/ppermute | solution.py:602
  75.0 13.2 %collective-permute-start.6 = (bf16[9,96,128]{2,1,0:T(8,128)(2,1)S(1)}, bf16[9,96,128]{2,1,0:T(8,128)(2,1)S(1)}, u32[]{:S(2)}, u32[]{:S(2)}) collective-permute-start(bf16[9,96,128]{2,1,0:T(8,128)(2,1)S(1)} %get-tuple-element.77), channel_id=1, source_target_pairs={{0,2},{2,0},{1,3},{3,1},{4,6},{6,4},{5,7},{7,5},{8,10},{10,8},{9,1... | collective-permute-start | bytes 663560 | tf_op jit(solution)/shard_map/ppermute | solution.py:602

commit v2 on v1

v2 whole, which is shorter than its diff:
```python
import functools

import jax
import jax.numpy as jnp
from jax import lax
from jax.experimental import pallas as pl
from jax.experimental.pallas import tpu as pltpu
from jax.sharding import Mesh
from jax.sharding import PartitionSpec as P

F32 = jnp.float32
BF16 = jnp.bfloat16
FSDP = ("fz", "fx")
TENSOR = ("ty", "tc")
AXES = (*FSDP, *TENSOR)
HBM = pl.BlockSpec(memory_space=pltpu.HBM)
VM = pl.BlockSpec(memory_space=pltpu.VMEM)
SM = pl.BlockSpec(memory_space=pltpu.SMEM)

GROUPS = 8
VEC = 96


def sds(shape, dtype=F32):
    return jax.ShapeDtypeStruct(shape, dtype)


def low_half(shape):
    return lax.broadcasted_iota(jnp.int32, shape, len(shape) - 1) < 64


def lane_iota(shape):
    return lax.broadcasted_iota(jnp.int32, shape, len(shape) - 1)


def dot(a, b, dims):
    return lax.dot_general(a, b, (dims, ((), ())), preferred_element_type=F32)


NT = ((1,), (1,))
NN = ((1,), (0,))
TN = ((0,), (0,))


def spread(x):
    lo = low_half((x.shape[0], 128))
    upper, lower = [], []
    for c in range(x.shape[1] // 128):
        xc = x[:, 128 * c : 128 * c + 128]
        turned = pltpu.roll(xc, 64, 1)
        upper += [jnp.where(lo, xc, 0.0).astype(BF16), jnp.where(lo, turned, 0.0).astype(BF16)]
        lower += [jnp.where(lo, 0.0, turned).astype(BF16), jnp.where(lo, 0.0, xc).astype(BF16)]
    return jnp.concatenate(
        [jnp.concatenate(upper, axis=1), jnp.concatenate(lower, axis=1)], axis=0
    )


def folded(pq):
    rows = pq.shape[0] // 2
    lo = low_half((rows, 128))
    out = []
    for c in range(pq.shape[1] // 256):
        p0, p1 = pq[:rows, 256 * c : 256 * c + 128], pq[:rows, 256 * c + 128 : 256 * c + 256]
        q0, q1 = pq[rows:, 256 * c : 256 * c + 128], pq[rows:, 256 * c + 128 : 256 * c + 256]
        out.append(jnp.where(lo, p0 + pltpu.roll(q0, 64, 1), pltpu.roll(p1, 64, 1) + q1))
    return jnp.concatenate(out, axis=1)


def slot_pos(k):
    return (k % 2) * 2 + (lax.axis_index("tc") ^ (k // 2))


def piece(refs, k, f, start, count):
    return refs[k // 2][f % 2, k % 2, f // 2, start : start + count, :]


def weights(get):
    return jnp.concatenate([jnp.concatenate([get(k, f) for k in range(4)], axis=0) for f in range(GROUPS)], axis=1)


def feature_rows(refs, row):
    lo = low_half((8, 128))
    first, second = [], []
    for c in range(GROUPS // 2):
        a = jnp.broadcast_to(piece(refs, 0, 2 * c, row, 1).astype(F32), (8, 128))
        b = jnp.broadcast_to(piece(refs, 0, 2 * c + 1, row, 1).astype(F32), (8, 128))
        first.append(jnp.where(lo, a, pltpu.roll(b, 64, 1)))
        second.append(jnp.where(lo, pltpu.roll(a, 64, 1), b))
    return jnp.concatenate(first, axis=1)[:1], jnp.concatenate(second, axis=1)[:1]


def rows_to_lanes(rows):
    turned = [rows, pltpu.roll(rows, 96, 1), pltpu.roll(rows, 64, 1), pltpu.roll(rows, 32, 1)]
    lane = lane_iota((1, 128))
    return [
        jnp.where(lane < 96, rows[0:1], turned[1][1:2]),
        jnp.where(lane < 64, turned[1][1:2], turned[2][2:3]),
        jnp.where(lane < 32, turned[2][2:3], turned[3][3:4]),
    ]


def lanes_to_rows(chunks):
    wide = [jnp.broadcast_to(chunk, (8, 128)) for chunk in chunks]
    lane = lane_iota((8, 128))
    r1 = jnp.where(lane < 32, pltpu.roll(wide[0], 32, 1), pltpu.roll(wide[1], 32, 1))
    r2 = jnp.where(lane < 64, pltpu.roll(wide[1], 64, 1), pltpu.roll(wide[2], 64, 1))
    r3 = pltpu.roll(wide[2], 96, 1)
    return [jnp.where(lane < 96, r, 0.0)[:1] for r in (wide[0], r1, r2, r3)]


def cmul(a, b):
    return a[0] * b[0] - a[1] * b[1], a[0] * b[1] + a[1] * b[0]


def tensor_pos():
    return lax.axis_index("ty") * 2 + lax.axis_index("tc")


def fsdp_pos():
    return lax.axis_index("fz") * 2 + lax.axis_index("fx")


def block_pos():
    return fsdp_pos() * 4 + tensor_pos()


def offsets_of(start_ref):
    return [start_ref[n : n + 1, :] for n in range(start_ref.shape[0])]


def starts_until(offsets, base, rows):
    at = (lax.broadcasted_iota(jnp.int32, (rows, 128), 0) + base).astype(F32)
    count = jnp.zeros((rows, 128), F32)
    for off in offsets:
        count = count + jnp.where((at >= off) & (off >= at[0:1]), 1.0, 0.0)
    return count


def no_start(offsets, base, rows):
    link = jnp.ones((1, 128), F32)
    first = (jnp.zeros((1, 128), jnp.int32) + base).astype(F32)
    for off in offsets:
        link = jnp.where((off >= first) & (off < first + rows), 0.0, link)
    return link


def expm1(x):
    series = x * (1 + x / 2 * (1 + x / 3 * (1 + x / 4 * (1 + x / 5 * (1 + x / 6 * (1 + x / 7))))))
    return jnp.where(jnp.abs(x) < 0.25, series, jnp.exp(x) - 1.0)


def discretize(decay_rate, lam_im, log_dt):
    step_size = jnp.exp(log_dt)
    lam_re = -decay_rate
    magnitude = jnp.exp(lam_re * step_size)
    phase = lam_im * step_size
    abar_re = magnitude * jnp.cos(phase)
    abar_im = magnitude * jnp.sin(phase)
    half_sin = jnp.sin(0.5 * phase)
    less_re = expm1(lam_re * step_size) * jnp.cos(phase) - 2.0 * half_sin * half_sin
    denom = lam_re * lam_re + lam_im * lam_im
    coef_re = (less_re * lam_re + abar_im * lam_im) / denom
    coef_im = (abar_im * lam_re - less_re * lam_im) / denom
    return abar_re, abar_im, coef_re, coef_im, step_size


def pack_kernel(*refs):
    *inputs, out_ref, square, four, glu_ref, halves, params, lengths, sems = refs
    seq_hbm, matrices, glu_hbm, features, states = inputs[0], inputs[1:5], inputs[5], inputs[6:10], inputs[10:13]
    units = pl.multiple_of(tensor_pos() * 128, 128)
    pairs = [(ref, four.at[k]) for k, ref in enumerate(matrices)]
    pairs += [(glu_hbm.at[:, pl.ds(units, 128)], glu_ref), (seq_hbm, lengths)]
    pairs += [(ref, halves.at[k]) for k, ref in enumerate(features)]
    pairs += [(ref, params.at[k]) for k, ref in enumerate(states)]
    copies = [pltpu.make_async_copy(source, target, sems.at[k]) for k, (source, target) in enumerate(pairs)]
    for copy in copies:
        copy.start()
    square[:, 96:128] = jnp.zeros((128, 32), F32)
    for copy in copies:
        copy.wait()
    vec = [
        jnp.concatenate([halves[0], halves[1]], axis=1).astype(F32),
        jnp.concatenate([halves[2], halves[3]], axis=1).astype(F32),
    ]
    for k in range(3):
        value = jnp.concatenate([params[k], jnp.zeros((1, 32), F32)], axis=1)
        for _ in range(3):
            part = value.astype(BF16).astype(F32)
            value = value - part
            vec.append(part)
    lane = lane_iota((1, 128))
    upper, lower, total = jnp.zeros((1, 128), jnp.int32), jnp.zeros((1, 128), jnp.int32), 0
    for n in range(lengths.shape[0]):
        upper = jnp.where(lane == n, total >> 8, upper)
        lower = jnp.where(lane == n, total & 255, lower)
        total = total + lengths[n]
    vec += [upper.astype(F32), lower.astype(F32)]
    vec.append(jnp.zeros((16 - len(vec), 128), F32))
    vec = jnp.concatenate(vec, axis=0).astype(BF16)
    pieces = []
    for k in (0, 2):
        square[0:64, 0:96] = four[k].astype(F32)
        square[64:128, 0:96] = four[k + 1].astype(F32)
        pieces.append(square[...].T[0:96].astype(BF16))
    packet = jnp.concatenate([pieces[0], vec, pieces[1], glu_ref[...]], axis=0)
    for z in range(GROUPS // 2):
        out_ref[z] = packet


def params_of(refs, vec_row):
    lane = lane_iota((8, 128))
    out = []
    for k, safe in enumerate((1.0, 0.0, 0.0)):
        rows = []
        for k4 in range(4):
            part = piece(refs, k4, 0, vec_row, 16).astype(F32)
            rows.append((part[2 + 3 * k : 3 + 3 * k] + part[3 + 3 * k : 4 + 3 * k]) + part[4 + 3 * k : 5 + 3 * k])
        value = jnp.concatenate(rows + [jnp.full((4, 128), safe, F32)], axis=0)
        out.append(jnp.where(lane < 96, value, safe))
    return out


def block_of(chunks_re, chunks_im, scratch):
    for half, chunks in ((0, chunks_re), (4, chunks_im)):
        for k, row in enumerate(lanes_to_rows(chunks)):
            scratch[pl.ds(half + slot_pos(k), 1), :] = row


def chunks_from(scratch, half):
    rows = [scratch[pl.ds(half + slot_pos(k), 1), :] for k in range(4)]
    return rows_to_lanes(jnp.concatenate([*rows, jnp.zeros((4, 128), F32)], axis=0))


def norm_kernel(x_ref, g_ref, xhat_ref, inv_ref, normed_ref, wide_ref, feat_ref, start_ref):
    rows, width = x_ref.shape
    x = x_ref[...].astype(F32)
    centered = x - jnp.sum(x, axis=1, keepdims=True) / width
    inverse = lax.rsqrt(jnp.sum(centered * centered, axis=1, keepdims=True) / width + 1e-05)
    xhat = centered * inverse
    xhat_ref[...] = xhat
    inv_ref[...] = jnp.broadcast_to(inverse, (rows, 128))
    scale, bias = feature_rows((g_ref,), VEC)
    feat_ref[0:1] = scale
    feat_ref[1:2], feat_ref[2:3] = feature_rows((g_ref,), VEC + 1)
    normed = (xhat * scale + bias).astype(BF16)
    normed_ref[...] = normed
    wide_ref[...] = spread(normed.astype(F32))
    upper, lower = (piece((g_ref,), 0, 0, VEC + 11 + k, 1).astype(F32) for k in range(2))
    starts = upper * 256.0 + lower
    for n in range(start_ref.shape[0]):
        start_ref[n : n + 1, :] = jnp.broadcast_to(starts[:, n : n + 1], (1, 128))


def first_kernel(blocks, wide_ref, start_ref, g0, g1, v_ref, lane_ref, row_ref, send_ref, scratch):
    refs = (g0, g1)
    rows = wide_ref.shape[0] // 2
    v_ref[...] = dot(wide_ref[...], weights(lambda k, f: piece(refs, k, f, 0, 96)), NT)

    decay, lam, log_dt = params_of(refs, VEC)
    abar_re, abar_im, coef_re, coef_im, step_size = discretize(decay, lam, log_dt)
    power = (abar_re, abar_im)
    per_row = [decay, lam, step_size, abar_re, abar_im, coef_re, coef_im]
    for _ in range(7):
        power = cmul(power, power)
    for half in (0, 1):
        for k in range(4):
            scratch[pl.ds(half * 4 + slot_pos(k), 1), :] = power[half][k : k + 1]
    for k, value in enumerate(per_row):
        row_ref[k] = value
    row_ref[len(per_row)] = scratch[...]
    abar = (rows_to_lanes(abar_re), rows_to_lanes(abar_im))
    coef = (rows_to_lanes(coef_re), rows_to_lanes(coef_im))
    for k, chunks in enumerate((*abar, *coef)):
        for c in range(3):
            lane_ref[k : k + 1, 128 * c : 128 * c + 128] = chunks[c]

    offsets = offsets_of(start_ref)
    count = starts_until(offsets, block_pos() * rows, rows)
    open_tail = jnp.where(count == count[rows - 1 : rows], 1.0, 0.0)
    last = ([], [])
    for c in range(3):
        lanes = slice(128 * c, 128 * c + 128)
        a = (abar[0][c], abar[1][c])
        eight, tail = eighth_powers(a, 7)
        b = (coef[0][c], coef[1][c])
        acc = (jnp.zeros((8, 128), F32), jnp.zeros((8, 128), F32))
        for blk in range(rows // 8):
            here = slice(8 * blk, 8 * blk + 8)
            there = slice(rows + 8 * blk, rows + 8 * blk + 8)
            drive = cmul(b, (v_ref[here, lanes], v_ref[there, lanes]))
            moved = cmul(eight, acc)
            acc = (moved[0] + drive[0] * open_tail[here], moved[1] + drive[1] * open_tail[here])
        total = cmul(tail, acc)
        last[0].append(column_sum(total[0]))
        last[1].append(column_sum(total[1]))
    block_of(last[0], last[1], scratch)
    packet = scratch[...]
    for d in range(blocks):
        send_ref[d] = packet


def local_scan_kernel(start_ref, v_ref, lane_ref, local_ref, power_ref):
    rows = v_ref.shape[0] // 2
    count = starts_until(offsets_of(start_ref), block_pos() * rows, rows)
    for c in range(3):
        lanes = slice(128 * c, 128 * c + 128)
        a = (lane_ref[0:1, lanes], lane_ref[1:2, lanes])
        b = (lane_ref[2:3, lanes], lane_ref[3:4, lanes])
        state = scan_chunk(cmul(b, (v_ref[:rows, lanes], v_ref[rows:, lanes])), a, count, False)
        local_ref[:rows, lanes] = state[0]
        local_ref[rows:, lanes] = state[1]
        eight, power = eighth_powers(a, 0)
        for blk in range(rows // 8):
            power_ref[8 * blk : 8 * blk + 8, lanes] = power[0]
            power_ref[rows + 8 * blk : rows + 8 * blk + 8, lanes] = power[1]
            if blk < rows // 8 - 1:
                power = cmul(power, eight)


def eighth_powers(a, top):
    sub = lax.broadcasted_iota(jnp.int32, (8, 128), 0)
    exponent = (7 - sub) if top == 7 else sub + 1
    a = (jnp.broadcast_to(a[0], (8, 128)), jnp.broadcast_to(a[1], (8, 128)))
    tile = (jnp.ones((8, 128), F32), jnp.zeros((8, 128), F32))
    for bit in range(4):
        if bit == 3:
            eight = a
        taken = (exponent & (1 << bit)) != 0
        more = cmul(tile, a)
        tile = (jnp.where(taken, more[0], tile[0]), jnp.where(taken, more[1], tile[1]))
        a = cmul(a, a)
    return eight, tile


def scan_chunk(value, a, count, reverse):
    rows = count.shape[0]
    at = lax.broadcasted_iota(jnp.int32, (rows, 128), 0)
    step = 1
    while step < rows:
        shift = rows - step if reverse else step
        other = pltpu.roll(count, shift, 0)
        inside = (at < rows - step) if reverse else (at >= step)
        linked = inside & (other == count)
        moved = (pltpu.roll(value[0], shift, 0), pltpu.roll(value[1], shift, 0))
        more = cmul(a, moved)
        value = (value[0] + jnp.where(linked, more[0], 0.0), value[1] + jnp.where(linked, more[1], 0.0))
        a = cmul(a, a)
        step *= 2
    return value


def carried(recv_ref, row_ref, offsets, rows, reverse, scratch):
    blocks = recv_ref.shape[0]
    power = row_ref[7]
    pre, pim = power[0:4], power[4:8]
    if reverse:
        pim = -pim
    place = block_pos()

    def turn(k, state):
        j = blocks - 1 - k if reverse else k
        link = no_start(offsets, j * rows, rows)
        got = recv_ref[j]
        new = cmul((pre * link, pim * link), state)
        return new[0] + got[0:4], new[1] + got[4:8]

    zero = jnp.zeros((4, 128), F32)
    out = lax.fori_loop(0, blocks - 1 - place if reverse else place, turn, (zero, zero))
    scratch[0:4, :] = out[0]
    scratch[4:8, :] = out[1]
    return chunks_from(scratch, 0), chunks_from(scratch, 4)


def column_sum(value):
    return jnp.sum(value, axis=0, keepdims=True)


def second_kernel(
    blocks, recv_ref, start_ref, x_ref, up_ref, normed_ref, lane_ref, row_ref, feat_ref, local_ref, power_ref, g0, g1, g2, g3,
    out_ref, state_ref, twice_ref, dstate_ref, enter_ref, dmixed_ref, act_ref, dlogit_ref, part_ref, send_ref,
    scratch, gate_ref, c_ref,
):
    rows, width = x_ref.shape
    x_pos, y_pos = lax.axis_index("fx"), lax.axis_index("ty")
    offsets = offsets_of(start_ref)
    base = block_pos() * rows
    count = starts_until(offsets, base, rows)
    for i, ref in enumerate((g0, g1, g2, g3)):
        y = y_pos ^ (i % 2)
        tens = y * 2 + (lax.axis_index("tc") ^ (i // 2))
        lanes = pl.ds(pl.multiple_of(tens * 128, 128), 128)
        for j in range(2):
            for z in range(GROUPS // 2):
                f = z * 2 + (x_pos ^ j)
                c_ref[f, (i // 2) * 2 + y] = ref[j, z, 0:96, :]
                gate_ref[pl.ds(pl.multiple_of(f * 64, 64), 64), lanes] = ref[j, z, 96:160, :]
    enter = carried(recv_ref, row_ref, offsets, rows, False, scratch)
    head = jnp.where(count == 0.0, 1.0, 0.0)
    for c in range(3):
        lanes = slice(128 * c, 128 * c + 128)
        power = (power_ref[:rows, lanes] * head, power_ref[rows:, lanes] * head)
        came = cmul(power, (enter[0][c], enter[1][c]))
        state = (local_ref[:rows, lanes] + came[0], local_ref[rows:, lanes] + came[1])
        state_ref[:rows, lanes] = state[0]
        state_ref[rows:, lanes] = state[1]
        twice_ref[:rows, lanes] = state[0].astype(BF16) * 2
        twice_ref[rows:, lanes] = state[1].astype(BF16) * -2
        enter_ref[0:1, lanes] = enter[0][c]
        enter_ref[1:2, lanes] = enter[1][c]
    readout = weights(lambda k, f: c_ref[f, k])
    scale, skip, gate_bias = (feat_ref[k : k + 1] for k in range(3))
    normed = normed_ref[...].astype(F32)
    mixed = folded(dot(twice_ref[...], readout, NN)) + skip * normed
    cdf = 0.5 * (1.0 + lax.erf(mixed * 0.7071067811865476))
    act_low = (mixed * cdf).astype(BF16)
    act_ref[...] = act_low
    act = act_low.astype(F32)
    w_gate = gate_ref[...]
    logit = dot(act_low, w_gate, NN) + gate_bias
    gate = 1.0 / (1.0 + jnp.exp(-logit))
    branch = (act * gate).astype(BF16).astype(F32)
    x = x_ref[...].astype(F32)
    out_ref[...] = (x + branch).astype(BF16)
    up = up_ref[...].astype(F32)
    dlogit = (up * act * gate * (1.0 - gate)).astype(BF16)
    dlogit_ref[...] = dlogit
    d_act = dot(dlogit, w_gate, NT) + up * gate
    slope = cdf + mixed * jnp.exp(-0.5 * mixed * mixed) * 0.3989422804014327
    d_mixed = d_act * slope
    dmixed_ref[...] = d_mixed
    part = [column_sum(d_mixed * normed), column_sum(dlogit.astype(F32)), column_sum(x * x), column_sum(branch * branch)]
    for k, value in enumerate(part):
        part_ref[k : k + 1, :] = value
    d_state = dot(spread(d_mixed.astype(BF16).astype(F32)), readout, NT)
    dstate_ref[:rows] = d_state[:rows] * 2.0
    dstate_ref[rows:] = d_state[rows:] * -2.0
    first = ([], [])
    for c in range(3):
        lanes = slice(128 * c, 128 * c + 128)
        a = (lane_ref[0:1, lanes], -lane_ref[1:2, lanes])
        eight, tail = eighth_powers(a, 0)
        acc = (jnp.zeros((8, 128), F32), jnp.zeros((8, 128), F32))
        for blk in range(rows // 8 - 1, -1, -1):
            here = slice(8 * blk, 8 * blk + 8)
            there = slice(rows + 8 * blk, rows + 8 * blk + 8)
            moved = cmul(eight, acc)
            acc = (moved[0] + dstate_ref[here, lanes] * head[here], moved[1] + dstate_ref[there, lanes] * head[here])
        total = cmul(tail, acc)
        first[0].append(column_sum(total[0]))
        first[1].append(column_sum(total[1]))
    block_of(first[0], first[1], scratch)
    packet = scratch[...]
    for d in range(blocks):
        send_ref[d] = packet


def readout_grad_kernel(twice_ref, dmixed_ref, act_ref, dlogit_ref, keep_ref, away_ref, dgate_ref):
    dy = dmixed_ref[...].astype(BF16).astype(F32)
    d_c = dot(twice_ref[...], spread(dy), TN).astype(BF16)
    dgate_ref[...] = dot(act_ref[...], dlogit_ref[...], TN).astype(BF16)
    for k in range(4):
        target = away_ref if k // 2 else keep_ref
        lanes = pl.ds(pl.multiple_of(slot_pos(k) * 128, 128), 128)
        for f in range(GROUPS):
            target[k % 2, f, 0:96, :] = d_c[96 * k : 96 * k + 96, 128 * f : 128 * f + 128]
            target[k % 2, f, 96:160, :] = dgate_ref[64 * f : 64 * f + 64, lanes]


def back_scan_kernel(start_ref, lane_ref, dstate_ref, local_ref):
    rows = dstate_ref.shape[0] // 2
    count = starts_until(offsets_of(start_ref), block_pos() * rows, rows)
    for c in range(3):
        lanes = slice(128 * c, 128 * c + 128)
        a = (lane_ref[0:1, lanes], -lane_ref[1:2, lanes])
        adj = scan_chunk((dstate_ref[:rows, lanes], dstate_ref[rows:, lanes]), a, count, True)
        local_ref[:rows, lanes] = adj[0]
        local_ref[rows:, lanes] = adj[1]


def split_rows(value):
    upper = value.astype(BF16)
    return jnp.concatenate([upper, (value - upper.astype(F32)).astype(BF16)], axis=0)


def third_kernel(
    recv_ref, start_ref, up_ref, wide_ref, xhat_ref, inv_ref, v_ref, lane_ref, row_ref, feat_ref, state_ref, local_ref, enter_ref,
    dmixed_ref, part_ref, g0, g1, gin_ref, keep_ref, away_ref, vec_ref, scratch, dv_ref,
):
    refs = (g0, g1)
    rows, width = up_ref.shape
    offsets = offsets_of(start_ref)
    base = block_pos() * rows
    count = starts_until(offsets, base, rows)
    later = carried(recv_ref, row_ref, offsets, rows, True, scratch)
    at = lax.broadcasted_iota(jnp.int32, (rows, 128), 0)
    before = jnp.where(at == 0, 0.0, pltpu.roll(count, 1, 0))
    keep = jnp.where(count == before, 1.0, 0.0)
    tail = jnp.where(count == count[rows - 1 : rows], 1.0, 0.0)
    sums = ([], [], [], [])
    for c in range(3):
        lanes = slice(128 * c, 128 * c + 128)
        a = (lane_ref[0:1, lanes], -lane_ref[1:2, lanes])
        eight, power = eighth_powers(a, 7)
        came = cmul(power, (later[0][c], later[1][c]))
        parts = ([], [])
        for blk in range(rows // 8 - 1, -1, -1):
            here = slice(8 * blk, 8 * blk + 8)
            there = slice(rows + 8 * blk, rows + 8 * blk + 8)
            parts[0].insert(0, local_ref[here, lanes] + came[0] * tail[here])
            parts[1].insert(0, local_ref[there, lanes] + came[1] * tail[here])
            came = cmul(came, eight)
        adj = (jnp.concatenate(parts[0], axis=0), jnp.concatenate(parts[1], axis=0))
        prev = (
            jnp.where(at == 0, enter_ref[0:1, lanes], pltpu.roll(state_ref[:rows, lanes], 1, 0)) * keep,
            jnp.where(at == 0, enter_ref[1:2, lanes], pltpu.roll(state_ref[rows:, lanes], 1, 0)) * keep,
        )
        v = (v_ref[:rows, lanes], v_ref[rows:, lanes])
        sums[0].append(column_sum(adj[0] * prev[0] + adj[1] * prev[1]))
        sums[1].append(column_sum(adj[1] * prev[0] - adj[0] * prev[1]))
        sums[2].append(column_sum(adj[0] * v[0] + adj[1] * v[1]))
        sums[3].append(column_sum(adj[1] * v[0] - adj[0] * v[1]))
        dv = cmul((lane_ref[2:3, lanes], -lane_ref[3:4, lanes]), adj)
        dv_ref[:rows, lanes] = dv[0].astype(BF16)
        dv_ref[rows:, lanes] = dv[1].astype(BF16)
    dv = dv_ref[...]
    d_b = dot(dv, wide_ref[...], TN).astype(BF16)
    for k in range(4):
        for f in range(GROUPS):
            block = d_b[96 * k : 96 * k + 96, 128 * f : 128 * f + 128]
            if k // 2:
                away_ref[(k % 2) * GROUPS + f] = block
            else:
                keep_ref[k % 2, f] = block
    scale, skip = feat_ref[0:1], feat_ref[1:2]
    d_normed = folded(dot(dv, weights(lambda k, f: piece(refs, k, f, 0, 96)), NN)) + dmixed_ref[...] * skip
    xhat = xhat_ref[...]
    d_xhat = d_normed * scale
    mean = jnp.sum(d_xhat, axis=1, keepdims=True) / width
    mean_hat = jnp.sum(d_xhat * xhat, axis=1, keepdims=True) / width
    gin_ref[...] = up_ref[...].astype(F32) + inv_ref[:, 0:1] * (d_xhat - mean - xhat * mean_hat)

    vector = [column_sum(d_normed * xhat), column_sum(d_normed), part_ref[0:1, :], part_ref[1:2, :]]
    for k, value in enumerate(vector):
        for c in range(4):
            vec_ref[4 * k + c : 4 * k + c + 1, :] = value[:, 128 * c : 128 * c + 128]
    g = [jnp.concatenate(lanes_to_rows(chunks) + [jnp.zeros((4, 128), F32)], axis=0) for chunks in sums]
    decay, lam, step, abar_re, abar_im, coef_re, coef_im = (row_ref[k] for k in range(7))
    d_abar, d_coef = (g[0], g[1]), (g[2], g[3])
    denom = decay * decay + lam * lam
    numer = (step * abar_re - coef_re, step * abar_im - coef_im)
    ratio = cmul(numer, (-decay / denom, -lam / denom))
    to_lam_a = cmul((step * abar_re, -step * abar_im), d_abar)
    to_lam_c = cmul((ratio[0], -ratio[1]), d_coef)
    g_decay = -(to_lam_a[0] + to_lam_c[0])
    g_lam = to_lam_a[1] + to_lam_c[1]
    slope = cmul((-decay, lam), (abar_re, abar_im))
    g_step = (slope[0] * d_abar[0] + slope[1] * d_abar[1] + abar_re * d_coef[0] + abar_im * d_coef[1]) * step
    for k, value in enumerate((g_decay, g_lam, g_step)):
        for i in range(4):
            vec_ref[pl.ds(16 + 4 * k + slot_pos(i), 1), :] = value[i : i + 1]
    for k in range(2):
        squares = part_ref[2 + k : 3 + k, :]
        total = squares[:, 0:128]
        for c in range(1, 4):
            total = total + squares[:, 128 * c : 128 * c + 128]
        vec_ref[28 + k : 29 + k, :] = total
    vec_ref[30:32, :] = jnp.zeros((2, 128), F32)
    away_ref[2 * GROUPS, 0:64, :] = split_rows(vec_ref[...])
    away_ref[2 * GROUPS, 64:96, :] = jnp.zeros((32, 128), BF16)


def added(a, b):
    return (a.astype(F32) + b.astype(F32)).astype(BF16)


def core_cw_kernel(keep_ref, got_ref, stay_ref, leave_ref):
    y = lax.axis_index("ty")
    for f in range(GROUPS):
        stay_ref[f] = added(keep_ref[y, f], got_ref[y, f])
        leave_ref[f] = added(keep_ref[1 - y, f], got_ref[1 - y, f])


def y_cw_kernel(keep_ref, got_ref, stay_ref, leave_ref):
    x = lax.axis_index("fx")
    for z in range(GROUPS // 2):
        stay_ref[z] = added(keep_ref[2 * z + x], got_ref[2 * z + x])
        leave_ref[z] = added(keep_ref[2 * z + 1 - x], got_ref[2 * z + 1 - x])


def joined(packet):
    return packet[0:32].astype(F32) + packet[32:64].astype(F32)


def core_b_kernel(keep_ref, vec_ref, got_ref, out_ref):
    total = split_rows(vec_ref[...] + joined(got_ref[2 * GROUPS, 0:64, :]))
    for x in range(2):
        for y in range(2):
            for z in range(GROUPS // 2):
                f = 2 * z + x
                out_ref[2 * x + y, 96 * z : 96 * z + 96, :] = added(keep_ref[y, f], got_ref[y * GROUPS + f])
            out_ref[2 * x + y, 384:448, :] = total


def last_add_kernel(cw_ref, gotcw_ref, gotb_ref, out_ref):
    vec = joined(gotb_ref[0, 384:448, :])
    for n in range(1, 4):
        vec = vec + joined(gotb_ref[n, 384:448, :])
    vec = split_rows(vec)
    for z in range(GROUPS // 2):
        here = slice(96 * z, 96 * z + 96)
        value = gotb_ref[0, here, :].astype(F32)
        for n in range(1, 4):
            value = value + gotb_ref[n, here, :].astype(F32)
        out_ref[z, 0:96, :] = value.astype(BF16)
        out_ref[z, 96:256, :] = added(cw_ref[z], gotcw_ref[z])
        out_ref[z, 256:320, :] = vec


def finish_vectors(vec, count_all, scale_ref, bias_ref, skip_ref, gbias_ref, decay_ref, lam_ref, step_ref, rms_ref, vec_ref):
    for k, ref in enumerate((scale_ref, bias_ref, skip_ref)):
        for c in range(4):
            ref[:, 128 * c : 128 * c + 128] = vec[4 * k + c : 4 * k + c + 1]
    for k, ref in enumerate((decay_ref, lam_ref, step_ref)):
        for c, chunk in enumerate(rows_to_lanes(vec[16 + 4 * k : 20 + 4 * k])):
            ref[128 * c : 128 * c + 128] = chunk.reshape(128)
    total = jnp.sum(vec[28:30], axis=1, keepdims=True)
    lane = lane_iota((1, 2))
    rms_ref[...] = jnp.sqrt(jnp.where(lane == 0, total[0:1], total[1:2]) / count_all)


def finish_kernel(
    count_all, got_ref, dre_ref, dim_ref, ore_ref, oim_ref, glu_ref, gbias_ref,
    scale_ref, bias_ref, skip_ref, decay_ref, lam_ref, step_ref, rms_ref, vec_ref, square,
):
    def total(start, count):
        value = got_ref[0, start : start + count, :].astype(F32)
        for z in range(1, GROUPS // 2):
            value = value + got_ref[z, start : start + count, :].astype(F32)
        return value

    for start, first_ref, second_ref in ((0, dre_ref, dim_ref), (96, ore_ref, oim_ref)):
        square[0:96, :] = total(start, 96)
        square[96:128, :] = jnp.zeros((32, 128), F32)
        turned = square[...].T
        first_ref[...] = turned[0:64, 0:96]
        second_ref[...] = turned[64:128, 0:96]
    glu_ref[...] = total(192, 64)
    vec = joined(got_ref[0, 256:320, :])
    for z in range(1, GROUPS // 2):
        vec = vec + joined(got_ref[z, 256:320, :])
    vec_ref[...] = vec
    finish_vectors(vec, count_all, scale_ref, bias_ref, skip_ref, None, decay_ref, lam_ref, step_ref, rms_ref, None)
    place = tensor_pos() * GROUPS + fsdp_pos()
    row = jnp.broadcast_to(vec_ref[pl.ds(12 + place // 8, 1), :], (8, 128))
    gbias_ref[...] = pltpu.roll(row, 128 - 16 * (place % 8), 1)[0:1, 0:16]


TAKES = {
    "pack": 1.5, "norm": 0.3, "first": 1.8, "local_scan": 1.3, "second": 3.0, "readout_grad": 0.7, "back_scan": 1.2, "third": 2.9,
    "finish": 0.7,
}


def call(kernel, outs, args, scratch=(), specs=None, limit=24):
    name = getattr(kernel, "func", kernel).__name__.removesuffix("_kernel")
    return pl.pallas_call(
        kernel,
        out_shape=outs,
        in_specs=specs or [VM] * len(args),
        out_specs=jax.tree.map(lambda _: VM, outs),
        scratch_shapes=list(scratch),
        compiler_params=pltpu.CompilerParams(vmem_limit_bytes=limit << 20),
        cost_estimate=pl.CostEstimate(flops=0, transcendentals=0, bytes_accessed=int(TAKES.get(name, 0.1) * 3.6e6)),
        name=name,
    )(*args)


def tied(value, other):
    return lax.optimization_barrier((value, other))[0]


def swap(value, axis):
    return lax.ppermute(value, axis, [(0, 1), (1, 0)])


def on_device(
    layer_in, grad_out, ln_scale, ln_bias, decay_rate, lam_im, log_dt, in_re, in_im, out_re, out_im, skip, glu_weight, glu_bias, seq_lengths
):
    rows, width = layer_in.shape
    fsdp = lax.axis_size(FSDP)
    blocks = fsdp * 4
    count_all = float(rows * blocks * width)
    fast = fsdp == GROUPS
    if fast:
        row = lambda v: v.reshape(1, -1)
        sent = call(
            pack_kernel,
            sds((GROUPS // 2, 272, 128), BF16),
            (seq_lengths, in_re.T, in_im.T, out_re.T, out_im.T, glu_weight.T, row(ln_scale), row(ln_bias), row(skip), row(glu_bias),
             row(decay_rate), row(lam_im), row(log_dt)),
            [pltpu.VMEM((128, 128), F32), pltpu.VMEM((4, 64, 96), BF16), pltpu.VMEM((64, 128), BF16), pltpu.VMEM((4, 1, 64), BF16),
             pltpu.VMEM((3, 1, 96), F32), pltpu.SMEM(seq_lengths.shape, jnp.int32), pltpu.SemaphoreType.DMA((13,))],
            [HBM] * 13,
            60,
        )
        mine = lax.all_to_all(sent, "fz", 0, 0, tiled=True)
        own_b, own_cw = lax.optimization_barrier((mine[:, :112], mine[:, 112:]))
        side_cw = swap(own_cw, "fx")
        own_b = lax.all_gather(own_b, ("fx", "ty"), axis=0)
        own_b, side_cw = lax.optimization_barrier((own_b, side_cw))
        own_b = own_b.reshape(2, 2, GROUPS // 2, 112, 128)
        g = (own_b, swap(own_b, "tc"))
        own_cw = jnp.stack([own_cw, side_cw])
        far_cw = swap(own_cw, "ty")
    else:
        g, g_cw = gathered(
            ln_scale, ln_bias, decay_rate, lam_im, log_dt, in_re, in_im, out_re, out_im, skip, glu_weight, glu_bias, seq_lengths
        )

    xhat, inverse, normed, wide, feat, starts = call(
        norm_kernel,
        (sds((rows, width)), sds((rows, 128)), sds((rows, width), BF16), sds((2 * rows, 2 * width), BF16), sds((8, width)),
         sds((seq_lengths.shape[0], 128))),
        (layer_in, g[0]),
    )
    v, lane, row_prm, carry = call(
        functools.partial(first_kernel, blocks),
        (sds((2 * rows, 384)), sds((8, 384)), sds((8, 8, 128)), sds((blocks, 8, 128))),
        (wide, starts, *g),
        [pltpu.VMEM((8, 128), F32)],
    )
    came = lax.all_to_all(carry, AXES, 0, 0, tiled=True)
    if fast:
        own_cw, far_cw = tied((own_cw, far_cw), came)
        g_cw = (own_cw, far_cw, swap(own_cw, "tc"), swap(far_cw, "tc"))
    local, power = call(
        local_scan_kernel, (sds((2 * rows, 384)), sds((2 * rows, 384))), (starts, tied(v, came), lane)
    )
    layer_out, state, twice, d_state, enter, d_mixed, act, dlogit, part, carry = call(
        functools.partial(second_kernel, blocks),
        (sds((rows, width), BF16), sds((2 * rows, 384)), sds((2 * rows, 384), BF16), sds((2 * rows, 384)), sds((8, 384)), sds((rows, width)),
         sds((rows, width), BF16), sds((rows, width), BF16), sds((8, width)), sds((blocks, 8, 128))),
        (came, starts, layer_in, grad_out, normed, lane, row_prm, feat, local, power, *g_cw),
        [pltpu.VMEM((8, 128), F32), pltpu.VMEM((width, width), BF16), pltpu.VMEM((GROUPS, 4, 96, 128), BF16)],
    )
    keep_cw, away_cw = call(
        readout_grad_kernel,
        (sds((2, GROUPS, 160, 128), BF16), sds((2, GROUPS, 160, 128), BF16)),
        (twice, d_mixed, act, dlogit),
        [pltpu.VMEM((width, width), BF16)],
    )
    local = call(back_scan_kernel, sds((2 * rows, 384)), (starts, lane, d_state))
    if fast:
        got_cw, local = lax.optimization_barrier((swap(away_cw, "tc"), local))
        stay_cw, leave_cw = call(core_cw_kernel, [sds((GROUPS, 160, 128), BF16)] * 2, (keep_cw, got_cw))
        far_cw = swap(leave_cw, "ty")
        carry = tied(carry, leave_cw)
    came = lax.all_to_all(carry, AXES, 0, 0, tiled=True)
    if fast:
        came, far_cw, stay_cw = lax.optimization_barrier((came, far_cw, stay_cw))
        stay_cw, leave_cw = call(y_cw_kernel, [sds((GROUPS // 2, 160, 128), BF16)] * 2, (stay_cw, far_cw))
        far_cw = swap(leave_cw, "fx")
        came = tied(came, leave_cw)
    grad_in, keep_b, away_b, vec = call(
        third_kernel,
        (sds((rows, width)), sds((2, GROUPS, 96, 128), BF16), sds((2 * GROUPS + 1, 96, 128), BF16), sds((32, 128))),
        (came, starts, grad_out, wide, xhat, inverse, v, lane, row_prm, feat, state, local, enter, d_mixed, part, *g),
        [pltpu.VMEM((8, 128), F32), pltpu.VMEM((2 * rows, 384), BF16)],
    )
    if not fast:
        return reduced(layer_out, grad_in, keep_cw, away_cw, keep_b, away_b, vec, count_all, fsdp, width)
    away_b, far_cw = lax.optimization_barrier((away_b, far_cw))
    got_b = swap(away_b, "tc")
    sent = call(core_b_kernel, sds((4, 448, 128), BF16), (keep_b, vec, got_b))
    got_b = lax.all_to_all(sent, ("fx", "ty"), 0, 0, tiled=True)
    sent = call(last_add_kernel, sds((GROUPS // 2, 320, 128), BF16), (stay_cw, far_cw, got_b))
    got = lax.all_to_all(sent, "fz", 0, 0, tiled=True)
    d_re, d_im, d_ore, d_oim, d_glu, d_gbias, d_scale, d_bias, d_skip, g_decay, g_lam, g_step, rms = call(
        functools.partial(finish_kernel, count_all),
        (*[sds((64, 96))] * 4, sds((64, 128)), sds((1, 16)), *[sds((1, 512))] * 3, *[sds((384,))] * 3, sds((1, 2))),
        (got,),
        [pltpu.VMEM((32, 128), F32), pltpu.VMEM((128, 128), F32)],
    )
    flat = lambda value: value.reshape(-1)
    return (
        layer_out, grad_in, flat(d_scale), flat(d_bias), g_decay, g_lam, g_step, d_re.T, d_im.T, d_ore.T, d_oim.T,
        flat(d_skip), d_glu.T, flat(d_gbias), flat(rms),
    )


def gathered(ln_scale, ln_bias, decay_rate, lam_im, log_dt, in_re, in_im, out_re, out_im, skip, glu_weight, glu_bias, seq_lengths):
    tens = tensor_pos()
    full = lambda value, axis: lax.all_gather(value, FSDP, axis=axis, tiled=True)

    def pair(first, second):
        halves = jnp.stack([first.reshape(-1, GROUPS, 64), second.reshape(-1, GROUPS, 64)], axis=2)
        return halves.reshape(-1, GROUPS, 128).swapaxes(0, 1)

    gate = lax.dynamic_slice_in_dim(full(glu_weight, 1), tens * 128, 128, 0).T.reshape(GROUPS, 64, 128)
    vectors = [pair(full(ln_scale, 0)[None], full(ln_bias, 0)[None]), pair(full(skip, 0)[None], full(glu_bias, 0)[None])]
    for value in (decay_rate, lam_im, log_dt):
        value = jnp.pad(value, (0, 32))
        for _ in range(3):
            piece = lax.reduce_precision(value, 8, 7)
            value = value - piece
            vectors.append(jnp.broadcast_to(piece.astype(BF16)[None, None], (GROUPS, 1, 128)))
    starts = jnp.cumsum(seq_lengths) - seq_lengths
    for value in (starts >> 8, starts & 255):
        value = jnp.pad(value, (0, 128 - value.shape[0])).astype(BF16)
        vectors.append(jnp.broadcast_to(value[None, None], (GROUPS, 1, 128)))
    vectors.append(jnp.zeros((GROUPS, 3, 128), BF16))
    packet = jnp.concatenate(
        [pair(full(in_re, 1), full(in_im, 1)), *vectors, pair(full(out_re, 1), full(out_im, 1)), gate],
        axis=1,
    )
    everyone = lax.all_gather(packet, TENSOR, axis=0).reshape(2, 2, GROUPS // 2, 2, 272, 128)
    x, y, core = (lax.axis_index(axis) for axis in ("fx", "ty", "tc"))
    of_core = lambda c: lax.dynamic_index_in_dim(everyone, c, 1, keepdims=False)
    g = [of_core(core ^ i).transpose(2, 0, 1, 3, 4)[:, :, :, :112] for i in range(2)]
    g_cw = []
    for i in range(4):
        picked = lax.dynamic_index_in_dim(of_core(core ^ (i // 2)), y ^ (i % 2), 0, keepdims=False)
        g_cw.append(jnp.stack([lax.dynamic_index_in_dim(picked, x ^ j, 1, keepdims=False)[:, 112:] for j in range(2)]))
    return g, g_cw


def reduced(layer_out, grad_in, keep_cw, away_cw, keep_b, away_b, vec, count_all, fsdp, width):
    tens, core = tensor_pos(), lax.axis_index("tc")
    blocks_b = away_b[: 2 * GROUPS].reshape(2, GROUPS, 96, 128)

    def canonical(keep, away):
        both = jnp.stack([keep, away]).astype(F32)
        both = jnp.concatenate([lax.dynamic_index_in_dim(both, core ^ i, 0) for i in range(2)], axis=0)
        return both.swapaxes(0, 1).reshape(4, *keep.shape[1:])

    def natural(keep, away):
        halves = canonical(keep, away).reshape(4, GROUPS, -1, 2, 64).transpose(3, 0, 2, 1, 4)
        return halves[0].reshape(-1, width), halves[1].reshape(-1, width)

    def scattered(value):
        value = lax.psum_scatter(value, TENSOR, scatter_dimension=0, tiled=True)
        return lax.psum_scatter(value, FSDP, scatter_dimension=1, tiled=True)

    d_re, d_im = natural(keep_b, blocks_b)
    d_ore, d_oim = natural(keep_cw[:, :, :96], away_cw[:, :, :96])
    d_glu = canonical(keep_cw[:, :, 96:], away_cw[:, :, 96:]).reshape(4, width, 128).swapaxes(1, 2).reshape(-1, width)
    vec = lax.psum(vec, AXES)
    states = lambda k: vec[16 + 4 * k : 20 + 4 * k, :96].reshape(-1)
    own = width // (4 * fsdp)
    place = tens * fsdp + fsdp_pos()
    d_gbias = lax.dynamic_slice_in_dim(vec[12:16].reshape(-1), place * own, own, 0)
    rms = jnp.sqrt(jnp.sum(vec[28:30], axis=1) / count_all)
    return (
        layer_out, grad_in, vec[0:4].reshape(-1), vec[4:8].reshape(-1), states(0), states(1), states(2), scattered(d_re), scattered(d_im),
        scattered(d_ore), scattered(d_oim), vec[8:12].reshape(-1), scattered(d_glu), d_gbias, rms,
    )


def solution(mesh):
    shape = (mesh.shape["fsdp"] // 2, 2, mesh.shape["tensor"] // 2, 2)
    split = Mesh(mesh.devices.reshape(shape), AXES)
    tokens, matrix = P(AXES, None), P(TENSOR, FSDP)
    return jax.shard_map(
        on_device,
        mesh=split,
        in_specs=(
            tokens, tokens, P(FSDP), P(FSDP), P(TENSOR), P(TENSOR), P(TENSOR), matrix, matrix, matrix, matrix,
            P(FSDP), P(None, FSDP), P(FSDP), P(),
        ),
        out_specs=(
            tokens, tokens, P(), P(), P(), P(), P(), matrix, matrix, matrix, matrix, P(), matrix, P((*TENSOR, *FSDP)), P(),
        ),
        check_vma=False,
    )
```

time: 115 us -> 95.7 us (0.83)
  waiting for transfers between devices: 27.3 us -> 15.3 us
  local copies, waits for them, and re-layouts: 6.07 us -> 0.03 us
  blocking collectives: 65.2 us -> 59.8 us
  starting transfers between devices: 3.09 us -> 7.78 us
  other arithmetic: 1.79 us -> 0.03 us
  Pallas kernels: 10 us -> 11.5 us
    ppermute x7 -> x9, waiting for transfers between devices: 27.3 us -> 12.1 us  [swap(): return lax.ppermute(value, axis, [(0, 1), (1, 0)])]
    all_to_all x2 -> x1, blocking collectives: 22 us -> 11.2 us  [on_device(): came = lax.all_to_all(carry, AXES, 0, 0, tiled=True)]
    all_gather x0 -> x1, blocking collectives: none -> 9.96 us  [on_device(): own_b = lax.all_gather(own_b, ('fx', 'ty'), axis=0)]
    unnamed x38 -> x4, local copies, waits for them, and re-layouts: 6.07 us -> 0.01 us
    all_to_all x2 -> x3, blocking collectives: 43.2 us -> 38.7 us  [the longest x1 15.6 us: on_device(): mine = lax.all_to_all(sent, 'fz', 0, 0, tiled=True)]
    all_to_all x0 -> x1, waiting for transfers between devices: none -> 3.22 us  [on_device(): came = lax.all_to_all(carry, AXES, 0, 0, tiled=True)]
    all_to_all x0 -> x1, starting transfers between devices: none -> 2.58 us  [on_device(): came = lax.all_to_all(carry, AXES, 0, 0, tiled=True)]
    ppermute x7 -> x9, starting transfers between devices: 3.09 us -> 5.2 us  [swap(): return lax.ppermute(value, axis, [(0, 1), (1, 0)])]
  transfers between devices with their start and end apart: 7 -> 10, of which waited for: 4 -> 7; matrix products, arithmetic and copies ran while one was open for 0% -> 0% of each run, Pallas kernels for 3% -> 6%
where the time goes in v2:
time: 95.7 us; the launch traced here: 95.3 us
  blocking collectives  59.8 us (62%)
  waiting for transfers between devices  15.3 us (16%)
  Pallas kernels  11.5 us (12%)
  starting transfers between devices  7.78 us (8%)
    all_to_all x1, blocking collectives, on_device(): mine = lax.all_to_all(sent, 'fz', 0, 0, tiled=True)  15.6 us
    all_to_all x1, blocking collectives, on_device(): got = lax.all_to_all(sent, 'fz', 0, 0, tiled=True)  12.2 us
    ppermute x9, waiting for transfers between devices, swap(): return lax.ppermute(value, axis, [(0, 1), (1, 0)])  12.1 us
    pallas_call x13, Pallas kernels, call(): pl.pallas_call(kernel, out_shape=outs, in_specs=specs or [VM] * len(args)...  11.5 us
    all_to_all x1, blocking collectives, on_device(): came = lax.all_to_all(carry, AXES, 0, 0, tiled=True)  11.2 us
    all_to_all x1, blocking collectives, on_device(): got_b = lax.all_to_all(sent, ('fx', 'ty'), 0, 0, tiled=True)  11 us
    all_gather x1, blocking collectives, on_device(): own_b = lax.all_gather(own_b, ('fx', 'ty'), axis=0)  9.96 us
    ppermute x9, starting transfers between devices, swap(): return lax.ppermute(value, axis, [(0, 1), (1, 0)])  5.2 us
  transfers between devices with their start and end apart: 10, of which 7 were waited for; matrix products, arithmetic and copies ran while one was open for 0% of the time, Pallas kernels for 6%

profile of v2, /device:TPU:0, one launch (start us, length us, event | category | flops | bytes accessed | tf_op | source)
XLA Modules:
  0.0 95.3 jit_solution(6416798799138050321)
XLA Ops:
  0.7 1.8 %pack.1 = bf16[4,272,128]{2,1,0:T(8,128)(2,1)} custom-call(s32[4]{0:T(128)} %refs_0_.1, bf16[64,96]{1,0:T(8,128)(2,1)} %bitcast.33, bf16[64,96]{1,0:T(8,128)(2,1)} %bitcast.34, bf16[64,96]{1,0:T(8,128)(2,1)} %bitcast.35, bf16[64,96]{1,0:T(8,128)(2,1)} %bitcast.36, bf16[64,512]{1,0:T(8,128)(2,1)} %bitcast.32, bf16[1,64]{1,0:T(2,128)(2,1)} %bitcast.37, ...), custom_call_target="tpu_custom_call" | custom-call | bytes 5400000 | tf_op jit(solution)/shard_map/pack/pallas_call | solution.py:666
  2.4 15.6 %all_to_all.25 = bf16[4,272,128]{2,1,0:T(8,128)(2,1)S(1)} all-to-all(bf16[4,272,128]{2,1,0:T(8,128)(2,1)} %pack.1), channel_id=1, replica_groups=mesh['fz'=4,'fx'=2,'ty'=2,'tc'=2] {'fz'}, dimensions={0} | all-to-all | bytes 557056 | tf_op jit(solution)/shard_map/all_to_all | solution.py:706
  18.0 1.6 %collective-permute-start = (bf16[4,160,128]{2,1,0:T(8,128)(2,1)S(1)}, bf16[4,160,128]{2,1,0:T(8,128)(2,1)S(1)}, u32[]{:S(2)}, u32[]{:S(2)}) collective-permute-start(bf16[4,160,128]{2,1,0:T(8,128)(2,1)S(1)} %slice.9), channel_id=1, source_target_pairs={{0,4},{4,0},{1,5},{5,1},{2,6},{6,2},{3,7},{7,3},{8,12},{12,8},{9,1... | collective-permute-start | bytes 491528 | tf_op jit(solution)/shard_map/ppermute | solution.py:683
  19.6 10.0 %all-gather = bf16[16,112,128]{2,1,0:T(8,128)(2,1)S(1)} all-gather(bf16[4,112,128]{2,1,0:T(8,128)(2,1)S(1)} %slice.8), channel_id=2, replica_groups=mesh['fz'=4,'fx'=2,'ty'=2,'tc'=2] {'fx','ty'}, dimensions={0}, use_global_device_ids=true | all-gather | bytes 573440 | tf_op jit(solution)/shard_map/all_gather | solution.py:709
  29.7 1.5 %collective-permute-start.2 = (bf16[2,4,160,128]{3,2,1,0:T(8,128)(2,1)S(1)}, bf16[2,4,160,128]{3,2,1,0:T(8,128)(2,1)S(1)}, u32[]{:S(2)}, u32[]{:S(2)}) collective-permute-start(bf16[2,4,160,128]{3,2,1,0:T(8,128)(2,1)S(1)} %pad_maximum_fusion.g0), channel_id=1, source_target_pairs={{0,2},{2,0},{1,3},{3,1},{4,6},{6,4},{5,7},{7,5},{8,10},{10,8},{9,1... | collective-permute-start | bytes 983048 | tf_op jit(solution)/shard_map/ppermute | solution.py:683
  31.5 1.3 %first.1 = (f32[256,384]{1,0:T(8,128)S(1)}, f32[8,384]{1,0:T(8,128)S(1)}, f32[8,8,128]{2,1,0:T(8,128)S(1)}, f32[32,8,128]{2,1,0:T(8,128)}) custom-call(bf16[256,1024]{1,0:T(8,128)(2,1)S(1)} %get-tuple-element.79.wide_ref, f32[4,128]{1,0:T(4,128)S(1)} %get-tuple-element.80.start_ref, bf16[2,2,4,112,128]{4,3,2,1,0:T(8,128)(2,1)S(1)} %bitcast.28, ...), custom_call_target="tpu_custom_call" | custom-call | bytes 6480000 | tf_op jit(solution)/shard_map/first/pallas_call | solution.py:666
  32.8 2.6 %all-to-all-start.1 = ((f32[32,8,128]{2,1,0:T(8,128)}), f32[32,8,128]{2,1,0:T(8,128)S(1)}, u32[]{:S(2)}, u32[]{:S(2)}) async-start(f32[32,8,128]{2,1,0:T(8,128)} %get-tuple-element.81), calls=%async_computation.1 | async-start | bytes 262144 | tf_op jit(solution)/shard_map/all_to_all | solution.py:732
  35.4 5.0 %collective-permute-done.2.g1 = bf16[2,4,160,128]{3,2,1,0:T(8,128)(2,1)S(1)} collective-permute-done((bf16[2,4,160,128]{3,2,1,0:T(8,128)(2,1)S(1)}, bf16[2,4,160,128]{3,2,1,0:T(8,128)(2,1)S(1)}, u32[]{:S(2)}, u32[]{:S(2)}) %collective-permute-start.2) | collective-permute-done | bytes 327712 | tf_op jit(solution)/shard_map/ppermute | solution.py:683
  40.4 3.2 %all-to-all-done.1.recv_ref = f32[32,8,128]{2,1,0:T(8,128)S(1)} async-done(((f32[32,8,128]{2,1,0:T(8,128)}), f32[32,8,128]{2,1,0:T(8,128)S(1)}, u32[]{:S(2)}, u32[]{:S(2)}) %all-to-all-start.1) | async-done | bytes 131104 | tf_op jit(solution)/shard_map/all_to_all | solution.py:732
  44.1 0.8 local_scan.1
  45.2 0.5 collective-permute-done.4.g3
  45.7 2.4 %second.1 = (bf16[128,512]{1,0:T(8,128)(2,1)}, f32[256,384]{1,0:T(8,128)S(1)}, bf16[256,384]{1,0:T(8,128)(2,1)S(1)}, f32[256,384]{1,0:T(8,128)S(1)}, f32[8,384]{...) custom-call(f32[32,8,128]{2,1,0:T(8,128)S(1)} %all-to-all-done.1.rec, ...), custom_call_target="tpu_custom_call" | custom-call | bytes 10800000 | tf_op jit(solution)/shard_map/second/pallas_call | solution.py:666
  48.1 0.7 readout_grad.1
  49.2 0.6 back_scan.1.local_ref
  49.8 1.2 %collective-permute-done.5.got_ref = bf16[2,8,160,128]{3,2,1,0:T(8,128)(2,1)S(1)} collective-permute-done((bf16[2,8,160,128]{3,2,1,0:T(8,128)(2,1)S(1)}, bf16[2,8,160,128]{3,2,1,0:T(8,128)(2,1)S(1)}, u32[]{:S(2)}, u32[]{:S(2)}) %collective-permute-start.5) | collective-permute-done | bytes 655392 | tf_op jit(solution)/shard_map/ppermute | solution.py:683
  51.2 0.5 collective-permute-start.6
  51.7 11.2 %all_to_all.26.recv_ref = f32[32,8,128]{2,1,0:T(8,128)S(1)} all-to-all(f32[32,8,128]{2,1,0:T(8,128)S(1)} %get-tuple-element.104), channel_id=1, replica_groups=mesh['fz'=4,'fx'=2,'ty'=2,'tc'=2] {'fz','fx','ty','tc'}, dimensions={0} | all-to-all | bytes 262144 | tf_op jit(solution)/shard_map/all_to_all | solution.py:758
  63.0 0.7 collective-permute-start.7
  63.7 2.4 %third.1 = (f32[128,512]{1,0:T(8,128)}, bf16[2,8,96,128]{3,2,1,0:T(8,128)(2,1)S(1)}, bf16[17,96,128]{2,1,0:T(8,128)(2,1)S(1)}, f32[32,128]{1,0:T(8,128)S(1)}) custom-call(f32[32,8,128]{2,1,0:T(8,128)S(1)} %all_to_all.26.recv_ref, f32[4,128]{1,0:T(4,128)S(1)} %get-tuple-element.80.start_ref, bf16[128,512]{1,0:T(8,128)(2,1)S(1)} %copy-done, ...), custom_call_target="tpu_custom_call" | custom-call | bytes 10440000 | tf_op jit(solution)/shard_map/third/pallas_call | solution.py:666
  66.1 3.3 %collective-permute-done.7.gotcw_ref = bf16[4,160,128]{2,1,0:T(8,128)(2,1)S(1)} collective-permute-done((bf16[4,160,128]{2,1,0:T(8,128)(2,1)S(1)}, bf16[4,160,128]{2,1,0:T(8,128)(2,1)S(1)}, u32[]{:S(2)}, u32[]{:S(2)}) %collective-permute-start.7) | collective-permute-done | bytes 163872 | tf_op jit(solution)/shard_map/ppermute | solution.py:683
  69.4 1.8 %collective-permute-done.8.got_ref = bf16[17,96,128]{2,1,0:T(8,128)(2,1)S(1)} collective-permute-done((bf16[17,96,128]{2,1,0:T(8,128)(2,1)S(1)}, bf16[17,96,128]{2,1,0:T(8,128)(2,1)S(1)}, u32[]{:S(2)}, u32[]{:S(2)}) %collective-permute-start.8) | collective-permute-done | bytes 417824 | tf_op jit(solution)/shard_map/ppermute | solution.py:683
  71.2 11.0 %all_to_all.27.gotb_ref = bf16[4,448,128]{2,1,0:T(8,128)(2,1)S(1)} all-to-all(bf16[4,448,128]{2,1,0:T(8,128)(2,1)S(1)} %core_b.1), channel_id=1, replica_groups=mesh['fz'=4,'fx'=2,'ty'=2,'tc'=2] {'fx','ty'}, dimensions={0} | all-to-all | bytes 917504 | tf_op jit(solution)/shard_map/all_to_all | solution.py:775
  82.3 12.2 %all_to_all.28.got_ref = bf16[4,320,128]{2,1,0:T(8,128)(2,1)S(1)} all-to-all(bf16[4,320,128]{2,1,0:T(8,128)(2,1)S(1)} %last_add.1), channel_id=1, replica_groups=mesh['fz'=4,'fx'=2,'ty'=2,'tc'=2] {'fz'}, dimensions={0} | all-to-all | bytes 655360 | tf_op jit(solution)/shard_map/all_to_all | solution.py:777
  94.5 0.8 finish.1
  (21 shorter events, 2.1 us)
Async XLA Ops:
  18.0 11.5 %collective-permute-start = (bf16[4,160,128]{2,1,0:T(8,128)(2,1)S(1)}, bf16[4,160,128]{2,1,0:T(8,128)(2,1)S(1)}, u32[]{:S(2)}, u32[]{:S(2)}) collective-permute-start(bf16[4,160,128]{2,1,0:T(8,128)(2,1)S(1)} %slice.9), channel_id=1, source_target_pairs={{0,4},{4,0},{1,5},{5,1},{2,6},{6,2},{3,7},{7,3},{8,12},{12,8},{9,1... | collective-permute-start | bytes 491528 | tf_op jit(solution)/shard_map/ppermute | solution.py:683
  29.5 2.0 %collective-permute-start.1 = (bf16[2,2,4,112,128]{4,3,2,1,0:T(8,128)(2,1)S(1)}, bf16[2,2,4,112,128]{4,3,2,1,0:T(8,128)(2,1)S(1)}, u32[]{:S(2)}, u32[]{:S(2)}) collective-permute-start(bf16[2,2,4,112,128]{4,3,2,1,0:T(8,128)(2,1)S(1)} %bitcast.26), channel_id=1, source_target_pairs={{0,1},{1,0},{2,3},{3,2},{4,5},{5,4},{6,7},{7,6},{8,9},{9,8},{10,11... | collective-permute-start | bytes 1376264 | tf_op jit(solution)/shard_map/ppermute | solution.py:683
  29.6 1.5 %copy-start.1 = (bf16[128,512]{1,0:T(8,128)(2,1)S(1)}, bf16[128,512]{1,0:T(8,128)(2,1)}, u32[]{:S(2)}) copy-start(bf16[128,512]{1,0:T(8,128)(2,1)} %x_ref.3) | copy-start | bytes 393220
  29.7 10.7 %collective-permute-start.2 = (bf16[2,4,160,128]{3,2,1,0:T(8,128)(2,1)S(1)}, bf16[2,4,160,128]{3,2,1,0:T(8,128)(2,1)S(1)}, u32[]{:S(2)}, u32[]{:S(2)}) collective-permute-start(bf16[2,4,160,128]{3,2,1,0:T(8,128)(2,1)S(1)} %pad_maximum_fusion.g0), channel_id=1, source_target_pairs={{0,2},{2,0},{1,3},{3,1},{4,6},{6,4},{5,7},{7,5},{8,10},{10,8},{9,1... | collective-permute-start | bytes 983048 | tf_op jit(solution)/shard_map/ppermute | solution.py:683
  32.8 10.8 %all-to-all-start.1 = ((f32[32,8,128]{2,1,0:T(8,128)}), f32[32,8,128]{2,1,0:T(8,128)S(1)}, u32[]{:S(2)}, u32[]{:S(2)}) async-start(f32[32,8,128]{2,1,0:T(8,128)} %get-tuple-element.81), calls=%async_computation.1 | async-start | bytes 262144 | tf_op jit(solution)/shard_map/all_to_all | solution.py:732
  43.6 1.6 %collective-permute-start.3 = (bf16[2,4,160,128]{3,2,1,0:T(8,128)(2,1)S(1)}, bf16[2,4,160,128]{3,2,1,0:T(8,128)(2,1)S(1)}, u32[]{:S(2)}, u32[]{:S(2)}) collective-permute-start(bf16[2,4,160,128]{3,2,1,0:T(8,128)(2,1)S(1)} %pad_maximum_fusion.g0), channel_id=1, source_target_pairs={{0,1},{1,0},{2,3},{3,2},{4,5},{5,4},{6,7},{7,6},{8,9},{9,8},{10,11... | collective-permute-start | bytes 983048 | tf_op jit(solution)/shard_map/ppermute | solution.py:683
  43.8 1.9 %collective-permute-start.4 = (bf16[2,4,160,128]{3,2,1,0:T(8,128)(2,1)S(1)}, bf16[2,4,160,128]{3,2,1,0:T(8,128)(2,1)S(1)}, u32[]{:S(2)}, u32[]{:S(2)}) collective-permute-start(bf16[2,4,160,128]{3,2,1,0:T(8,128)(2,1)S(1)} %collective-permute-done.2.g1), channel_id=1, source_target_pairs={{0,1},{1,0},{2,3},{3,2},{4,5},{5,4},{6,7},{7,6},{8,9},{9,8},{10,11... | collective-permute-start | bytes 983048 | tf_op jit(solution)/shard_map/ppermute | solution.py:683
  44.1 1.6 %copy-start = (bf16[128,512]{1,0:T(8,128)(2,1)S(1)}, bf16[128,512]{1,0:T(8,128)(2,1)}, u32[]{:S(2)}) copy-start(bf16[128,512]{1,0:T(8,128)(2,1)} %up_ref.3) | copy-start | bytes 393220
  48.9 2.2 %collective-permute-start.5 = (bf16[2,8,160,128]{3,2,1,0:T(8,128)(2,1)S(1)}, bf16[2,8,160,128]{3,2,1,0:T(8,128)(2,1)S(1)}, u32[]{:S(2)}, u32[]{:S(2)}) collective-permute-start(bf16[2,8,160,128]{3,2,1,0:T(8,128)(2,1)S(1)} %get-tuple-element.100), channel_id=1, source_target_pairs={{0,1},{1,0},{2,3},{3,2},{4,5},{5,4},{6,7},{7,6},{8,9},{9,8},{10,11... | collective-permute-start | bytes 1966088 | tf_op jit(solution)/shard_map/ppermute | solution.py:683
  51.2 11.7 %collective-permute-start.6 = (bf16[8,160,128]{2,1,0:T(8,128)(2,1)S(1)}, bf16[8,160,128]{2,1,0:T(8,128)(2,1)S(1)}, u32[]{:S(2)}, u32[]{:S(2)}) collective-permute-start(bf16[8,160,128]{2,1,0:T(8,128)(2,1)S(1)} %get-tuple-element.103), channel_id=1, source_target_pairs={{0,2},{2,0},{1,3},{3,1},{4,6},{6,4},{5,7},{7,5},{8,10},{10,8},{9,1... | collective-permute-start | bytes 983048 | tf_op jit(solution)/shard_map/ppermute | solution.py:683
  63.0 6.4 %collective-permute-start.7 = (bf16[4,160,128]{2,1,0:T(8,128)(2,1)S(1)}, bf16[4,160,128]{2,1,0:T(8,128)(2,1)S(1)}, u32[]{:S(2)}, u32[]{:S(2)}) collective-permute-start(bf16[4,160,128]{2,1,0:T(8,128)(2,1)S(1)} %get-tuple-element.109), channel_id=1, source_target_pairs={{0,4},{4,0},{1,5},{5,1},{2,6},{6,2},{3,7},{7,3},{8,12},{12,8},{9,1... | collective-permute-start | bytes 491528 | tf_op jit(solution)/shard_map/ppermute | solution.py:683
  69.4 1.8 %collective-permute-start.8 = (bf16[17,96,128]{2,1,0:T(8,128)(2,1)S(1)}, bf16[17,96,128]{2,1,0:T(8,128)(2,1)S(1)}, u32[]{:S(2)}, u32[]{:S(2)}) collective-permute-start(bf16[17,96,128]{2,1,0:T(8,128)(2,1)S(1)} %get-tuple-element.123), channel_id=1, source_target_pairs={{0,1},{1,0},{2,3},{3,2},{4,5},{5,4},{6,7},{7,6},{8,9},{9,8},{10,11... | collective-permute-start | bytes 1253384 | tf_op jit(solution)/shard_map/ppermute | solution.py:683

commit v3 on v2

--- a/solution.py
+++ b/solution.py
@@ -42,12 +42,18 @@
 TN = ((0,), (0,))
 
 
+def flipped():
+    return lax.axis_index("fx") == 1
+
+
 def spread(x):
     lo = low_half((x.shape[0], 128))
+    flip = flipped()
     upper, lower = [], []
     for c in range(x.shape[1] // 128):
         xc = x[:, 128 * c : 128 * c + 128]
         turned = pltpu.roll(xc, 64, 1)
+        xc, turned = jnp.where(flip, turned, xc), jnp.where(flip, xc, turned)
         upper += [jnp.where(lo, xc, 0.0).astype(BF16), jnp.where(lo, turned, 0.0).astype(BF16)]
         lower += [jnp.where(lo, 0.0, turned).astype(BF16), jnp.where(lo, 0.0, xc).astype(BF16)]
     return jnp.concatenate(
@@ -58,16 +64,18 @@
 def folded(pq):
     rows = pq.shape[0] // 2
     lo = low_half((rows, 128))
+    flip = flipped()
     out = []
     for c in range(pq.shape[1] // 256):
         p0, p1 = pq[:rows, 256 * c : 256 * c + 128], pq[:rows, 256 * c + 128 : 256 * c + 256]
         q0, q1 = pq[rows:, 256 * c : 256 * c + 128], pq[rows:, 256 * c + 128 : 256 * c + 256]
-        out.append(jnp.where(lo, p0 + pltpu.roll(q0, 64, 1), pltpu.roll(p1, 64, 1) + q1))
+        even = jnp.where(lo, p0, q1) + jnp.where(lo, pltpu.roll(q0, 64, 1), pltpu.roll(p1, 64, 1))
+        out.append(jnp.where(flip, pltpu.roll(even, 64, 1), even))
     return jnp.concatenate(out, axis=1)
 
 
 def slot_pos(k):
-    return (k % 2) * 2 + (lax.axis_index("tc") ^ (k // 2))
+    return tensor_pos() ^ ((k % 2) * 2 + k // 2)
 
 
 def piece(refs, k, f, start, count):
@@ -80,10 +88,12 @@
 
 def feature_rows(refs, row):
     lo = low_half((8, 128))
+    flip = flipped()
     first, second = [], []
     for c in range(GROUPS // 2):
         a = jnp.broadcast_to(piece(refs, 0, 2 * c, row, 1).astype(F32), (8, 128))
         b = jnp.broadcast_to(piece(refs, 0, 2 * c + 1, row, 1).astype(F32), (8, 128))
+        a, b = jnp.where(flip, b, a), jnp.where(flip, a, b)
         first.append(jnp.where(lo, a, pltpu.roll(b, 64, 1)))
         second.append(jnp.where(lo, pltpu.roll(a, 64, 1), b))
     return jnp.concatenate(first, axis=1)[:1], jnp.concatenate(second, axis=1)[:1]
@@ -231,18 +241,20 @@
     return rows_to_lanes(jnp.concatenate([*rows, jnp.zeros((4, 128), F32)], axis=0))
 
 
-def norm_kernel(x_ref, g_ref, xhat_ref, inv_ref, normed_ref, wide_ref, feat_ref, start_ref):
+def standardize_kernel(x_ref, xhat_ref, inv_ref):
     rows, width = x_ref.shape
     x = x_ref[...].astype(F32)
     centered = x - jnp.sum(x, axis=1, keepdims=True) / width
     inverse = lax.rsqrt(jnp.sum(centered * centered, axis=1, keepdims=True) / width + 1e-05)
-    xhat = centered * inverse
-    xhat_ref[...] = xhat
+    xhat_ref[...] = centered * inverse
     inv_ref[...] = jnp.broadcast_to(inverse, (rows, 128))
+
+
+def norm_kernel(xhat_ref, g_ref, normed_ref, wide_ref, feat_ref, start_ref):
     scale, bias = feature_rows((g_ref,), VEC)
     feat_ref[0:1] = scale
     feat_ref[1:2], feat_ref[2:3] = feature_rows((g_ref,), VEC + 1)
-    normed = (xhat * scale + bias).astype(BF16)
+    normed = (xhat_ref[...] * scale + bias).astype(BF16)
     normed_ref[...] = normed
     wide_ref[...] = spread(normed.astype(F32))
     upper, lower = (piece((g_ref,), 0, 0, VEC + 11 + k, 1).astype(F32) for k in range(2))
@@ -299,22 +311,28 @@
         send_ref[d] = packet
 
 
-def local_scan_kernel(start_ref, v_ref, lane_ref, local_ref, power_ref):
+def states_kernel(recv_ref, start_ref, v_ref, lane_ref, row_ref, state_ref, twice_ref, enter_ref, scratch):
     rows = v_ref.shape[0] // 2
-    count = starts_until(offsets_of(start_ref), block_pos() * rows, rows)
+    offsets = offsets_of(start_ref)
+    base = block_pos() * rows
+    count = starts_until(offsets, base, rows)
+    enter = carried(recv_ref, row_ref, offsets, rows, False, scratch)
+    keep_first = no_start(offsets, base, 1)
+    top = lax.broadcasted_iota(jnp.int32, (rows, 128), 0) == 0
     for c in range(3):
         lanes = slice(128 * c, 128 * c + 128)
         a = (lane_ref[0:1, lanes], lane_ref[1:2, lanes])
         b = (lane_ref[2:3, lanes], lane_ref[3:4, lanes])
-        state = scan_chunk(cmul(b, (v_ref[:rows, lanes], v_ref[rows:, lanes])), a, count, False)
-        local_ref[:rows, lanes] = state[0]
-        local_ref[rows:, lanes] = state[1]
-        eight, power = eighth_powers(a, 0)
-        for blk in range(rows // 8):
-            power_ref[8 * blk : 8 * blk + 8, lanes] = power[0]
-            power_ref[rows + 8 * blk : rows + 8 * blk + 8, lanes] = power[1]
-            if blk < rows // 8 - 1:
-                power = cmul(power, eight)
+        drive = cmul(b, (v_ref[:rows, lanes], v_ref[rows:, lanes]))
+        came = cmul((a[0] * keep_first, a[1] * keep_first), (enter[0][c], enter[1][c]))
+        drive = (drive[0] + jnp.where(top, came[0], 0.0), drive[1] + jnp.where(top, came[1], 0.0))
+        state = scan_chunk(drive, a, count, False)
+        state_ref[:rows, lanes] = state[0]
+        state_ref[rows:, lanes] = state[1]
+        twice_ref[:rows, lanes] = state[0].astype(BF16) * 2
+        twice_ref[rows:, lanes] = state[1].astype(BF16) * -2
+        enter_ref[0:1, lanes] = enter[0][c]
+        enter_ref[1:2, lanes] = enter[1][c]
 
 
 def eighth_powers(a, top):
@@ -376,38 +394,20 @@
 
 
 def second_kernel(
-    blocks, recv_ref, start_ref, x_ref, up_ref, normed_ref, lane_ref, row_ref, feat_ref, local_ref, power_ref, g0, g1, g2, g3,
-    out_ref, state_ref, twice_ref, dstate_ref, enter_ref, dmixed_ref, act_ref, dlogit_ref, part_ref, send_ref,
-    scratch, gate_ref, c_ref,
+    blocks, twice_ref, start_ref, up_ref, normed_ref, lane_ref, feat_ref, g0, g1, g2, g3,
+    branch_ref, dstate_ref, dmixed_ref, act_ref, dlogit_ref, send_ref, scratch, gate_ref,
 ):
-    rows, width = x_ref.shape
-    x_pos, y_pos = lax.axis_index("fx"), lax.axis_index("ty")
+    rows, width = up_ref.shape
     offsets = offsets_of(start_ref)
-    base = block_pos() * rows
-    count = starts_until(offsets, base, rows)
-    for i, ref in enumerate((g0, g1, g2, g3)):
-        y = y_pos ^ (i % 2)
-        tens = y * 2 + (lax.axis_index("tc") ^ (i // 2))
-        lanes = pl.ds(pl.multiple_of(tens * 128, 128), 128)
-        for j in range(2):
-            for z in range(GROUPS // 2):
-                f = z * 2 + (x_pos ^ j)
-                c_ref[f, (i // 2) * 2 + y] = ref[j, z, 0:96, :]
-                gate_ref[pl.ds(pl.multiple_of(f * 64, 64), 64), lanes] = ref[j, z, 96:160, :]
-    enter = carried(recv_ref, row_ref, offsets, rows, False, scratch)
+    count = starts_until(offsets, block_pos() * rows, rows)
+    slots = (g0, g1, g2, g3)
+    for k in range(4):
+        lanes = pl.ds(pl.multiple_of(slot_pos(k) * 128, 128), 128)
+        for f in range(GROUPS):
+            place = (f // 2) * 2 + (lax.axis_index("fx") ^ (f % 2))
+            gate_ref[pl.ds(pl.multiple_of(place * 64, 64), 64), lanes] = slots[k][f % 2, f // 2, 96:160, :]
     head = jnp.where(count == 0.0, 1.0, 0.0)
-    for c in range(3):
-        lanes = slice(128 * c, 128 * c + 128)
-        power = (power_ref[:rows, lanes] * head, power_ref[rows:, lanes] * head)
-        came = cmul(power, (enter[0][c], enter[1][c]))
-        state = (local_ref[:rows, lanes] + came[0], local_ref[rows:, lanes] + came[1])
-        state_ref[:rows, lanes] = state[0]
-        state_ref[rows:, lanes] = state[1]
-        twice_ref[:rows, lanes] = state[0].astype(BF16) * 2
-        twice_ref[rows:, lanes] = state[1].astype(BF16) * -2
-        enter_ref[0:1, lanes] = enter[0][c]
-        enter_ref[1:2, lanes] = enter[1][c]
-    readout = weights(lambda k, f: c_ref[f, k])
+    readout = weights(lambda k, f: slots[k][f % 2, f // 2, 0:96, :])
     scale, skip, gate_bias = (feat_ref[k : k + 1] for k in range(3))
     normed = normed_ref[...].astype(F32)
     mixed = folded(dot(twice_ref[...], readout, NN)) + skip * normed
@@ -418,9 +418,7 @@
     w_gate = gate_ref[...]
     logit = dot(act_low, w_gate, NN) + gate_bias
     gate = 1.0 / (1.0 + jnp.exp(-logit))
-    branch = (act * gate).astype(BF16).astype(F32)
-    x = x_ref[...].astype(F32)
-    out_ref[...] = (x + branch).astype(BF16)
+    branch_ref[...] = (act * gate).astype(BF16)
     up = up_ref[...].astype(F32)
     dlogit = (up * act * gate * (1.0 - gate)).astype(BF16)
     dlogit_ref[...] = dlogit
@@ -428,9 +426,6 @@
     slope = cdf + mixed * jnp.exp(-0.5 * mixed * mixed) * 0.3989422804014327
     d_mixed = d_act * slope
     dmixed_ref[...] = d_mixed
-    part = [column_sum(d_mixed * normed), column_sum(dlogit.astype(F32)), column_sum(x * x), column_sum(branch * branch)]
-    for k, value in enumerate(part):
-        part_ref[k : k + 1, :] = value
     d_state = dot(spread(d_mixed.astype(BF16).astype(F32)), readout, NT)
     dstate_ref[:rows] = d_state[:rows] * 2.0
     dstate_ref[rows:] = d_state[rows:] * -2.0
@@ -454,6 +449,15 @@
         send_ref[d] = packet
 
 
+def sums_kernel(x_ref, branch_ref, normed_ref, dmixed_ref, dlogit_ref, out_ref, part_ref):
+    x = x_ref[...].astype(F32)
+    branch = branch_ref[...].astype(F32)
+    out_ref[...] = (x + branch).astype(BF16)
+    skip = column_sum(dmixed_ref[...] * normed_ref[...].astype(F32))
+    for k, value in enumerate((skip, column_sum(dlogit_ref[...].astype(F32)), column_sum(x * x), column_sum(branch * branch))):
+        part_ref[k : k + 1, :] = value
+
+
 def readout_grad_kernel(twice_ref, dmixed_ref, act_ref, dlogit_ref, keep_ref, away_ref, dgate_ref):
     dy = dmixed_ref[...].astype(BF16).astype(F32)
     d_c = dot(twice_ref[...], spread(dy), TN).astype(BF16)
@@ -463,7 +467,8 @@
         lanes = pl.ds(pl.multiple_of(slot_pos(k) * 128, 128), 128)
         for f in range(GROUPS):
             target[k % 2, f, 0:96, :] = d_c[96 * k : 96 * k + 96, 128 * f : 128 * f + 128]
-            target[k % 2, f, 96:160, :] = dgate_ref[64 * f : 64 * f + 64, lanes]
+            rows = pl.ds(pl.multiple_of(((f // 2) * 2 + (lax.axis_index("fx") ^ (f % 2))) * 64, 64), 64)
+            target[k % 2, f, 96:160, :] = dgate_ref[rows, lanes]
 
 
 def back_scan_kernel(start_ref, lane_ref, dstate_ref, local_ref):
@@ -484,7 +489,7 @@
 
 def third_kernel(
     recv_ref, start_ref, up_ref, wide_ref, xhat_ref, inv_ref, v_ref, lane_ref, row_ref, feat_ref, state_ref, local_ref, enter_ref,
-    dmixed_ref, part_ref, g0, g1, gin_ref, keep_ref, away_ref, vec_ref, scratch, dv_ref,
+    dmixed_ref, part_ref, g0, g1, gin_ref, keep_ref, away_ref, scratch, dv_ref, vec_ref,
 ):
     refs = (g0, g1)
     rows, width = up_ref.shape
@@ -527,10 +532,8 @@
     for k in range(4):
         for f in range(GROUPS):
             block = d_b[96 * k : 96 * k + 96, 128 * f : 128 * f + 128]
-            if k // 2:
-                away_ref[(k % 2) * GROUPS + f] = block
-            else:
-                keep_ref[k % 2, f] = block
+            target = away_ref if k // 2 else keep_ref
+            target[(k % 2) * GROUPS + f] = block
     scale, skip = feat_ref[0:1], feat_ref[1:2]
     d_normed = folded(dot(dv, weights(lambda k, f: piece(refs, k, f, 0, 96)), NN)) + dmixed_ref[...] * skip
     xhat = xhat_ref[...]
@@ -565,8 +568,9 @@
             total = total + squares[:, 128 * c : 128 * c + 128]
         vec_ref[28 + k : 29 + k, :] = total
     vec_ref[30:32, :] = jnp.zeros((2, 128), F32)
-    away_ref[2 * GROUPS, 0:64, :] = split_rows(vec_ref[...])
-    away_ref[2 * GROUPS, 64:96, :] = jnp.zeros((32, 128), BF16)
+    for ref in (keep_ref, away_ref):
+        ref[2 * GROUPS, 0:64, :] = split_rows(vec_ref[...])
+        ref[2 * GROUPS, 64:96, :] = jnp.zeros((32, 128), BF16)
 
 
 def added(a, b):
@@ -574,44 +578,39 @@
 
 
 def core_cw_kernel(keep_ref, got_ref, stay_ref, leave_ref):
-    y = lax.axis_index("ty")
     for f in range(GROUPS):
-        stay_ref[f] = added(keep_ref[y, f], got_ref[y, f])
-        leave_ref[f] = added(keep_ref[1 - y, f], got_ref[1 - y, f])
-
-
-def y_cw_kernel(keep_ref, got_ref, stay_ref, leave_ref):
-    x = lax.axis_index("fx")
-    for z in range(GROUPS // 2):
-        stay_ref[z] = added(keep_ref[2 * z + x], got_ref[2 * z + x])
-        leave_ref[z] = added(keep_ref[2 * z + 1 - x], got_ref[2 * z + 1 - x])
+        stay_ref[f] = added(keep_ref[0, f], got_ref[0, f])
+        leave_ref[f] = added(keep_ref[1, f], got_ref[1, f])
 
 
 def joined(packet):
     return packet[0:32].astype(F32) + packet[32:64].astype(F32)
 
 
-def core_b_kernel(keep_ref, vec_ref, got_ref, out_ref):
-    total = split_rows(vec_ref[...] + joined(got_ref[2 * GROUPS, 0:64, :]))
-    for x in range(2):
-        for y in range(2):
-            for z in range(GROUPS // 2):
-                f = 2 * z + x
-                out_ref[2 * x + y, 96 * z : 96 * z + 96, :] = added(keep_ref[y, f], got_ref[y * GROUPS + f])
-            out_ref[2 * x + y, 384:448, :] = total
-
-
-def last_add_kernel(cw_ref, gotcw_ref, gotb_ref, out_ref):
-    vec = joined(gotb_ref[0, 384:448, :])
-    for n in range(1, 4):
-        vec = vec + joined(gotb_ref[n, 384:448, :])
-    vec = split_rows(vec)
+def core_b_kernel(keep_ref, got_ref, stay_ref, y_ref, x_ref, xy_ref):
+    total = split_rows(joined(keep_ref[2 * GROUPS, 0:64, :]) + joined(got_ref[2 * GROUPS, 0:64, :]))
+    for ref, m, j in ((stay_ref, 0, 0), (y_ref, 1, 0), (x_ref, 0, 1), (xy_ref, 1, 1)):
+        for z in range(GROUPS // 2):
+            block = m * GROUPS + 2 * z + j
+            ref[96 * z : 96 * z + 96, :] = added(keep_ref[block], got_ref[block])
+        ref[384:448, :] = total
+
+
+def y_cw_kernel(keep_ref, got_ref, stay_ref, leave_ref):
+    for z in range(GROUPS // 2):
+        f, other = 2 * z, 2 * z + 1
+        stay_ref[z] = added(keep_ref[f], got_ref[f])
+        leave_ref[z] = added(keep_ref[other], got_ref[other])
+
+
+def plane_add_kernel(cw_ref, gotcw_ref, stay_ref, y_ref, x_ref, xy_ref, out_ref):
+    def total(read):
+        return (read(stay_ref) + read(y_ref)) + (read(x_ref) + read(xy_ref))
+
+    vec = split_rows(total(lambda ref: joined(ref[384:448, :])))
     for z in range(GROUPS // 2):
         here = slice(96 * z, 96 * z + 96)
-        value = gotb_ref[0, here, :].astype(F32)
-        for n in range(1, 4):
-            value = value + gotb_ref[n, here, :].astype(F32)
-        out_ref[z, 0:96, :] = value.astype(BF16)
+        out_ref[z, 0:96, :] = total(lambda ref, here=here: ref[here, :].astype(F32)).astype(BF16)
         out_ref[z, 96:256, :] = added(cw_ref[z], gotcw_ref[z])
         out_ref[z, 256:320, :] = vec
 
@@ -656,8 +655,8 @@
 
 
 TAKES = {
-    "pack": 1.5, "norm": 0.3, "first": 1.8, "local_scan": 1.3, "second": 3.0, "readout_grad": 0.7, "back_scan": 1.2, "third": 2.9,
-    "finish": 0.7,
+    "pack": 1.5, "standardize": 0.2, "norm": 0.2, "first": 1.3, "states": 1.2, "second": 1.9, "readout_grad": 0.7, "back_scan": 0.7,
+    "sums": 0.3, "third": 2.1, "finish": 0.7,
 }
 
 
@@ -681,6 +680,10 @@
 
 def swap(value, axis):
     return lax.ppermute(value, axis, [(0, 1), (1, 0)])
+
+
+def across(value):
+    return lax.ppermute(value, ("fx", "ty"), [(n, 3 - n) for n in range(4)])
 
 
 def on_device(
@@ -705,23 +708,23 @@
         )
         mine = lax.all_to_all(sent, "fz", 0, 0, tiled=True)
         own_b, own_cw = lax.optimization_barrier((mine[:, :112], mine[:, 112:]))
-        side_cw = swap(own_cw, "fx")
-        own_b = lax.all_gather(own_b, ("fx", "ty"), axis=0)
-        own_b, side_cw = lax.optimization_barrier((own_b, side_cw))
-        own_b = own_b.reshape(2, 2, GROUPS // 2, 112, 128)
+        plane_b = [own_b, swap(own_b, "ty"), swap(own_b, "fx"), across(own_b)]
+        plane_b, side_cw = lax.optimization_barrier((plane_b, swap(own_cw, "fx")))
+        side_cw = jnp.stack([own_cw, side_cw])
+        far_cw = swap(side_cw, "ty")
+        own_b = jnp.stack(plane_b).reshape(2, 2, GROUPS // 2, 112, 128)
         g = (own_b, swap(own_b, "tc"))
-        own_cw = jnp.stack([own_cw, side_cw])
-        far_cw = swap(own_cw, "ty")
     else:
         g, g_cw = gathered(
             ln_scale, ln_bias, decay_rate, lam_im, log_dt, in_re, in_im, out_re, out_im, skip, glu_weight, glu_bias, seq_lengths
         )
 
-    xhat, inverse, normed, wide, feat, starts = call(
+    xhat, inverse = call(standardize_kernel, (sds((rows, width)), sds((rows, 128))), (layer_in,))
+    normed, wide, feat, starts = call(
         norm_kernel,
-        (sds((rows, width)), sds((rows, 128)), sds((rows, width), BF16), sds((2 * rows, 2 * width), BF16), sds((8, width)),
+        (sds((rows, width), BF16), sds((2 * rows, 2 * width), BF16), sds((8, width)),
          sds((seq_lengths.shape[0], 128))),
-        (layer_in, g[0]),
+        (xhat, g[0]),
     )
     v, lane, row_prm, carry = call(
         functools.partial(first_kernel, blocks),
@@ -731,17 +734,20 @@
     )
     came = lax.all_to_all(carry, AXES, 0, 0, tiled=True)
     if fast:
-        own_cw, far_cw = tied((own_cw, far_cw), came)
-        g_cw = (own_cw, far_cw, swap(own_cw, "tc"), swap(far_cw, "tc"))
-    local, power = call(
-        local_scan_kernel, (sds((2 * rows, 384)), sds((2 * rows, 384))), (starts, tied(v, came), lane)
-    )
-    layer_out, state, twice, d_state, enter, d_mixed, act, dlogit, part, carry = call(
+        side_cw, far_cw = tied((side_cw, far_cw), came)
+        g_cw = (side_cw, far_cw, swap(side_cw, "tc"), swap(far_cw, "tc"))
+    state, twice, enter = call(
+        states_kernel,
+        (sds((2 * rows, 384)), sds((2 * rows, 384), BF16), sds((8, 384))),
+        (came, starts, v, lane, row_prm),
+        [pltpu.VMEM((8, 128), F32)],
+    )
+    branch, d_state, d_mixed, act, dlogit, carry = call(
         functools.partial(second_kernel, blocks),
-        (sds((rows, width), BF16), sds((2 * rows, 384)), sds((2 * rows, 384), BF16), sds((2 * rows, 384)), sds((8, 384)), sds((rows, width)),
-         sds((rows, width), BF16), sds((rows, width), BF16), sds((8, width)), sds((blocks, 8, 128))),
-        (came, starts, layer_in, grad_out, normed, lane, row_prm, feat, local, power, *g_cw),
-        [pltpu.VMEM((8, 128), F32), pltpu.VMEM((width, width), BF16), pltpu.VMEM((GROUPS, 4, 96, 128), BF16)],
+        (sds((rows, width), BF16), sds((2 * rows, 384)), sds((rows, width)), sds((rows, width), BF16), sds((rows, width), BF16),
+         sds((blocks, 8, 128))),
+        (twice, starts, grad_out, normed, lane, feat, *g_cw),
+        [pltpu.VMEM((8, 128), F32), pltpu.VMEM((width, width), BF16)],
     )
     keep_cw, away_cw = call(
         readout_grad_kernel,
@@ -750,8 +756,11 @@
         [pltpu.VMEM((width, width), BF16)],
     )
     local = call(back_scan_kernel, sds((2 * rows, 384)), (starts, lane, d_state))
+    layer_out, part = call(
+        sums_kernel, (sds((rows, width), BF16), sds((8, width))), (layer_in, branch, normed, d_mixed, dlogit)
+    )
     if fast:
-        got_cw, local = lax.optimization_barrier((swap(away_cw, "tc"), local))
+        got_cw, local, part = lax.optimization_barrier((swap(away_cw, "tc"), local, part))
         stay_cw, leave_cw = call(core_cw_kernel, [sds((GROUPS, 160, 128), BF16)] * 2, (keep_cw, got_cw))
         far_cw = swap(leave_cw, "ty")
         carry = tied(carry, leave_cw)
@@ -761,19 +770,20 @@
         stay_cw, leave_cw = call(y_cw_kernel, [sds((GROUPS // 2, 160, 128), BF16)] * 2, (stay_cw, far_cw))
         far_cw = swap(leave_cw, "fx")
         came = tied(came, leave_cw)
-    grad_in, keep_b, away_b, vec = call(
+    grad_in, keep_b, away_b = call(
         third_kernel,
-        (sds((rows, width)), sds((2, GROUPS, 96, 128), BF16), sds((2 * GROUPS + 1, 96, 128), BF16), sds((32, 128))),
+        (sds((rows, width)), sds((2 * GROUPS + 1, 96, 128), BF16), sds((2 * GROUPS + 1, 96, 128), BF16)),
         (came, starts, grad_out, wide, xhat, inverse, v, lane, row_prm, feat, state, local, enter, d_mixed, part, *g),
-        [pltpu.VMEM((8, 128), F32), pltpu.VMEM((2 * rows, 384), BF16)],
+        [pltpu.VMEM((8, 128), F32), pltpu.VMEM((2 * rows, 384), BF16), pltpu.VMEM((32, 128), F32)],
     )
     if not fast:
-        return reduced(layer_out, grad_in, keep_cw, away_cw, keep_b, away_b, vec, count_all, fsdp, width)
-    away_b, far_cw = lax.optimization_barrier((away_b, far_cw))
-    got_b = swap(away_b, "tc")
-    sent = call(core_b_kernel, sds((4, 448, 128), BF16), (keep_b, vec, got_b))
-    got_b = lax.all_to_all(sent, ("fx", "ty"), 0, 0, tiled=True)
-    sent = call(last_add_kernel, sds((GROUPS // 2, 320, 128), BF16), (stay_cw, far_cw, got_b))
+        return reduced(layer_out, grad_in, keep_cw, away_cw, keep_b, away_b, count_all, fsdp, width)
+    stay_b, y_b, x_b, xy_b = call(core_b_kernel, [sds((448, 128), BF16)] * 4, (keep_b, swap(away_b, "tc")))
+    sent = call(
+        plane_add_kernel,
+        sds((GROUPS // 2, 320, 128), BF16),
+        (stay_cw, far_cw, stay_b, swap(y_b, "ty"), swap(x_b, "fx"), across(xy_b)),
+    )
     got = lax.all_to_all(sent, "fz", 0, 0, tiled=True)
     d_re, d_im, d_ore, d_oim, d_glu, d_gbias, d_scale, d_bias, d_skip, g_decay, g_lam, g_step, rms = call(
         functools.partial(finish_kernel, count_all),
@@ -815,22 +825,29 @@
     )
     everyone = lax.all_gather(packet, TENSOR, axis=0).reshape(2, 2, GROUPS // 2, 2, 272, 128)
     x, y, core = (lax.axis_index(axis) for axis in ("fx", "ty", "tc"))
-    of_core = lambda c: lax.dynamic_index_in_dim(everyone, c, 1, keepdims=False)
-    g = [of_core(core ^ i).transpose(2, 0, 1, 3, 4)[:, :, :, :112] for i in range(2)]
-    g_cw = []
-    for i in range(4):
-        picked = lax.dynamic_index_in_dim(of_core(core ^ (i // 2)), y ^ (i % 2), 0, keepdims=False)
-        g_cw.append(jnp.stack([lax.dynamic_index_in_dim(picked, x ^ j, 1, keepdims=False)[:, 112:] for j in range(2)]))
+    own_x = lambda value, axis: jnp.stack([lax.dynamic_index_in_dim(value, x ^ j, axis, keepdims=False) for j in range(2)])
+    g, g_cw = [], []
+    for i in range(2):
+        both = lax.dynamic_index_in_dim(everyone, core ^ i, 1, keepdims=False)
+        slots = [own_x(lax.dynamic_index_in_dim(both, y ^ m, 0, keepdims=False), 1) for m in range(2)]
+        g.append(jnp.stack(slots, axis=1)[:, :, :, :112])
+        g_cw += [slot[:, :, 112:] for slot in slots]
     return g, g_cw
 
 
-def reduced(layer_out, grad_in, keep_cw, away_cw, keep_b, away_b, vec, count_all, fsdp, width):
-    tens, core = tensor_pos(), lax.axis_index("tc")
-    blocks_b = away_b[: 2 * GROUPS].reshape(2, GROUPS, 96, 128)
+def reduced(layer_out, grad_in, keep_cw, away_cw, keep_b, away_b, count_all, fsdp, width):
+    tens = tensor_pos()
+    x, y, core = (lax.axis_index(axis) for axis in ("fx", "ty", "tc"))
+    vec = joined(keep_b[2 * GROUPS, :64])
+    keep_b, away_b = (value[: 2 * GROUPS].reshape(2, GROUPS, 96, 128) for value in (keep_b, away_b))
+
+    def ordered(value, own, axis):
+        return jnp.concatenate([lax.dynamic_index_in_dim(value, own ^ n, axis) for n in range(2)], axis=axis)
 
     def canonical(keep, away):
         both = jnp.stack([keep, away]).astype(F32)
-        both = jnp.concatenate([lax.dynamic_index_in_dim(both, core ^ i, 0) for i in range(2)], axis=0)
+        both = both.reshape(2, 2, GROUPS // 2, 2, *keep.shape[2:])
+        both = ordered(ordered(ordered(both, core, 0), y, 1), x, 3)
         return both.swapaxes(0, 1).reshape(4, *keep.shape[1:])
 
     def natural(keep, away):
@@ -841,7 +858,7 @@
         value = lax.psum_scatter(value, TENSOR, scatter_dimension=0, tiled=True)
         return lax.psum_scatter(value, FSDP, scatter_dimension=1, tiled=True)
 
-    d_re, d_im = natural(keep_b, blocks_b)
+    d_re, d_im = natural(keep_b, away_b)
     d_ore, d_oim = natural(keep_cw[:, :, :96], away_cw[:, :, :96])
     d_glu = canonical(keep_cw[:, :, 96:], away_cw[:, :, 96:]).reshape(4, width, 128).swapaxes(1, 2).reshape(-1, width)
     vec = lax.psum(vec, AXES)

time: 95.7 us -> 89.6 us (0.936)
  blocking collectives: 59.8 us -> 39.1 us
  starting transfers between devices: 7.78 us -> 15.9 us
  waiting for transfers between devices: 15.3 us -> 21.7 us
    all_to_all x1 -> x0, blocking collectives: 11 us -> none  [on_device(): got_b = lax.all_to_all(sent, ('fx', 'ty'), 0, 0, tiled=True)]
    all_gather x1 -> x0, blocking collectives: 9.96 us -> none  [on_device(): own_b = lax.all_gather(own_b, ('fx', 'ty'), axis=0)]
    ppermute x0 -> x2, waiting for transfers between devices: none -> 5.27 us  [across(): return lax.ppermute(value, ('fx', 'ty'), [(n, 3 - n) for n in range(4)])]
    ppermute x0 -> x2, starting transfers between devices: none -> 3.64 us  [across(): return lax.ppermute(value, ('fx', 'ty'), [(n, 3 - n) for n in range(4)])]
    ppermute x9 -> x13, starting transfers between devices: 5.2 us -> 7.92 us  [swap(): return lax.ppermute(value, axis, [(0, 1), (1, 0)])]
    all_to_all x1, waiting for transfers between devices: 3.22 us -> 5.39 us  [on_device(): came = lax.all_to_all(carry, AXES, 0, 0, tiled=True)]
    all_to_all x1, starting transfers between devices: 2.58 us -> 4.3 us  [on_device(): came = lax.all_to_all(carry, AXES, 0, 0, tiled=True)]
    ppermute x9 -> x13, waiting for transfers between devices: 12.1 us -> 11.1 us  [swap(): return lax.ppermute(value, axis, [(0, 1), (1, 0)])]
  transfers between devices with their start and end apart: 10 -> 16, of which waited for: 7 -> 13; matrix products, arithmetic and copies ran while one was open for 0% -> 0% of each run, Pallas kernels for 6% -> 4%
where the time goes in v3:
time: 89.6 us; the launch traced here: 89.2 us
  blocking collectives  39.1 us (44%)
  waiting for transfers between devices  21.7 us (24%)
  starting transfers between devices  15.9 us (18%)
  Pallas kernels  11.6 us (13%)
    all_to_all x1, blocking collectives, on_device(): mine = lax.all_to_all(sent, 'fz', 0, 0, tiled=True)  15.6 us
    all_to_all x1, blocking collectives, on_device(): got = lax.all_to_all(sent, 'fz', 0, 0, tiled=True)  12.7 us
    pallas_call x15, Pallas kernels, call(): pl.pallas_call(kernel, out_shape=outs, in_specs=specs or [VM] * len(args)...  11.6 us
    ppermute x13, waiting for transfers between devices, swap(): return lax.ppermute(value, axis, [(0, 1), (1, 0)])  11.1 us
    all_to_all x1, blocking collectives, on_device(): came = lax.all_to_all(carry, AXES, 0, 0, tiled=True)  10.9 us
    ppermute x13, starting transfers between devices, swap(): return lax.ppermute(value, axis, [(0, 1), (1, 0)])  7.92 us
    all_to_all x1, waiting for transfers between devices, on_device(): came = lax.all_to_all(carry, AXES, 0, 0, tiled=True)  5.39 us
    ppermute x2, waiting for transfers between devices, across(): return lax.ppermute(value, ('fx', 'ty'), [(n, 3 - n) for n in range(4)])  5.27 us
  transfers between devices with their start and end apart: 16, of which 13 were waited for; matrix products, arithmetic and copies ran while one was open for 0% of the time, Pallas kernels for 4%

profile of v3, /device:TPU:0, one launch (start us, length us, event | category | flops | bytes accessed | tf_op | source)
XLA Modules:
  0.0 89.2 jit_solution(13903606667101798083)
XLA Ops:
  0.7 1.8 %pack.1 = bf16[4,272,128]{2,1,0:T(8,128)(2,1)} custom-call(s32[4]{0:T(128)} %refs_0_.1, bf16[64,96]{1,0:T(8,128)(2,1)} %bitcast.40, bf16[64,96]{1,0:T(8,128)(2,1)} %bitcast.41, bf16[64,96]{1,0:T(8,128)(2,1)} %bitcast.42, bf16[64,96]{1,0:T(8,128)(2,1)} %bitcast.43, bf16[64,512]{1,0:T(8,128)(2,1)} %bitcast.39, bf16[1,64]{1,0:T(2,128)(2,1)} %bitcast.44, ...), custom_call_target="tpu_custom_call" | custom-call | bytes 5400000 | tf_op jit(solution)/shard_map/pack/pallas_call | solution.py:665
  2.4 15.6 %all_to_all.20 = bf16[4,272,128]{2,1,0:T(8,128)(2,1)S(1)} all-to-all(bf16[4,272,128]{2,1,0:T(8,128)(2,1)} %pack.1), channel_id=1, replica_groups=mesh['fz'=4,'fx'=2,'ty'=2,'tc'=2] {'fz'}, dimensions={0} | all-to-all | bytes 557056 | tf_op jit(solution)/shard_map/all_to_all | solution.py:709
  18.0 1.6 %collective-permute-start.3 = (bf16[4,160,128]{2,1,0:T(8,128)(2,1)S(1)}, bf16[4,160,128]{2,1,0:T(8,128)(2,1)S(1)}, u32[]{:S(2)}, u32[]{:S(2)}) collective-permute-start(bf16[4,160,128]{2,1,0:T(8,128)(2,1)S(1)} %slice.9), channel_id=1, source_target_pairs={{0,4},{4,0},{1,5},{5,1},{2,6},{6,2},{3,7},{7,3},{8,12},{12,8},{9,1... | collective-permute-start | bytes 491528 | tf_op jit(solution)/shard_map/ppermute | solution.py:682
  19.6 1.5 %collective-permute-start.2 = (bf16[4,112,128]{2,1,0:T(8,128)(2,1)S(1)}, bf16[4,112,128]{2,1,0:T(8,128)(2,1)S(1)}, u32[]{:S(2)}, u32[]{:S(2)}) collective-permute-start(bf16[4,112,128]{2,1,0:T(8,128)(2,1)S(1)} %slice.8), channel_id=1, source_target_pairs={{0,6},{2,4},{4,2},{6,0},{1,7},{3,5},{5,3},{7,1},{8,14},{10,12},{12... | collective-permute-start | bytes 344072 | tf_op jit(solution)/shard_map/ppermute | solution.py:686
  21.0 1.5 %collective-permute-start.1 = (bf16[4,112,128]{2,1,0:T(8,128)(2,1)S(1)}, bf16[4,112,128]{2,1,0:T(8,128)(2,1)S(1)}, u32[]{:S(2)}, u32[]{:S(2)}) collective-permute-start(bf16[4,112,128]{2,1,0:T(8,128)(2,1)S(1)} %slice.8), channel_id=1, source_target_pairs={{0,4},{4,0},{1,5},{5,1},{2,6},{6,2},{3,7},{7,3},{8,12},{12,8},{9,1... | collective-permute-start | bytes 344072 | tf_op jit(solution)/shard_map/ppermute | solution.py:682
  23.0 3.5 %collective-permute-done.2 = bf16[4,112,128]{2,1,0:T(8,128)(2,1)S(1)} collective-permute-done((bf16[4,112,128]{2,1,0:T(8,128)(2,1)S(1)}, bf16[4,112,128]{2,1,0:T(8,128)(2,1)S(1)}, u32[]{:S(2)}, u32[]{:S(2)}) %collective-permute-start.2) | collective-permute-done | bytes 114720 | tf_op jit(solution)/shard_map/ppermute | solution.py:686
  28.0 1.0 %collective-permute-start.5 = (bf16[2,4,160,128]{3,2,1,0:T(8,128)(2,1)S(1)}, bf16[2,4,160,128]{3,2,1,0:T(8,128)(2,1)S(1)}, u32[]{:S(2)}, u32[]{:S(2)}) collective-permute-start(bf16[2,4,160,128]{3,2,1,0:T(8,128)(2,1)S(1)} %pad_maximum_fusion.1.g0), channel_id=1, source_target_pairs={{0,2},{2,0},{1,3},{3,1},{4,6},{6,4},{5,7},{7,5},{8,10},{10,8},{9,1... | collective-permute-start | bytes 983048 | tf_op jit(solution)/shard_map/ppermute | solution.py:682
  29.7 1.3 %first.1 = (f32[256,384]{1,0:T(8,128)S(1)}, f32[8,384]{1,0:T(8,128)S(1)}, f32[8,8,128]{2,1,0:T(8,128)S(1)}, f32[32,8,128]{2,1,0:T(8,128)}) custom-call(bf16[256,1024]{1,0:T(8,128)(2,1)S(1)} %get-tuple-element.86.wide_ref, f32[4,128]{1,0:T(4,128)S(1)} %get-tuple-element.87.start_ref, bf16[2,2,4,112,128]{4,3,2,1,0:T(8,128)(2,1)S(1)} %bitcast.31, ...), custom_call_target="tpu_custom_call" | custom-call | bytes 4680000 | tf_op jit(solution)/shard_map/first/pallas_call | solution.py:665
  31.0 4.3 %all-to-all-start.1 = ((f32[32,8,128]{2,1,0:T(8,128)}), f32[32,8,128]{2,1,0:T(8,128)S(1)}, u32[]{:S(2)}, u32[]{:S(2)}) async-start(f32[32,8,128]{2,1,0:T(8,128)} %get-tuple-element.88), calls=%async_computation.1 | async-start | bytes 262144 | tf_op jit(solution)/shard_map/all_to_all | solution.py:735
  35.3 2.8 %collective-permute-done.5.g1 = bf16[2,4,160,128]{3,2,1,0:T(8,128)(2,1)S(1)} collective-permute-done((bf16[2,4,160,128]{3,2,1,0:T(8,128)(2,1)S(1)}, bf16[2,4,160,128]{3,2,1,0:T(8,128)(2,1)S(1)}, u32[]{:S(2)}, u32[]{:S(2)}) %collective-permute-start.5) | collective-permute-done | bytes 327712 | tf_op jit(solution)/shard_map/ppermute | solution.py:682
  38.1 5.4 %all-to-all-done.1.recv_ref = f32[32,8,128]{2,1,0:T(8,128)S(1)} async-done(((f32[32,8,128]{2,1,0:T(8,128)}), f32[32,8,128]{2,1,0:T(8,128)S(1)}, u32[]{:S(2)}, u32[]{:S(2)}) %all-to-all-start.1) | async-done | bytes 131104 | tf_op jit(solution)/shard_map/all_to_all | solution.py:735
  44.0 0.8 states.1
  45.6 1.7 %second.1 = (bf16[128,512]{1,0:T(8,128)(2,1)S(1)}, f32[256,384]{1,0:T(8,128)S(1)}, f32[128,512]{1,0:T(8,128)S(1)}, bf16[128,512]{1,0:T(8,128)(2,1)S(1)}, bf16[12...) custom-call(bf16[256,384]{1,0:T(8,128)(2,1)S(1)} %get-tuple-element.92.twice_ref, ...), custom_call_target="tpu_custom_call" | custom-call | bytes 6840000 | tf_op jit(solution)/shard_map/second/pallas_call | solution.py:665
  48.3 0.8 sums.1
  50.8 10.9 %all_to_all.21.recv_ref = f32[32,8,128]{2,1,0:T(8,128)S(1)} all-to-all(f32[32,8,128]{2,1,0:T(8,128)S(1)} %get-tuple-element.110), channel_id=1, replica_groups=mesh['fz'=4,'fx'=2,'ty'=2,'tc'=2] {'fz','fx','ty','tc'}, dimensions={0} | all-to-all | bytes 262144 | tf_op jit(solution)/shard_map/all_to_all | solution.py:767
  61.7 2.4 %third.1 = (f32[128,512]{1,0:T(8,128)}, bf16[17,96,128]{2,1,0:T(8,128)(2,1)S(1)}, bf16[17,96,128]{2,1,0:T(8,128)(2,1)S(1)}) custom-call(f32[32,8,128]{2,1,0:T(8,128)S(1)} %all_to_all.21.recv_ref, f32[4,128]{1,0:T(4,128)S(1)} %get-tuple-element.87.start_ref, bf16[128,512]{1,0:T(8,128)(2,1)S(1)} %copy-done.1, ...), custom_call_target="tpu_custom_call" | custom-call | bytes 7560000 | tf_op jit(solution)/shard_map/third/pallas_call | solution.py:665
  64.8 1.1 %collective-permute-done.11.got_ref = bf16[17,96,128]{2,1,0:T(8,128)(2,1)S(1)} collective-permute-done((bf16[17,96,128]{2,1,0:T(8,128)(2,1)S(1)}, bf16[17,96,128]{2,1,0:T(8,128)(2,1)S(1)}, u32[]{:S(2)}, u32[]{:S(2)}) %collective-permute-start.11) | collective-permute-done | bytes 417824 | tf_op jit(solution)/shard_map/ppermute | solution.py:682
  66.5 0.9 %collective-permute-start.13 = (bf16[448,128]{1,0:T(8,128)(2,1)S(1)}, bf16[448,128]{1,0:T(8,128)(2,1)S(1)}, u32[]{:S(2)}, u32[]{:S(2)}) collective-permute-start(bf16[448,128]{1,0:T(8,128)(2,1)S(1)} %get-tuple-element.128), channel_id=1, source_target_pairs={{0,4},{4,0},{1,5},{5,1},{2,6},{6,2},{3,7},{7,3},{8,12},{12,8},{9,1... | collective-permute-start | bytes 344072 | tf_op jit(solution)/shard_map/ppermute | solution.py:682
  67.4 2.1 %collective-permute-start.14 = (bf16[448,128]{1,0:T(8,128)(2,1)S(1)}, bf16[448,128]{1,0:T(8,128)(2,1)S(1)}, u32[]{:S(2)}, u32[]{:S(2)}) collective-permute-start(bf16[448,128]{1,0:T(8,128)(2,1)S(1)} %get-tuple-element.129), channel_id=1, source_target_pairs={{0,6},{2,4},{4,2},{6,0},{1,7},{3,5},{5,3},{7,1},{8,14},{10,12},{12... | collective-permute-start | bytes 344072 | tf_op jit(solution)/shard_map/ppermute | solution.py:686
  69.6 1.8 %collective-permute-done.10.gotcw_ref = bf16[4,160,128]{2,1,0:T(8,128)(2,1)S(1)} collective-permute-done((bf16[4,160,128]{2,1,0:T(8,128)(2,1)S(1)}, bf16[4,160,128]{2,1,0:T(8,128)(2,1)S(1)}, u32[]{:S(2)}, u32[]{:S(2)}) %collective-permute-start.10) | collective-permute-done | bytes 163872 | tf_op jit(solution)/shard_map/ppermute | solution.py:682
  71.4 2.5 %collective-permute-done.13.x_ref = bf16[448,128]{1,0:T(8,128)(2,1)S(1)} collective-permute-done((bf16[448,128]{1,0:T(8,128)(2,1)S(1)}, bf16[448,128]{1,0:T(8,128)(2,1)S(1)}, u32[]{:S(2)}, u32[]{:S(2)}) %collective-permute-start.13) | collective-permute-done | bytes 114720 | tf_op jit(solution)/shard_map/ppermute | solution.py:682
  73.9 1.7 %collective-permute-done.14.xy_ref = bf16[448,128]{1,0:T(8,128)(2,1)S(1)} collective-permute-done((bf16[448,128]{1,0:T(8,128)(2,1)S(1)}, bf16[448,128]{1,0:T(8,128)(2,1)S(1)}, u32[]{:S(2)}, u32[]{:S(2)}) %collective-permute-start.14) | collective-permute-done | bytes 114720 | tf_op jit(solution)/shard_map/ppermute | solution.py:686
  75.7 12.7 %all_to_all.22.got_ref = bf16[4,320,128]{2,1,0:T(8,128)(2,1)S(1)} all-to-all(bf16[4,320,128]{2,1,0:T(8,128)(2,1)S(1)} %plane_add.1), channel_id=1, replica_groups=mesh['fz'=4,'fx'=2,'ty'=2,'tc'=2] {'fz'}, dimensions={0} | all-to-all | bytes 655360 | tf_op jit(solution)/shard_map/all_to_all | solution.py:787
  88.4 0.8 finish.1
  (34 shorter events, 8.1 us)
Async XLA Ops:
  18.0 9.8 %collective-permute-start.3 = (bf16[4,160,128]{2,1,0:T(8,128)(2,1)S(1)}, bf16[4,160,128]{2,1,0:T(8,128)(2,1)S(1)}, u32[]{:S(2)}, u32[]{:S(2)}) collective-permute-start(bf16[4,160,128]{2,1,0:T(8,128)(2,1)S(1)} %slice.9), channel_id=1, source_target_pairs={{0,4},{4,0},{1,5},{5,1},{2,6},{6,2},{3,7},{7,3},{8,12},{12,8},{9,1... | collective-permute-start | bytes 491528 | tf_op jit(solution)/shard_map/ppermute | solution.py:682
  19.6 7.0 %collective-permute-start.2 = (bf16[4,112,128]{2,1,0:T(8,128)(2,1)S(1)}, bf16[4,112,128]{2,1,0:T(8,128)(2,1)S(1)}, u32[]{:S(2)}, u32[]{:S(2)}) collective-permute-start(bf16[4,112,128]{2,1,0:T(8,128)(2,1)S(1)} %slice.8), channel_id=1, source_target_pairs={{0,6},{2,4},{4,2},{6,0},{1,7},{3,5},{5,3},{7,1},{8,14},{10,12},{12... | collective-permute-start | bytes 344072 | tf_op jit(solution)/shard_map/ppermute | solution.py:686
  21.0 6.2 %collective-permute-start.1 = (bf16[4,112,128]{2,1,0:T(8,128)(2,1)S(1)}, bf16[4,112,128]{2,1,0:T(8,128)(2,1)S(1)}, u32[]{:S(2)}, u32[]{:S(2)}) collective-permute-start(bf16[4,112,128]{2,1,0:T(8,128)(2,1)S(1)} %slice.8), channel_id=1, source_target_pairs={{0,4},{4,0},{1,5},{5,1},{2,6},{6,2},{3,7},{7,3},{8,12},{12,8},{9,1... | collective-permute-start | bytes 344072 | tf_op jit(solution)/shard_map/ppermute | solution.py:682
  22.5 5.2 %collective-permute-start = (bf16[4,112,128]{2,1,0:T(8,128)(2,1)S(1)}, bf16[4,112,128]{2,1,0:T(8,128)(2,1)S(1)}, u32[]{:S(2)}, u32[]{:S(2)}) collective-permute-start(bf16[4,112,128]{2,1,0:T(8,128)(2,1)S(1)} %slice.8), channel_id=1, source_target_pairs={{0,2},{2,0},{1,3},{3,1},{4,6},{6,4},{5,7},{7,5},{8,10},{10,8},{9,1... | collective-permute-start | bytes 344072 | tf_op jit(solution)/shard_map/ppermute | solution.py:682
  27.8 1.9 %collective-permute-start.4 = (bf16[2,2,4,112,128]{4,3,2,1,0:T(8,128)(2,1)S(1)}, bf16[2,2,4,112,128]{4,3,2,1,0:T(8,128)(2,1)S(1)}, u32[]{:S(2)}, u32[]{:S(2)}) collective-permute-start(bf16[2,2,4,112,128]{4,3,2,1,0:T(8,128)(2,1)S(1)} %bitcast.29), channel_id=1, source_target_pairs={{0,1},{1,0},{2,3},{3,2},{4,5},{5,4},{6,7},{7,6},{8,9},{9,8},{10,11... | collective-permute-start | bytes 1376264 | tf_op jit(solution)/shard_map/ppermute | solution.py:682
  27.9 1.0 %copy-start = (bf16[128,512]{1,0:T(8,128)(2,1)S(1)}, bf16[128,512]{1,0:T(8,128)(2,1)}, u32[]{:S(2)}) copy-start(bf16[128,512]{1,0:T(8,128)(2,1)} %x_ref.3) | copy-start | bytes 393220
  28.0 10.2 %collective-permute-start.5 = (bf16[2,4,160,128]{3,2,1,0:T(8,128)(2,1)S(1)}, bf16[2,4,160,128]{3,2,1,0:T(8,128)(2,1)S(1)}, u32[]{:S(2)}, u32[]{:S(2)}) collective-permute-start(bf16[2,4,160,128]{3,2,1,0:T(8,128)(2,1)S(1)} %pad_maximum_fusion.1.g0), channel_id=1, source_target_pairs={{0,2},{2,0},{1,3},{3,1},{4,6},{6,4},{5,7},{7,5},{8,10},{10,8},{9,1... | collective-permute-start | bytes 983048 | tf_op jit(solution)/shard_map/ppermute | solution.py:682
  31.0 12.5 %all-to-all-start.1 = ((f32[32,8,128]{2,1,0:T(8,128)}), f32[32,8,128]{2,1,0:T(8,128)S(1)}, u32[]{:S(2)}, u32[]{:S(2)}) async-start(f32[32,8,128]{2,1,0:T(8,128)} %get-tuple-element.88), calls=%async_computation.1 | async-start | bytes 262144 | tf_op jit(solution)/shard_map/all_to_all | solution.py:735
  43.5 1.6 %collective-permute-start.6 = (bf16[2,4,160,128]{3,2,1,0:T(8,128)(2,1)S(1)}, bf16[2,4,160,128]{3,2,1,0:T(8,128)(2,1)S(1)}, u32[]{:S(2)}, u32[]{:S(2)}) collective-permute-start(bf16[2,4,160,128]{3,2,1,0:T(8,128)(2,1)S(1)} %pad_maximum_fusion.1.g0), channel_id=1, source_target_pairs={{0,1},{1,0},{2,3},{3,2},{4,5},{5,4},{6,7},{7,6},{8,9},{9,8},{10,11... | collective-permute-start | bytes 983048 | tf_op jit(solution)/shard_map/ppermute | solution.py:682
  43.8 1.9 %collective-permute-start.7 = (bf16[2,4,160,128]{3,2,1,0:T(8,128)(2,1)S(1)}, bf16[2,4,160,128]{3,2,1,0:T(8,128)(2,1)S(1)}, u32[]{:S(2)}, u32[]{:S(2)}) collective-permute-start(bf16[2,4,160,128]{3,2,1,0:T(8,128)(2,1)S(1)} %collective-permute-done.5.g1), channel_id=1, source_target_pairs={{0,1},{1,0},{2,3},{3,2},{4,5},{5,4},{6,7},{7,6},{8,9},{9,8},{10,11... | collective-permute-start | bytes 983048 | tf_op jit(solution)/shard_map/ppermute | solution.py:682
  44.0 1.6 %copy-start.1 = (bf16[128,512]{1,0:T(8,128)(2,1)S(1)}, bf16[128,512]{1,0:T(8,128)(2,1)}, u32[]{:S(2)}) copy-start(bf16[128,512]{1,0:T(8,128)(2,1)} %up_ref.3) | copy-start | bytes 393220
  48.0 2.2 %collective-permute-start.8 = (bf16[2,8,160,128]{3,2,1,0:T(8,128)(2,1)S(1)}, bf16[2,8,160,128]{3,2,1,0:T(8,128)(2,1)S(1)}, u32[]{:S(2)}, u32[]{:S(2)}) collective-permute-start(bf16[2,8,160,128]{3,2,1,0:T(8,128)(2,1)S(1)} %get-tuple-element.105), channel_id=1, source_target_pairs={{0,1},{1,0},{2,3},{3,2},{4,5},{5,4},{6,7},{7,6},{8,9},{9,8},{10,11... | collective-permute-start | bytes 1966088 | tf_op jit(solution)/shard_map/ppermute | solution.py:682
  50.3 11.4 %collective-permute-start.9 = (bf16[8,160,128]{2,1,0:T(8,128)(2,1)S(1)}, bf16[8,160,128]{2,1,0:T(8,128)(2,1)S(1)}, u32[]{:S(2)}, u32[]{:S(2)}) collective-permute-start(bf16[8,160,128]{2,1,0:T(8,128)(2,1)S(1)} %get-tuple-element.109), channel_id=1, source_target_pairs={{0,2},{2,0},{1,3},{3,1},{4,6},{6,4},{5,7},{7,5},{8,10},{10,8},{9,1... | collective-permute-start | bytes 983048 | tf_op jit(solution)/shard_map/ppermute | solution.py:682
  64.2 1.8 %collective-permute-start.11 = (bf16[17,96,128]{2,1,0:T(8,128)(2,1)S(1)}, bf16[17,96,128]{2,1,0:T(8,128)(2,1)S(1)}, u32[]{:S(2)}, u32[]{:S(2)}) collective-permute-start(bf16[17,96,128]{2,1,0:T(8,128)(2,1)S(1)} %get-tuple-element.125), channel_id=1, source_target_pairs={{0,1},{1,0},{2,3},{3,2},{4,5},{5,4},{6,7},{7,6},{8,9},{9,8},{10,11... | collective-permute-start | bytes 1253384 | tf_op jit(solution)/shard_map/ppermute | solution.py:682
  64.4 7.0 %collective-permute-start.10 = (bf16[4,160,128]{2,1,0:T(8,128)(2,1)S(1)}, bf16[4,160,128]{2,1,0:T(8,128)(2,1)S(1)}, u32[]{:S(2)}, u32[]{:S(2)}) collective-permute-start(bf16[4,160,128]{2,1,0:T(8,128)(2,1)S(1)} %get-tuple-element.115), channel_id=1, source_target_pairs={{0,4},{4,0},{1,5},{5,1},{2,6},{6,2},{3,7},{7,3},{8,12},{12,8},{9,1... | collective-permute-start | bytes 491528 | tf_op jit(solution)/shard_map/ppermute | solution.py:682
  66.0 5.4 %collective-permute-start.12 = (bf16[448,128]{1,0:T(8,128)(2,1)S(1)}, bf16[448,128]{1,0:T(8,128)(2,1)S(1)}, u32[]{:S(2)}, u32[]{:S(2)}) collective-permute-start(bf16[448,128]{1,0:T(8,128)(2,1)S(1)} %get-tuple-element.127), channel_id=1, source_target_pairs={{0,2},{2,0},{1,3},{3,1},{4,6},{6,4},{5,7},{7,5},{8,10},{10,8},{9,1... | collective-permute-start | bytes 344072 | tf_op jit(solution)/shard_map/ppermute | solution.py:682
  66.5 7.3 %collective-permute-start.13 = (bf16[448,128]{1,0:T(8,128)(2,1)S(1)}, bf16[448,128]{1,0:T(8,128)(2,1)S(1)}, u32[]{:S(2)}, u32[]{:S(2)}) collective-permute-start(bf16[448,128]{1,0:T(8,128)(2,1)S(1)} %get-tuple-element.128), channel_id=1, source_target_pairs={{0,4},{4,0},{1,5},{5,1},{2,6},{6,2},{3,7},{7,3},{8,12},{12,8},{9,1... | collective-permute-start | bytes 344072 | tf_op jit(solution)/shard_map/ppermute | solution.py:682
  67.4 8.1 %collective-permute-start.14 = (bf16[448,128]{1,0:T(8,128)(2,1)S(1)}, bf16[448,128]{1,0:T(8,128)(2,1)S(1)}, u32[]{:S(2)}, u32[]{:S(2)}) collective-permute-start(bf16[448,128]{1,0:T(8,128)(2,1)S(1)} %get-tuple-element.129), channel_id=1, source_target_pairs={{0,6},{2,4},{4,2},{6,0},{1,7},{3,5},{5,3},{7,1},{8,14},{10,12},{12... | collective-permute-start | bytes 344072 | tf_op jit(solution)/shard_map/ppermute | solution.py:686

commit v4 on v3

v4 whole, which is shorter than its diff:
```python
import functools

import jax
import jax.numpy as jnp
from jax import lax
from jax.experimental import pallas as pl
from jax.experimental.pallas import tpu as pltpu
from jax.sharding import Mesh
from jax.sharding import PartitionSpec as P

F32 = jnp.float32
BF16 = jnp.bfloat16
FSDP = ("fz", "fx")
TENSOR = ("ty", "tc")
AXES = (*FSDP, *TENSOR)
HBM = pl.BlockSpec(memory_space=pltpu.HBM)
VM = pl.BlockSpec(memory_space=pltpu.VMEM)
SM = pl.BlockSpec(memory_space=pltpu.SMEM)

GROUPS = 8
VEC = 96


def sds(shape, dtype=F32):
    return jax.ShapeDtypeStruct(shape, dtype)


def low_half(shape):
    return lax.broadcasted_iota(jnp.int32, shape, len(shape) - 1) < 64


def lane_iota(shape):
    return lax.broadcasted_iota(jnp.int32, shape, len(shape) - 1)


def dot(a, b, dims):
    return lax.dot_general(a, b, (dims, ((), ())), preferred_element_type=F32)


NT = ((1,), (1,))
NN = ((1,), (0,))
TN = ((0,), (0,))


def flipped():
    return lax.axis_index("fx") == 1


def spread(x):
    lo = low_half((x.shape[0], 128))
    flip = flipped()
    upper, lower = [], []
    for c in range(x.shape[1] // 128):
        xc = x[:, 128 * c : 128 * c + 128]
        turned = pltpu.roll(xc, 64, 1)
        xc, turned = jnp.where(flip, turned, xc), jnp.where(flip, xc, turned)
        upper += [jnp.where(lo, xc, 0.0).astype(BF16), jnp.where(lo, turned, 0.0).astype(BF16)]
        lower += [jnp.where(lo, 0.0, turned).astype(BF16), jnp.where(lo, 0.0, xc).astype(BF16)]
    return jnp.concatenate(
        [jnp.concatenate(upper, axis=1), jnp.concatenate(lower, axis=1)], axis=0
    )


def folded(lhs, parts):
    rows = lhs.shape[0] // 2
    lo = low_half((rows, 128))
    flip = flipped()
    out = []
    for part in parts:
        pq = dot(lhs, part, NN)
        p0, p1, q0, q1 = pq[:rows, :128], pq[:rows, 128:], pq[rows:, :128], pq[rows:, 128:]
        even = jnp.where(lo, p0, q1) + jnp.where(lo, pltpu.roll(q0, 64, 1), pltpu.roll(p1, 64, 1))
        out.append(jnp.where(flip, pltpu.roll(even, 64, 1), even))
    return jnp.concatenate(out, axis=1)


def slot_pos(m, core):
    return (lax.axis_index("ty") ^ m) * 2 + (lax.axis_index("tc") ^ core)


def own_rows(rows):
    return pl.ds(pl.multiple_of(lax.axis_index("tc") * rows, rows), rows)


def other_rows(rows):
    return pl.ds(pl.multiple_of((1 - lax.axis_index("tc")) * rows, rows), rows)


def piece(ref, m, f, start, count):
    return ref[f % 2, m, f // 2, start : start + count, :]


def weights(get):
    none = jnp.zeros((32, 128), BF16)
    block = lambda f: jnp.concatenate([get(0, f), none, get(1, f), none], axis=0)
    return [jnp.concatenate([block(f), block(f + 1)], axis=1) for f in range(0, GROUPS, 2)]


def feature_rows(ref, row):
    lo = low_half((8, 128))
    flip = flipped()
    first, second = [], []
    for c in range(GROUPS // 2):
        a = jnp.broadcast_to(piece(ref, 0, 2 * c, row, 1).astype(F32), (8, 128))
        b = jnp.broadcast_to(piece(ref, 0, 2 * c + 1, row, 1).astype(F32), (8, 128))
        a, b = jnp.where(flip, b, a), jnp.where(flip, a, b)
        first.append(jnp.where(lo, a, pltpu.roll(b, 64, 1)))
        second.append(jnp.where(lo, pltpu.roll(a, 64, 1), b))
    return jnp.concatenate(first, axis=1)[:1], jnp.concatenate(second, axis=1)[:1]


def cmul(a, b):
    return a[0] * b[0] - a[1] * b[1], a[0] * b[1] + a[1] * b[0]


def tensor_pos():
    return lax.axis_index("ty") * 2 + lax.axis_index("tc")


def fsdp_pos():
    return lax.axis_index("fz") * 2 + lax.axis_index("fx")


def pair_pos():
    return fsdp_pos() * 2 + lax.axis_index("ty")


def offsets_of(start_ref):
    return [start_ref[n : n + 1, :] for n in range(start_ref.shape[0])]


def starts_until(offsets, base, rows):
    at = (lax.broadcasted_iota(jnp.int32, (rows, 128), 0) + base).astype(F32)
    count = jnp.zeros((rows, 128), F32)
    for off in offsets:
        count = count + jnp.where((at >= off) & (off >= at[0:1]), 1.0, 0.0)
    return count


def no_start(offsets, base, rows):
    link = jnp.ones((1, 128), F32)
    first = (jnp.zeros((1, 128), jnp.int32) + base).astype(F32)
    for off in offsets:
        link = jnp.where((off >= first) & (off < first + rows), 0.0, link)
    return link


def expm1(x):
    series = x * (1 + x / 2 * (1 + x / 3 * (1 + x / 4 * (1 + x / 5 * (1 + x / 6 * (1 + x / 7))))))
    return jnp.where(jnp.abs(x) < 0.25, series, jnp.exp(x) - 1.0)


def discretize(decay_rate, lam_im, log_dt):
    step_size = jnp.exp(log_dt)
    lam_re = -decay_rate
    magnitude = jnp.exp(lam_re * step_size)
    phase = lam_im * step_size
    abar_re = magnitude * jnp.cos(phase)
    abar_im = magnitude * jnp.sin(phase)
    half_sin = jnp.sin(0.5 * phase)
    less_re = expm1(lam_re * step_size) * jnp.cos(phase) - 2.0 * half_sin * half_sin
    denom = lam_re * lam_re + lam_im * lam_im
    coef_re = (less_re * lam_re + abar_im * lam_im) / denom
    coef_im = (abar_im * lam_re - less_re * lam_im) / denom
    return abar_re, abar_im, coef_re, coef_im, step_size


def pack_kernel(*refs):
    *inputs, out_ref, square, four, glu_ref, halves, params, lengths, sems = refs
    seq_hbm, matrices, glu_hbm, features, states = inputs[0], inputs[1:5], inputs[5], inputs[6:10], inputs[10:13]
    units = pl.multiple_of(tensor_pos() * 128, 128)
    pairs = [(ref, four.at[k]) for k, ref in enumerate(matrices)]
    pairs += [(glu_hbm.at[:, pl.ds(units, 128)], glu_ref), (seq_hbm, lengths)]
    pairs += [(ref, halves.at[k]) for k, ref in enumerate(features)]
    pairs += [(ref, params.at[k]) for k, ref in enumerate(states)]
    copies = [pltpu.make_async_copy(source, target, sems.at[k]) for k, (source, target) in enumerate(pairs)]
    for copy in copies:
        copy.start()
    square[:, 96:128] = jnp.zeros((128, 32), F32)
    for copy in copies:
        copy.wait()
    vec = [
        jnp.concatenate([halves[0], halves[1]], axis=1).astype(F32),
        jnp.concatenate([halves[2], halves[3]], axis=1).astype(F32),
    ]
    for k in range(3):
        value = jnp.concatenate([params[k], jnp.zeros((1, 32), F32)], axis=1)
        for _ in range(3):
            part = value.astype(BF16).astype(F32)
            value = value - part
            vec.append(part)
    lane = lane_iota((1, 128))
    upper, lower, total = jnp.zeros((1, 128), jnp.int32), jnp.zeros((1, 128), jnp.int32), 0
    for n in range(lengths.shape[0]):
        upper = jnp.where(lane == n, total >> 8, upper)
        lower = jnp.where(lane == n, total & 255, lower)
        total = total + lengths[n]
    vec += [upper.astype(F32), lower.astype(F32)]
    vec.append(jnp.zeros((16 - len(vec), 128), F32))
    vec = jnp.concatenate(vec, axis=0).astype(BF16)
    pieces = []
    for k in (0, 2):
        square[0:64, 0:96] = four[k].astype(F32)
        square[64:128, 0:96] = four[k + 1].astype(F32)
        pieces.append(square[...].T[0:96].astype(BF16))
    packet = jnp.concatenate([pieces[0], vec, pieces[1], glu_ref[...]], axis=0)
    for z in range(GROUPS // 2):
        out_ref[z] = packet


def params_of(ref, vec_row):
    lane = lane_iota((8, 128))
    out = []
    for k, safe in enumerate((1.0, 0.0, 0.0)):
        rows = []
        for m in range(2):
            part = piece(ref, m, 0, vec_row, 16).astype(F32)
            rows.append((part[2 + 3 * k : 3 + 3 * k] + part[3 + 3 * k : 4 + 3 * k]) + part[4 + 3 * k : 5 + 3 * k])
        value = jnp.concatenate(rows + [jnp.full((6, 128), safe, F32)], axis=0)
        out.append(jnp.where(lane < 96, value, safe))
    return out


def carry_block(re_rows, im_rows, scratch):
    for m in range(2):
        y = lax.axis_index("ty") ^ m
        scratch[pl.ds(y, 1), :] = re_rows[m]
        scratch[pl.ds(2 + y, 1), :] = im_rows[m]


def standardize_kernel(x_ref, other_ref, xhat_ref, inv_ref):
    rows, width = x_ref.shape
    for ref, where, own in ((x_ref, own_rows(rows), True), (other_ref, other_rows(rows), False)):
        x = ref[...].astype(F32)
        centered = x - jnp.sum(x, axis=1, keepdims=True) / width
        inverse = lax.rsqrt(jnp.sum(centered * centered, axis=1, keepdims=True) / width + 1e-05)
        xhat_ref[where, :] = centered * inverse
        if own:
            inv_ref[...] = jnp.broadcast_to(inverse, (rows, 128))


def norm_kernel(xhat_ref, g_ref, normed_ref, wide_ref, feat_ref, start_ref):
    scale, bias = feature_rows(g_ref, VEC)
    feat_ref[0:1] = scale
    feat_ref[1:2], feat_ref[2:3] = feature_rows(g_ref, VEC + 1)
    normed = (xhat_ref[...] * scale + bias).astype(BF16)
    normed_ref[...] = normed
    wide_ref[...] = spread(normed.astype(F32))
    upper, lower = (piece(g_ref, 0, 0, VEC + 11 + k, 1).astype(F32) for k in range(2))
    starts = upper * 256.0 + lower
    for n in range(start_ref.shape[0]):
        start_ref[n : n + 1, :] = jnp.broadcast_to(starts[:, n : n + 1], (1, 128))


def first_kernel(pairs, wide_ref, start_ref, g_ref, v_ref, lane_ref, row_ref, send_ref, scratch):
    rows = wide_ref.shape[0] // 2
    b_all = jnp.concatenate(weights(lambda m, f: piece(g_ref, m, f, 0, 96)), axis=1)
    v_ref[...] = dot(wide_ref[...], b_all, NT)

    decay, lam, log_dt = params_of(g_ref, VEC)
    abar_re, abar_im, coef_re, coef_im, step_size = discretize(decay, lam, log_dt)
    power = (abar_re, abar_im)
    for _ in range(8):
        power = cmul(power, power)
    scratch[...] = jnp.zeros((8, 128), F32)
    carry_block([power[0][m : m + 1] for m in range(2)], [power[1][m : m + 1] for m in range(2)], scratch)
    for k, value in enumerate((decay, lam, step_size, abar_re, abar_im, coef_re, coef_im, scratch[...])):
        row_ref[k] = value
    for k, value in enumerate((abar_re, abar_im, coef_re, coef_im)):
        for m in range(2):
            lane_ref[k : k + 1, 128 * m : 128 * m + 128] = value[m : m + 1]

    count = starts_until(offsets_of(start_ref), pair_pos() * rows, rows)
    open_tail = jnp.where(count == count[rows - 1 : rows], 1.0, 0.0)
    last = ([], [])
    for m in range(2):
        lanes = slice(128 * m, 128 * m + 128)
        eight, tail = eighth_powers((abar_re[m : m + 1], abar_im[m : m + 1]), 7)
        b = (coef_re[m : m + 1], coef_im[m : m + 1])
        acc = (jnp.zeros((8, 128), F32), jnp.zeros((8, 128), F32))
        for blk in range(rows // 8):
            here = slice(8 * blk, 8 * blk + 8)
            there = slice(rows + 8 * blk, rows + 8 * blk + 8)
            drive = cmul(b, (v_ref[here, lanes], v_ref[there, lanes]))
            moved = cmul(eight, acc)
            acc = (moved[0] + drive[0] * open_tail[here], moved[1] + drive[1] * open_tail[here])
        total = cmul(tail, acc)
        last[0].append(column_sum(total[0]))
        last[1].append(column_sum(total[1]))
    carry_block(last[0], last[1], scratch)
    packet = scratch[...]
    for d in range(pairs):
        send_ref[d] = packet


def eighth_powers(a, top):
    sub = lax.broadcasted_iota(jnp.int32, (8, 128), 0)
    exponent = (7 - sub) if top == 7 else sub + 1
    a = (jnp.broadcast_to(a[0], (8, 128)), jnp.broadcast_to(a[1], (8, 128)))
    tile = (jnp.ones((8, 128), F32), jnp.zeros((8, 128), F32))
    for bit in range(4):
        if bit == 3:
            eight = a
        taken = (exponent & (1 << bit)) != 0
        more = cmul(tile, a)
        tile = (jnp.where(taken, more[0], tile[0]), jnp.where(taken, more[1], tile[1]))
        a = cmul(a, a)
    return eight, tile


def scan_chunk(value, a, count, reverse):
    rows = count.shape[0]
    at = lax.broadcasted_iota(jnp.int32, (rows, 128), 0)
    step = 1
    while step < rows:
        shift = rows - step if reverse else step
        other = pltpu.roll(count, shift, 0)
        inside = (at < rows - step) if reverse else (at >= step)
        linked = inside & (other == count)
        moved = (pltpu.roll(value[0], shift, 0), pltpu.roll(value[1], shift, 0))
        more = cmul(a, moved)
        value = (value[0] + jnp.where(linked, more[0], 0.0), value[1] + jnp.where(linked, more[1], 0.0))
        a = cmul(a, a)
        step *= 2
    return value


def carried(recv_ref, row_ref, offsets, rows, reverse, scratch):
    pairs = recv_ref.shape[0]
    power = row_ref[7]
    pre, pim = power[0:2], power[2:4]
    if reverse:
        pim = -pim
    place = pair_pos()

    def turn(k, state):
        j = pairs - 1 - k if reverse else k
        link = no_start(offsets, j * rows, rows)
        got = recv_ref[j]
        new = cmul((pre * link, pim * link), state)
        return new[0] + got[0:2], new[1] + got[2:4]

    zero = jnp.zeros((2, 128), F32)
    out = lax.fori_loop(0, pairs - 1 - place if reverse else place, turn, (zero, zero))
    scratch[0:2, :] = out[0]
    scratch[2:4, :] = out[1]
    own = [lax.axis_index("ty") ^ m for m in range(2)]
    return [scratch[pl.ds(y, 1), :] for y in own], [scratch[pl.ds(2 + y, 1), :] for y in own]


def column_sum(value):
    return jnp.sum(value, axis=0, keepdims=True)


def states_kernel(recv_ref, start_ref, v_ref, lane_ref, row_ref, state_ref, twice_ref, enter_ref, scratch):
    rows = v_ref.shape[0] // 2
    half = rows // 2
    offsets = offsets_of(start_ref)
    base = pair_pos() * rows
    count = starts_until(offsets, base, rows)
    enter = carried(recv_ref, row_ref, offsets, rows, False, scratch)
    top = lax.broadcasted_iota(jnp.int32, (half, 128), 0) == 0
    links = (no_start(offsets, base, 1), jnp.where(count[half : half + 1] == count[half - 1 : half], 1.0, 0.0))
    for m in range(2):
        lanes = slice(128 * m, 128 * m + 128)
        a = (lane_ref[0:1, lanes], lane_ref[1:2, lanes])
        b = (lane_ref[2:3, lanes], lane_ref[3:4, lanes])
        before = (enter[0][m], enter[1][m])
        enter_ref[0:1, lanes] = before[0]
        enter_ref[1:2, lanes] = before[1]
        for h in range(2):
            here = slice(half * h, half * h + half)
            there = slice(rows + half * h, rows + half * h + half)
            drive = cmul(b, (v_ref[here, lanes], v_ref[there, lanes]))
            came = cmul((a[0] * links[h], a[1] * links[h]), before)
            drive = (drive[0] + jnp.where(top, came[0], 0.0), drive[1] + jnp.where(top, came[1], 0.0))
            state = scan_chunk(drive, a, count[here], False)
            before = (state[0][half - 1 : half], state[1][half - 1 : half])
            state_ref[here, lanes] = state[0]
            state_ref[there, lanes] = state[1]
            twice_ref[here, lanes] = state[0].astype(BF16) * 2
            twice_ref[there, lanes] = state[1].astype(BF16) * -2


def readout_kernel(twice_ref, c0_ref, c1_ref, own_ref, away_ref, scratch):
    rows = own_ref.shape[0]
    slots = (c0_ref, c1_ref)
    scratch[...] = folded(twice_ref[...], weights(lambda m, f: slots[m][f % 2, f // 2, 0:96, :]))
    own_ref[...] = scratch[own_rows(rows), :]
    away_ref[...] = scratch[other_rows(rows), :]


def second_kernel(
    own_ref, got_ref, up_ref, normed_ref, feat_ref, g0, g1, g2, g3,
    branch_ref, dmixed_ref, dlogit_ref, mine_ref, away_ref, gate_ref, all_ref,
):
    rows, width = up_ref.shape
    for core, slots in enumerate(((g0, g1), (g2, g3))):
        for m in range(2):
            lanes = pl.ds(pl.multiple_of(slot_pos(m, core) * 128, 128), 128)
            for f in range(GROUPS):
                place = (f // 2) * 2 + (lax.axis_index("fx") ^ (f % 2))
                gate_ref[pl.ds(pl.multiple_of(place * 64, 64), 64), lanes] = slots[m][f % 2, f // 2, 96:160, :]
    skip, gate_bias = feat_ref[1:2], feat_ref[2:3]
    normed = normed_ref[own_rows(rows), :].astype(F32)
    mixed = (own_ref[...] + got_ref[...]) + skip * normed
    cdf = 0.5 * (1.0 + lax.erf(mixed * 0.7071067811865476))
    act_low = (mixed * cdf).astype(BF16)
    act = act_low.astype(F32)
    w_gate = gate_ref[...]
    logit = dot(act_low, w_gate, NN) + gate_bias
    gate = 1.0 / (1.0 + jnp.exp(-logit))
    branch_ref[...] = (act * gate).astype(BF16)
    up = up_ref[...].astype(F32)
    dlogit = (up * act * gate * (1.0 - gate)).astype(BF16)
    dlogit_ref[...] = dlogit
    all_ref[...] = dlogit
    d_act = dot(dlogit, w_gate, NT) + up * gate
    slope = cdf + mixed * jnp.exp(-0.5 * mixed * mixed) * 0.3989422804014327
    d_mixed = d_act * slope
    dmixed_ref[...] = d_mixed
    for core, ref in enumerate((mine_ref, away_ref)):
        ref[:, 0:width] = d_mixed.astype(BF16)
        ref[:, width : 2 * width] = act_low
        for m in range(2):
            lanes = pl.ds(pl.multiple_of(slot_pos(m, core) * 128, 128), 128)
            ref[:, 2 * width + 128 * m : 2 * width + 128 * m + 128] = all_ref[:, lanes]


def sums_kernel(x_ref, branch_ref, normed_ref, dmixed_ref, dlogit_ref, out_ref, part_ref):
    x = x_ref[...].astype(F32)
    branch = branch_ref[...].astype(F32)
    out_ref[...] = (x + branch).astype(BF16)
    skip = column_sum(dmixed_ref[...] * normed_ref[own_rows(x_ref.shape[0]), :].astype(F32))
    for k, value in enumerate((skip, column_sum(dlogit_ref[...].astype(F32)), column_sum(x * x), column_sum(branch * branch))):
        part_ref[k : k + 1, :] = value


def back_kernel(
    pairs, mine_ref, got_ref, twice_ref, start_ref, lane_ref, c0_ref, c1_ref,
    dstate_ref, send_ref, stay_ref, leave_ref, dy_ref, dgate_ref, scratch,
):
    rows, width = dy_ref.shape
    half = rows // 2
    dy_ref[own_rows(half), :] = mine_ref[:, 0:width]
    dy_ref[other_rows(half), :] = got_ref[:, 0:width]
    slots = (c0_ref, c1_ref)
    c_all = jnp.concatenate(weights(lambda m, f: slots[m][f % 2, f // 2, 0:96, :]), axis=1)
    spread_dy = spread(dy_ref[...].astype(F32))
    d_state = dot(spread_dy, c_all, NT)
    dstate_ref[:rows] = d_state[:rows] * 2.0
    dstate_ref[rows:] = d_state[rows:] * -2.0
    count = starts_until(offsets_of(start_ref), pair_pos() * rows, rows)
    head = jnp.where(count == 0.0, 1.0, 0.0)
    first = ([], [])
    for m in range(2):
        lanes = slice(128 * m, 128 * m + 128)
        eight, tail = eighth_powers((lane_ref[0:1, lanes], -lane_ref[1:2, lanes]), 0)
        acc = (jnp.zeros((8, 128), F32), jnp.zeros((8, 128), F32))
        for blk in range(rows // 8 - 1, -1, -1):
            here = slice(8 * blk, 8 * blk + 8)
            there = slice(rows + 8 * blk, rows + 8 * blk + 8)
            moved = cmul(eight, acc)
            acc = (moved[0] + dstate_ref[here, lanes] * head[here], moved[1] + dstate_ref[there, lanes] * head[here])
        total = cmul(tail, acc)
        first[0].append(column_sum(total[0]))
        first[1].append(column_sum(total[1]))
    scratch[...] = jnp.zeros((8, 128), F32)
    carry_block(first[0], first[1], scratch)
    packet = scratch[...]
    for d in range(pairs):
        send_ref[d] = packet
    d_c = dot(twice_ref[...], spread_dy, TN).astype(BF16)
    act = slice(width, 2 * width)
    units = slice(2 * width, 2 * width + 256)
    d_gate = dot(mine_ref[:, act], mine_ref[:, units], TN) + dot(got_ref[:, act], got_ref[:, units], TN)
    dgate_ref[...] = d_gate.astype(BF16)
    for m, ref in enumerate((stay_ref, leave_ref)):
        for f in range(GROUPS):
            ref[f, 0:96, :] = d_c[128 * m : 128 * m + 96, 128 * f : 128 * f + 128]
            place = pl.ds(pl.multiple_of(((f // 2) * 2 + (lax.axis_index("fx") ^ (f % 2))) * 64, 64), 64)
            ref[f, 96:160, :] = dgate_ref[place, 128 * m : 128 * m + 128]


def split_rows(value):
    upper = value.astype(BF16)
    return jnp.concatenate([upper, (value - upper.astype(F32)).astype(BF16)], axis=0)


def third_kernel(
    recv_ref, start_ref, wide_ref, xhat_ref, v_ref, lane_ref, row_ref, feat_ref, state_ref, dstate_ref, enter_ref, dmixed_ref,
    part_ref, g_ref, stay_ref, y_ref, x_ref, xy_ref, dn_ref, dnaway_ref, scratch, dv_ref, all_ref, vec_ref,
):
    rows, width = xhat_ref.shape
    half = rows // 2
    offsets = offsets_of(start_ref)
    base = pair_pos() * rows
    count = starts_until(offsets, base, rows)
    later = carried(recv_ref, row_ref, offsets, rows, True, scratch)
    at = lax.broadcasted_iota(jnp.int32, (half, 128), 0)
    top, bottom = at == 0, at == half - 1
    before = jnp.where(lax.broadcasted_iota(jnp.int32, (rows, 128), 0) == 0, 0.0, pltpu.roll(count, 1, 0))
    keep = jnp.where(count == before, 1.0, 0.0)
    sums = ([], [], [], [])
    for m in range(2):
        lanes = slice(128 * m, 128 * m + 128)
        a = (lane_ref[0:1, lanes], -lane_ref[1:2, lanes])
        b = (lane_ref[2:3, lanes], -lane_ref[3:4, lanes])
        came = (later[0][m], later[1][m])
        totals = None
        for h in (1, 0):
            here = slice(half * h, half * h + half)
            there = slice(rows + half * h, rows + half * h + half)
            start = (
                dstate_ref[here, lanes] + jnp.where(bottom, came[0], 0.0),
                dstate_ref[there, lanes] + jnp.where(bottom, came[1], 0.0),
            )
            adj = scan_chunk(start, a, count[here], True)
            if h:
                link = keep[half : half + 1]
                came = cmul((a[0] * link, a[1] * link), (adj[0][0:1], adj[1][0:1]))
                edge = (state_ref[half - 1 : half, lanes], state_ref[rows + half - 1 : rows + half, lanes])
            else:
                edge = (enter_ref[0:1, lanes], enter_ref[1:2, lanes])
            prev = (
                jnp.where(top, edge[0], pltpu.roll(state_ref[here, lanes], 1, 0)) * keep[here],
                jnp.where(top, edge[1], pltpu.roll(state_ref[there, lanes], 1, 0)) * keep[here],
            )
            v = (v_ref[here, lanes], v_ref[there, lanes])
            new = [
                column_sum(adj[0] * prev[0] + adj[1] * prev[1]),
                column_sum(adj[1] * prev[0] - adj[0] * prev[1]),
                column_sum(adj[0] * v[0] + adj[1] * v[1]),
                column_sum(adj[1] * v[0] - adj[0] * v[1]),
            ]
            totals = new if totals is None else [p + q for p, q in zip(totals, new)]
            dv = cmul(b, adj)
            dv_ref[here, lanes] = dv[0].astype(BF16)
            dv_ref[there, lanes] = dv[1].astype(BF16)
        for k in range(4):
            sums[k].append(totals[k])
    dv = dv_ref[...]
    d_b = dot(dv, wide_ref[...], TN).astype(BF16)
    for ref, m, j in ((stay_ref, 0, 0), (y_ref, 1, 0), (x_ref, 0, 1), (xy_ref, 1, 1)):
        for z in range(GROUPS // 2):
            f = 2 * z + j
            ref[96 * z : 96 * z + 96, :] = d_b[128 * m : 128 * m + 96, 128 * f : 128 * f + 128]
    all_ref[...] = folded(dv, weights(lambda m, f: piece(g_ref, m, f, 0, 96)))
    dnaway_ref[...] = all_ref[other_rows(half), :]
    own = all_ref[own_rows(half), :] + dmixed_ref[...] * feat_ref[1:2]
    dn_ref[...] = own
    all_ref[own_rows(half), :] = own
    d_normed = all_ref[...]
    vector = [column_sum(d_normed * xhat_ref[...]), column_sum(d_normed), part_ref[0:1, :], part_ref[1:2, :]]
    for k, value in enumerate(vector):
        for c in range(4):
            vec_ref[4 * k + c : 4 * k + c + 1, :] = value[:, 128 * c : 128 * c + 128]
    g = [jnp.concatenate(pair + [jnp.zeros((6, 128), F32)], axis=0) for pair in sums]
    decay, lam, step, abar_re, abar_im, coef_re, coef_im = (row_ref[k] for k in range(7))
    d_abar, d_coef = (g[0], g[1]), (g[2], g[3])
    denom = decay * decay + lam * lam
    numer = (step * abar_re - coef_re, step * abar_im - coef_im)
    ratio = cmul(numer, (-decay / denom, -lam / denom))
    to_lam_a = cmul((step * abar_re, -step * abar_im), d_abar)
    to_lam_c = cmul((ratio[0], -ratio[1]), d_coef)
    g_decay = -(to_lam_a[0] + to_lam_c[0])
    g_lam = to_lam_a[1] + to_lam_c[1]
    slope = cmul((-decay, lam), (abar_re, abar_im))
    g_step = (slope[0] * d_abar[0] + slope[1] * d_abar[1] + abar_re * d_coef[0] + abar_im * d_coef[1]) * step
    vec_ref[16:32, :] = jnp.zeros((16, 128), F32)
    for k, value in enumerate((g_decay, g_lam, g_step)):
        for m in range(2):
            vec_ref[pl.ds(16 + 4 * k + slot_pos(m, 0), 1), :] = value[m : m + 1]
    for k in range(2):
        squares = part_ref[2 + k : 3 + k, :]
        total = squares[:, 0:128]
        for c in range(1, 4):
            total = total + squares[:, 128 * c : 128 * c + 128]
        vec_ref[28 + k : 29 + k, :] = total
    vec_ref[30:32, :] = jnp.zeros((2, 128), F32)
    vec = split_rows(vec_ref[...])
    for ref in (stay_ref, y_ref, x_ref, xy_ref):
        ref[384:448, :] = vec


def input_grad_kernel(dn_ref, got_ref, up_ref, xhat_ref, inv_ref, feat_ref, gin_ref):
    rows, width = up_ref.shape
    xhat = xhat_ref[own_rows(rows), :]
    d_xhat = (dn_ref[...] + got_ref[...]) * feat_ref[0:1]
    mean = jnp.sum(d_xhat, axis=1, keepdims=True) / width
    mean_hat = jnp.sum(d_xhat * xhat, axis=1, keepdims=True) / width
    gin_ref[...] = up_ref[...].astype(F32) + inv_ref[:, 0:1] * (d_xhat - mean - xhat * mean_hat)


def added(a, b):
    return (a.astype(F32) + b.astype(F32)).astype(BF16)


def joined(packet):
    return packet[0:32].astype(F32) + packet[32:64].astype(F32)


def y_cw_kernel(keep_ref, got_ref, stay_ref, leave_ref):
    for z in range(GROUPS // 2):
        f, other = 2 * z, 2 * z + 1
        stay_ref[z] = added(keep_ref[f], got_ref[f])
        leave_ref[z] = added(keep_ref[other], got_ref[other])


def plane_add_kernel(cw_ref, gotcw_ref, stay_ref, y_ref, x_ref, xy_ref, out_ref):
    def total(read):
        return (read(stay_ref) + read(y_ref)) + (read(x_ref) + read(xy_ref))

    vec = split_rows(total(lambda ref: joined(ref[384:448, :])))
    for z in range(GROUPS // 2):
        here = slice(96 * z, 96 * z + 96)
        out_ref[z, 0:96, :] = total(lambda ref, here=here: ref[here, :].astype(F32)).astype(BF16)
        out_ref[z, 96:256, :] = added(cw_ref[z], gotcw_ref[z])
        out_ref[z, 256:320, :] = vec


def vectors_kernel(got_ref, vec_ref):
    vec = joined(got_ref[0, 256:320, :])
    for z in range(1, GROUPS // 2):
        vec = vec + joined(got_ref[z, 256:320, :])
    vec_ref[...] = vec


def rows_to_lanes(rows):
    turned = [rows, pltpu.roll(rows, 96, 1), pltpu.roll(rows, 64, 1), pltpu.roll(rows, 32, 1)]
    lane = lane_iota((1, 128))
    return [
        jnp.where(lane < 96, rows[0:1], turned[1][1:2]),
        jnp.where(lane < 64, turned[1][1:2], turned[2][2:3]),
        jnp.where(lane < 32, turned[2][2:3], turned[3][3:4]),
    ]


def matrices_kernel(got_ref, dre_ref, dim_ref, ore_ref, oim_ref, glu_ref, square):
    def total(start, count):
        value = got_ref[0, start : start + count, :].astype(F32)
        for z in range(1, GROUPS // 2):
            value = value + got_ref[z, start : start + count, :].astype(F32)
        return value

    for start, first_ref, second_ref in ((0, dre_ref, dim_ref), (96, ore_ref, oim_ref)):
        square[0:96, :] = total(start, 96)
        square[96:128, :] = jnp.zeros((32, 128), F32)
        turned = square[...].T
        first_ref[...] = turned[0:64, 0:96]
        second_ref[...] = turned[64:128, 0:96]
    glu_ref[...] = total(192, 64)


def finish_kernel(
    count_all, own_ref, other_ref, gbias_ref, scale_ref, bias_ref, skip_ref, decay_ref, lam_ref, step_ref, rms_ref, vec_ref
):
    vec = own_ref[...] + other_ref[...]
    vec_ref[...] = vec
    for k, ref in enumerate((scale_ref, bias_ref, skip_ref)):
        for c in range(4):
            ref[:, 128 * c : 128 * c + 128] = vec[4 * k + c : 4 * k + c + 1]
    for k, ref in enumerate((decay_ref, lam_ref, step_ref)):
        for c, chunk in enumerate(rows_to_lanes(vec[16 + 4 * k : 20 + 4 * k])):
            ref[128 * c : 128 * c + 128] = chunk.reshape(128)
    total = jnp.sum(vec[28:30], axis=1, keepdims=True)
    lane = lane_iota((1, 2))
    rms_ref[...] = jnp.sqrt(jnp.where(lane == 0, total[0:1], total[1:2]) / count_all)
    place = tensor_pos() * GROUPS + fsdp_pos()
    row = jnp.broadcast_to(vec_ref[pl.ds(12 + place // 8, 1), :], (8, 128))
    gbias_ref[...] = pltpu.roll(row, 128 - 16 * (place % 8), 1)[0:1, 0:16]


TAKES = {
    "pack": 1.5, "standardize": 0.4, "norm": 0.4, "first": 1.4, "states": 1.5, "readout": 0.5, "second": 1.2, "sums": 0.7, "back": 1.6,
    "third": 2.4, "input_grad": 0.5, "matrices": 0.5, "finish": 0.4,
}


def call(kernel, outs, args, scratch=(), specs=None, limit=24):
    name = getattr(kernel, "func", kernel).__name__.removesuffix("_kernel")
    return pl.pallas_call(
        kernel,
        out_shape=outs,
        in_specs=specs or [VM] * len(args),
        out_specs=jax.tree.map(lambda _: VM, outs),
        scratch_shapes=list(scratch),
        compiler_params=pltpu.CompilerParams(vmem_limit_bytes=limit << 20),
        cost_estimate=pl.CostEstimate(flops=0, transcendentals=0, bytes_accessed=int(TAKES.get(name, 0.1) * 3.6e6)),
        name=name,
    )(*args)


def tied(value, other):
    return lax.optimization_barrier((value, other))[0]


def swap(value, axis):
    return lax.ppermute(value, axis, [(0, 1), (1, 0)])


def across(value):
    return lax.ppermute(value, ("fx", "ty"), [(n, 3 - n) for n in range(4)])


def on_device(
    layer_in, grad_out, ln_scale, ln_bias, decay_rate, lam_im, log_dt, in_re, in_im, out_re, out_im, skip, glu_weight, glu_bias, seq_lengths
):
    rows, width = layer_in.shape
    fsdp = lax.axis_size(FSDP)
    pairs, pair = fsdp * 2, 2 * rows
    count_all = float(rows * pairs * 2 * width)
    fast = fsdp == GROUPS
    same_core = (*FSDP, "ty")
    if fast:
        row = lambda v: v.reshape(1, -1)
        sent = call(
            pack_kernel,
            sds((GROUPS // 2, 272, 128), BF16),
            (seq_lengths, in_re.T, in_im.T, out_re.T, out_im.T, glu_weight.T, row(ln_scale), row(ln_bias), row(skip), row(glu_bias),
             row(decay_rate), row(lam_im), row(log_dt)),
            [pltpu.VMEM((128, 128), F32), pltpu.VMEM((4, 64, 96), BF16), pltpu.VMEM((64, 128), BF16), pltpu.VMEM((4, 1, 64), BF16),
             pltpu.VMEM((3, 1, 96), F32), pltpu.SMEM(seq_lengths.shape, jnp.int32), pltpu.SemaphoreType.DMA((13,))],
            [HBM] * 13,
            60,
        )
        mine = lax.all_to_all(sent, "fz", 0, 0, tiled=True)
        own_b, own_cw = lax.optimization_barrier((mine[:, :112], mine[:, 112:]))
        plane_b = [own_b, swap(own_b, "ty"), swap(own_b, "fx"), across(own_b)]
        plane_b, side_cw = lax.optimization_barrier((plane_b, swap(own_cw, "fx")))
        side_cw = jnp.stack([own_cw, side_cw])
        far_cw = swap(side_cw, "ty")
        g = jnp.stack(plane_b).reshape(2, 2, GROUPS // 2, 112, 128)
    else:
        g, g_cw = gathered(
            ln_scale, ln_bias, decay_rate, lam_im, log_dt, in_re, in_im, out_re, out_im, skip, glu_weight, glu_bias, seq_lengths
        )

    xhat, inverse = call(standardize_kernel, (sds((pair, width)), sds((rows, 128))), (layer_in, swap(layer_in, "tc")))
    normed, wide, feat, starts = call(
        norm_kernel,
        (sds((pair, width), BF16), sds((2 * pair, 2 * width), BF16), sds((8, width)), sds((seq_lengths.shape[0], 128))),
        (xhat, g),
    )
    v, lane, row_prm, carry = call(
        functools.partial(first_kernel, pairs),
        (sds((2 * pair, 256)), sds((8, 256)), sds((8, 8, 128)), sds((pairs, 8, 128))),
        (wide, starts, g),
        [pltpu.VMEM((8, 128), F32)],
    )
    came = lax.all_to_all(carry, same_core, 0, 0, tiled=True)
    if fast:
        g_cw = tied((side_cw, far_cw), came)
    state, twice, enter = call(
        states_kernel,
        (sds((2 * pair, 256)), sds((2 * pair, 256), BF16), sds((8, 256))),
        (came, starts, v, lane, row_prm),
        [pltpu.VMEM((8, 128), F32)],
    )
    if fast:
        far = tied(g_cw, twice)
        g_cw = (*g_cw, swap(far[0], "tc"), swap(far[1], "tc"))
    own, away = call(
        readout_kernel, (sds((rows, width)), sds((rows, width))), (twice, *g_cw[:2]), [pltpu.VMEM((pair, width), F32)]
    )
    branch, d_mixed, dlogit, kept, away = call(
        second_kernel,
        (sds((rows, width), BF16), sds((rows, width)), sds((rows, width), BF16), *[sds((rows, 2 * width + 256), BF16)] * 2),
        (own, swap(away, "tc"), grad_out, normed, feat, *g_cw),
        [pltpu.VMEM((width, width), BF16), pltpu.VMEM((rows, width), BF16)],
    )
    got = swap(away, "tc")
    layer_out, part = call(
        sums_kernel, (sds((rows, width), BF16), sds((8, width))), (layer_in, branch, normed, d_mixed, dlogit)
    )
    got, part = lax.optimization_barrier((got, part))
    d_state, carry, stay_cw, leave_cw = call(
        functools.partial(back_kernel, pairs),
        (sds((2 * pair, 256)), sds((pairs, 8, 128)), sds((GROUPS, 160, 128), BF16), sds((GROUPS, 160, 128), BF16)),
        (kept, got, twice, starts, lane, *g_cw[:2]),
        [pltpu.VMEM((pair, width), BF16), pltpu.VMEM((width, 256), BF16), pltpu.VMEM((8, 128), F32)],
    )
    if fast:
        far_cw = swap(leave_cw, "ty")
    came = lax.all_to_all(carry, same_core, 0, 0, tiled=True)
    if fast:
        came, far_cw, stay_cw = lax.optimization_barrier((came, far_cw, stay_cw))
        stay_cw, leave_cw = call(y_cw_kernel, [sds((GROUPS // 2, 160, 128), BF16)] * 2, (stay_cw, far_cw))
        far_cw = swap(leave_cw, "fx")
        came = tied(came, leave_cw)
    stay_b, y_b, x_b, xy_b, d_normed, away = call(
        third_kernel,
        (*[sds((448, 128), BF16)] * 4, sds((rows, width)), sds((rows, width))),
        (came, starts, wide, xhat, v, lane, row_prm, feat, state, d_state, enter, d_mixed, part, g),
        [pltpu.VMEM((8, 128), F32), pltpu.VMEM((2 * pair, 256), BF16), pltpu.VMEM((pair, width), F32), pltpu.VMEM((32, 128), F32)],
    )
    input_grad = lambda away: call(
        input_grad_kernel, sds((rows, width)), (d_normed, swap(away, "tc"), grad_out, xhat, inverse, feat)
    )
    if not fast:
        grad_in = input_grad(away)
        return reduced(layer_out, grad_in, stay_cw, leave_cw, (stay_b, y_b, x_b, xy_b), count_all, fsdp, width)
    sent = call(
        plane_add_kernel,
        sds((GROUPS // 2, 320, 128), BF16),
        (stay_cw, far_cw, stay_b, swap(y_b, "ty"), swap(x_b, "fx"), across(xy_b)),
    )
    got = lax.all_to_all(sent, "fz", 0, 0, tiled=True)
    grad_in = input_grad(tied(away, got))
    vec = call(vectors_kernel, sds((32, 128)), (got,))
    other = swap(vec, "tc")
    d_re, d_im, d_ore, d_oim, d_glu = call(
        matrices_kernel, (*[sds((64, 96))] * 4, sds((64, 128))), (got,), [pltpu.VMEM((128, 128), F32)]
    )
    d_gbias, d_scale, d_bias, d_skip, g_decay, g_lam, g_step, rms = call(
        functools.partial(finish_kernel, count_all),
        (sds((1, 16)), *[sds((1, 512))] * 3, *[sds((384,))] * 3, sds((1, 2))),
        (vec, other),
        [pltpu.VMEM((32, 128), F32)],
    )
    flat = lambda value: value.reshape(-1)
    return (
        layer_out, grad_in, flat(d_scale), flat(d_bias), g_decay, g_lam, g_step, d_re.T, d_im.T, d_ore.T, d_oim.T,
        flat(d_skip), d_glu.T, flat(d_gbias), flat(rms),
    )


def gathered(ln_scale, ln_bias, decay_rate, lam_im, log_dt, in_re, in_im, out_re, out_im, skip, glu_weight, glu_bias, seq_lengths):
    tens = tensor_pos()
    full = lambda value, axis: lax.all_gather(value, FSDP, axis=axis, tiled=True)

    def pair(first, second):
        halves = jnp.stack([first.reshape(-1, GROUPS, 64), second.reshape(-1, GROUPS, 64)], axis=2)
        return halves.reshape(-1, GROUPS, 128).swapaxes(0, 1)

    gate = lax.dynamic_slice_in_dim(full(glu_weight, 1), tens * 128, 128, 0).T.reshape(GROUPS, 64, 128)
    vectors = [pair(full(ln_scale, 0)[None], full(ln_bias, 0)[None]), pair(full(skip, 0)[None], full(glu_bias, 0)[None])]
    for value in (decay_rate, lam_im, log_dt):
        value = jnp.pad(value, (0, 32))
        for _ in range(3):
            piece = lax.reduce_precision(value, 8, 7)
            value = value - piece
            vectors.append(jnp.broadcast_to(piece.astype(BF16)[None, None], (GROUPS, 1, 128)))
    starts = jnp.cumsum(seq_lengths) - seq_lengths
    for value in (starts >> 8, starts & 255):
        value = jnp.pad(value, (0, 128 - value.shape[0])).astype(BF16)
        vectors.append(jnp.broadcast_to(value[None, None], (GROUPS, 1, 128)))
    vectors.append(jnp.zeros((GROUPS, 3, 128), BF16))
    packet = jnp.concatenate(
        [pair(full(in_re, 1), full(in_im, 1)), *vectors, pair(full(out_re, 1), full(out_im, 1)), gate],
        axis=1,
    )
    everyone = lax.all_gather(packet, TENSOR, axis=0).reshape(2, 2, GROUPS // 2, 2, 272, 128)
    x, y, core = (lax.axis_index(axis) for axis in ("fx", "ty", "tc"))
    own_x = lambda value, axis: jnp.stack([lax.dynamic_index_in_dim(value, x ^ j, axis, keepdims=False) for j in range(2)])
    g_cw = []
    for i in range(2):
        both = lax.dynamic_index_in_dim(everyone, core ^ i, 1, keepdims=False)
        slots = [own_x(lax.dynamic_index_in_dim(both, y ^ m, 0, keepdims=False), 1) for m in range(2)]
        g_cw += [slot[:, :, 112:] for slot in slots]
        if i == 0:
            g = jnp.stack(slots, axis=1)[:, :, :, :112]
    return g, g_cw


def reduced(layer_out, grad_in, stay_cw, leave_cw, plane_b, count_all, fsdp, width):
    tens = tensor_pos()
    x = lax.axis_index("fx")

    def canonical(slots):
        out = jnp.zeros((4, GROUPS, *slots[0].shape[2:]), F32)
        for m, slot in enumerate(slots):
            parts = [lax.dynamic_index_in_dim(slot.astype(F32), x ^ n, 1) for n in range(2)]
            block = jnp.concatenate(parts, axis=1).reshape(1, GROUPS, *slot.shape[2:])
            out = lax.dynamic_update_slice_in_dim(out, block, slot_pos(m, 0), 0)
        return out

    def natural(slots):
        halves = canonical(slots).reshape(4, GROUPS, -1, 2, 64).transpose(3, 0, 2, 1, 4)
        return halves[0].reshape(-1, width), halves[1].reshape(-1, width)

    def scattered(value):
        value = lax.psum_scatter(value, TENSOR, scatter_dimension=0, tiled=True)
        return lax.psum_scatter(value, FSDP, scatter_dimension=1, tiled=True)

    blocks = [value[:384].reshape(GROUPS // 2, 96, 128) for value in plane_b]
    d_re, d_im = natural([jnp.stack([blocks[m], blocks[2 + m]], axis=1) for m in range(2)])
    cw = [value.reshape(GROUPS // 2, 2, 160, 128) for value in (stay_cw, leave_cw)]
    d_ore, d_oim = natural([value[:, :, :96] for value in cw])
    d_glu = canonical([value[:, :, 96:] for value in cw]).reshape(4, width, 128).swapaxes(1, 2).reshape(-1, width)
    vec = lax.psum(joined(plane_b[0][384:448]), AXES)
    states = lambda k: vec[16 + 4 * k : 20 + 4 * k, :96].reshape(-1)
    own = width // (4 * fsdp)
    place = tens * fsdp + fsdp_pos()
    d_gbias = lax.dynamic_slice_in_dim(vec[12:16].reshape(-1), place * own, own, 0)
    rms = jnp.sqrt(jnp.sum(vec[28:30], axis=1) / count_all)
    return (
        layer_out, grad_in, vec[0:4].reshape(-1), vec[4:8].reshape(-1), states(0), states(1), states(2), scattered(d_re), scattered(d_im),
        scattered(d_ore), scattered(d_oim), vec[8:12].reshape(-1), scattered(d_glu), d_gbias, rms,
    )


def solution(mesh):
    shape = (mesh.shape["fsdp"] // 2, 2, mesh.shape["tensor"] // 2, 2)
    split = Mesh(mesh.devices.reshape(shape), AXES)
    tokens, matrix = P(AXES, None), P(TENSOR, FSDP)
    return jax.shard_map(
        on_device,
        mesh=split,
        in_specs=(
            tokens, tokens, P(FSDP), P(FSDP), P(TENSOR), P(TENSOR), P(TENSOR), matrix, matrix, matrix, matrix,
            P(FSDP), P(None, FSDP), P(FSDP), P(),
        ),
        out_specs=(
            tokens, tokens, P(), P(), P(), P(), P(), matrix, matrix, matrix, matrix, P(), matrix, P((*TENSOR, *FSDP)), P(),
        ),
        check_vma=False,
    )
```

time: 89.6 us -> 86.5 us (0.965)
  waiting for transfers between devices: 21.7 us -> 12 us
  blocking collectives: 39.1 us -> 48 us
  starting transfers between devices: 15.9 us -> 13 us
    all_to_all x1 -> x2, blocking collectives: 10.9 us -> 22 us  [on_device(): came = lax.all_to_all(carry, same_core, 0, 0, tiled=True)]
    all_to_all x1 -> x0, waiting for transfers between devices: 5.39 us -> none  [on_device(): came = lax.all_to_all(carry, AXES, 0, 0, tiled=True)]
    ppermute x13 -> x15, waiting for transfers between devices: 11.1 us -> 6.55 us  [swap(): return lax.ppermute(value, axis, [(0, 1), (1, 0)])]
    all_to_all x1 -> x0, starting transfers between devices: 4.3 us -> none  [on_device(): came = lax.all_to_all(carry, AXES, 0, 0, tiled=True)]
    all_to_all x1, blocking collectives: 12.7 us -> 10.4 us  [on_device(): got = lax.all_to_all(sent, 'fz', 0, 0, tiled=True)]
    ppermute x13 -> x15, starting transfers between devices: 7.92 us -> 10.2 us  [swap(): return lax.ppermute(value, axis, [(0, 1), (1, 0)])]
    pallas_call x15 -> x16, Pallas kernels: 11.6 us -> 12.2 us  [call(): pl.pallas_call(kernel, out_shape=outs, in_specs=specs or [VM] * len(args)...]
  transfers between devices with their start and end apart: 16 -> 17, of which waited for: 13 -> 8; matrix products, arithmetic and copies ran while one was open for 0% -> 0% of each run, Pallas kernels for 4% -> 9%
where the time goes in v4:
time: 86.5 us; the launch traced here: 86.1 us
  blocking collectives  48 us (55%)
  starting transfers between devices  13 us (15%)
  Pallas kernels  12.2 us (14%)
  waiting for transfers between devices  12 us (14%)
    all_to_all x2, blocking collectives, on_device(): came = lax.all_to_all(carry, same_core, 0, 0, tiled=True)  22 us
    all_to_all x1, blocking collectives, on_device(): mine = lax.all_to_all(sent, 'fz', 0, 0, tiled=True)  15.6 us
    pallas_call x16, Pallas kernels, call(): pl.pallas_call(kernel, out_shape=outs, in_specs=specs or [VM] * len(args)...  12.2 us
    all_to_all x1, blocking collectives, on_device(): got = lax.all_to_all(sent, 'fz', 0, 0, tiled=True)  10.4 us
    ppermute x15, starting transfers between devices, swap(): return lax.ppermute(value, axis, [(0, 1), (1, 0)])  10.2 us
    ppermute x15, waiting for transfers between devices, swap(): return lax.ppermute(value, axis, [(0, 1), (1, 0)])  6.55 us
    ppermute x2, waiting for transfers between devices, across(): return lax.ppermute(value, ('fx', 'ty'), [(n, 3 - n) for n in range(4)])  5.48 us
    ppermute x2, starting transfers between devices, across(): return lax.ppermute(value, ('fx', 'ty'), [(n, 3 - n) for n in range(4)])  2.82 us
  transfers between devices with their start and end apart: 17, of which 8 were waited for; matrix products, arithmetic and copies ran while one was open for 0% of the time, Pallas kernels for 9%

profile of v4, /device:TPU:0, one launch (start us, length us, event | category | flops | bytes accessed | tf_op | source)
XLA Modules:
  0.0 86.1 jit_solution(15077783143308696323)
XLA Ops:
  0.7 1.8 %pack.1 = bf16[4,272,128]{2,1,0:T(8,128)(2,1)} custom-call(s32[4]{0:T(128)} %refs_0_.1, bf16[64,96]{1,0:T(8,128)(2,1)} %bitcast.39, bf16[64,96]{1,0:T(8,128)(2,1)} %bitcast.40, bf16[64,96]{1,0:T(8,128)(2,1)} %bitcast.41, bf16[64,96]{1,0:T(8,128)(2,1)} %bitcast.42, bf16[64,512]{1,0:T(8,128)(2,1)} %bitcast.38, bf16[1,64]{1,0:T(2,128)(2,1)} %bitcast.43, ...), custom_call_target="tpu_custom_call" | custom-call | bytes 5400000 | tf_op jit(solution)/shard_map/pack/pallas_call | solution.py:682
  2.4 15.6 %all_to_all.20 = bf16[4,272,128]{2,1,0:T(8,128)(2,1)S(1)} all-to-all(bf16[4,272,128]{2,1,0:T(8,128)(2,1)} %pack.1), channel_id=1, replica_groups=mesh['fz'=4,'fx'=2,'ty'=2,'tc'=2] {'fz'}, dimensions={0} | all-to-all | bytes 557056 | tf_op jit(solution)/shard_map/all_to_all | solution.py:727
  18.0 1.6 %collective-permute-start.4 = (bf16[4,160,128]{2,1,0:T(8,128)(2,1)S(1)}, bf16[4,160,128]{2,1,0:T(8,128)(2,1)S(1)}, u32[]{:S(2)}, u32[]{:S(2)}) collective-permute-start(bf16[4,160,128]{2,1,0:T(8,128)(2,1)S(1)} %slice.9), channel_id=1, source_target_pairs={{0,4},{4,0},{1,5},{5,1},{2,6},{6,2},{3,7},{7,3},{8,12},{12,8},{9,1... | collective-permute-start | bytes 491528 | tf_op jit(solution)/shard_map/ppermute | solution.py:699
  19.6 1.5 %collective-permute-start.3 = (bf16[4,112,128]{2,1,0:T(8,128)(2,1)S(1)}, bf16[4,112,128]{2,1,0:T(8,128)(2,1)S(1)}, u32[]{:S(2)}, u32[]{:S(2)}) collective-permute-start(bf16[4,112,128]{2,1,0:T(8,128)(2,1)S(1)} %slice.8), channel_id=1, source_target_pairs={{0,6},{2,4},{4,2},{6,0},{1,7},{3,5},{5,3},{7,1},{8,14},{10,12},{12... | collective-permute-start | bytes 344072 | tf_op jit(solution)/shard_map/ppermute | solution.py:703
  21.1 1.5 %collective-permute-start.2 = (bf16[4,112,128]{2,1,0:T(8,128)(2,1)S(1)}, bf16[4,112,128]{2,1,0:T(8,128)(2,1)S(1)}, u32[]{:S(2)}, u32[]{:S(2)}) collective-permute-start(bf16[4,112,128]{2,1,0:T(8,128)(2,1)S(1)} %slice.8), channel_id=1, source_target_pairs={{0,4},{4,0},{1,5},{5,1},{2,6},{6,2},{3,7},{7,3},{8,12},{12,8},{9,1... | collective-permute-start | bytes 344072 | tf_op jit(solution)/shard_map/ppermute | solution.py:699
  23.1 3.5 %collective-permute-done.3 = bf16[4,112,128]{2,1,0:T(8,128)(2,1)S(1)} collective-permute-done((bf16[4,112,128]{2,1,0:T(8,128)(2,1)S(1)}, bf16[4,112,128]{2,1,0:T(8,128)(2,1)S(1)}, u32[]{:S(2)}, u32[]{:S(2)}) %collective-permute-start.3) | collective-permute-done | bytes 114720 | tf_op jit(solution)/shard_map/ppermute | solution.py:703
  27.2 1.1 %collective-permute-done.1 = bf16[4,112,128]{2,1,0:T(8,128)(2,1)S(1)} collective-permute-done((bf16[4,112,128]{2,1,0:T(8,128)(2,1)S(1)}, bf16[4,112,128]{2,1,0:T(8,128)(2,1)S(1)}, u32[]{:S(2)}, u32[]{:S(2)}) %collective-permute-start.1) | collective-permute-done | bytes 114720 | tf_op jit(solution)/shard_map/ppermute | solution.py:699
  28.4 1.3 %collective-permute-start.5 = (bf16[2,4,160,128]{3,2,1,0:T(8,128)(2,1)S(1)}, bf16[2,4,160,128]{3,2,1,0:T(8,128)(2,1)S(1)}, u32[]{:S(2)}, u32[]{:S(2)}) collective-permute-start(bf16[2,4,160,128]{3,2,1,0:T(8,128)(2,1)S(1)} %pad_maximum_fusion.1.c0_ref.g0), channel_id=1, source_target_pairs={{0,2},{2,0},{1,3},{3,1},{4,6},{6,4},{5,7},{7,5},{8,10},{10,8},{9,1... | collective-permute-start | bytes 983048 | tf_op jit(solution)/shard_map/ppermute | solution.py:699
  30.8 11.5 %all_to_all.21.recv_ref = f32[16,8,128]{2,1,0:T(8,128)S(1)} all-to-all(f32[16,8,128]{2,1,0:T(8,128)S(1)} %get-tuple-element.89), channel_id=1, replica_groups=mesh['fz'=4,'fx'=2,'ty'=2,'tc'=2] {'fz','fx','ty'}, dimensions={0} | all-to-all | bytes 131072 | tf_op jit(solution)/shard_map/all_to_all | solution.py:751
  42.3 1.0 %states.1 = (f32[512,256]{1,0:T(8,128)S(1)}, bf16[512,256]{1,0:T(8,128)(2,1)S(1)}, f32[8,256]{1,0:T(8,128)S(1)}) custom-call(f32[16,8,128]{2,1,0:T(8,128)S(1)} %all_to_all.21.recv_ref, f32[4,128]{1,0:T(4,128)S(1)} %get-tuple-element.88.start_ref, f32[512,256]{1,0:T(8,128)S(1)} %get-tuple-element.90.v_ref, f32[8,256]{1,0:T(8,128)S(1)} %get-tuple-element.91.lane_ref, ...), custom_call_target="tpu_custom_call" | custom-call | bytes 5400000 | tf_op jit(solution)/shard_map/states/pallas_call | solution.py:682
  44.8 1.4 %collective-permute-done.6.got_ref = f32[128,512]{1,0:T(8,128)S(1)} collective-permute-done((f32[128,512]{1,0:T(8,128)S(1)}, f32[128,512]{1,0:T(8,128)S(1)}, u32[]{:S(2)}, u32[]{:S(2)}) %collective-permute-start.6) | collective-permute-done | bytes 262176 | tf_op jit(solution)/shard_map/ppermute | solution.py:699
  47.2 0.8 sums.1
  47.9 0.7 collective-permute-done.9.got_ref
  48.6 1.0 %back.1 = (f32[512,256]{1,0:T(8,128)S(1)}, f32[16,8,128]{2,1,0:T(8,128)S(1)}, bf16[8,160,128]{2,1,0:T(8,128)(2,1)S(1)}, bf16[8,160,128]{2,1,0:T(8,128)(2,1)S(1)}) custom-call(bf16[128,1280]{1,0:T(8,128)(2,1)S(1)} %get-tuple-element.107.mine_ref, bf16[128,1280]{1,0:T(8,128)(2,1)S(1)} %collective-permute-done.9.got_ref, ...), custom_call_target="tpu_custom_call" | custom-call | bytes 5760000 | tf_op jit(solution)/shard_map/back/pallas_call | solution.py:682
  49.7 0.9 %collective-permute-start.10 = (bf16[8,160,128]{2,1,0:T(8,128)(2,1)S(1)}, bf16[8,160,128]{2,1,0:T(8,128)(2,1)S(1)}, u32[]{:S(2)}, u32[]{:S(2)}) collective-permute-start(bf16[8,160,128]{2,1,0:T(8,128)(2,1)S(1)} %get-tuple-element.112), channel_id=1, source_target_pairs={{0,2},{2,0},{1,3},{3,1},{4,6},{6,4},{5,7},{7,5},{8,10},{10,8},{9,1... | collective-permute-start | bytes 983048 | tf_op jit(solution)/shard_map/ppermute | solution.py:699
  50.6 10.5 %all_to_all.22.recv_ref = f32[16,8,128]{2,1,0:T(8,128)S(1)} all-to-all(f32[16,8,128]{2,1,0:T(8,128)S(1)} %get-tuple-element.111), channel_id=1, replica_groups=mesh['fz'=4,'fx'=2,'ty'=2,'tc'=2] {'fz','fx','ty'}, dimensions={0} | all-to-all | bytes 131072 | tf_op jit(solution)/shard_map/all_to_all | solution.py:785
  61.9 2.6 %third.1 = (bf16[448,128]{1,0:T(8,128)(2,1)S(1)}, bf16[448,128]{1,0:T(8,128)(2,1)S(1)}, bf16[448,128]{1,0:T(8,128)(2,1)S(1)}, bf16[448,128]{1,0:T(8,128)(2,1)S(1...) custom-call(f32[16,8,128]{2,1,0:T(8,128)S(1)} %all_to_all.22.recv_ref, f32[4,128]{1,0:T(4,128)S(1)} %get-tuple-element.88.start_ref, ...), custom_call_target="tpu_custom_call" | custom-call | bytes 8640000 | tf_op jit(solution)/shard_map/third/pallas_call | solution.py:682
  65.2 1.6 %collective-permute-start.13 = (bf16[448,128]{1,0:T(8,128)(2,1)S(1)}, bf16[448,128]{1,0:T(8,128)(2,1)S(1)}, u32[]{:S(2)}, u32[]{:S(2)}) collective-permute-start(bf16[448,128]{1,0:T(8,128)(2,1)S(1)} %get-tuple-element.128), channel_id=1, source_target_pairs={{0,4},{4,0},{1,5},{5,1},{2,6},{6,2},{3,7},{7,3},{8,12},{12,8},{9,1... | collective-permute-start | bytes 344072 | tf_op jit(solution)/shard_map/ppermute | solution.py:699
  66.8 1.3 %collective-permute-start.14 = (bf16[448,128]{1,0:T(8,128)(2,1)S(1)}, bf16[448,128]{1,0:T(8,128)(2,1)S(1)}, u32[]{:S(2)}, u32[]{:S(2)}) collective-permute-start(bf16[448,128]{1,0:T(8,128)(2,1)S(1)} %get-tuple-element.129), channel_id=1, source_target_pairs={{0,6},{2,4},{4,2},{6,0},{1,7},{3,5},{5,3},{7,1},{8,14},{10,12},{12... | collective-permute-start | bytes 344072 | tf_op jit(solution)/shard_map/ppermute | solution.py:703
  68.1 2.4 %collective-permute-done.12.y_ref = bf16[448,128]{1,0:T(8,128)(2,1)S(1)} collective-permute-done((bf16[448,128]{1,0:T(8,128)(2,1)S(1)}, bf16[448,128]{1,0:T(8,128)(2,1)S(1)}, u32[]{:S(2)}, u32[]{:S(2)}) %collective-permute-start.12) | collective-permute-done | bytes 114720 | tf_op jit(solution)/shard_map/ppermute | solution.py:699
  70.5 1.9 %collective-permute-done.14.xy_ref = bf16[448,128]{1,0:T(8,128)(2,1)S(1)} collective-permute-done((bf16[448,128]{1,0:T(8,128)(2,1)S(1)}, bf16[448,128]{1,0:T(8,128)(2,1)S(1)}, u32[]{:S(2)}, u32[]{:S(2)}) %collective-permute-start.14) | collective-permute-done | bytes 114720 | tf_op jit(solution)/shard_map/ppermute | solution.py:703
  72.6 10.4 %all_to_all.23.got_ref = bf16[4,320,128]{2,1,0:T(8,128)(2,1)S(1)} all-to-all(bf16[4,320,128]{2,1,0:T(8,128)(2,1)S(1)} %plane_add.1), channel_id=1, replica_groups=mesh['fz'=4,'fx'=2,'ty'=2,'tc'=2] {'fz'}, dimensions={0} | all-to-all | bytes 655360 | tf_op jit(solution)/shard_map/all_to_all | solution.py:808
  83.5 0.8 matrices.1
  85.2 0.9 %input_grad.1 = f32[128,512]{1,0:T(8,128)} custom-call(f32[128,512]{1,0:T(8,128)S(1)} %get-tuple-element.123.dn_ref, f32[128,512]{1,0:T(8,128)S(1)} %collective-permute-done.15.got_ref, bf16[128,512]{1,0:T(8,128)(2,1)S(1)} %copy-done, f32[256,512]{1,0:T(8,128)S(1)} %get-tuple-element.80.xhat_ref, f32[128,128]{1,0:T(8,128)S(1)} %get-tuple-element.131.inv_ref, ...), custom_call_target="tpu_custom_call" | custom-call | bytes 1800000 | tf_op jit(solution)/shard_map/input_grad/pallas_call | solution.py:682
  (38 shorter events, 7.7 us)
Async XLA Ops:
  18.0 5.1 %copy-start.1 = (bf16[128,512]{1,0:T(8,128)(2,1)S(1)}, bf16[128,512]{1,0:T(8,128)(2,1)}, u32[]{:S(2)}) copy-start(bf16[128,512]{1,0:T(8,128)(2,1)} %x_ref.3) | copy-start | bytes 393220
  18.0 10.3 %collective-permute-start.4 = (bf16[4,160,128]{2,1,0:T(8,128)(2,1)S(1)}, bf16[4,160,128]{2,1,0:T(8,128)(2,1)S(1)}, u32[]{:S(2)}, u32[]{:S(2)}) collective-permute-start(bf16[4,160,128]{2,1,0:T(8,128)(2,1)S(1)} %slice.9), channel_id=1, source_target_pairs={{0,4},{4,0},{1,5},{5,1},{2,6},{6,2},{3,7},{7,3},{8,12},{12,8},{9,1... | collective-permute-start | bytes 491528 | tf_op jit(solution)/shard_map/ppermute | solution.py:699
  19.6 7.0 %collective-permute-start.3 = (bf16[4,112,128]{2,1,0:T(8,128)(2,1)S(1)}, bf16[4,112,128]{2,1,0:T(8,128)(2,1)S(1)}, u32[]{:S(2)}, u32[]{:S(2)}) collective-permute-start(bf16[4,112,128]{2,1,0:T(8,128)(2,1)S(1)} %slice.8), channel_id=1, source_target_pairs={{0,6},{2,4},{4,2},{6,0},{1,7},{3,5},{5,3},{7,1},{8,14},{10,12},{12... | collective-permute-start | bytes 344072 | tf_op jit(solution)/shard_map/ppermute | solution.py:703
  21.1 6.2 %collective-permute-start.2 = (bf16[4,112,128]{2,1,0:T(8,128)(2,1)S(1)}, bf16[4,112,128]{2,1,0:T(8,128)(2,1)S(1)}, u32[]{:S(2)}, u32[]{:S(2)}) collective-permute-start(bf16[4,112,128]{2,1,0:T(8,128)(2,1)S(1)} %slice.8), channel_id=1, source_target_pairs={{0,4},{4,0},{1,5},{5,1},{2,6},{6,2},{3,7},{7,3},{8,12},{12,8},{9,1... | collective-permute-start | bytes 344072 | tf_op jit(solution)/shard_map/ppermute | solution.py:699
  22.5 5.8 %collective-permute-start.1 = (bf16[4,112,128]{2,1,0:T(8,128)(2,1)S(1)}, bf16[4,112,128]{2,1,0:T(8,128)(2,1)S(1)}, u32[]{:S(2)}, u32[]{:S(2)}) collective-permute-start(bf16[4,112,128]{2,1,0:T(8,128)(2,1)S(1)} %slice.8), channel_id=1, source_target_pairs={{0,2},{2,0},{1,3},{3,1},{4,6},{6,4},{5,7},{7,5},{8,10},{10,8},{9,1... | collective-permute-start | bytes 344072 | tf_op jit(solution)/shard_map/ppermute | solution.py:699
  23.1 6.6 %collective-permute-start = (bf16[128,512]{1,0:T(8,128)(2,1)S(1)}, bf16[128,512]{1,0:T(8,128)(2,1)S(1)}, u32[]{:S(2)}, u32[]{:S(2)}) collective-permute-start(bf16[128,512]{1,0:T(8,128)(2,1)S(1)} %copy-done.1), channel_id=1, source_target_pairs={{0,1},{1,0},{2,3},{3,2},{4,5},{5,4},{6,7},{7,6},{8,9},{9,8},{10,11... | collective-permute-start | bytes 393224 | tf_op jit(solution)/shard_map/ppermute | solution.py:699
  28.4 15.0 %collective-permute-start.5 = (bf16[2,4,160,128]{3,2,1,0:T(8,128)(2,1)S(1)}, bf16[2,4,160,128]{3,2,1,0:T(8,128)(2,1)S(1)}, u32[]{:S(2)}, u32[]{:S(2)}) collective-permute-start(bf16[2,4,160,128]{3,2,1,0:T(8,128)(2,1)S(1)} %pad_maximum_fusion.1.c0_ref.g0), channel_id=1, source_target_pairs={{0,2},{2,0},{1,3},{3,1},{4,6},{6,4},{5,7},{7,5},{8,10},{10,8},{9,1... | collective-permute-start | bytes 983048 | tf_op jit(solution)/shard_map/ppermute | solution.py:699
  43.4 2.9 %copy-start = (bf16[128,512]{1,0:T(8,128)(2,1)S(1)}, bf16[128,512]{1,0:T(8,128)(2,1)}, u32[]{:S(2)}) copy-start(bf16[128,512]{1,0:T(8,128)(2,1)} %up_ref.3) | copy-start | bytes 393220
  43.4 2.9 %collective-permute-start.7 = (bf16[2,4,160,128]{3,2,1,0:T(8,128)(2,1)S(1)}, bf16[2,4,160,128]{3,2,1,0:T(8,128)(2,1)S(1)}, u32[]{:S(2)}, u32[]{:S(2)}) collective-permute-start(bf16[2,4,160,128]{3,2,1,0:T(8,128)(2,1)S(1)} %pad_maximum_fusion.1.c0_ref.g0), channel_id=1, source_target_pairs={{0,1},{1,0},{2,3},{3,2},{4,5},{5,4},{6,7},{7,6},{8,9},{9,8},{10,11... | collective-permute-start | bytes 983048 | tf_op jit(solution)/shard_map/ppermute | solution.py:699
  43.5 2.8 %collective-permute-start.8 = (bf16[2,4,160,128]{3,2,1,0:T(8,128)(2,1)S(1)}, bf16[2,4,160,128]{3,2,1,0:T(8,128)(2,1)S(1)}, u32[]{:S(2)}, u32[]{:S(2)}) collective-permute-start(bf16[2,4,160,128]{3,2,1,0:T(8,128)(2,1)S(1)} %collective-permute-done.5.c1_ref.g1), channel_id=1, source_target_pairs={{0,1},{1,0},{2,3},{3,2},{4,5},{5,4},{6,7},{7,6},{8,9},{9,8},{10,11... | collective-permute-start | bytes 983048 | tf_op jit(solution)/shard_map/ppermute | solution.py:699
  44.7 1.6 %collective-permute-start.6 = (f32[128,512]{1,0:T(8,128)S(1)}, f32[128,512]{1,0:T(8,128)S(1)}, u32[]{:S(2)}, u32[]{:S(2)}) collective-permute-start(f32[128,512]{1,0:T(8,128)S(1)} %get-tuple-element.98), channel_id=1, source_target_pairs={{0,1},{1,0},{2,3},{3,2},{4,5},{5,4},{6,7},{7,6},{8,9},{9,8},{10,11... | collective-permute-start | bytes 786440 | tf_op jit(solution)/shard_map/ppermute | solution.py:699
  47.0 1.7 %collective-permute-start.9 = (bf16[128,1280]{1,0:T(8,128)(2,1)S(1)}, bf16[128,1280]{1,0:T(8,128)(2,1)S(1)}, u32[]{:S(2)}, u32[]{:S(2)}) collective-permute-start(bf16[128,1280]{1,0:T(8,128)(2,1)S(1)} %get-tuple-element.108), channel_id=1, source_target_pairs={{0,1},{1,0},{2,3},{3,2},{4,5},{5,4},{6,7},{7,6},{8,9},{9,8},{10,11... | collective-permute-start | bytes 983048 | tf_op jit(solution)/shard_map/ppermute | solution.py:699
  49.7 11.5 %collective-permute-start.10 = (bf16[8,160,128]{2,1,0:T(8,128)(2,1)S(1)}, bf16[8,160,128]{2,1,0:T(8,128)(2,1)S(1)}, u32[]{:S(2)}, u32[]{:S(2)}) collective-permute-start(bf16[8,160,128]{2,1,0:T(8,128)(2,1)S(1)} %get-tuple-element.112), channel_id=1, source_target_pairs={{0,2},{2,0},{1,3},{3,1},{4,6},{6,4},{5,7},{7,5},{8,10},{10,8},{9,1... | collective-permute-start | bytes 983048 | tf_op jit(solution)/shard_map/ppermute | solution.py:699
  61.2 11.3 %collective-permute-start.11 = (bf16[4,160,128]{2,1,0:T(8,128)(2,1)S(1)}, bf16[4,160,128]{2,1,0:T(8,128)(2,1)S(1)}, u32[]{:S(2)}, u32[]{:S(2)}) collective-permute-start(bf16[4,160,128]{2,1,0:T(8,128)(2,1)S(1)} %get-tuple-element.117), channel_id=1, source_target_pairs={{0,4},{4,0},{1,5},{5,1},{2,6},{6,2},{3,7},{7,3},{8,12},{12,8},{9,1... | collective-permute-start | bytes 491528 | tf_op jit(solution)/shard_map/ppermute | solution.py:699
  64.6 6.0 %collective-permute-start.12 = (bf16[448,128]{1,0:T(8,128)(2,1)S(1)}, bf16[448,128]{1,0:T(8,128)(2,1)S(1)}, u32[]{:S(2)}, u32[]{:S(2)}) collective-permute-start(bf16[448,128]{1,0:T(8,128)(2,1)S(1)} %get-tuple-element.127), channel_id=1, source_target_pairs={{0,2},{2,0},{1,3},{3,1},{4,6},{6,4},{5,7},{7,5},{8,10},{10,8},{9,1... | collective-permute-start | bytes 344072 | tf_op jit(solution)/shard_map/ppermute | solution.py:699
  65.2 5.4 %collective-permute-start.13 = (bf16[448,128]{1,0:T(8,128)(2,1)S(1)}, bf16[448,128]{1,0:T(8,128)(2,1)S(1)}, u32[]{:S(2)}, u32[]{:S(2)}) collective-permute-start(bf16[448,128]{1,0:T(8,128)(2,1)S(1)} %get-tuple-element.128), channel_id=1, source_target_pairs={{0,4},{4,0},{1,5},{5,1},{2,6},{6,2},{3,7},{7,3},{8,12},{12,8},{9,1... | collective-permute-start | bytes 344072 | tf_op jit(solution)/shard_map/ppermute | solution.py:699
  66.8 5.7 %collective-permute-start.14 = (bf16[448,128]{1,0:T(8,128)(2,1)S(1)}, bf16[448,128]{1,0:T(8,128)(2,1)S(1)}, u32[]{:S(2)}, u32[]{:S(2)}) collective-permute-start(bf16[448,128]{1,0:T(8,128)(2,1)S(1)} %get-tuple-element.129), channel_id=1, source_target_pairs={{0,6},{2,4},{4,2},{6,0},{1,7},{3,5},{5,3},{7,1},{8,14},{10,12},{12... | collective-permute-start | bytes 344072 | tf_op jit(solution)/shard_map/ppermute | solution.py:703
  82.9 2.2 %collective-permute-start.15 = (f32[128,512]{1,0:T(8,128)S(1)}, f32[128,512]{1,0:T(8,128)S(1)}, u32[]{:S(2)}, u32[]{:S(2)}) collective-permute-start(f32[128,512]{1,0:T(8,128)S(1)} %get-tuple-element.130), channel_id=1, source_target_pairs={{0,1},{1,0},{2,3},{3,2},{4,5},{5,4},{6,7},{7,6},{8,9},{9,8},{10,11... | collective-permute-start | bytes 786440 | tf_op jit(solution)/shard_map/ppermute | solution.py:699
  83.0 1.5 %collective-permute-start.16 = (f32[32,128]{1,0:T(8,128)S(1)}, f32[32,128]{1,0:T(8,128)S(1)}, u32[]{:S(2)}, u32[]{:S(2)}) collective-permute-start(f32[32,128]{1,0:T(8,128)S(1)} %vectors.1.own_ref), channel_id=1, source_target_pairs={{0,1},{1,0},{2,3},{3,2},{4,5},{5,4},{6,7},{7,6},{8,9},{9,8},{10,11... | collective-permute-start | bytes 49160 | tf_op jit(solution)/shard_map/ppermute | solution.py:699

commit v5 on v4

--- a/solution.py
+++ b/solution.py
@@ -46,32 +46,8 @@
     return lax.axis_index("fx") == 1
 
 
-def spread(x):
-    lo = low_half((x.shape[0], 128))
-    flip = flipped()
-    upper, lower = [], []
-    for c in range(x.shape[1] // 128):
-        xc = x[:, 128 * c : 128 * c + 128]
-        turned = pltpu.roll(xc, 64, 1)
-        xc, turned = jnp.where(flip, turned, xc), jnp.where(flip, xc, turned)
-        upper += [jnp.where(lo, xc, 0.0).astype(BF16), jnp.where(lo, turned, 0.0).astype(BF16)]
-        lower += [jnp.where(lo, 0.0, turned).astype(BF16), jnp.where(lo, 0.0, xc).astype(BF16)]
-    return jnp.concatenate(
-        [jnp.concatenate(upper, axis=1), jnp.concatenate(lower, axis=1)], axis=0
-    )
-
-
-def folded(lhs, parts):
-    rows = lhs.shape[0] // 2
-    lo = low_half((rows, 128))
-    flip = flipped()
-    out = []
-    for part in parts:
-        pq = dot(lhs, part, NN)
-        p0, p1, q0, q1 = pq[:rows, :128], pq[:rows, 128:], pq[rows:, :128], pq[rows:, 128:]
-        even = jnp.where(lo, p0, q1) + jnp.where(lo, pltpu.roll(q0, 64, 1), pltpu.roll(p1, 64, 1))
-        out.append(jnp.where(flip, pltpu.roll(even, 64, 1), even))
-    return jnp.concatenate(out, axis=1)
+def part_lanes(part, m):
+    return slice(256 * part + 128 * m, 256 * part + 128 * m + 128)
 
 
 def slot_pos(m, core):
@@ -90,10 +66,24 @@
     return ref[f % 2, m, f // 2, start : start + count, :]
 
 
-def weights(get):
-    none = jnp.zeros((32, 128), BF16)
-    block = lambda f: jnp.concatenate([get(0, f), none, get(1, f), none], axis=0)
-    return [jnp.concatenate([block(f), block(f + 1)], axis=1) for f in range(0, GROUPS, 2)]
+def natural(get, ref):
+    lo = low_half((96, 128))
+    for m in range(2):
+        for part in range(2):
+            lanes = part_lanes(part, m)
+            ref[lanes.start + 96 : lanes.stop, :] = jnp.zeros((32, 512), BF16)
+        for z in range(GROUPS // 2):
+            even, odd = get(m, z, 0).astype(F32), get(m, z, 1).astype(F32)
+            here = slice(128 * z, 128 * z + 128)
+            ref[128 * m : 128 * m + 96, here] = jnp.where(lo, even, pltpu.roll(odd, 64, 1)).astype(BF16)
+            ref[256 + 128 * m : 256 + 128 * m + 96, here] = jnp.where(lo, pltpu.roll(even, 64, 1), odd).astype(BF16)
+
+
+def packets(value, m, z):
+    lo = low_half((96, 128))
+    here = slice(128 * z, 128 * z + 128)
+    re, im = value[128 * m : 128 * m + 96, here], value[256 + 128 * m : 256 + 128 * m + 96, here]
+    return jnp.where(lo, re, pltpu.roll(im, 64, 1)), jnp.where(lo, pltpu.roll(re, 64, 1), im)
 
 
 def feature_rows(ref, row):
@@ -239,23 +229,22 @@
             inv_ref[...] = jnp.broadcast_to(inverse, (rows, 128))
 
 
-def norm_kernel(xhat_ref, g_ref, normed_ref, wide_ref, feat_ref, start_ref):
+def norm_kernel(xhat_ref, g_ref, normed_ref, feat_ref, start_ref):
     scale, bias = feature_rows(g_ref, VEC)
     feat_ref[0:1] = scale
     feat_ref[1:2], feat_ref[2:3] = feature_rows(g_ref, VEC + 1)
     normed = (xhat_ref[...] * scale + bias).astype(BF16)
     normed_ref[...] = normed
-    wide_ref[...] = spread(normed.astype(F32))
     upper, lower = (piece(g_ref, 0, 0, VEC + 11 + k, 1).astype(F32) for k in range(2))
     starts = upper * 256.0 + lower
     for n in range(start_ref.shape[0]):
         start_ref[n : n + 1, :] = jnp.broadcast_to(starts[:, n : n + 1], (1, 128))
 
 
-def first_kernel(pairs, wide_ref, start_ref, g_ref, v_ref, lane_ref, row_ref, send_ref, scratch):
-    rows = wide_ref.shape[0] // 2
-    b_all = jnp.concatenate(weights(lambda m, f: piece(g_ref, m, f, 0, 96)), axis=1)
-    v_ref[...] = dot(wide_ref[...], b_all, NT)
+def first_kernel(pairs, normed_ref, start_ref, g_ref, b_ref, v_ref, lane_ref, row_ref, send_ref, scratch):
+    rows = normed_ref.shape[0]
+    natural(lambda m, z, x: g_ref[lax.axis_index("fx") ^ x, m, z, 0:96, :], b_ref)
+    v_ref[...] = dot(normed_ref[...], b_ref[...], NT)
 
     decay, lam, log_dt = params_of(g_ref, VEC)
     abar_re, abar_im, coef_re, coef_im, step_size = discretize(decay, lam, log_dt)
@@ -274,14 +263,12 @@
     open_tail = jnp.where(count == count[rows - 1 : rows], 1.0, 0.0)
     last = ([], [])
     for m in range(2):
-        lanes = slice(128 * m, 128 * m + 128)
-        eight, tail = eighth_powers((abar_re[m : m + 1], abar_im[m : m + 1]), 7)
+        eight, tail = eighth_powers((abar_re[m : m + 1], abar_im[m : m + 1]), lambda sub: 7 - sub)
         b = (coef_re[m : m + 1], coef_im[m : m + 1])
         acc = (jnp.zeros((8, 128), F32), jnp.zeros((8, 128), F32))
         for blk in range(rows // 8):
             here = slice(8 * blk, 8 * blk + 8)
-            there = slice(rows + 8 * blk, rows + 8 * blk + 8)
-            drive = cmul(b, (v_ref[here, lanes], v_ref[there, lanes]))
+            drive = cmul(b, (v_ref[here, part_lanes(0, m)], v_ref[here, part_lanes(1, m)]))
             moved = cmul(eight, acc)
             acc = (moved[0] + drive[0] * open_tail[here], moved[1] + drive[1] * open_tail[here])
         total = cmul(tail, acc)
@@ -293,9 +280,8 @@
         send_ref[d] = packet
 
 
-def eighth_powers(a, top):
-    sub = lax.broadcasted_iota(jnp.int32, (8, 128), 0)
-    exponent = (7 - sub) if top == 7 else sub + 1
+def eighth_powers(a, exponent_of):
+    exponent = exponent_of(lax.broadcasted_iota(jnp.int32, (8, 128), 0))
     a = (jnp.broadcast_to(a[0], (8, 128)), jnp.broadcast_to(a[1], (8, 128)))
     tile = (jnp.ones((8, 128), F32), jnp.zeros((8, 128), F32))
     for bit in range(4):
@@ -308,21 +294,47 @@
     return eight, tile
 
 
-def scan_chunk(value, a, count, reverse):
-    rows = count.shape[0]
-    at = lax.broadcasted_iota(jnp.int32, (rows, 128), 0)
-    step = 1
-    while step < rows:
-        shift = rows - step if reverse else step
-        other = pltpu.roll(count, shift, 0)
-        inside = (at < rows - step) if reverse else (at >= step)
-        linked = inside & (other == count)
-        moved = (pltpu.roll(value[0], shift, 0), pltpu.roll(value[1], shift, 0))
-        more = cmul(a, moved)
-        value = (value[0] + jnp.where(linked, more[0], 0.0), value[1] + jnp.where(linked, more[1], 0.0))
-        a = cmul(a, a)
-        step *= 2
-    return value
+def all_rows(row):
+    return jnp.broadcast_to(row, (8, 128))
+
+
+def scan(read, powers, carry, count, reverse, emit):
+    groups = count.shape[0] // 8
+    sub = lax.broadcasted_iota(jnp.int32, (8, 128), 0)
+    steps, eights, tiles = [], [], []
+    for a in powers:
+        squared = cmul(a, a)
+        steps.append((a, squared, cmul(squared, squared)))
+        eight, tile = eighth_powers(a, (lambda sub: 8 - sub) if reverse else (lambda sub: sub + 1))
+        eights.append(eight)
+        tiles.append(tile)
+    carry = [(all_rows(c[0]), all_rows(c[1])) for c in carry]
+    edge = 0 if reverse else 7
+    seen = all_rows(count[8 * groups - 1 :]) if reverse else jnp.zeros((8, 128), F32)
+    for b in range(groups - 1, -1, -1) if reverse else range(groups):
+        here = count[8 * b : 8 * b + 8]
+        links = []
+        for k in (1, 2, 4):
+            other = pltpu.roll(here, 8 - k if reverse else k, 0)
+            links.append(((sub < 8 - k) if reverse else (sub >= k)) & (other == here))
+        came = here == seen
+        last = all_rows(here[edge : edge + 1])
+        through = last == seen
+        seen = last
+        for m in range(2):
+            value = read(b, m)
+            for k, link, a in zip((1, 2, 4), links, steps[m]):
+                shift = 8 - k if reverse else k
+                more = cmul(a, (pltpu.roll(value[0], shift, 0), pltpu.roll(value[1], shift, 0)))
+                value = (value[0] + jnp.where(link, more[0], 0.0), value[1] + jnp.where(link, more[1], 0.0))
+            more = cmul(tiles[m], carry[m])
+            done = (value[0] + jnp.where(came, more[0], 0.0), value[1] + jnp.where(came, more[1], 0.0))
+            more = cmul(eights[m], carry[m])
+            carry[m] = (
+                all_rows(value[0][edge : edge + 1]) + jnp.where(through, more[0], 0.0),
+                all_rows(value[1][edge : edge + 1]) + jnp.where(through, more[1], 0.0),
+            )
+            emit(b, m, done)
 
 
 def carried(recv_ref, row_ref, offsets, rows, reverse, scratch):
@@ -352,55 +364,50 @@
     return jnp.sum(value, axis=0, keepdims=True)
 
 
-def states_kernel(recv_ref, start_ref, v_ref, lane_ref, row_ref, state_ref, twice_ref, enter_ref, scratch):
-    rows = v_ref.shape[0] // 2
-    half = rows // 2
+def states_kernel(
+    recv_ref, start_ref, v_ref, lane_ref, row_ref, cw_ref, state_ref, twice_ref, enter_ref, c_ref, scratch
+):
+    rows = v_ref.shape[0]
     offsets = offsets_of(start_ref)
-    base = pair_pos() * rows
-    count = starts_until(offsets, base, rows)
+    count = starts_until(offsets, pair_pos() * rows, rows)
     enter = carried(recv_ref, row_ref, offsets, rows, False, scratch)
-    top = lax.broadcasted_iota(jnp.int32, (half, 128), 0) == 0
-    links = (no_start(offsets, base, 1), jnp.where(count[half : half + 1] == count[half - 1 : half], 1.0, 0.0))
-    for m in range(2):
-        lanes = slice(128 * m, 128 * m + 128)
-        a = (lane_ref[0:1, lanes], lane_ref[1:2, lanes])
-        b = (lane_ref[2:3, lanes], lane_ref[3:4, lanes])
-        before = (enter[0][m], enter[1][m])
-        enter_ref[0:1, lanes] = before[0]
-        enter_ref[1:2, lanes] = before[1]
-        for h in range(2):
-            here = slice(half * h, half * h + half)
-            there = slice(rows + half * h, rows + half * h + half)
-            drive = cmul(b, (v_ref[here, lanes], v_ref[there, lanes]))
-            came = cmul((a[0] * links[h], a[1] * links[h]), before)
-            drive = (drive[0] + jnp.where(top, came[0], 0.0), drive[1] + jnp.where(top, came[1], 0.0))
-            state = scan_chunk(drive, a, count[here], False)
-            before = (state[0][half - 1 : half], state[1][half - 1 : half])
-            state_ref[here, lanes] = state[0]
-            state_ref[there, lanes] = state[1]
-            twice_ref[here, lanes] = state[0].astype(BF16) * 2
-            twice_ref[there, lanes] = state[1].astype(BF16) * -2
-
-
-def readout_kernel(twice_ref, c0_ref, c1_ref, own_ref, away_ref, scratch):
+    for part in range(2):
+        for m in range(2):
+            enter_ref[0:1, part_lanes(part, m)] = enter[part][m]
+    powers = [(lane_ref[0:1, 128 * m : 128 * m + 128], lane_ref[1:2, 128 * m : 128 * m + 128]) for m in range(2)]
+
+    def read(b, m):
+        here, lanes = slice(8 * b, 8 * b + 8), slice(128 * m, 128 * m + 128)
+        return cmul((lane_ref[2:3, lanes], lane_ref[3:4, lanes]), (v_ref[here, part_lanes(0, m)], v_ref[here, part_lanes(1, m)]))
+
+    def emit(b, m, value):
+        for part in range(2):
+            state_ref[8 * b : 8 * b + 8, part_lanes(part, m)] = value[part]
+
+    scan(read, powers, [(enter[0][m], enter[1][m]) for m in range(2)], count, False, emit)
+    twice_ref[:, 0:256] = state_ref[:, 0:256].astype(BF16) * 2
+    twice_ref[:, 256:512] = state_ref[:, 256:512].astype(BF16) * -2
+    natural(lambda m, z, x: cw_ref[lax.axis_index("fx") ^ x, m, z, 0:96, :], c_ref)
+
+
+def readout_kernel(twice_ref, c_ref, own_ref, away_ref, scratch):
     rows = own_ref.shape[0]
-    slots = (c0_ref, c1_ref)
-    scratch[...] = folded(twice_ref[...], weights(lambda m, f: slots[m][f % 2, f // 2, 0:96, :]))
+    scratch[...] = dot(twice_ref[...], c_ref[...], NN)
     own_ref[...] = scratch[own_rows(rows), :]
     away_ref[...] = scratch[other_rows(rows), :]
 
 
 def second_kernel(
-    own_ref, got_ref, up_ref, normed_ref, feat_ref, g0, g1, g2, g3,
+    own_ref, got_ref, up_ref, normed_ref, feat_ref, cw_ref, othercw_ref,
     branch_ref, dmixed_ref, dlogit_ref, mine_ref, away_ref, gate_ref, all_ref,
 ):
     rows, width = up_ref.shape
-    for core, slots in enumerate(((g0, g1), (g2, g3))):
+    for core, ref in enumerate((cw_ref, othercw_ref)):
         for m in range(2):
             lanes = pl.ds(pl.multiple_of(slot_pos(m, core) * 128, 128), 128)
             for f in range(GROUPS):
                 place = (f // 2) * 2 + (lax.axis_index("fx") ^ (f % 2))
-                gate_ref[pl.ds(pl.multiple_of(place * 64, 64), 64), lanes] = slots[m][f % 2, f // 2, 96:160, :]
+                gate_ref[pl.ds(pl.multiple_of(place * 64, 64), 64), lanes] = piece(ref, m, f, 96, 64)
     skip, gate_bias = feat_ref[1:2], feat_ref[2:3]
     normed = normed_ref[own_rows(rows), :].astype(F32)
     mixed = (own_ref[...] + got_ref[...]) + skip * normed
@@ -437,31 +444,30 @@
 
 
 def back_kernel(
-    pairs, mine_ref, got_ref, twice_ref, start_ref, lane_ref, c0_ref, c1_ref,
-    dstate_ref, send_ref, stay_ref, leave_ref, dy_ref, dgate_ref, scratch,
+    pairs, mine_ref, got_ref, twice_ref, start_ref, lane_ref, c_ref,
+    dstate_ref, send_ref, stay_ref, leave_ref, dy_ref, dgate_ref, scratch, all_ref,
 ):
     rows, width = dy_ref.shape
     half = rows // 2
     dy_ref[own_rows(half), :] = mine_ref[:, 0:width]
     dy_ref[other_rows(half), :] = got_ref[:, 0:width]
-    slots = (c0_ref, c1_ref)
-    c_all = jnp.concatenate(weights(lambda m, f: slots[m][f % 2, f // 2, 0:96, :]), axis=1)
-    spread_dy = spread(dy_ref[...].astype(F32))
-    d_state = dot(spread_dy, c_all, NT)
-    dstate_ref[:rows] = d_state[:rows] * 2.0
-    dstate_ref[rows:] = d_state[rows:] * -2.0
+    d_state = dot(dy_ref[...], c_ref[...], NT)
+    dstate_ref[:, 0:256] = d_state[:, 0:256] * 2.0
+    dstate_ref[:, 256:512] = d_state[:, 256:512] * -2.0
     count = starts_until(offsets_of(start_ref), pair_pos() * rows, rows)
     head = jnp.where(count == 0.0, 1.0, 0.0)
     first = ([], [])
     for m in range(2):
         lanes = slice(128 * m, 128 * m + 128)
-        eight, tail = eighth_powers((lane_ref[0:1, lanes], -lane_ref[1:2, lanes]), 0)
+        eight, tail = eighth_powers((lane_ref[0:1, lanes], -lane_ref[1:2, lanes]), lambda sub: sub + 1)
         acc = (jnp.zeros((8, 128), F32), jnp.zeros((8, 128), F32))
         for blk in range(rows // 8 - 1, -1, -1):
             here = slice(8 * blk, 8 * blk + 8)
-            there = slice(rows + 8 * blk, rows + 8 * blk + 8)
             moved = cmul(eight, acc)
-            acc = (moved[0] + dstate_ref[here, lanes] * head[here], moved[1] + dstate_ref[there, lanes] * head[here])
+            acc = (
+                moved[0] + dstate_ref[here, part_lanes(0, m)] * head[here],
+                moved[1] + dstate_ref[here, part_lanes(1, m)] * head[here],
+            )
         total = cmul(tail, acc)
         first[0].append(column_sum(total[0]))
         first[1].append(column_sum(total[1]))
@@ -470,16 +476,19 @@
     packet = scratch[...]
     for d in range(pairs):
         send_ref[d] = packet
-    d_c = dot(twice_ref[...], spread_dy, TN).astype(BF16)
+    d_c = dot(twice_ref[...], dy_ref[...], TN)
     act = slice(width, 2 * width)
     units = slice(2 * width, 2 * width + 256)
     d_gate = dot(mine_ref[:, act], mine_ref[:, units], TN) + dot(got_ref[:, act], got_ref[:, units], TN)
     dgate_ref[...] = d_gate.astype(BF16)
-    for m, ref in enumerate((stay_ref, leave_ref)):
-        for f in range(GROUPS):
-            ref[f, 0:96, :] = d_c[128 * m : 128 * m + 96, 128 * f : 128 * f + 128]
-            place = pl.ds(pl.multiple_of(((f // 2) * 2 + (lax.axis_index("fx") ^ (f % 2))) * 64, 64), 64)
-            ref[f, 96:160, :] = dgate_ref[place, 128 * m : 128 * m + 128]
+    for m in range(2):
+        for z in range(GROUPS // 2):
+            for x, packet in enumerate(packets(d_c, m, z)):
+                j = lax.axis_index("fx") ^ x
+                all_ref[j, m, z, 0:96, :] = packet.astype(BF16)
+                all_ref[j, m, z, 96:160, :] = dgate_ref[128 * z + 64 * x : 128 * z + 64 * x + 64, 128 * m : 128 * m + 128]
+    stay_ref[...] = all_ref[0]
+    leave_ref[...] = all_ref[1]
 
 
 def split_rows(value):
@@ -488,64 +497,56 @@
 
 
 def third_kernel(
-    recv_ref, start_ref, wide_ref, xhat_ref, v_ref, lane_ref, row_ref, feat_ref, state_ref, dstate_ref, enter_ref, dmixed_ref,
-    part_ref, g_ref, stay_ref, y_ref, x_ref, xy_ref, dn_ref, dnaway_ref, scratch, dv_ref, all_ref, vec_ref,
+    recv_ref, start_ref, normed_ref, xhat_ref, v_ref, lane_ref, row_ref, feat_ref, state_ref, dstate_ref, enter_ref, dmixed_ref,
+    part_ref, b_ref, stay_ref, y_ref, x_ref, xy_ref, dn_ref, dnaway_ref, scratch, dv_ref, all_ref, vec_ref,
 ):
     rows, width = xhat_ref.shape
     half = rows // 2
     offsets = offsets_of(start_ref)
-    base = pair_pos() * rows
-    count = starts_until(offsets, base, rows)
+    count = starts_until(offsets, pair_pos() * rows, rows)
     later = carried(recv_ref, row_ref, offsets, rows, True, scratch)
-    at = lax.broadcasted_iota(jnp.int32, (half, 128), 0)
-    top, bottom = at == 0, at == half - 1
-    before = jnp.where(lax.broadcasted_iota(jnp.int32, (rows, 128), 0) == 0, 0.0, pltpu.roll(count, 1, 0))
-    keep = jnp.where(count == before, 1.0, 0.0)
-    sums = ([], [], [], [])
-    for m in range(2):
-        lanes = slice(128 * m, 128 * m + 128)
-        a = (lane_ref[0:1, lanes], -lane_ref[1:2, lanes])
-        b = (lane_ref[2:3, lanes], -lane_ref[3:4, lanes])
-        came = (later[0][m], later[1][m])
-        totals = None
-        for h in (1, 0):
-            here = slice(half * h, half * h + half)
-            there = slice(rows + half * h, rows + half * h + half)
-            start = (
-                dstate_ref[here, lanes] + jnp.where(bottom, came[0], 0.0),
-                dstate_ref[there, lanes] + jnp.where(bottom, came[1], 0.0),
-            )
-            adj = scan_chunk(start, a, count[here], True)
-            if h:
-                link = keep[half : half + 1]
-                came = cmul((a[0] * link, a[1] * link), (adj[0][0:1], adj[1][0:1]))
-                edge = (state_ref[half - 1 : half, lanes], state_ref[rows + half - 1 : rows + half, lanes])
-            else:
-                edge = (enter_ref[0:1, lanes], enter_ref[1:2, lanes])
-            prev = (
-                jnp.where(top, edge[0], pltpu.roll(state_ref[here, lanes], 1, 0)) * keep[here],
-                jnp.where(top, edge[1], pltpu.roll(state_ref[there, lanes], 1, 0)) * keep[here],
-            )
-            v = (v_ref[here, lanes], v_ref[there, lanes])
-            new = [
-                column_sum(adj[0] * prev[0] + adj[1] * prev[1]),
-                column_sum(adj[1] * prev[0] - adj[0] * prev[1]),
-                column_sum(adj[0] * v[0] + adj[1] * v[1]),
-                column_sum(adj[1] * v[0] - adj[0] * v[1]),
-            ]
-            totals = new if totals is None else [p + q for p, q in zip(totals, new)]
-            dv = cmul(b, adj)
-            dv_ref[here, lanes] = dv[0].astype(BF16)
-            dv_ref[there, lanes] = dv[1].astype(BF16)
-        for k in range(4):
-            sums[k].append(totals[k])
+    sub = lax.broadcasted_iota(jnp.int32, (8, 128), 0)
+    none = jnp.zeros((1, 128), F32)
+    totals = [[jnp.zeros((8, 128), F32) for _ in range(4)] for _ in range(2)]
+    powers = [(lane_ref[0:1, 128 * m : 128 * m + 128], -lane_ref[1:2, 128 * m : 128 * m + 128]) for m in range(2)]
+
+    def read(b, m):
+        value = [dstate_ref[8 * b : 8 * b + 8, part_lanes(part, m)] for part in range(2)]
+        if b == rows // 8 - 1:
+            value = [value[part] + jnp.where(sub == 7, later[part][m], 0.0) for part in range(2)]
+        return tuple(value)
+
+    def emit(b, m, adj):
+        here, lanes = slice(8 * b, 8 * b + 8), slice(128 * m, 128 * m + 128)
+        seen = count[8 * b - 1 : 8 * b] if b else none
+        keep = count[here] == jnp.where(sub == 0, seen, pltpu.roll(count[here], 1, 0))
+        prev = []
+        for part in range(2):
+            edge = state_ref[8 * b - 1 : 8 * b, part_lanes(part, m)] if b else enter_ref[0:1, part_lanes(part, m)]
+            moved = jnp.where(sub == 0, edge, pltpu.roll(state_ref[here, part_lanes(part, m)], 1, 0))
+            prev.append(jnp.where(keep, moved, 0.0))
+        v = (v_ref[here, part_lanes(0, m)], v_ref[here, part_lanes(1, m)])
+        for k, (p, q) in enumerate((prev, v)):
+            totals[m][2 * k] = totals[m][2 * k] + (adj[0] * p + adj[1] * q)
+            totals[m][2 * k + 1] = totals[m][2 * k + 1] + (adj[1] * p - adj[0] * q)
+        dv = cmul((lane_ref[2:3, lanes], -lane_ref[3:4, lanes]), adj)
+        for part in range(2):
+            dvf_ref[here, part_lanes(part, m)] = dv[part]
+
+    dvf_ref = all_ref
+    scan(read, powers, [(none, none), (none, none)], count, True, emit)
+    sums = [[column_sum(totals[m][k]) for m in range(2)] for k in range(4)]
+    dv_ref[...] = dvf_ref[...].astype(BF16)
     dv = dv_ref[...]
-    d_b = dot(dv, wide_ref[...], TN).astype(BF16)
-    for ref, m, j in ((stay_ref, 0, 0), (y_ref, 1, 0), (x_ref, 0, 1), (xy_ref, 1, 1)):
+    d_b = dot(dv, normed_ref[...], TN)
+    flip = flipped()
+    for m, (near, side) in enumerate(((stay_ref, x_ref), (y_ref, xy_ref))):
         for z in range(GROUPS // 2):
-            f = 2 * z + j
-            ref[96 * z : 96 * z + 96, :] = d_b[128 * m : 128 * m + 96, 128 * f : 128 * f + 128]
-    all_ref[...] = folded(dv, weights(lambda m, f: piece(g_ref, m, f, 0, 96)))
+            even, odd = packets(d_b, m, z)
+            here = slice(96 * z, 96 * z + 96)
+            near[here, :] = jnp.where(flip, odd, even).astype(BF16)
+            side[here, :] = jnp.where(flip, even, odd).astype(BF16)
+    all_ref[...] = dot(dv, b_ref[...], NN)
     dnaway_ref[...] = all_ref[other_rows(half), :]
     own = all_ref[own_rows(half), :] + dmixed_ref[...] * feat_ref[1:2]
     dn_ref[...] = own
@@ -583,7 +584,7 @@
         ref[384:448, :] = vec
 
 
-def input_grad_kernel(dn_ref, got_ref, up_ref, xhat_ref, inv_ref, feat_ref, gin_ref):
+def input_grad(dn_ref, got_ref, up_ref, xhat_ref, inv_ref, feat_ref, gin_ref):
     rows, width = up_ref.shape
     xhat = xhat_ref[own_rows(rows), :]
     d_xhat = (dn_ref[...] + got_ref[...]) * feat_ref[0:1]
@@ -592,6 +593,10 @@
     gin_ref[...] = up_ref[...].astype(F32) + inv_ref[:, 0:1] * (d_xhat - mean - xhat * mean_hat)
 
 
+def input_grad_kernel(*refs):
+    input_grad(*refs)
+
+
 def added(a, b):
     return (a.astype(F32) + b.astype(F32)).astype(BF16)
 
@@ -600,11 +605,9 @@
     return packet[0:32].astype(F32) + packet[32:64].astype(F32)
 
 
-def y_cw_kernel(keep_ref, got_ref, stay_ref, leave_ref):
-    for z in range(GROUPS // 2):
-        f, other = 2 * z, 2 * z + 1
-        stay_ref[z] = added(keep_ref[f], got_ref[f])
-        leave_ref[z] = added(keep_ref[other], got_ref[other])
+def middle_kernel(keep_ref, got_ref, stay_ref, leave_ref):
+    stay_ref[...] = added(keep_ref[0], got_ref[0])
+    leave_ref[...] = added(keep_ref[1], got_ref[1])
 
 
 def plane_add_kernel(cw_ref, gotcw_ref, stay_ref, y_ref, x_ref, xy_ref, out_ref):
@@ -653,8 +656,10 @@
 
 
 def finish_kernel(
-    count_all, own_ref, other_ref, gbias_ref, scale_ref, bias_ref, skip_ref, decay_ref, lam_ref, step_ref, rms_ref, vec_ref
+    count_all, own_ref, other_ref, dn_ref, got_ref, up_ref, xhat_ref, inv_ref, feat_ref,
+    gin_ref, gbias_ref, scale_ref, bias_ref, skip_ref, decay_ref, lam_ref, step_ref, rms_ref, vec_ref,
 ):
+    input_grad(dn_ref, got_ref, up_ref, xhat_ref, inv_ref, feat_ref, gin_ref)
     vec = own_ref[...] + other_ref[...]
     vec_ref[...] = vec
     for k, ref in enumerate((scale_ref, bias_ref, skip_ref)):
@@ -672,8 +677,8 @@
 
 
 TAKES = {
-    "pack": 1.5, "standardize": 0.4, "norm": 0.4, "first": 1.4, "states": 1.5, "readout": 0.5, "second": 1.2, "sums": 0.7, "back": 1.6,
-    "third": 2.4, "input_grad": 0.5, "matrices": 0.5, "finish": 0.4,
+    "pack": 1.5, "standardize": 0.4, "norm": 0.4, "first": 0.6, "states": 0.9, "readout": 0.4, "second": 0.7, "sums": 0.7, "back": 0.8,
+    "third": 1.5, "input_grad": 0.5, "matrices": 0.5, "finish": 0.4,
 }
 
 
@@ -727,46 +732,46 @@
         mine = lax.all_to_all(sent, "fz", 0, 0, tiled=True)
         own_b, own_cw = lax.optimization_barrier((mine[:, :112], mine[:, 112:]))
         plane_b = [own_b, swap(own_b, "ty"), swap(own_b, "fx"), across(own_b)]
-        plane_b, side_cw = lax.optimization_barrier((plane_b, swap(own_cw, "fx")))
+        xhat, inverse = call(standardize_kernel, (sds((pair, width)), sds((rows, 128))), (layer_in, swap(layer_in, "tc")))
+        plane_b, side_cw, xhat = lax.optimization_barrier((plane_b, swap(own_cw, "ty"), xhat))
         side_cw = jnp.stack([own_cw, side_cw])
-        far_cw = swap(side_cw, "ty")
+        far_cw = swap(side_cw, "fx")
         g = jnp.stack(plane_b).reshape(2, 2, GROUPS // 2, 112, 128)
     else:
-        g, g_cw = gathered(
+        xhat, inverse = call(standardize_kernel, (sds((pair, width)), sds((rows, 128))), (layer_in, swap(layer_in, "tc")))
+        g, cw, other_cw = gathered(
             ln_scale, ln_bias, decay_rate, lam_im, log_dt, in_re, in_im, out_re, out_im, skip, glu_weight, glu_bias, seq_lengths
         )
 
-    xhat, inverse = call(standardize_kernel, (sds((pair, width)), sds((rows, 128))), (layer_in, swap(layer_in, "tc")))
-    normed, wide, feat, starts = call(
+    normed, feat, starts = call(
         norm_kernel,
-        (sds((pair, width), BF16), sds((2 * pair, 2 * width), BF16), sds((8, width)), sds((seq_lengths.shape[0], 128))),
+        (sds((pair, width), BF16), sds((8, width)), sds((seq_lengths.shape[0], 128))),
         (xhat, g),
     )
-    v, lane, row_prm, carry = call(
+    b_all, v, lane, row_prm, carry = call(
         functools.partial(first_kernel, pairs),
-        (sds((2 * pair, 256)), sds((8, 256)), sds((8, 8, 128)), sds((pairs, 8, 128))),
-        (wide, starts, g),
+        (sds((512, width), BF16), sds((pair, 512)), sds((8, 256)), sds((8, 8, 128)), sds((pairs, 8, 128))),
+        (normed, starts, g),
         [pltpu.VMEM((8, 128), F32)],
     )
     came = lax.all_to_all(carry, same_core, 0, 0, tiled=True)
     if fast:
-        g_cw = tied((side_cw, far_cw), came)
-    state, twice, enter = call(
+        cw = jnp.stack(tied((side_cw, far_cw), came))
+    state, twice, enter, c_all = call(
         states_kernel,
-        (sds((2 * pair, 256)), sds((2 * pair, 256), BF16), sds((8, 256))),
-        (came, starts, v, lane, row_prm),
+        (sds((pair, 512)), sds((pair, 512), BF16), sds((8, 512)), sds((512, width), BF16)),
+        (came, starts, v, lane, row_prm, cw),
         [pltpu.VMEM((8, 128), F32)],
     )
     if fast:
-        far = tied(g_cw, twice)
-        g_cw = (*g_cw, swap(far[0], "tc"), swap(far[1], "tc"))
+        other_cw = swap(tied(cw, twice), "tc")
     own, away = call(
-        readout_kernel, (sds((rows, width)), sds((rows, width))), (twice, *g_cw[:2]), [pltpu.VMEM((pair, width), F32)]
+        readout_kernel, (sds((rows, width)), sds((rows, width))), (twice, c_all), [pltpu.VMEM((pair, width), F32)]
     )
     branch, d_mixed, dlogit, kept, away = call(
         second_kernel,
         (sds((rows, width), BF16), sds((rows, width)), sds((rows, width), BF16), *[sds((rows, 2 * width + 256), BF16)] * 2),
-        (own, swap(away, "tc"), grad_out, normed, feat, *g_cw),
+        (own, swap(away, "tc"), grad_out, normed, feat, cw, other_cw),
         [pltpu.VMEM((width, width), BF16), pltpu.VMEM((rows, width), BF16)],
     )
     got = swap(away, "tc")
@@ -776,29 +781,29 @@
     got, part = lax.optimization_barrier((got, part))
     d_state, carry, stay_cw, leave_cw = call(
         functools.partial(back_kernel, pairs),
-        (sds((2 * pair, 256)), sds((pairs, 8, 128)), sds((GROUPS, 160, 128), BF16), sds((GROUPS, 160, 128), BF16)),
-        (kept, got, twice, starts, lane, *g_cw[:2]),
-        [pltpu.VMEM((pair, width), BF16), pltpu.VMEM((width, 256), BF16), pltpu.VMEM((8, 128), F32)],
+        (sds((pair, 512)), sds((pairs, 8, 128)), *[sds((2, GROUPS // 2, 160, 128), BF16)] * 2),
+        (kept, got, twice, starts, lane, c_all),
+        [pltpu.VMEM((pair, width), BF16), pltpu.VMEM((width, 256), BF16), pltpu.VMEM((8, 128), F32),
+         pltpu.VMEM((2, 2, GROUPS // 2, 160, 128), BF16)],
     )
     if fast:
-        far_cw = swap(leave_cw, "ty")
+        far_cw = swap(leave_cw, "fx")
     came = lax.all_to_all(carry, same_core, 0, 0, tiled=True)
     if fast:
         came, far_cw, stay_cw = lax.optimization_barrier((came, far_cw, stay_cw))
-        stay_cw, leave_cw = call(y_cw_kernel, [sds((GROUPS // 2, 160, 128), BF16)] * 2, (stay_cw, far_cw))
-        far_cw = swap(leave_cw, "fx")
+        stay_cw, leave_cw = call(middle_kernel, [sds((GROUPS // 2, 160, 128), BF16)] * 2, (stay_cw, far_cw))
+        far_cw = swap(leave_cw, "ty")
         came = tied(came, leave_cw)
     stay_b, y_b, x_b, xy_b, d_normed, away = call(
         third_kernel,
         (*[sds((448, 128), BF16)] * 4, sds((rows, width)), sds((rows, width))),
-        (came, starts, wide, xhat, v, lane, row_prm, feat, state, d_state, enter, d_mixed, part, g),
-        [pltpu.VMEM((8, 128), F32), pltpu.VMEM((2 * pair, 256), BF16), pltpu.VMEM((pair, width), F32), pltpu.VMEM((32, 128), F32)],
-    )
-    input_grad = lambda away: call(
-        input_grad_kernel, sds((rows, width)), (d_normed, swap(away, "tc"), grad_out, xhat, inverse, feat)
+        (came, starts, normed, xhat, v, lane, row_prm, feat, state, d_state, enter, d_mixed, part, b_all),
+        [pltpu.VMEM((8, 128), F32), pltpu.VMEM((pair, 512), BF16), pltpu.VMEM((pair, width), F32), pltpu.VMEM((32, 128), F32)],
     )
     if not fast:
-        grad_in = input_grad(away)
+        grad_in = call(
+            input_grad_kernel, sds((rows, width)), (d_normed, swap(away, "tc"), grad_out, xhat, inverse, feat)
+        )
         return reduced(layer_out, grad_in, stay_cw, leave_cw, (stay_b, y_b, x_b, xy_b), count_all, fsdp, width)
     sent = call(
         plane_add_kernel,
@@ -806,16 +811,16 @@
         (stay_cw, far_cw, stay_b, swap(y_b, "ty"), swap(x_b, "fx"), across(xy_b)),
     )
     got = lax.all_to_all(sent, "fz", 0, 0, tiled=True)
-    grad_in = input_grad(tied(away, got))
+    away = swap(tied(away, got), "tc")
     vec = call(vectors_kernel, sds((32, 128)), (got,))
     other = swap(vec, "tc")
     d_re, d_im, d_ore, d_oim, d_glu = call(
         matrices_kernel, (*[sds((64, 96))] * 4, sds((64, 128))), (got,), [pltpu.VMEM((128, 128), F32)]
     )
-    d_gbias, d_scale, d_bias, d_skip, g_decay, g_lam, g_step, rms = call(
+    grad_in, d_gbias, d_scale, d_bias, d_skip, g_decay, g_lam, g_step, rms = call(
         functools.partial(finish_kernel, count_all),
-        (sds((1, 16)), *[sds((1, 512))] * 3, *[sds((384,))] * 3, sds((1, 2))),
-        (vec, other),
+        (sds((rows, width)), sds((1, 16)), *[sds((1, 512))] * 3, *[sds((384,))] * 3, sds((1, 2))),
+        (vec, other, d_normed, away, grad_out, xhat, inverse, feat),
         [pltpu.VMEM((32, 128), F32)],
     )
     flat = lambda value: value.reshape(-1)
@@ -853,14 +858,13 @@
     everyone = lax.all_gather(packet, TENSOR, axis=0).reshape(2, 2, GROUPS // 2, 2, 272, 128)
     x, y, core = (lax.axis_index(axis) for axis in ("fx", "ty", "tc"))
     own_x = lambda value, axis: jnp.stack([lax.dynamic_index_in_dim(value, x ^ j, axis, keepdims=False) for j in range(2)])
-    g_cw = []
     for i in range(2):
         both = lax.dynamic_index_in_dim(everyone, core ^ i, 1, keepdims=False)
         slots = [own_x(lax.dynamic_index_in_dim(both, y ^ m, 0, keepdims=False), 1) for m in range(2)]
-        g_cw += [slot[:, :, 112:] for slot in slots]
+        slots = jnp.stack(slots, axis=1)
         if i == 0:
-            g = jnp.stack(slots, axis=1)[:, :, :, :112]
-    return g, g_cw
+            g, cw = slots[:, :, :, :112], slots[:, :, :, 112:]
+    return g, cw, slots[:, :, :, 112:]
 
 
 def reduced(layer_out, grad_in, stay_cw, leave_cw, plane_b, count_all, fsdp, width):
@@ -885,7 +889,7 @@
 
     blocks = [value[:384].reshape(GROUPS // 2, 96, 128) for value in plane_b]
     d_re, d_im = natural([jnp.stack([blocks[m], blocks[2 + m]], axis=1) for m in range(2)])
-    cw = [value.reshape(GROUPS // 2, 2, 160, 128) for value in (stay_cw, leave_cw)]
+    cw = jnp.stack([stay_cw, leave_cw]).transpose(1, 2, 0, 3, 4)
     d_ore, d_oim = natural([value[:, :, :96] for value in cw])
     d_glu = canonical([value[:, :, 96:] for value in cw]).reshape(4, width, 128).swapaxes(1, 2).reshape(-1, width)
     vec = lax.psum(joined(plane_b[0][384:448]), AXES)

time: 86.5 us -> 83.6 us (0.966)
  Pallas kernels: 12.2 us -> 9.8 us
    pallas_call x16 -> x15, Pallas kernels: 12.2 us -> 9.8 us  [call(): pl.pallas_call(kernel, out_shape=outs, in_specs=specs or [VM] * len(args)...]
    ppermute x2, waiting for transfers between devices: 5.48 us -> 4.32 us  [across(): return lax.ppermute(value, ('fx', 'ty'), [(n, 3 - n) for n in range(4)])]
    ppermute x15 -> x14, waiting for transfers between devices: 6.55 us -> 7.42 us  [swap(): return lax.ppermute(value, axis, [(0, 1), (1, 0)])]
    ppermute x15 -> x14, starting transfers between devices: 10.2 us -> 9.8 us  [swap(): return lax.ppermute(value, axis, [(0, 1), (1, 0)])]
  transfers between devices with their start and end apart: 17 -> 16, of which waited for: 8 -> 8; matrix products, arithmetic and copies ran while one was open for 0% -> 0% of each run, Pallas kernels for 9% -> 6%
where the time goes in v5:
time: 83.6 us; the launch traced here: 83.2 us
  blocking collectives  47.5 us (57%)
  starting transfers between devices  13.2 us (16%)
  waiting for transfers between devices  11.7 us (14%)
  Pallas kernels  9.8 us (12%)
    all_to_all x2, blocking collectives, on_device(): came = lax.all_to_all(carry, same_core, 0, 0, tiled=True)  21.6 us
    all_to_all x1, blocking collectives, on_device(): mine = lax.all_to_all(sent, 'fz', 0, 0, tiled=True)  15.6 us
    all_to_all x1, blocking collectives, on_device(): got = lax.all_to_all(sent, 'fz', 0, 0, tiled=True)  10.4 us
    ppermute x14, starting transfers between devices, swap(): return lax.ppermute(value, axis, [(0, 1), (1, 0)])  9.8 us
    pallas_call x15, Pallas kernels, call(): pl.pallas_call(kernel, out_shape=outs, in_specs=specs or [VM] * len(args)...  9.8 us
    ppermute x14, waiting for transfers between devices, swap(): return lax.ppermute(value, axis, [(0, 1), (1, 0)])  7.42 us
    ppermute x2, waiting for transfers between devices, across(): return lax.ppermute(value, ('fx', 'ty'), [(n, 3 - n) for n in range(4)])  4.32 us
    ppermute x2, starting transfers between devices, across(): return lax.ppermute(value, ('fx', 'ty'), [(n, 3 - n) for n in range(4)])  3.42 us
  transfers between devices with their start and end apart: 16, of which 8 were waited for; matrix products, arithmetic and copies ran while one was open for 0% of the time, Pallas kernels for 6%

profile of v5, /device:TPU:0, one launch (start us, length us, event | category | flops | bytes accessed | tf_op | source)
XLA Modules:
  0.0 83.2 jit_solution(12284785359174422478)
XLA Ops:
  0.7 1.8 %pack.1 = bf16[4,272,128]{2,1,0:T(8,128)(2,1)} custom-call(s32[4]{0:T(128)} %refs_0_.1, bf16[64,96]{1,0:T(8,128)(2,1)} %bitcast.42, bf16[64,96]{1,0:T(8,128)(2,1)} %bitcast.43, bf16[64,96]{1,0:T(8,128)(2,1)} %bitcast.44, bf16[64,96]{1,0:T(8,128)(2,1)} %bitcast.45, bf16[64,512]{1,0:T(8,128)(2,1)} %bitcast.41, bf16[1,64]{1,0:T(2,128)(2,1)} %bitcast.46, ...), custom_call_target="tpu_custom_call" | custom-call | bytes 5400000 | tf_op jit(solution)/shard_map/pack/pallas_call | solution.py:687
  2.4 15.6 %all_to_all.20 = bf16[4,272,128]{2,1,0:T(8,128)(2,1)S(1)} all-to-all(bf16[4,272,128]{2,1,0:T(8,128)(2,1)} %pack.1), channel_id=1, replica_groups=mesh['fz'=4,'fx'=2,'ty'=2,'tc'=2] {'fz'}, dimensions={0} | all-to-all | bytes 557056 | tf_op jit(solution)/shard_map/all_to_all | solution.py:732
  18.0 1.6 %collective-permute-start.3 = (bf16[4,160,128]{2,1,0:T(8,128)(2,1)S(1)}, bf16[4,160,128]{2,1,0:T(8,128)(2,1)S(1)}, u32[]{:S(2)}, u32[]{:S(2)}) collective-permute-start(bf16[4,160,128]{2,1,0:T(8,128)(2,1)S(1)} %slice.9), channel_id=1, source_target_pairs={{0,2},{2,0},{1,3},{3,1},{4,6},{6,4},{5,7},{7,5},{8,10},{10,8},{9,1... | collective-permute-start | bytes 491528 | tf_op jit(solution)/shard_map/ppermute | solution.py:704
  19.6 1.7 %collective-permute-start.2 = (bf16[4,112,128]{2,1,0:T(8,128)(2,1)S(1)}, bf16[4,112,128]{2,1,0:T(8,128)(2,1)S(1)}, u32[]{:S(2)}, u32[]{:S(2)}) collective-permute-start(bf16[4,112,128]{2,1,0:T(8,128)(2,1)S(1)} %slice.8), channel_id=1, source_target_pairs={{0,6},{2,4},{4,2},{6,0},{1,7},{3,5},{5,3},{7,1},{8,14},{10,12},{12... | collective-permute-start | bytes 344072 | tf_op jit(solution)/shard_map/ppermute | solution.py:708
  21.9 1.2 %collective-permute-start = (bf16[4,112,128]{2,1,0:T(8,128)(2,1)S(1)}, bf16[4,112,128]{2,1,0:T(8,128)(2,1)S(1)}, u32[]{:S(2)}, u32[]{:S(2)}) collective-permute-start(bf16[4,112,128]{2,1,0:T(8,128)(2,1)S(1)} %slice.8), channel_id=1, source_target_pairs={{0,2},{2,0},{1,3},{3,1},{4,6},{6,4},{5,7},{7,5},{8,10},{10,8},{9,1... | collective-permute-start | bytes 344072 | tf_op jit(solution)/shard_map/ppermute | solution.py:704
  23.4 3.1 %collective-permute-done.2 = bf16[4,112,128]{2,1,0:T(8,128)(2,1)S(1)} collective-permute-done((bf16[4,112,128]{2,1,0:T(8,128)(2,1)S(1)}, bf16[4,112,128]{2,1,0:T(8,128)(2,1)S(1)}, u32[]{:S(2)}, u32[]{:S(2)}) %collective-permute-start.2) | collective-permute-done | bytes 114720 | tf_op jit(solution)/shard_map/ppermute | solution.py:708
  26.5 1.5 %collective-permute-done.1 = bf16[4,112,128]{2,1,0:T(8,128)(2,1)S(1)} collective-permute-done((bf16[4,112,128]{2,1,0:T(8,128)(2,1)S(1)}, bf16[4,112,128]{2,1,0:T(8,128)(2,1)S(1)}, u32[]{:S(2)}, u32[]{:S(2)}) %collective-permute-start.1) | collective-permute-done | bytes 114720 | tf_op jit(solution)/shard_map/ppermute | solution.py:704
  28.6 1.6 %collective-permute-start.5 = (bf16[2,4,160,128]{3,2,1,0:T(8,128)(2,1)S(1)}, bf16[2,4,160,128]{3,2,1,0:T(8,128)(2,1)S(1)}, u32[]{:S(2)}, u32[]{:S(2)}) collective-permute-start(bf16[2,4,160,128]{3,2,1,0:T(8,128)(2,1)S(1)} %pad_maximum_fusion.2), channel_id=1, source_target_pairs={{0,4},{4,0},{1,5},{5,1},{2,6},{6,2},{3,7},{7,3},{8,12},{12,8},{9,1... | collective-permute-start | bytes 983048 | tf_op jit(solution)/shard_map/ppermute | solution.py:704
  30.9 11.0 %all_to_all.21.recv_ref = f32[16,8,128]{2,1,0:T(8,128)S(1)} all-to-all(f32[16,8,128]{2,1,0:T(8,128)S(1)} %get-tuple-element.92), channel_id=1, replica_groups=mesh['fz'=4,'fx'=2,'ty'=2,'tc'=2] {'fz','fx','ty'}, dimensions={0} | all-to-all | bytes 131072 | tf_op jit(solution)/shard_map/all_to_all | solution.py:757
  42.0 0.9 %states.1 = (f32[256,512]{1,0:T(8,128)S(1)}, bf16[256,512]{1,0:T(8,128)(2,1)S(1)}, f32[8,512]{1,0:T(8,128)S(1)}, bf16[512,512]{1,0:T(8,128)(2,1)S(1)}) custom-call(f32[16,8,128]{2,1,0:T(8,128)S(1)} %all_to_all.21.recv_ref, f32[4,128]{1,0:T(4,128)S(1)} %get-tuple-element.91.start_ref, f32[256,512]{1,0:T(8,128)S(1)} %get-tuple-element.93.v_ref, ...), custom_call_target="tpu_custom_call" | custom-call | bytes 3240000 | tf_op jit(solution)/shard_map/states/pallas_call | solution.py:687
  43.9 1.5 %collective-permute-done.6.got_ref = f32[128,512]{1,0:T(8,128)S(1)} collective-permute-done((f32[128,512]{1,0:T(8,128)S(1)}, f32[128,512]{1,0:T(8,128)S(1)}, u32[]{:S(2)}, u32[]{:S(2)}) %collective-permute-start.6) | collective-permute-done | bytes 262176 | tf_op jit(solution)/shard_map/ppermute | solution.py:704
  46.3 0.8 sums.1
  47.8 0.8 back.1
  48.6 0.7 collective-permute-start.9
  49.3 10.6 %all_to_all.22.recv_ref = f32[16,8,128]{2,1,0:T(8,128)S(1)} all-to-all(f32[16,8,128]{2,1,0:T(8,128)S(1)} %get-tuple-element.113), channel_id=1, replica_groups=mesh['fz'=4,'fx'=2,'ty'=2,'tc'=2] {'fz','fx','ty'}, dimensions={0} | all-to-all | bytes 131072 | tf_op jit(solution)/shard_map/all_to_all | solution.py:791
  60.0 0.9 %collective-permute-start.10 = (bf16[4,160,128]{2,1,0:T(8,128)(2,1)S(1)}, bf16[4,160,128]{2,1,0:T(8,128)(2,1)S(1)}, u32[]{:S(2)}, u32[]{:S(2)}) collective-permute-start(bf16[4,160,128]{2,1,0:T(8,128)(2,1)S(1)} %get-tuple-element.119), channel_id=1, source_target_pairs={{0,2},{2,0},{1,3},{3,1},{4,6},{6,4},{5,7},{7,5},{8,10},{10,8},{9,1... | collective-permute-start | bytes 491528 | tf_op jit(solution)/shard_map/ppermute | solution.py:704
  60.9 1.8 %third.1 = (bf16[448,128]{1,0:T(8,128)(2,1)S(1)}, bf16[448,128]{1,0:T(8,128)(2,1)S(1)}, bf16[448,128]{1,0:T(8,128)(2,1)S(1)}, bf16[448,128]{1,0:T(8,128)(2,1)S(1...) custom-call(f32[16,8,128]{2,1,0:T(8,128)S(1)} %all_to_all.22.recv_ref, f32[4,128]{1,0:T(4,128)S(1)} %get-tuple-element.91.start_ref, ...), custom_call_target="tpu_custom_call" | custom-call | bytes 5400000 | tf_op jit(solution)/shard_map/third/pallas_call | solution.py:687
  62.7 1.2 %collective-permute-start.11 = (bf16[448,128]{1,0:T(8,128)(2,1)S(1)}, bf16[448,128]{1,0:T(8,128)(2,1)S(1)}, u32[]{:S(2)}, u32[]{:S(2)}) collective-permute-start(bf16[448,128]{1,0:T(8,128)(2,1)S(1)} %get-tuple-element.128), channel_id=1, source_target_pairs={{0,2},{2,0},{1,3},{3,1},{4,6},{6,4},{5,7},{7,5},{8,10},{10,8},{9,1... | collective-permute-start | bytes 344072 | tf_op jit(solution)/shard_map/ppermute | solution.py:704
  64.5 1.7 %collective-permute-start.13 = (bf16[448,128]{1,0:T(8,128)(2,1)S(1)}, bf16[448,128]{1,0:T(8,128)(2,1)S(1)}, u32[]{:S(2)}, u32[]{:S(2)}) collective-permute-start(bf16[448,128]{1,0:T(8,128)(2,1)S(1)} %get-tuple-element.130), channel_id=1, source_target_pairs={{0,6},{2,4},{4,2},{6,0},{1,7},{3,5},{5,3},{7,1},{8,14},{10,12},{12... | collective-permute-start | bytes 344072 | tf_op jit(solution)/shard_map/ppermute | solution.py:708
  66.2 2.8 %collective-permute-done.11.y_ref = bf16[448,128]{1,0:T(8,128)(2,1)S(1)} collective-permute-done((bf16[448,128]{1,0:T(8,128)(2,1)S(1)}, bf16[448,128]{1,0:T(8,128)(2,1)S(1)}, u32[]{:S(2)}, u32[]{:S(2)}) %collective-permute-start.11) | collective-permute-done | bytes 114720 | tf_op jit(solution)/shard_map/ppermute | solution.py:704
  69.1 1.2 %collective-permute-done.13.xy_ref = bf16[448,128]{1,0:T(8,128)(2,1)S(1)} collective-permute-done((bf16[448,128]{1,0:T(8,128)(2,1)S(1)}, bf16[448,128]{1,0:T(8,128)(2,1)S(1)}, u32[]{:S(2)}, u32[]{:S(2)}) %collective-permute-start.13) | collective-permute-done | bytes 114720 | tf_op jit(solution)/shard_map/ppermute | solution.py:708
  70.4 10.4 %all_to_all.23.got_ref = bf16[4,320,128]{2,1,0:T(8,128)(2,1)S(1)} all-to-all(bf16[4,320,128]{2,1,0:T(8,128)(2,1)S(1)} %plane_add.1), channel_id=1, replica_groups=mesh['fz'=4,'fx'=2,'ty'=2,'tc'=2] {'fz'}, dimensions={0} | all-to-all | bytes 655360 | tf_op jit(solution)/shard_map/all_to_all | solution.py:813
  81.3 0.8 matrices.1
  82.3 0.9 %finish.1 = (f32[128,512]{1,0:T(8,128)}, f32[1,16]{1,0:T(1,128)}, f32[1,512]{1,0:T(1,128)}, f32[1,512]{1,0:T(1,128)}, f32[1,512]{1,0:T(1,128)}, /*index=5*/f32[3...) custom-call(f32[32,128]{1,0:T(8,128)S(1)} %vectors.1.own_ref, f32[32,128]{1,0:T(8,128)S(1)} %collective-permute-done.14.other_ref, ...), custom_call_target="tpu_custom_call" | custom-call | bytes 1440000 | tf_op jit(solution)/shard_map/finish/pallas_call | solution.py:687
  (36 shorter events, 6.5 us)
Async XLA Ops:
  18.0 1.6 %copy-start.1 = (bf16[128,512]{1,0:T(8,128)(2,1)S(1)}, bf16[128,512]{1,0:T(8,128)(2,1)}, u32[]{:S(2)}) copy-start(bf16[128,512]{1,0:T(8,128)(2,1)} %x_ref.3) | copy-start | bytes 393220
  18.0 10.5 %collective-permute-start.3 = (bf16[4,160,128]{2,1,0:T(8,128)(2,1)S(1)}, bf16[4,160,128]{2,1,0:T(8,128)(2,1)S(1)}, u32[]{:S(2)}, u32[]{:S(2)}) collective-permute-start(bf16[4,160,128]{2,1,0:T(8,128)(2,1)S(1)} %slice.9), channel_id=1, source_target_pairs={{0,2},{2,0},{1,3},{3,1},{4,6},{6,4},{5,7},{7,5},{8,10},{10,8},{9,1... | collective-permute-start | bytes 491528 | tf_op jit(solution)/shard_map/ppermute | solution.py:704
  19.6 3.5 %collective-permute-start.4 = (bf16[128,512]{1,0:T(8,128)(2,1)S(1)}, bf16[128,512]{1,0:T(8,128)(2,1)S(1)}, u32[]{:S(2)}, u32[]{:S(2)}) collective-permute-start(bf16[128,512]{1,0:T(8,128)(2,1)S(1)} %copy-done.1), channel_id=1, source_target_pairs={{0,1},{1,0},{2,3},{3,2},{4,5},{5,4},{6,7},{7,6},{8,9},{9,8},{10,11... | collective-permute-start | bytes 393224 | tf_op jit(solution)/shard_map/ppermute | solution.py:704
  19.6 6.8 %collective-permute-start.2 = (bf16[4,112,128]{2,1,0:T(8,128)(2,1)S(1)}, bf16[4,112,128]{2,1,0:T(8,128)(2,1)S(1)}, u32[]{:S(2)}, u32[]{:S(2)}) collective-permute-start(bf16[4,112,128]{2,1,0:T(8,128)(2,1)S(1)} %slice.8), channel_id=1, source_target_pairs={{0,6},{2,4},{4,2},{6,0},{1,7},{3,5},{5,3},{7,1},{8,14},{10,12},{12... | collective-permute-start | bytes 344072 | tf_op jit(solution)/shard_map/ppermute | solution.py:708
  21.3 6.6 %collective-permute-start.1 = (bf16[4,112,128]{2,1,0:T(8,128)(2,1)S(1)}, bf16[4,112,128]{2,1,0:T(8,128)(2,1)S(1)}, u32[]{:S(2)}, u32[]{:S(2)}) collective-permute-start(bf16[4,112,128]{2,1,0:T(8,128)(2,1)S(1)} %slice.8), channel_id=1, source_target_pairs={{0,4},{4,0},{1,5},{5,1},{2,6},{6,2},{3,7},{7,3},{8,12},{12,8},{9,1... | collective-permute-start | bytes 344072 | tf_op jit(solution)/shard_map/ppermute | solution.py:704
  21.9 6.6 %collective-permute-start = (bf16[4,112,128]{2,1,0:T(8,128)(2,1)S(1)}, bf16[4,112,128]{2,1,0:T(8,128)(2,1)S(1)}, u32[]{:S(2)}, u32[]{:S(2)}) collective-permute-start(bf16[4,112,128]{2,1,0:T(8,128)(2,1)S(1)} %slice.8), channel_id=1, source_target_pairs={{0,2},{2,0},{1,3},{3,1},{4,6},{6,4},{5,7},{7,5},{8,10},{10,8},{9,1... | collective-permute-start | bytes 344072 | tf_op jit(solution)/shard_map/ppermute | solution.py:704
  28.6 13.4 %collective-permute-start.5 = (bf16[2,4,160,128]{3,2,1,0:T(8,128)(2,1)S(1)}, bf16[2,4,160,128]{3,2,1,0:T(8,128)(2,1)S(1)}, u32[]{:S(2)}, u32[]{:S(2)}) collective-permute-start(bf16[2,4,160,128]{3,2,1,0:T(8,128)(2,1)S(1)} %pad_maximum_fusion.2), channel_id=1, source_target_pairs={{0,4},{4,0},{1,5},{5,1},{2,6},{6,2},{3,7},{7,3},{8,12},{12,8},{9,1... | collective-permute-start | bytes 983048 | tf_op jit(solution)/shard_map/ppermute | solution.py:704
  42.9 2.5 %collective-permute-start.7 = (bf16[2,2,4,160,128]{4,3,2,1,0:T(8,128)(2,1)S(1)}, bf16[2,2,4,160,128]{4,3,2,1,0:T(8,128)(2,1)S(1)}, u32[]{:S(2)}, u32[]{:S(2)}) collective-permute-start(bf16[2,2,4,160,128]{4,3,2,1,0:T(8,128)(2,1)S(1)} %pad_maximum_fusion.cw_ref), channel_id=1, source_target_pairs={{0,1},{1,0},{2,3},{3,2},{4,5},{5,4},{6,7},{7,6},{8,9},{9,8},{10,11... | collective-permute-start | bytes 1966088 | tf_op jit(solution)/shard_map/ppermute | solution.py:704
  43.0 2.5 %copy-start = (bf16[128,512]{1,0:T(8,128)(2,1)S(1)}, bf16[128,512]{1,0:T(8,128)(2,1)}, u32[]{:S(2)}) copy-start(bf16[128,512]{1,0:T(8,128)(2,1)} %up_ref.3) | copy-start | bytes 393220
  43.3 2.1 %collective-permute-start.6 = (f32[128,512]{1,0:T(8,128)S(1)}, f32[128,512]{1,0:T(8,128)S(1)}, u32[]{:S(2)}, u32[]{:S(2)}) collective-permute-start(f32[128,512]{1,0:T(8,128)S(1)} %get-tuple-element.102), channel_id=1, source_target_pairs={{0,1},{1,0},{2,3},{3,2},{4,5},{5,4},{6,7},{7,6},{8,9},{9,8},{10,11... | collective-permute-start | bytes 786440 | tf_op jit(solution)/shard_map/ppermute | solution.py:704
  46.1 1.7 %collective-permute-start.8 = (bf16[128,1280]{1,0:T(8,128)(2,1)S(1)}, bf16[128,1280]{1,0:T(8,128)(2,1)S(1)}, u32[]{:S(2)}, u32[]{:S(2)}) collective-permute-start(bf16[128,1280]{1,0:T(8,128)(2,1)S(1)} %get-tuple-element.110), channel_id=1, source_target_pairs={{0,1},{1,0},{2,3},{3,2},{4,5},{5,4},{6,7},{7,6},{8,9},{9,8},{10,11... | collective-permute-start | bytes 983048 | tf_op jit(solution)/shard_map/ppermute | solution.py:704
  48.6 11.3 %collective-permute-start.9 = (bf16[2,4,160,128]{3,2,1,0:T(8,128)(2,1)S(1)}, bf16[2,4,160,128]{3,2,1,0:T(8,128)(2,1)S(1)}, u32[]{:S(2)}, u32[]{:S(2)}) collective-permute-start(bf16[2,4,160,128]{3,2,1,0:T(8,128)(2,1)S(1)} %get-tuple-element.114), channel_id=1, source_target_pairs={{0,4},{4,0},{1,5},{5,1},{2,6},{6,2},{3,7},{7,3},{8,12},{12,8},{9,1... | collective-permute-start | bytes 983048 | tf_op jit(solution)/shard_map/ppermute | solution.py:704
  60.0 10.3 %collective-permute-start.10 = (bf16[4,160,128]{2,1,0:T(8,128)(2,1)S(1)}, bf16[4,160,128]{2,1,0:T(8,128)(2,1)S(1)}, u32[]{:S(2)}, u32[]{:S(2)}) collective-permute-start(bf16[4,160,128]{2,1,0:T(8,128)(2,1)S(1)} %get-tuple-element.119), channel_id=1, source_target_pairs={{0,2},{2,0},{1,3},{3,1},{4,6},{6,4},{5,7},{7,5},{8,10},{10,8},{9,1... | collective-permute-start | bytes 491528 | tf_op jit(solution)/shard_map/ppermute | solution.py:704
  62.7 6.4 %collective-permute-start.11 = (bf16[448,128]{1,0:T(8,128)(2,1)S(1)}, bf16[448,128]{1,0:T(8,128)(2,1)S(1)}, u32[]{:S(2)}, u32[]{:S(2)}) collective-permute-start(bf16[448,128]{1,0:T(8,128)(2,1)S(1)} %get-tuple-element.128), channel_id=1, source_target_pairs={{0,2},{2,0},{1,3},{3,1},{4,6},{6,4},{5,7},{7,5},{8,10},{10,8},{9,1... | collective-permute-start | bytes 344072 | tf_op jit(solution)/shard_map/ppermute | solution.py:704
  63.9 5.1 %collective-permute-start.12 = (bf16[448,128]{1,0:T(8,128)(2,1)S(1)}, bf16[448,128]{1,0:T(8,128)(2,1)S(1)}, u32[]{:S(2)}, u32[]{:S(2)}) collective-permute-start(bf16[448,128]{1,0:T(8,128)(2,1)S(1)} %get-tuple-element.129), channel_id=1, source_target_pairs={{0,4},{4,0},{1,5},{5,1},{2,6},{6,2},{3,7},{7,3},{8,12},{12,8},{9,1... | collective-permute-start | bytes 344072 | tf_op jit(solution)/shard_map/ppermute | solution.py:704
  64.5 5.7 %collective-permute-start.13 = (bf16[448,128]{1,0:T(8,128)(2,1)S(1)}, bf16[448,128]{1,0:T(8,128)(2,1)S(1)}, u32[]{:S(2)}, u32[]{:S(2)}) collective-permute-start(bf16[448,128]{1,0:T(8,128)(2,1)S(1)} %get-tuple-element.130), channel_id=1, source_target_pairs={{0,6},{2,4},{4,2},{6,0},{1,7},{3,5},{5,3},{7,1},{8,14},{10,12},{12... | collective-permute-start | bytes 344072 | tf_op jit(solution)/shard_map/ppermute | solution.py:708
  80.8 1.6 %collective-permute-start.15 = (f32[128,512]{1,0:T(8,128)S(1)}, f32[128,512]{1,0:T(8,128)S(1)}, u32[]{:S(2)}, u32[]{:S(2)}) collective-permute-start(f32[128,512]{1,0:T(8,128)S(1)} %get-tuple-element.133), channel_id=1, source_target_pairs={{0,1},{1,0},{2,3},{3,2},{4,5},{5,4},{6,7},{7,6},{8,9},{9,8},{10,11... | collective-permute-start | bytes 786440 | tf_op jit(solution)/shard_map/ppermute | solution.py:704
  80.8 1.5 %collective-permute-start.14 = (f32[32,128]{1,0:T(8,128)S(1)}, f32[32,128]{1,0:T(8,128)S(1)}, u32[]{:S(2)}, u32[]{:S(2)}) collective-permute-start(f32[32,128]{1,0:T(8,128)S(1)} %vectors.1.own_ref), channel_id=1, source_target_pairs={{0,1},{1,0},{2,3},{3,2},{4,5},{5,4},{6,7},{7,6},{8,9},{9,8},{10,11... | collective-permute-start | bytes 49160 | tf_op jit(solution)/shard_map/ppermute | solution.py:704

commit v6 on v5

--- a/solution.py
+++ b/solution.py
@@ -277,7 +277,7 @@
     carry_block(last[0], last[1], scratch)
     packet = scratch[...]
     for d in range(pairs):
-        send_ref[d] = packet
+        send_ref[d] = packet[0:4]
 
 
 def eighth_powers(a, exponent_of):
@@ -475,7 +475,7 @@
     carry_block(first[0], first[1], scratch)
     packet = scratch[...]
     for d in range(pairs):
-        send_ref[d] = packet
+        send_ref[d] = packet[0:4]
     d_c = dot(twice_ref[...], dy_ref[...], TN)
     act = slice(width, 2 * width)
     units = slice(2 * width, 2 * width + 256)
@@ -491,9 +491,14 @@
     leave_ref[...] = all_ref[1]
 
 
-def split_rows(value):
-    upper = value.astype(BF16)
-    return jnp.concatenate([upper, (value - upper.astype(F32)).astype(BF16)], axis=0)
+def packed(vec):
+    upper = vec.astype(BF16).astype(F32)
+    return jnp.concatenate([upper, vec - upper], axis=0).astype(BF16)
+
+
+def unpacked(packet):
+    value = packet.astype(F32)
+    return value[0:24] + value[24:48]
 
 
 def third_kernel(
@@ -568,20 +573,20 @@
     g_lam = to_lam_a[1] + to_lam_c[1]
     slope = cmul((-decay, lam), (abar_re, abar_im))
     g_step = (slope[0] * d_abar[0] + slope[1] * d_abar[1] + abar_re * d_coef[0] + abar_im * d_coef[1]) * step
-    vec_ref[16:32, :] = jnp.zeros((16, 128), F32)
     for k, value in enumerate((g_decay, g_lam, g_step)):
         for m in range(2):
-            vec_ref[pl.ds(16 + 4 * k + slot_pos(m, 0), 1), :] = value[m : m + 1]
+            vec_ref[pl.ds(16 + 2 * k + (lax.axis_index("ty") ^ m), 1), :] = value[m : m + 1]
+    folds = []
     for k in range(2):
         squares = part_ref[2 + k : 3 + k, :]
-        total = squares[:, 0:128]
-        for c in range(1, 4):
-            total = total + squares[:, 128 * c : 128 * c + 128]
-        vec_ref[28 + k : 29 + k, :] = total
-    vec_ref[30:32, :] = jnp.zeros((2, 128), F32)
-    vec = split_rows(vec_ref[...])
+        total = (squares[:, 0:128] + squares[:, 128:256]) + (squares[:, 256:384] + squares[:, 384:512])
+        total = jnp.broadcast_to(total, (8, 128))
+        folds.append(total + pltpu.roll(total, 64, 1))
+    vec_ref[22:23, :] = jnp.where(low_half((1, 128)), folds[0][:1], folds[1][:1])
+    vec_ref[23:24, :] = jnp.zeros((1, 128), F32)
+    vec = packed(vec_ref[...])
     for ref in (stay_ref, y_ref, x_ref, xy_ref):
-        ref[384:448, :] = vec
+        ref[384:432, :] = vec
 
 
 def input_grad(dn_ref, got_ref, up_ref, xhat_ref, inv_ref, feat_ref, gin_ref):
@@ -601,10 +606,6 @@
     return (a.astype(F32) + b.astype(F32)).astype(BF16)
 
 
-def joined(packet):
-    return packet[0:32].astype(F32) + packet[32:64].astype(F32)
-
-
 def middle_kernel(keep_ref, got_ref, stay_ref, leave_ref):
     stay_ref[...] = added(keep_ref[0], got_ref[0])
     leave_ref[...] = added(keep_ref[1], got_ref[1])
@@ -614,18 +615,18 @@
     def total(read):
         return (read(stay_ref) + read(y_ref)) + (read(x_ref) + read(xy_ref))
 
-    vec = split_rows(total(lambda ref: joined(ref[384:448, :])))
+    vec = packed(total(lambda ref: unpacked(ref[384:432, :])))
     for z in range(GROUPS // 2):
         here = slice(96 * z, 96 * z + 96)
         out_ref[z, 0:96, :] = total(lambda ref, here=here: ref[here, :].astype(F32)).astype(BF16)
         out_ref[z, 96:256, :] = added(cw_ref[z], gotcw_ref[z])
-        out_ref[z, 256:320, :] = vec
+        out_ref[z, 256:304, :] = vec
 
 
 def vectors_kernel(got_ref, vec_ref):
-    vec = joined(got_ref[0, 256:320, :])
+    vec = unpacked(got_ref[0, 256:304, :])
     for z in range(1, GROUPS // 2):
-        vec = vec + joined(got_ref[z, 256:320, :])
+        vec = vec + unpacked(got_ref[z, 256:304, :])
     vec_ref[...] = vec
 
 
@@ -660,17 +661,21 @@
     gin_ref, gbias_ref, scale_ref, bias_ref, skip_ref, decay_ref, lam_ref, step_ref, rms_ref, vec_ref,
 ):
     input_grad(dn_ref, got_ref, up_ref, xhat_ref, inv_ref, feat_ref, gin_ref)
-    vec = own_ref[...] + other_ref[...]
+    own, other = own_ref[...], other_ref[...]
+    vec = own + other
     vec_ref[...] = vec
+    first, second = jnp.where(lax.axis_index("tc") == 0, own, other), jnp.where(lax.axis_index("tc") == 0, other, own)
     for k, ref in enumerate((scale_ref, bias_ref, skip_ref)):
         for c in range(4):
             ref[:, 128 * c : 128 * c + 128] = vec[4 * k + c : 4 * k + c + 1]
     for k, ref in enumerate((decay_ref, lam_ref, step_ref)):
-        for c, chunk in enumerate(rows_to_lanes(vec[16 + 4 * k : 20 + 4 * k])):
+        at = 16 + 2 * k
+        by_pos = [first[at : at + 1], second[at : at + 1], first[at + 1 : at + 2], second[at + 1 : at + 2]]
+        for c, chunk in enumerate(rows_to_lanes(jnp.concatenate(by_pos + [jnp.zeros((4, 128), F32)], axis=0))):
             ref[128 * c : 128 * c + 128] = chunk.reshape(128)
-    total = jnp.sum(vec[28:30], axis=1, keepdims=True)
-    lane = lane_iota((1, 2))
-    rms_ref[...] = jnp.sqrt(jnp.where(lane == 0, total[0:1], total[1:2]) / count_all)
+    squares = vec[22:23]
+    total = [jnp.sum(jnp.where(low_half((1, 128)) == low, squares, 0.0), axis=1, keepdims=True) for low in (True, False)]
+    rms_ref[...] = jnp.sqrt(jnp.where(lane_iota((1, 2)) == 0, total[0], total[1]) / count_all)
     place = tensor_pos() * GROUPS + fsdp_pos()
     row = jnp.broadcast_to(vec_ref[pl.ds(12 + place // 8, 1), :], (8, 128))
     gbias_ref[...] = pltpu.roll(row, 128 - 16 * (place % 8), 1)[0:1, 0:16]
@@ -750,7 +755,7 @@
     )
     b_all, v, lane, row_prm, carry = call(
         functools.partial(first_kernel, pairs),
-        (sds((512, width), BF16), sds((pair, 512)), sds((8, 256)), sds((8, 8, 128)), sds((pairs, 8, 128))),
+        (sds((512, width), BF16), sds((pair, 512)), sds((8, 256)), sds((8, 8, 128)), sds((pairs, 4, 128))),
         (normed, starts, g),
         [pltpu.VMEM((8, 128), F32)],
     )
@@ -781,7 +786,7 @@
     got, part = lax.optimization_barrier((got, part))
     d_state, carry, stay_cw, leave_cw = call(
         functools.partial(back_kernel, pairs),
-        (sds((pair, 512)), sds((pairs, 8, 128)), *[sds((2, GROUPS // 2, 160, 128), BF16)] * 2),
+        (sds((pair, 512)), sds((pairs, 4, 128)), *[sds((2, GROUPS // 2, 160, 128), BF16)] * 2),
         (kept, got, twice, starts, lane, c_all),
         [pltpu.VMEM((pair, width), BF16), pltpu.VMEM((width, 256), BF16), pltpu.VMEM((8, 128), F32),
          pltpu.VMEM((2, 2, GROUPS // 2, 160, 128), BF16)],
@@ -796,23 +801,26 @@
         came = tied(came, leave_cw)
     stay_b, y_b, x_b, xy_b, d_normed, away = call(
         third_kernel,
-        (*[sds((448, 128), BF16)] * 4, sds((rows, width)), sds((rows, width))),
+        (*[sds((432, 128), BF16)] * 4, sds((rows, width)), sds((rows, width))),
         (came, starts, normed, xhat, v, lane, row_prm, feat, state, d_state, enter, d_mixed, part, b_all),
-        [pltpu.VMEM((8, 128), F32), pltpu.VMEM((pair, 512), BF16), pltpu.VMEM((pair, width), F32), pltpu.VMEM((32, 128), F32)],
+        [pltpu.VMEM((8, 128), F32), pltpu.VMEM((pair, 512), BF16), pltpu.VMEM((pair, width), F32), pltpu.VMEM((24, 128), F32)],
     )
     if not fast:
         grad_in = call(
             input_grad_kernel, sds((rows, width)), (d_normed, swap(away, "tc"), grad_out, xhat, inverse, feat)
         )
         return reduced(layer_out, grad_in, stay_cw, leave_cw, (stay_b, y_b, x_b, xy_b), count_all, fsdp, width)
+    xy_b = across(xy_b)
+    x_b = swap(x_b, "fx")
+    y_b = swap(y_b, "ty")
     sent = call(
         plane_add_kernel,
-        sds((GROUPS // 2, 320, 128), BF16),
-        (stay_cw, far_cw, stay_b, swap(y_b, "ty"), swap(x_b, "fx"), across(xy_b)),
+        sds((GROUPS // 2, 304, 128), BF16),
+        (stay_cw, far_cw, stay_b, y_b, x_b, xy_b),
     )
     got = lax.all_to_all(sent, "fz", 0, 0, tiled=True)
     away = swap(tied(away, got), "tc")
-    vec = call(vectors_kernel, sds((32, 128)), (got,))
+    vec = call(vectors_kernel, sds((24, 128)), (got,))
     other = swap(vec, "tc")
     d_re, d_im, d_ore, d_oim, d_glu = call(
         matrices_kernel, (*[sds((64, 96))] * 4, sds((64, 128))), (got,), [pltpu.VMEM((128, 128), F32)]
@@ -821,7 +829,7 @@
         functools.partial(finish_kernel, count_all),
         (sds((rows, width)), sds((1, 16)), *[sds((1, 512))] * 3, *[sds((384,))] * 3, sds((1, 2))),
         (vec, other, d_normed, away, grad_out, xhat, inverse, feat),
-        [pltpu.VMEM((32, 128), F32)],
+        [pltpu.VMEM((24, 128), F32)],
     )
     flat = lambda value: value.reshape(-1)
     return (
@@ -892,12 +900,16 @@
     cw = jnp.stack([stay_cw, leave_cw]).transpose(1, 2, 0, 3, 4)
     d_ore, d_oim = natural([value[:, :, :96] for value in cw])
     d_glu = canonical([value[:, :, 96:] for value in cw]).reshape(4, width, 128).swapaxes(1, 2).reshape(-1, width)
-    vec = lax.psum(joined(plane_b[0][384:448]), AXES)
-    states = lambda k: vec[16 + 4 * k : 20 + 4 * k, :96].reshape(-1)
+    vec = unpacked(plane_b[0][384:432])
+    by_pos = lax.dynamic_update_slice_in_dim(
+        jnp.zeros((3, 2, 2, 96), F32), vec[16:22, :96].reshape(3, 2, 1, 96), lax.axis_index("tc"), 2
+    )
+    vec, by_pos = lax.psum((vec, by_pos), AXES)
+    states = lambda k: by_pos[k].reshape(-1)
     own = width // (4 * fsdp)
     place = tens * fsdp + fsdp_pos()
     d_gbias = lax.dynamic_slice_in_dim(vec[12:16].reshape(-1), place * own, own, 0)
-    rms = jnp.sqrt(jnp.sum(vec[28:30], axis=1) / count_all)
+    rms = jnp.sqrt(jnp.sum(vec[22].reshape(2, 64), axis=1) / count_all)
     return (
         layer_out, grad_in, vec[0:4].reshape(-1), vec[4:8].reshape(-1), states(0), states(1), states(2), scattered(d_re), scattered(d_im),
         scattered(d_ore), scattered(d_oim), vec[8:12].reshape(-1), scattered(d_glu), d_gbias, rms,

time: 83.6 us -> 82.9 us (level)
  no operation moved by 1% of the time
where the time goes in v6:
time: 82.9 us; the launch traced here: 82.5 us
  blocking collectives  47 us (57%)
  starting transfers between devices  13 us (16%)
  waiting for transfers between devices  11.7 us (14%)
  Pallas kernels  9.8 us (12%)
    all_to_all x2, blocking collectives, on_device(): came = lax.all_to_all(carry, same_core, 0, 0, tiled=True)  21.2 us
    all_to_all x1, blocking collectives, on_device(): mine = lax.all_to_all(sent, 'fz', 0, 0, tiled=True)  15.6 us
    all_to_all x1, blocking collectives, on_device(): got = lax.all_to_all(sent, 'fz', 0, 0, tiled=True)  10.2 us
    pallas_call x15, Pallas kernels, call(): pl.pallas_call(kernel, out_shape=outs, in_specs=specs or [VM] * len(args)...  9.8 us
    ppermute x14, starting transfers between devices, swap(): return lax.ppermute(value, axis, [(0, 1), (1, 0)])  9.72 us
    ppermute x14, waiting for transfers between devices, swap(): return lax.ppermute(value, axis, [(0, 1), (1, 0)])  7.39 us
    ppermute x2, waiting for transfers between devices, across(): return lax.ppermute(value, ('fx', 'ty'), [(n, 3 - n) for n in range(4)])  4.33 us
    ppermute x2, starting transfers between devices, across(): return lax.ppermute(value, ('fx', 'ty'), [(n, 3 - n) for n in range(4)])  3.33 us
  transfers between devices with their start and end apart: 16, of which 8 were waited for; matrix products, arithmetic and copies ran while one was open for 0% of the time, Pallas kernels for 6%

profile of v6, /device:TPU:0, one launch (start us, length us, event | category | flops | bytes accessed | tf_op | source)
XLA Modules:
  0.0 82.5 jit_solution(10899414301730868598)
XLA Ops:
  0.7 1.8 %pack.1 = bf16[4,272,128]{2,1,0:T(8,128)(2,1)} custom-call(s32[4]{0:T(128)} %refs_0_.1, bf16[64,96]{1,0:T(8,128)(2,1)} %bitcast.42, bf16[64,96]{1,0:T(8,128)(2,1)} %bitcast.43, bf16[64,96]{1,0:T(8,128)(2,1)} %bitcast.44, bf16[64,96]{1,0:T(8,128)(2,1)} %bitcast.45, bf16[64,512]{1,0:T(8,128)(2,1)} %bitcast.41, bf16[1,64]{1,0:T(2,128)(2,1)} %bitcast.46, ...), custom_call_target="tpu_custom_call" | custom-call | bytes 5400000 | tf_op jit(solution)/shard_map/pack/pallas_call | solution.py:692
  2.4 15.6 %all_to_all.20 = bf16[4,272,128]{2,1,0:T(8,128)(2,1)S(1)} all-to-all(bf16[4,272,128]{2,1,0:T(8,128)(2,1)} %pack.1), channel_id=1, replica_groups=mesh['fz'=4,'fx'=2,'ty'=2,'tc'=2] {'fz'}, dimensions={0} | all-to-all | bytes 557056 | tf_op jit(solution)/shard_map/all_to_all | solution.py:737
  18.0 1.6 %collective-permute-start.3 = (bf16[4,160,128]{2,1,0:T(8,128)(2,1)S(1)}, bf16[4,160,128]{2,1,0:T(8,128)(2,1)S(1)}, u32[]{:S(2)}, u32[]{:S(2)}) collective-permute-start(bf16[4,160,128]{2,1,0:T(8,128)(2,1)S(1)} %slice.9), channel_id=1, source_target_pairs={{0,2},{2,0},{1,3},{3,1},{4,6},{6,4},{5,7},{7,5},{8,10},{10,8},{9,1... | collective-permute-start | bytes 491528 | tf_op jit(solution)/shard_map/ppermute | solution.py:709
  19.6 1.7 %collective-permute-start.2 = (bf16[4,112,128]{2,1,0:T(8,128)(2,1)S(1)}, bf16[4,112,128]{2,1,0:T(8,128)(2,1)S(1)}, u32[]{:S(2)}, u32[]{:S(2)}) collective-permute-start(bf16[4,112,128]{2,1,0:T(8,128)(2,1)S(1)} %slice.8), channel_id=1, source_target_pairs={{0,6},{2,4},{4,2},{6,0},{1,7},{3,5},{5,3},{7,1},{8,14},{10,12},{12... | collective-permute-start | bytes 344072 | tf_op jit(solution)/shard_map/ppermute | solution.py:713
  21.9 1.2 %collective-permute-start = (bf16[4,112,128]{2,1,0:T(8,128)(2,1)S(1)}, bf16[4,112,128]{2,1,0:T(8,128)(2,1)S(1)}, u32[]{:S(2)}, u32[]{:S(2)}) collective-permute-start(bf16[4,112,128]{2,1,0:T(8,128)(2,1)S(1)} %slice.8), channel_id=1, source_target_pairs={{0,2},{2,0},{1,3},{3,1},{4,6},{6,4},{5,7},{7,5},{8,10},{10,8},{9,1... | collective-permute-start | bytes 344072 | tf_op jit(solution)/shard_map/ppermute | solution.py:709
  23.4 3.1 %collective-permute-done.2 = bf16[4,112,128]{2,1,0:T(8,128)(2,1)S(1)} collective-permute-done((bf16[4,112,128]{2,1,0:T(8,128)(2,1)S(1)}, bf16[4,112,128]{2,1,0:T(8,128)(2,1)S(1)}, u32[]{:S(2)}, u32[]{:S(2)}) %collective-permute-start.2) | collective-permute-done | bytes 114720 | tf_op jit(solution)/shard_map/ppermute | solution.py:713
  26.5 1.5 %collective-permute-done.1 = bf16[4,112,128]{2,1,0:T(8,128)(2,1)S(1)} collective-permute-done((bf16[4,112,128]{2,1,0:T(8,128)(2,1)S(1)}, bf16[4,112,128]{2,1,0:T(8,128)(2,1)S(1)}, u32[]{:S(2)}, u32[]{:S(2)}) %collective-permute-start.1) | collective-permute-done | bytes 114720 | tf_op jit(solution)/shard_map/ppermute | solution.py:709
  28.6 1.6 %collective-permute-start.5 = (bf16[2,4,160,128]{3,2,1,0:T(8,128)(2,1)S(1)}, bf16[2,4,160,128]{3,2,1,0:T(8,128)(2,1)S(1)}, u32[]{:S(2)}, u32[]{:S(2)}) collective-permute-start(bf16[2,4,160,128]{3,2,1,0:T(8,128)(2,1)S(1)} %pad_maximum_fusion.2), channel_id=1, source_target_pairs={{0,4},{4,0},{1,5},{5,1},{2,6},{6,2},{3,7},{7,3},{8,12},{12,8},{9,1... | collective-permute-start | bytes 983048 | tf_op jit(solution)/shard_map/ppermute | solution.py:709
  30.9 10.9 %all_to_all.21.recv_ref = f32[16,4,128]{2,1,0:T(4,128)S(1)} all-to-all(f32[16,4,128]{2,1,0:T(4,128)S(1)} %get-tuple-element.92), channel_id=1, replica_groups=mesh['fz'=4,'fx'=2,'ty'=2,'tc'=2] {'fz','fx','ty'}, dimensions={0} | all-to-all | bytes 65536 | tf_op jit(solution)/shard_map/all_to_all | solution.py:762
  41.9 0.9 %states.1 = (f32[256,512]{1,0:T(8,128)S(1)}, bf16[256,512]{1,0:T(8,128)(2,1)S(1)}, f32[8,512]{1,0:T(8,128)S(1)}, bf16[512,512]{1,0:T(8,128)(2,1)S(1)}) custom-call(f32[16,4,128]{2,1,0:T(4,128)S(1)} %all_to_all.21.recv_ref, f32[4,128]{1,0:T(4,128)S(1)} %get-tuple-element.91.start_ref, f32[256,512]{1,0:T(8,128)S(1)} %get-tuple-element.93.v_ref, ...), custom_call_target="tpu_custom_call" | custom-call | bytes 3240000 | tf_op jit(solution)/shard_map/states/pallas_call | solution.py:692
  43.7 1.5 %collective-permute-done.6.got_ref = f32[128,512]{1,0:T(8,128)S(1)} collective-permute-done((f32[128,512]{1,0:T(8,128)S(1)}, f32[128,512]{1,0:T(8,128)S(1)}, u32[]{:S(2)}, u32[]{:S(2)}) %collective-permute-start.6) | collective-permute-done | bytes 262176 | tf_op jit(solution)/shard_map/ppermute | solution.py:709
  46.2 0.8 sums.1
  46.9 0.7 collective-permute-done.8.got_ref
  47.6 0.8 back.1
  49.1 10.3 %all_to_all.22.recv_ref = f32[16,4,128]{2,1,0:T(4,128)S(1)} all-to-all(f32[16,4,128]{2,1,0:T(4,128)S(1)} %get-tuple-element.113), channel_id=1, replica_groups=mesh['fz'=4,'fx'=2,'ty'=2,'tc'=2] {'fz','fx','ty'}, dimensions={0} | all-to-all | bytes 65536 | tf_op jit(solution)/shard_map/all_to_all | solution.py:796
  59.5 0.8 collective-permute-start.10
  60.3 1.8 %third.1 = (bf16[432,128]{1,0:T(8,128)(2,1)S(1)}, bf16[432,128]{1,0:T(8,128)(2,1)S(1)}, bf16[432,128]{1,0:T(8,128)(2,1)S(1)}, bf16[432,128]{1,0:T(8,128)(2,1)S(1...) custom-call(f32[16,4,128]{2,1,0:T(4,128)S(1)} %all_to_all.22.recv_ref, f32[4,128]{1,0:T(4,128)S(1)} %get-tuple-element.91.start_ref, ...), custom_call_target="tpu_custom_call" | custom-call | bytes 5400000 | tf_op jit(solution)/shard_map/third/pallas_call | solution.py:692
  62.1 1.4 %collective-permute-start.11 = (bf16[432,128]{1,0:T(8,128)(2,1)S(1)}, bf16[432,128]{1,0:T(8,128)(2,1)S(1)}, u32[]{:S(2)}, u32[]{:S(2)}) collective-permute-start(bf16[432,128]{1,0:T(8,128)(2,1)S(1)} %get-tuple-element.128), channel_id=1, source_target_pairs={{0,2},{2,0},{1,3},{3,1},{4,6},{6,4},{5,7},{7,5},{8,10},{10,8},{9,1... | collective-permute-start | bytes 331784 | tf_op jit(solution)/shard_map/ppermute | solution.py:709
  64.1 1.6 %collective-permute-start.13 = (bf16[432,128]{1,0:T(8,128)(2,1)S(1)}, bf16[432,128]{1,0:T(8,128)(2,1)S(1)}, u32[]{:S(2)}, u32[]{:S(2)}) collective-permute-start(bf16[432,128]{1,0:T(8,128)(2,1)S(1)} %get-tuple-element.130), channel_id=1, source_target_pairs={{0,6},{2,4},{4,2},{6,0},{1,7},{3,5},{5,3},{7,1},{8,14},{10,12},{12... | collective-permute-start | bytes 331784 | tf_op jit(solution)/shard_map/ppermute | solution.py:713
  65.7 2.8 %collective-permute-done.11.y_ref = bf16[432,128]{1,0:T(8,128)(2,1)S(1)} collective-permute-done((bf16[432,128]{1,0:T(8,128)(2,1)S(1)}, bf16[432,128]{1,0:T(8,128)(2,1)S(1)}, u32[]{:S(2)}, u32[]{:S(2)}) %collective-permute-start.11) | collective-permute-done | bytes 110624 | tf_op jit(solution)/shard_map/ppermute | solution.py:709
  68.5 1.2 %collective-permute-done.13.xy_ref = bf16[432,128]{1,0:T(8,128)(2,1)S(1)} collective-permute-done((bf16[432,128]{1,0:T(8,128)(2,1)S(1)}, bf16[432,128]{1,0:T(8,128)(2,1)S(1)}, u32[]{:S(2)}, u32[]{:S(2)}) %collective-permute-start.13) | collective-permute-done | bytes 110624 | tf_op jit(solution)/shard_map/ppermute | solution.py:713
  69.8 10.2 %all_to_all.23.got_ref = bf16[4,304,128]{2,1,0:T(8,128)(2,1)S(1)} all-to-all(bf16[4,304,128]{2,1,0:T(8,128)(2,1)S(1)} %plane_add.1), channel_id=1, replica_groups=mesh['fz'=4,'fx'=2,'ty'=2,'tc'=2] {'fz'}, dimensions={0} | all-to-all | bytes 622592 | tf_op jit(solution)/shard_map/all_to_all | solution.py:821
  80.6 0.8 matrices.1
  81.6 0.9 %finish.1 = (f32[128,512]{1,0:T(8,128)}, f32[1,16]{1,0:T(1,128)}, f32[1,512]{1,0:T(1,128)}, f32[1,512]{1,0:T(1,128)}, f32[1,512]{1,0:T(1,128)}, /*index=5*/f32[3...) custom-call(f32[24,128]{1,0:T(8,128)S(1)} %vectors.1.own_ref, f32[24,128]{1,0:T(8,128)S(1)} %collective-permute-done.14.other_ref, ...), custom_call_target="tpu_custom_call" | custom-call | bytes 1440000 | tf_op jit(solution)/shard_map/finish/pallas_call | solution.py:692
  (36 shorter events, 6.4 us)
Async XLA Ops:
  18.0 1.6 %copy-start.1 = (bf16[128,512]{1,0:T(8,128)(2,1)S(1)}, bf16[128,512]{1,0:T(8,128)(2,1)}, u32[]{:S(2)}) copy-start(bf16[128,512]{1,0:T(8,128)(2,1)} %x_ref.3) | copy-start | bytes 393220
  18.0 10.5 %collective-permute-start.3 = (bf16[4,160,128]{2,1,0:T(8,128)(2,1)S(1)}, bf16[4,160,128]{2,1,0:T(8,128)(2,1)S(1)}, u32[]{:S(2)}, u32[]{:S(2)}) collective-permute-start(bf16[4,160,128]{2,1,0:T(8,128)(2,1)S(1)} %slice.9), channel_id=1, source_target_pairs={{0,2},{2,0},{1,3},{3,1},{4,6},{6,4},{5,7},{7,5},{8,10},{10,8},{9,1... | collective-permute-start | bytes 491528 | tf_op jit(solution)/shard_map/ppermute | solution.py:709
  19.6 3.5 %collective-permute-start.4 = (bf16[128,512]{1,0:T(8,128)(2,1)S(1)}, bf16[128,512]{1,0:T(8,128)(2,1)S(1)}, u32[]{:S(2)}, u32[]{:S(2)}) collective-permute-start(bf16[128,512]{1,0:T(8,128)(2,1)S(1)} %copy-done.1), channel_id=1, source_target_pairs={{0,1},{1,0},{2,3},{3,2},{4,5},{5,4},{6,7},{7,6},{8,9},{9,8},{10,11... | collective-permute-start | bytes 393224 | tf_op jit(solution)/shard_map/ppermute | solution.py:709
  19.6 6.8 %collective-permute-start.2 = (bf16[4,112,128]{2,1,0:T(8,128)(2,1)S(1)}, bf16[4,112,128]{2,1,0:T(8,128)(2,1)S(1)}, u32[]{:S(2)}, u32[]{:S(2)}) collective-permute-start(bf16[4,112,128]{2,1,0:T(8,128)(2,1)S(1)} %slice.8), channel_id=1, source_target_pairs={{0,6},{2,4},{4,2},{6,0},{1,7},{3,5},{5,3},{7,1},{8,14},{10,12},{12... | collective-permute-start | bytes 344072 | tf_op jit(solution)/shard_map/ppermute | solution.py:713
  21.3 6.6 %collective-permute-start.1 = (bf16[4,112,128]{2,1,0:T(8,128)(2,1)S(1)}, bf16[4,112,128]{2,1,0:T(8,128)(2,1)S(1)}, u32[]{:S(2)}, u32[]{:S(2)}) collective-permute-start(bf16[4,112,128]{2,1,0:T(8,128)(2,1)S(1)} %slice.8), channel_id=1, source_target_pairs={{0,4},{4,0},{1,5},{5,1},{2,6},{6,2},{3,7},{7,3},{8,12},{12,8},{9,1... | collective-permute-start | bytes 344072 | tf_op jit(solution)/shard_map/ppermute | solution.py:709
  21.9 6.6 %collective-permute-start = (bf16[4,112,128]{2,1,0:T(8,128)(2,1)S(1)}, bf16[4,112,128]{2,1,0:T(8,128)(2,1)S(1)}, u32[]{:S(2)}, u32[]{:S(2)}) collective-permute-start(bf16[4,112,128]{2,1,0:T(8,128)(2,1)S(1)} %slice.8), channel_id=1, source_target_pairs={{0,2},{2,0},{1,3},{3,1},{4,6},{6,4},{5,7},{7,5},{8,10},{10,8},{9,1... | collective-permute-start | bytes 344072 | tf_op jit(solution)/shard_map/ppermute | solution.py:709
  28.6 13.2 %collective-permute-start.5 = (bf16[2,4,160,128]{3,2,1,0:T(8,128)(2,1)S(1)}, bf16[2,4,160,128]{3,2,1,0:T(8,128)(2,1)S(1)}, u32[]{:S(2)}, u32[]{:S(2)}) collective-permute-start(bf16[2,4,160,128]{3,2,1,0:T(8,128)(2,1)S(1)} %pad_maximum_fusion.2), channel_id=1, source_target_pairs={{0,4},{4,0},{1,5},{5,1},{2,6},{6,2},{3,7},{7,3},{8,12},{12,8},{9,1... | collective-permute-start | bytes 983048 | tf_op jit(solution)/shard_map/ppermute | solution.py:709
  42.7 2.5 %collective-permute-start.7 = (bf16[2,2,4,160,128]{4,3,2,1,0:T(8,128)(2,1)S(1)}, bf16[2,2,4,160,128]{4,3,2,1,0:T(8,128)(2,1)S(1)}, u32[]{:S(2)}, u32[]{:S(2)}) collective-permute-start(bf16[2,2,4,160,128]{4,3,2,1,0:T(8,128)(2,1)S(1)} %pad_maximum_fusion.cw_ref), channel_id=1, source_target_pairs={{0,1},{1,0},{2,3},{3,2},{4,5},{5,4},{6,7},{7,6},{8,9},{9,8},{10,11... | collective-permute-start | bytes 1966088 | tf_op jit(solution)/shard_map/ppermute | solution.py:709
  42.8 2.5 %copy-start = (bf16[128,512]{1,0:T(8,128)(2,1)S(1)}, bf16[128,512]{1,0:T(8,128)(2,1)}, u32[]{:S(2)}) copy-start(bf16[128,512]{1,0:T(8,128)(2,1)} %up_ref.3) | copy-start | bytes 393220
  43.2 2.1 %collective-permute-start.6 = (f32[128,512]{1,0:T(8,128)S(1)}, f32[128,512]{1,0:T(8,128)S(1)}, u32[]{:S(2)}, u32[]{:S(2)}) collective-permute-start(f32[128,512]{1,0:T(8,128)S(1)} %get-tuple-element.102), channel_id=1, source_target_pairs={{0,1},{1,0},{2,3},{3,2},{4,5},{5,4},{6,7},{7,6},{8,9},{9,8},{10,11... | collective-permute-start | bytes 786440 | tf_op jit(solution)/shard_map/ppermute | solution.py:709
  46.0 1.7 %collective-permute-start.8 = (bf16[128,1280]{1,0:T(8,128)(2,1)S(1)}, bf16[128,1280]{1,0:T(8,128)(2,1)S(1)}, u32[]{:S(2)}, u32[]{:S(2)}) collective-permute-start(bf16[128,1280]{1,0:T(8,128)(2,1)S(1)} %get-tuple-element.110), channel_id=1, source_target_pairs={{0,1},{1,0},{2,3},{3,2},{4,5},{5,4},{6,7},{7,6},{8,9},{9,8},{10,11... | collective-permute-start | bytes 983048 | tf_op jit(solution)/shard_map/ppermute | solution.py:709
  48.4 11.0 %collective-permute-start.9 = (bf16[2,4,160,128]{3,2,1,0:T(8,128)(2,1)S(1)}, bf16[2,4,160,128]{3,2,1,0:T(8,128)(2,1)S(1)}, u32[]{:S(2)}, u32[]{:S(2)}) collective-permute-start(bf16[2,4,160,128]{3,2,1,0:T(8,128)(2,1)S(1)} %get-tuple-element.114), channel_id=1, source_target_pairs={{0,4},{4,0},{1,5},{5,1},{2,6},{6,2},{3,7},{7,3},{8,12},{12,8},{9,1... | collective-permute-start | bytes 983048 | tf_op jit(solution)/shard_map/ppermute | solution.py:709
  59.5 10.2 %collective-permute-start.10 = (bf16[4,160,128]{2,1,0:T(8,128)(2,1)S(1)}, bf16[4,160,128]{2,1,0:T(8,128)(2,1)S(1)}, u32[]{:S(2)}, u32[]{:S(2)}) collective-permute-start(bf16[4,160,128]{2,1,0:T(8,128)(2,1)S(1)} %get-tuple-element.119), channel_id=1, source_target_pairs={{0,2},{2,0},{1,3},{3,1},{4,6},{6,4},{5,7},{7,5},{8,10},{10,8},{9,1... | collective-permute-start | bytes 491528 | tf_op jit(solution)/shard_map/ppermute | solution.py:709
  62.1 6.4 %collective-permute-start.11 = (bf16[432,128]{1,0:T(8,128)(2,1)S(1)}, bf16[432,128]{1,0:T(8,128)(2,1)S(1)}, u32[]{:S(2)}, u32[]{:S(2)}) collective-permute-start(bf16[432,128]{1,0:T(8,128)(2,1)S(1)} %get-tuple-element.128), channel_id=1, source_target_pairs={{0,2},{2,0},{1,3},{3,1},{4,6},{6,4},{5,7},{7,5},{8,10},{10,8},{9,1... | collective-permute-start | bytes 331784 | tf_op jit(solution)/shard_map/ppermute | solution.py:709
  63.5 5.0 %collective-permute-start.12 = (bf16[432,128]{1,0:T(8,128)(2,1)S(1)}, bf16[432,128]{1,0:T(8,128)(2,1)S(1)}, u32[]{:S(2)}, u32[]{:S(2)}) collective-permute-start(bf16[432,128]{1,0:T(8,128)(2,1)S(1)} %get-tuple-element.129), channel_id=1, source_target_pairs={{0,4},{4,0},{1,5},{5,1},{2,6},{6,2},{3,7},{7,3},{8,12},{12,8},{9,1... | collective-permute-start | bytes 331784 | tf_op jit(solution)/shard_map/ppermute | solution.py:709
  64.1 5.6 %collective-permute-start.13 = (bf16[432,128]{1,0:T(8,128)(2,1)S(1)}, bf16[432,128]{1,0:T(8,128)(2,1)S(1)}, u32[]{:S(2)}, u32[]{:S(2)}) collective-permute-start(bf16[432,128]{1,0:T(8,128)(2,1)S(1)} %get-tuple-element.130), channel_id=1, source_target_pairs={{0,6},{2,4},{4,2},{6,0},{1,7},{3,5},{5,3},{7,1},{8,14},{10,12},{12... | collective-permute-start | bytes 331784 | tf_op jit(solution)/shard_map/ppermute | solution.py:713
  80.1 1.6 %collective-permute-start.15 = (f32[128,512]{1,0:T(8,128)S(1)}, f32[128,512]{1,0:T(8,128)S(1)}, u32[]{:S(2)}, u32[]{:S(2)}) collective-permute-start(f32[128,512]{1,0:T(8,128)S(1)} %get-tuple-element.133), channel_id=1, source_target_pairs={{0,1},{1,0},{2,3},{3,2},{4,5},{5,4},{6,7},{7,6},{8,9},{9,8},{10,11... | collective-permute-start | bytes 786440 | tf_op jit(solution)/shard_map/ppermute | solution.py:709
  80.1 1.5 %collective-permute-start.14 = (f32[24,128]{1,0:T(8,128)S(1)}, f32[24,128]{1,0:T(8,128)S(1)}, u32[]{:S(2)}, u32[]{:S(2)}) collective-permute-start(f32[24,128]{1,0:T(8,128)S(1)} %vectors.1.own_ref), channel_id=1, source_target_pairs={{0,1},{1,0},{2,3},{3,2},{4,5},{5,4},{6,7},{7,6},{8,9},{9,8},{10,11... | collective-permute-start | bytes 36872 | tf_op jit(solution)/shard_map/ppermute | solution.py:709

commit v7 on v6

--- a/solution.py
+++ b/solution.py
@@ -119,8 +119,33 @@
     return [start_ref[n : n + 1, :] for n in range(start_ref.shape[0])]
 
 
+STEPS = 16
+
+
+def in_tiles(ref, rows, value):
+    for c in range(4):
+        ref[c, rows, :] = value[:, 128 * c : 128 * c + 128]
+
+
+def of_tiles(ref, rows):
+    return jnp.concatenate([ref[c, rows, :] for c in range(4)], axis=1)
+
+
+def interleaved(ref, b):
+    groups = [of_tiles(ref, pl.ds((n // STEPS) * 128 + n % STEPS, 8, stride=STEPS)) for n in (b, b + 1)]
+    return jnp.concatenate(groups, axis=0)
+
+
+def in_order(source, target):
+    for g in range(target.shape[0] // 8):
+        h, s, i = g // STEPS, g % STEPS // 2, 8 * (g % 2)
+        target[8 * g : 8 * g + 8, :] = of_tiles(source, pl.ds(128 * h + 8 * i + s, 8, stride=8))
+
+
 def starts_until(offsets, base, rows):
-    at = (lax.broadcasted_iota(jnp.int32, (rows, 128), 0) + base).astype(F32)
+    row = lax.broadcasted_iota(jnp.int32, (rows, 128), 0)
+    token = (row & ~127) + (row & 7) * STEPS + ((row & 127) >> 3)
+    at = (token + base).astype(F32)
     count = jnp.zeros((rows, 128), F32)
     for off in offsets:
         count = count + jnp.where((at >= off) & (off >= at[0:1]), 1.0, 0.0)
@@ -156,7 +181,7 @@
 
 
 def pack_kernel(*refs):
-    *inputs, out_ref, square, four, glu_ref, halves, params, lengths, sems = refs
+    *inputs, out_ref, start_ref, square, four, glu_ref, halves, params, lengths, sems = refs
     seq_hbm, matrices, glu_hbm, features, states = inputs[0], inputs[1:5], inputs[5], inputs[6:10], inputs[10:13]
     units = pl.multiple_of(tensor_pos() * 128, 128)
     pairs = [(ref, four.at[k]) for k, ref in enumerate(matrices)]
@@ -179,13 +204,10 @@
             part = value.astype(BF16).astype(F32)
             value = value - part
             vec.append(part)
-    lane = lane_iota((1, 128))
-    upper, lower, total = jnp.zeros((1, 128), jnp.int32), jnp.zeros((1, 128), jnp.int32), 0
+    total = 0
     for n in range(lengths.shape[0]):
-        upper = jnp.where(lane == n, total >> 8, upper)
-        lower = jnp.where(lane == n, total & 255, lower)
+        start_ref[n : n + 1, :] = jnp.full((1, 128), total, jnp.int32).astype(F32)
         total = total + lengths[n]
-    vec += [upper.astype(F32), lower.astype(F32)]
     vec.append(jnp.zeros((16 - len(vec), 128), F32))
     vec = jnp.concatenate(vec, axis=0).astype(BF16)
     pieces = []
@@ -218,30 +240,33 @@
         scratch[pl.ds(2 + y, 1), :] = im_rows[m]
 
 
-def standardize_kernel(x_ref, other_ref, xhat_ref, inv_ref):
+def standardize_kernel(x_ref, other_ref, up_ref, start_ref, xhat_ref, up_out_ref, inv_ref, count_ref, tiles, inverses):
     rows, width = x_ref.shape
+    in_tiles(tiles, slice(0, rows), up_ref[...].astype(F32))
+    for b in range(0, rows // 8, 2):
+        up_out_ref[8 * b : 8 * b + 16, :] = interleaved(tiles, b)
     for ref, where, own in ((x_ref, own_rows(rows), True), (other_ref, other_rows(rows), False)):
         x = ref[...].astype(F32)
         centered = x - jnp.sum(x, axis=1, keepdims=True) / width
         inverse = lax.rsqrt(jnp.sum(centered * centered, axis=1, keepdims=True) / width + 1e-05)
-        xhat_ref[where, :] = centered * inverse
+        in_tiles(tiles, where, centered * inverse)
         if own:
-            inv_ref[...] = jnp.broadcast_to(inverse, (rows, 128))
-
-
-def norm_kernel(xhat_ref, g_ref, normed_ref, feat_ref, start_ref):
+            inverses[...] = jnp.broadcast_to(inverse, (rows, 128))
+    for b in range(0, 2 * rows // 8, 2):
+        xhat_ref[8 * b : 8 * b + 16, :] = interleaved(tiles, b)
+    for b in range(rows // 8):
+        inv_ref[8 * b : 8 * b + 8, :] = inverses[pl.ds(b, 8, stride=STEPS), :]
+    count_ref[...] = starts_until(offsets_of(start_ref), pair_pos() * 2 * rows, 2 * rows)
+
+
+def norm_kernel(xhat_ref, g_ref, normed_ref, feat_ref):
     scale, bias = feature_rows(g_ref, VEC)
     feat_ref[0:1] = scale
     feat_ref[1:2], feat_ref[2:3] = feature_rows(g_ref, VEC + 1)
-    normed = (xhat_ref[...] * scale + bias).astype(BF16)
-    normed_ref[...] = normed
-    upper, lower = (piece(g_ref, 0, 0, VEC + 11 + k, 1).astype(F32) for k in range(2))
-    starts = upper * 256.0 + lower
-    for n in range(start_ref.shape[0]):
-        start_ref[n : n + 1, :] = jnp.broadcast_to(starts[:, n : n + 1], (1, 128))
-
-
-def first_kernel(pairs, normed_ref, start_ref, g_ref, b_ref, v_ref, lane_ref, row_ref, send_ref, scratch):
+    normed_ref[...] = (xhat_ref[...] * scale + bias).astype(BF16)
+
+
+def first_kernel(pairs, normed_ref, count_ref, g_ref, b_ref, v_ref, lane_ref, row_ref, send_ref, scratch):
     rows = normed_ref.shape[0]
     natural(lambda m, z, x: g_ref[lax.axis_index("fx") ^ x, m, z, 0:96, :], b_ref)
     v_ref[...] = dot(normed_ref[...], b_ref[...], NT)
@@ -259,82 +284,95 @@
         for m in range(2):
             lane_ref[k : k + 1, 128 * m : 128 * m + 128] = value[m : m + 1]
 
-    count = starts_until(offsets_of(start_ref), pair_pos() * rows, rows)
+    count = count_ref[...]
     open_tail = jnp.where(count == count[rows - 1 : rows], 1.0, 0.0)
     last = ([], [])
     for m in range(2):
-        eight, tail = eighth_powers((abar_re[m : m + 1], abar_im[m : m + 1]), lambda sub: 7 - sub)
+        a = (all_rows(abar_re[m : m + 1]), all_rows(abar_im[m : m + 1]))
         b = (coef_re[m : m + 1], coef_im[m : m + 1])
-        acc = (jnp.zeros((8, 128), F32), jnp.zeros((8, 128), F32))
-        for blk in range(rows // 8):
-            here = slice(8 * blk, 8 * blk + 8)
-            drive = cmul(b, (v_ref[here, part_lanes(0, m)], v_ref[here, part_lanes(1, m)]))
-            moved = cmul(eight, acc)
-            acc = (moved[0] + drive[0] * open_tail[here], moved[1] + drive[1] * open_tail[here])
-        total = cmul(tail, acc)
-        last[0].append(column_sum(total[0]))
-        last[1].append(column_sum(total[1]))
+        sixteen = squared(a, 4)
+        tile = tile_powers(sixteen, lambda sub: 7 - sub)
+        halves = []
+        for h in range(2):
+            acc = (jnp.zeros((8, 128), F32), jnp.zeros((8, 128), F32))
+            for blk in range(STEPS * h, STEPS * h + STEPS):
+                here = slice(8 * blk, 8 * blk + 8)
+                drive = cmul(b, (v_ref[here, part_lanes(0, m)], v_ref[here, part_lanes(1, m)]))
+                moved = cmul(a, acc)
+                acc = (moved[0] + drive[0] * open_tail[here], moved[1] + drive[1] * open_tail[here])
+            total = cmul(tile, acc)
+            halves.append((column_sum(total[0]), column_sum(total[1])))
+        moved = cmul(squared((sixteen[0][:1], sixteen[1][:1]), 3), halves[0])
+        last[0].append(moved[0] + halves[1][0])
+        last[1].append(moved[1] + halves[1][1])
     carry_block(last[0], last[1], scratch)
     packet = scratch[...]
     for d in range(pairs):
         send_ref[d] = packet[0:4]
 
 
-def eighth_powers(a, exponent_of):
+def squared(a, times):
+    for _ in range(times):
+        a = cmul(a, a)
+    return a
+
+
+def tile_powers(a, exponent_of):
     exponent = exponent_of(lax.broadcasted_iota(jnp.int32, (8, 128), 0))
-    a = (jnp.broadcast_to(a[0], (8, 128)), jnp.broadcast_to(a[1], (8, 128)))
     tile = (jnp.ones((8, 128), F32), jnp.zeros((8, 128), F32))
     for bit in range(4):
-        if bit == 3:
-            eight = a
         taken = (exponent & (1 << bit)) != 0
         more = cmul(tile, a)
         tile = (jnp.where(taken, more[0], tile[0]), jnp.where(taken, more[1], tile[1]))
         a = cmul(a, a)
-    return eight, tile
+    return tile
 
 
 def all_rows(row):
     return jnp.broadcast_to(row, (8, 128))
 
 
+def plus(value, link, more):
+    return value[0] + jnp.where(link, more[0], 0.0), value[1] + jnp.where(link, more[1], 0.0)
+
+
 def scan(read, powers, carry, count, reverse, emit):
-    groups = count.shape[0] // 8
     sub = lax.broadcasted_iota(jnp.int32, (8, 128), 0)
-    steps, eights, tiles = [], [], []
+    order = range(STEPS - 1, -1, -1) if reverse else range(STEPS)
+    end = 0 if reverse else 7
+    back = lambda k: 8 - k if reverse else k
+    carry = [(all_rows(c[0]), all_rows(c[1])) for c in carry]
+    entries, ends, upto = [], [], []
     for a in powers:
-        squared = cmul(a, a)
-        steps.append((a, squared, cmul(squared, squared)))
-        eight, tile = eighth_powers(a, (lambda sub: 8 - sub) if reverse else (lambda sub: sub + 1))
-        eights.append(eight)
-        tiles.append(tile)
-    carry = [(all_rows(c[0]), all_rows(c[1])) for c in carry]
-    edge = 0 if reverse else 7
-    seen = all_rows(count[8 * groups - 1 :]) if reverse else jnp.zeros((8, 128), F32)
-    for b in range(groups - 1, -1, -1) if reverse else range(groups):
-        here = count[8 * b : 8 * b + 8]
-        links = []
-        for k in (1, 2, 4):
-            other = pltpu.roll(here, 8 - k if reverse else k, 0)
-            links.append(((sub < 8 - k) if reverse else (sub >= k)) & (other == here))
-        came = here == seen
-        last = all_rows(here[edge : edge + 1])
-        through = last == seen
-        seen = last
+        a = (all_rows(a[0]), all_rows(a[1]))
+        power = [a]
+        for _ in range(STEPS - 1):
+            power.append(cmul(power[-1], a))
+        upto.append(power)
+        ends.append((power[-1], squared(power[-1], 1), squared(power[-1], 2)))
+        entries.append(tile_powers(power[-1], (lambda sub: 8 - sub) if reverse else (lambda sub: sub + 1)))
+    seen = jnp.zeros((8, 128), F32)
+    for h in (1, 0) if reverse else (0, 1):
+        counts = [count[8 * b : 8 * b + 8] for b in range(STEPS * h, STEPS * h + STEPS)]
+        last = counts[order[-1]]
+        near = jnp.where(sub == 7 - end, seen, pltpu.roll(last, back(1), 0))
         for m in range(2):
-            value = read(b, m)
-            for k, link, a in zip((1, 2, 4), links, steps[m]):
-                shift = 8 - k if reverse else k
-                more = cmul(a, (pltpu.roll(value[0], shift, 0), pltpu.roll(value[1], shift, 0)))
-                value = (value[0] + jnp.where(link, more[0], 0.0), value[1] + jnp.where(link, more[1], 0.0))
-            more = cmul(tiles[m], carry[m])
-            done = (value[0] + jnp.where(came, more[0], 0.0), value[1] + jnp.where(came, more[1], 0.0))
-            more = cmul(eights[m], carry[m])
-            carry[m] = (
-                all_rows(value[0][edge : edge + 1]) + jnp.where(through, more[0], 0.0),
-                all_rows(value[1][edge : edge + 1]) + jnp.where(through, more[1], 0.0),
-            )
-            emit(b, m, done)
+            values, before = {}, None
+            for i in order:
+                value = read(STEPS * h + i, m)
+                if before is not None:
+                    value = plus(value, counts[i] == counts[before], cmul(upto[m][0], values[before]))
+                values[i], before = value, i
+            tip = values[before]
+            for k, power in zip((1, 2, 4), ends[m]):
+                link = ((sub < 8 - k) if reverse else (sub >= k)) & (pltpu.roll(last, back(k), 0) == last)
+                tip = plus(tip, link, cmul(power, (pltpu.roll(tip[0], back(k), 0), pltpu.roll(tip[1], back(k), 0))))
+            tip = plus(tip, last == seen, cmul(entries[m], carry[m]))
+            comes = tuple(jnp.where(sub == 7 - end, carry[m][p], pltpu.roll(tip[p], back(1), 0)) for p in range(2))
+            for n, i in enumerate(order):
+                emit(STEPS * h + i, m, plus(values[i], counts[i] == near, cmul(upto[m][n], comes)))
+            carry[m] = (all_rows(tip[0][end : end + 1]), all_rows(tip[1][end : end + 1]))
+        seen = all_rows(last[end : end + 1])
 
 
 def carried(recv_ref, row_ref, offsets, rows, reverse, scratch):
@@ -345,15 +383,29 @@
         pim = -pim
     place = pair_pos()
 
-    def turn(k, state):
-        j = pairs - 1 - k if reverse else k
-        link = no_start(offsets, j * rows, rows)
-        got = recv_ref[j]
-        new = cmul((pre * link, pim * link), state)
-        return new[0] + got[0:2], new[1] + got[2:4]
-
     zero = jnp.zeros((2, 128), F32)
-    out = lax.fori_loop(0, pairs - 1 - place if reverse else place, turn, (zero, zero))
+    if pairs <= 32:
+        first = lax.broadcasted_iota(jnp.int32, (pairs, 128), 0).astype(F32) * rows
+        links = jnp.ones((pairs, 128), F32)
+        for off in offsets:
+            links = jnp.where((off >= first) & (off < first + rows), 0.0, links)
+        out = (zero, zero)
+        for j in range(pairs - 1, 0, -1) if reverse else range(pairs - 1):
+            link = links[j : j + 1]
+            got = recv_ref[j]
+            new = cmul((pre * link, pim * link), out)
+            reached = (j > place) if reverse else (j < place)
+            out = (jnp.where(reached, new[0] + got[0:2], out[0]), jnp.where(reached, new[1] + got[2:4], out[1]))
+    else:
+
+        def turn(k, state):
+            j = pairs - 1 - k if reverse else k
+            link = no_start(offsets, j * rows, rows)
+            got = recv_ref[j]
+            new = cmul((pre * link, pim * link), state)
+            return new[0] + got[0:2], new[1] + got[2:4]
+
+        out = lax.fori_loop(0, pairs - 1 - place if reverse else place, turn, (zero, zero))
     scratch[0:2, :] = out[0]
     scratch[2:4, :] = out[1]
     own = [lax.axis_index("ty") ^ m for m in range(2)]
@@ -365,12 +417,11 @@
 
 
 def states_kernel(
-    recv_ref, start_ref, v_ref, lane_ref, row_ref, cw_ref, state_ref, twice_ref, enter_ref, c_ref, scratch
+    recv_ref, start_ref, count_ref, v_ref, lane_ref, row_ref, cw_ref, state_ref, twice_ref, enter_ref, c_ref, scratch
 ):
     rows = v_ref.shape[0]
-    offsets = offsets_of(start_ref)
-    count = starts_until(offsets, pair_pos() * rows, rows)
-    enter = carried(recv_ref, row_ref, offsets, rows, False, scratch)
+    count = count_ref[...]
+    enter = carried(recv_ref, row_ref, offsets_of(start_ref), rows, False, scratch)
     for part in range(2):
         for m in range(2):
             enter_ref[0:1, part_lanes(part, m)] = enter[part][m]
@@ -418,7 +469,7 @@
     logit = dot(act_low, w_gate, NN) + gate_bias
     gate = 1.0 / (1.0 + jnp.exp(-logit))
     branch_ref[...] = (act * gate).astype(BF16)
-    up = up_ref[...].astype(F32)
+    up = up_ref[...]
     dlogit = (up * act * gate * (1.0 - gate)).astype(BF16)
     dlogit_ref[...] = dlogit
     all_ref[...] = dlogit
@@ -434,17 +485,19 @@
             ref[:, 2 * width + 128 * m : 2 * width + 128 * m + 128] = all_ref[:, lanes]
 
 
-def sums_kernel(x_ref, branch_ref, normed_ref, dmixed_ref, dlogit_ref, out_ref, part_ref):
+def sums_kernel(x_ref, branch_ref, normed_ref, dmixed_ref, dlogit_ref, out_ref, part_ref, tiles, ordered):
     x = x_ref[...].astype(F32)
     branch = branch_ref[...].astype(F32)
-    out_ref[...] = (x + branch).astype(BF16)
+    in_tiles(tiles, slice(None), branch)
+    in_order(tiles, ordered)
+    out_ref[...] = (x + ordered[...]).astype(BF16)
     skip = column_sum(dmixed_ref[...] * normed_ref[own_rows(x_ref.shape[0]), :].astype(F32))
     for k, value in enumerate((skip, column_sum(dlogit_ref[...].astype(F32)), column_sum(x * x), column_sum(branch * branch))):
         part_ref[k : k + 1, :] = value
 
 
 def back_kernel(
-    pairs, mine_ref, got_ref, twice_ref, start_ref, lane_ref, c_ref,
+    pairs, mine_ref, got_ref, twice_ref, count_ref, lane_ref, c_ref,
     dstate_ref, send_ref, stay_ref, leave_ref, dy_ref, dgate_ref, scratch, all_ref,
 ):
     rows, width = dy_ref.shape
@@ -454,23 +507,30 @@
     d_state = dot(dy_ref[...], c_ref[...], NT)
     dstate_ref[:, 0:256] = d_state[:, 0:256] * 2.0
     dstate_ref[:, 256:512] = d_state[:, 256:512] * -2.0
-    count = starts_until(offsets_of(start_ref), pair_pos() * rows, rows)
+    count = count_ref[...]
     head = jnp.where(count == 0.0, 1.0, 0.0)
     first = ([], [])
     for m in range(2):
         lanes = slice(128 * m, 128 * m + 128)
-        eight, tail = eighth_powers((lane_ref[0:1, lanes], -lane_ref[1:2, lanes]), lambda sub: sub + 1)
-        acc = (jnp.zeros((8, 128), F32), jnp.zeros((8, 128), F32))
-        for blk in range(rows // 8 - 1, -1, -1):
-            here = slice(8 * blk, 8 * blk + 8)
-            moved = cmul(eight, acc)
-            acc = (
-                moved[0] + dstate_ref[here, part_lanes(0, m)] * head[here],
-                moved[1] + dstate_ref[here, part_lanes(1, m)] * head[here],
-            )
-        total = cmul(tail, acc)
-        first[0].append(column_sum(total[0]))
-        first[1].append(column_sum(total[1]))
+        a = (all_rows(lane_ref[0:1, lanes]), all_rows(-lane_ref[1:2, lanes]))
+        sixteen = squared(a, 4)
+        tile = tile_powers(sixteen, lambda sub: sub)
+        halves = []
+        for h in range(2):
+            acc = (jnp.zeros((8, 128), F32), jnp.zeros((8, 128), F32))
+            for blk in range(STEPS * h + STEPS - 1, STEPS * h - 1, -1):
+                here = slice(8 * blk, 8 * blk + 8)
+                moved = cmul(a, acc)
+                acc = (
+                    moved[0] + dstate_ref[here, part_lanes(0, m)] * head[here],
+                    moved[1] + dstate_ref[here, part_lanes(1, m)] * head[here],
+                )
+            total = cmul(tile, acc)
+            halves.append((column_sum(total[0]), column_sum(total[1])))
+        moved = cmul(squared((sixteen[0][:1], sixteen[1][:1]), 3), halves[1])
+        total = cmul((a[0][:1], a[1][:1]), (moved[0] + halves[0][0], moved[1] + halves[0][1]))
+        first[0].append(total[0])
+        first[1].append(total[1])
     scratch[...] = jnp.zeros((8, 128), F32)
     carry_block(first[0], first[1], scratch)
     packet = scratch[...]
@@ -502,14 +562,13 @@
 
 
 def third_kernel(
-    recv_ref, start_ref, normed_ref, xhat_ref, v_ref, lane_ref, row_ref, feat_ref, state_ref, dstate_ref, enter_ref, dmixed_ref,
+    recv_ref, start_ref, count_ref, normed_ref, xhat_ref, v_ref, lane_ref, row_ref, feat_ref, state_ref, dstate_ref, enter_ref, dmixed_ref,
     part_ref, b_ref, stay_ref, y_ref, x_ref, xy_ref, dn_ref, dnaway_ref, scratch, dv_ref, all_ref, vec_ref,
 ):
-    rows, width = xhat_ref.shape
+    rows, width = normed_ref.shape
     half = rows // 2
-    offsets = offsets_of(start_ref)
-    count = starts_until(offsets, pair_pos() * rows, rows)
-    later = carried(recv_ref, row_ref, offsets, rows, True, scratch)
+    count = count_ref[...]
+    later = carried(recv_ref, row_ref, offsets_of(start_ref), rows, True, scratch)
     sub = lax.broadcasted_iota(jnp.int32, (8, 128), 0)
     none = jnp.zeros((1, 128), F32)
     totals = [[jnp.zeros((8, 128), F32) for _ in range(4)] for _ in range(2)]
@@ -523,13 +582,18 @@
 
     def emit(b, m, adj):
         here, lanes = slice(8 * b, 8 * b + 8), slice(128 * m, 128 * m + 128)
-        seen = count[8 * b - 1 : 8 * b] if b else none
-        keep = count[here] == jnp.where(sub == 0, seen, pltpu.roll(count[here], 1, 0))
-        prev = []
-        for part in range(2):
-            edge = state_ref[8 * b - 1 : 8 * b, part_lanes(part, m)] if b else enter_ref[0:1, part_lanes(part, m)]
-            moved = jnp.where(sub == 0, edge, pltpu.roll(state_ref[here, part_lanes(part, m)], 1, 0))
-            prev.append(jnp.where(keep, moved, 0.0))
+        h, i = b // STEPS, b % STEPS
+        if i:
+            same = count[here] == count[8 * b - 8 : 8 * b]
+            moved = [state_ref[8 * b - 8 : 8 * b, part_lanes(part, m)] for part in range(2)]
+        else:
+            end = slice(8 * (b + STEPS - 1), 8 * (b + STEPS))
+            same = count[here] == jnp.where(sub == 0, count[127:128] if h else none, pltpu.roll(count[end], 1, 0))
+            moved = []
+            for part in range(2):
+                edge = state_ref[127:128, part_lanes(part, m)] if h else enter_ref[0:1, part_lanes(part, m)]
+                moved.append(jnp.where(sub == 0, edge, pltpu.roll(state_ref[end, part_lanes(part, m)], 1, 0)))
+        prev = [jnp.where(same, part, 0.0) for part in moved]
         v = (v_ref[here, part_lanes(0, m)], v_ref[here, part_lanes(1, m)])
         for k, (p, q) in enumerate((prev, v)):
             totals[m][2 * k] = totals[m][2 * k] + (adj[0] * p + adj[1] * q)
@@ -552,12 +616,12 @@
             near[here, :] = jnp.where(flip, odd, even).astype(BF16)
             side[here, :] = jnp.where(flip, even, odd).astype(BF16)
     all_ref[...] = dot(dv, b_ref[...], NN)
-    dnaway_ref[...] = all_ref[other_rows(half), :]
+    away = all_ref[other_rows(half), :]
+    dnaway_ref[...] = away
     own = all_ref[own_rows(half), :] + dmixed_ref[...] * feat_ref[1:2]
     dn_ref[...] = own
-    all_ref[own_rows(half), :] = own
-    d_normed = all_ref[...]
-    vector = [column_sum(d_normed * xhat_ref[...]), column_sum(d_normed), part_ref[0:1, :], part_ref[1:2, :]]
+    to_scale = column_sum(own * xhat_ref[own_rows(half), :]) + column_sum(away * xhat_ref[other_rows(half), :])
+    vector = [to_scale, column_sum(own) + column_sum(away), part_ref[0:1, :], part_ref[1:2, :]]
     for k, value in enumerate(vector):
         for c in range(4):
             vec_ref[4 * k + c : 4 * k + c + 1, :] = value[:, 128 * c : 128 * c + 128]
@@ -589,13 +653,15 @@
         ref[384:432, :] = vec
 
 
-def input_grad(dn_ref, got_ref, up_ref, xhat_ref, inv_ref, feat_ref, gin_ref):
+def input_grad(dn_ref, got_ref, up_ref, xhat_ref, inv_ref, feat_ref, gin_ref, tiles):
     rows, width = up_ref.shape
     xhat = xhat_ref[own_rows(rows), :]
     d_xhat = (dn_ref[...] + got_ref[...]) * feat_ref[0:1]
     mean = jnp.sum(d_xhat, axis=1, keepdims=True) / width
     mean_hat = jnp.sum(d_xhat * xhat, axis=1, keepdims=True) / width
-    gin_ref[...] = up_ref[...].astype(F32) + inv_ref[:, 0:1] * (d_xhat - mean - xhat * mean_hat)
+    in_tiles(tiles, slice(None), inv_ref[:, 0:1] * (d_xhat - mean - xhat * mean_hat))
+    in_order(tiles, gin_ref)
+    gin_ref[...] = gin_ref[...] + up_ref[...].astype(F32)
 
 
 def input_grad_kernel(*refs):
@@ -658,9 +724,9 @@
 
 def finish_kernel(
     count_all, own_ref, other_ref, dn_ref, got_ref, up_ref, xhat_ref, inv_ref, feat_ref,
-    gin_ref, gbias_ref, scale_ref, bias_ref, skip_ref, decay_ref, lam_ref, step_ref, rms_ref, vec_ref,
+    gin_ref, gbias_ref, scale_ref, bias_ref, skip_ref, decay_ref, lam_ref, step_ref, rms_ref, vec_ref, tiles,
 ):
-    input_grad(dn_ref, got_ref, up_ref, xhat_ref, inv_ref, feat_ref, gin_ref)
+    input_grad(dn_ref, got_ref, up_ref, xhat_ref, inv_ref, feat_ref, gin_ref, tiles)
     own, other = own_ref[...], other_ref[...]
     vec = own + other
     vec_ref[...] = vec
@@ -713,6 +779,16 @@
     return lax.ppermute(value, ("fx", "ty"), [(n, 3 - n) for n in range(4)])
 
 
+def standardized(layer_in, grad_out, starts):
+    rows, width = layer_in.shape
+    return call(
+        standardize_kernel,
+        (sds((2 * rows, width)), sds((rows, width)), sds((rows, 128)), sds((2 * rows, 128))),
+        (layer_in, swap(layer_in, "tc"), grad_out, starts),
+        [pltpu.VMEM((4, 2 * rows, 128), F32), pltpu.VMEM((rows, 128), F32)],
+    )
+
+
 def on_device(
     layer_in, grad_out, ln_scale, ln_bias, decay_rate, lam_im, log_dt, in_re, in_im, out_re, out_im, skip, glu_weight, glu_bias, seq_lengths
 ):
@@ -724,9 +800,9 @@
     same_core = (*FSDP, "ty")
     if fast:
         row = lambda v: v.reshape(1, -1)
-        sent = call(
+        sent, starts = call(
             pack_kernel,
-            sds((GROUPS // 2, 272, 128), BF16),
+            (sds((GROUPS // 2, 272, 128), BF16), sds((seq_lengths.shape[0], 128))),
             (seq_lengths, in_re.T, in_im.T, out_re.T, out_im.T, glu_weight.T, row(ln_scale), row(ln_bias), row(skip), row(glu_bias),
              row(decay_rate), row(lam_im), row(log_dt)),
             [pltpu.VMEM((128, 128), F32), pltpu.VMEM((4, 64, 96), BF16), pltpu.VMEM((64, 128), BF16), pltpu.VMEM((4, 1, 64), BF16),
@@ -737,26 +813,23 @@
         mine = lax.all_to_all(sent, "fz", 0, 0, tiled=True)
         own_b, own_cw = lax.optimization_barrier((mine[:, :112], mine[:, 112:]))
         plane_b = [own_b, swap(own_b, "ty"), swap(own_b, "fx"), across(own_b)]
-        xhat, inverse = call(standardize_kernel, (sds((pair, width)), sds((rows, 128))), (layer_in, swap(layer_in, "tc")))
+        xhat, up, inverse, count = standardized(layer_in, grad_out, starts)
         plane_b, side_cw, xhat = lax.optimization_barrier((plane_b, swap(own_cw, "ty"), xhat))
         side_cw = jnp.stack([own_cw, side_cw])
         far_cw = swap(side_cw, "fx")
         g = jnp.stack(plane_b).reshape(2, 2, GROUPS // 2, 112, 128)
     else:
-        xhat, inverse = call(standardize_kernel, (sds((pair, width)), sds((rows, 128))), (layer_in, swap(layer_in, "tc")))
+        starts = jnp.broadcast_to((jnp.cumsum(seq_lengths) - seq_lengths).astype(F32)[:, None], (seq_lengths.shape[0], 128))
+        xhat, up, inverse, count = standardized(layer_in, grad_out, starts)
         g, cw, other_cw = gathered(
-            ln_scale, ln_bias, decay_rate, lam_im, log_dt, in_re, in_im, out_re, out_im, skip, glu_weight, glu_bias, seq_lengths
+            ln_scale, ln_bias, decay_rate, lam_im, log_dt, in_re, in_im, out_re, out_im, skip, glu_weight, glu_bias
         )
 
-    normed, feat, starts = call(
-        norm_kernel,
-        (sds((pair, width), BF16), sds((8, width)), sds((seq_lengths.shape[0], 128))),
-        (xhat, g),
-    )
+    normed, feat = call(norm_kernel, (sds((pair, width), BF16), sds((8, width))), (xhat, g))
     b_all, v, lane, row_prm, carry = call(
         functools.partial(first_kernel, pairs),
         (sds((512, width), BF16), sds((pair, 512)), sds((8, 256)), sds((8, 8, 128)), sds((pairs, 4, 128))),
-        (normed, starts, g),
+        (normed, count, g),
         [pltpu.VMEM((8, 128), F32)],
     )
     came = lax.all_to_all(carry, same_core, 0, 0, tiled=True)
@@ -765,7 +838,7 @@
     state, twice, enter, c_all = call(
         states_kernel,
         (sds((pair, 512)), sds((pair, 512), BF16), sds((8, 512)), sds((512, width), BF16)),
-        (came, starts, v, lane, row_prm, cw),
+        (came, starts, count, v, lane, row_prm, cw),
         [pltpu.VMEM((8, 128), F32)],
     )
     if fast:
@@ -776,18 +849,21 @@
     branch, d_mixed, dlogit, kept, away = call(
         second_kernel,
         (sds((rows, width), BF16), sds((rows, width)), sds((rows, width), BF16), *[sds((rows, 2 * width + 256), BF16)] * 2),
-        (own, swap(away, "tc"), grad_out, normed, feat, cw, other_cw),
+        (own, swap(away, "tc"), up, normed, feat, cw, other_cw),
         [pltpu.VMEM((width, width), BF16), pltpu.VMEM((rows, width), BF16)],
     )
     got = swap(away, "tc")
     layer_out, part = call(
-        sums_kernel, (sds((rows, width), BF16), sds((8, width))), (layer_in, branch, normed, d_mixed, dlogit)
+        sums_kernel,
+        (sds((rows, width), BF16), sds((8, width))),
+        (layer_in, branch, normed, d_mixed, dlogit),
+        [pltpu.VMEM((4, rows, 128), F32), pltpu.VMEM((rows, width), F32)],
     )
     got, part = lax.optimization_barrier((got, part))
     d_state, carry, stay_cw, leave_cw = call(
         functools.partial(back_kernel, pairs),
         (sds((pair, 512)), sds((pairs, 4, 128)), *[sds((2, GROUPS // 2, 160, 128), BF16)] * 2),
-        (kept, got, twice, starts, lane, c_all),
+        (kept, got, twice, count, lane, c_all),
         [pltpu.VMEM((pair, width), BF16), pltpu.VMEM((width, 256), BF16), pltpu.VMEM((8, 128), F32),
          pltpu.VMEM((2, 2, GROUPS // 2, 160, 128), BF16)],
     )
@@ -802,12 +878,15 @@
     stay_b, y_b, x_b, xy_b, d_normed, away = call(
         third_kernel,
         (*[sds((432, 128), BF16)] * 4, sds((rows, width)), sds((rows, width))),
-        (came, starts, normed, xhat, v, lane, row_prm, feat, state, d_state, enter, d_mixed, part, b_all),
+        (came, starts, count, normed, xhat, v, lane, row_prm, feat, state, d_state, enter, d_mixed, part, b_all),
         [pltpu.VMEM((8, 128), F32), pltpu.VMEM((pair, 512), BF16), pltpu.VMEM((pair, width), F32), pltpu.VMEM((24, 128), F32)],
     )
     if not fast:
         grad_in = call(
-            input_grad_kernel, sds((rows, width)), (d_normed, swap(away, "tc"), grad_out, xhat, inverse, feat)
+            input_grad_kernel,
+            sds((rows, width)),
+            (d_normed, swap(away, "tc"), grad_out, xhat, inverse, feat),
+            [pltpu.VMEM((4, rows, 128), F32)],
         )
         return reduced(layer_out, grad_in, stay_cw, leave_cw, (stay_b, y_b, x_b, xy_b), count_all, fsdp, width)
     xy_b = across(xy_b)
@@ -829,7 +908,7 @@
         functools.partial(finish_kernel, count_all),
         (sds((rows, width)), sds((1, 16)), *[sds((1, 512))] * 3, *[sds((384,))] * 3, sds((1, 2))),
         (vec, other, d_normed, away, grad_out, xhat, inverse, feat),
-        [pltpu.VMEM((24, 128), F32)],
+        [pltpu.VMEM((24, 128), F32), pltpu.VMEM((4, rows, 128), F32)],
     )
     flat = lambda value: value.reshape(-1)
     return (
@@ -838,7 +917,7 @@
     )
 
 
-def gathered(ln_scale, ln_bias, decay_rate, lam_im, log_dt, in_re, in_im, out_re, out_im, skip, glu_weight, glu_bias, seq_lengths):
+def gathered(ln_scale, ln_bias, decay_rate, lam_im, log_dt, in_re, in_im, out_re, out_im, skip, glu_weight, glu_bias):
     tens = tensor_pos()
     full = lambda value, axis: lax.all_gather(value, FSDP, axis=axis, tiled=True)
 
@@ -854,11 +933,7 @@
             piece = lax.reduce_precision(value, 8, 7)
             value = value - piece
             vectors.append(jnp.broadcast_to(piece.astype(BF16)[None, None], (GROUPS, 1, 128)))
-    starts = jnp.cumsum(seq_lengths) - seq_lengths
-    for value in (starts >> 8, starts & 255):
-        value = jnp.pad(value, (0, 128 - value.shape[0])).astype(BF16)
-        vectors.append(jnp.broadcast_to(value[None, None], (GROUPS, 1, 128)))
-    vectors.append(jnp.zeros((GROUPS, 3, 128), BF16))
+    vectors.append(jnp.zeros((GROUPS, 5, 128), BF16))
     packet = jnp.concatenate(
         [pair(full(in_re, 1), full(in_im, 1)), *vectors, pair(full(out_re, 1), full(out_im, 1)), gate],
         axis=1,

time: 82.9 us -> 82.4 us (level)
    ppermute x14, waiting for transfers between devices: 7.39 us -> 9.14 us  [swap(): return lax.ppermute(value, axis, [(0, 1), (1, 0)])]
    ppermute x2, waiting for transfers between devices: 4.33 us -> 2.66 us  [across(): return lax.ppermute(value, ('fx', 'ty'), [(n, 3 - n) for n in range(4)])]
  transfers between devices with their start and end apart: 16 -> 16, of which waited for: 8 -> 7; matrix products, arithmetic and copies ran while one was open for 0% -> 0% of each run, Pallas kernels for 6% -> 5%
where the time goes in v7:
time: 82.4 us; the launch traced here: 82 us
  blocking collectives  46.8 us (57%)
  starting transfers between devices  13.1 us (16%)
  waiting for transfers between devices  11.8 us (14%)
  Pallas kernels  9.28 us (11%)
    all_to_all x2, blocking collectives, on_device(): came = lax.all_to_all(carry, same_core, 0, 0, tiled=True)  21 us
    all_to_all x1, blocking collectives, on_device(): mine = lax.all_to_all(sent, 'fz', 0, 0, tiled=True)  15.6 us
    all_to_all x1, blocking collectives, on_device(): got = lax.all_to_all(sent, 'fz', 0, 0, tiled=True)  10.2 us
    ppermute x14, starting transfers between devices, swap(): return lax.ppermute(value, axis, [(0, 1), (1, 0)])  9.76 us
    pallas_call x15, Pallas kernels, call(): pl.pallas_call(kernel, out_shape=outs, in_specs=specs or [VM] * len(args)...  9.28 us
    ppermute x14, waiting for transfers between devices, swap(): return lax.ppermute(value, axis, [(0, 1), (1, 0)])  9.14 us
    ppermute x2, starting transfers between devices, across(): return lax.ppermute(value, ('fx', 'ty'), [(n, 3 - n) for n in range(4)])  3.36 us
    ppermute x2, waiting for transfers between devices, across(): return lax.ppermute(value, ('fx', 'ty'), [(n, 3 - n) for n in range(4)])  2.66 us
  transfers between devices with their start and end apart: 16, of which 7 were waited for; matrix products, arithmetic and copies ran while one was open for 0% of the time, Pallas kernels for 5%

profile of v7, /device:TPU:0, one launch (start us, length us, event | category | flops | bytes accessed | tf_op | source)
XLA Modules:
  0.0 82.0 jit_solution(11692409528268020358)
XLA Ops:
  0.7 1.8 %pack.1 = (bf16[4,272,128]{2,1,0:T(8,128)(2,1)}, f32[4,128]{1,0:T(4,128)}) custom-call(s32[4]{0:T(128)} %refs_0_.1, bf16[64,96]{1,0:T(8,128)(2,1)} %bitcast.42, bf16[64,96]{1,0:T(8,128)(2,1)} %bitcast.43, bf16[64,96]{1,0:T(8,128)(2,1)} %bitcast.44, bf16[64,96]{1,0:T(8,128)(2,1)} %bitcast.45, bf16[64,512]{1,0:T(8,128)(2,1)} %bitcast.41, ...), custom_call_target="tpu_custom_call" | custom-call | bytes 5400000 | tf_op jit(solution)/shard_map/pack/pallas_call | solution.py:758
  2.4 15.6 %all_to_all.20 = bf16[4,272,128]{2,1,0:T(8,128)(2,1)S(1)} all-to-all(bf16[4,272,128]{2,1,0:T(8,128)(2,1)} %get-tuple-element.85), channel_id=1, replica_groups=mesh['fz'=4,'fx'=2,'ty'=2,'tc'=2] {'fz'}, dimensions={0} | all-to-all | bytes 557056 | tf_op jit(solution)/shard_map/all_to_all | solution.py:813
  18.0 1.6 %collective-permute-start.3 = (bf16[4,160,128]{2,1,0:T(8,128)(2,1)S(1)}, bf16[4,160,128]{2,1,0:T(8,128)(2,1)S(1)}, u32[]{:S(2)}, u32[]{:S(2)}) collective-permute-start(bf16[4,160,128]{2,1,0:T(8,128)(2,1)S(1)} %slice.9), channel_id=1, source_target_pairs={{0,2},{2,0},{1,3},{3,1},{4,6},{6,4},{5,7},{7,5},{8,10},{10,8},{9,1... | collective-permute-start | bytes 491528 | tf_op jit(solution)/shard_map/ppermute | solution.py:775
  19.6 1.7 %collective-permute-start.2 = (bf16[4,112,128]{2,1,0:T(8,128)(2,1)S(1)}, bf16[4,112,128]{2,1,0:T(8,128)(2,1)S(1)}, u32[]{:S(2)}, u32[]{:S(2)}) collective-permute-start(bf16[4,112,128]{2,1,0:T(8,128)(2,1)S(1)} %slice.8), channel_id=1, source_target_pairs={{0,6},{2,4},{4,2},{6,0},{1,7},{3,5},{5,3},{7,1},{8,14},{10,12},{12... | collective-permute-start | bytes 344072 | tf_op jit(solution)/shard_map/ppermute | solution.py:779
  21.9 1.2 %collective-permute-start = (bf16[4,112,128]{2,1,0:T(8,128)(2,1)S(1)}, bf16[4,112,128]{2,1,0:T(8,128)(2,1)S(1)}, u32[]{:S(2)}, u32[]{:S(2)}) collective-permute-start(bf16[4,112,128]{2,1,0:T(8,128)(2,1)S(1)} %slice.8), channel_id=1, source_target_pairs={{0,2},{2,0},{1,3},{3,1},{4,6},{6,4},{5,7},{7,5},{8,10},{10,8},{9,1... | collective-permute-start | bytes 344072 | tf_op jit(solution)/shard_map/ppermute | solution.py:775
  23.1 0.7 standardize.1
  23.8 2.7 %collective-permute-done.2 = bf16[4,112,128]{2,1,0:T(8,128)(2,1)S(1)} collective-permute-done((bf16[4,112,128]{2,1,0:T(8,128)(2,1)S(1)}, bf16[4,112,128]{2,1,0:T(8,128)(2,1)S(1)}, u32[]{:S(2)}, u32[]{:S(2)}) %collective-permute-start.2) | collective-permute-done | bytes 114720 | tf_op jit(solution)/shard_map/ppermute | solution.py:779
  26.5 1.4 %collective-permute-done.1 = bf16[4,112,128]{2,1,0:T(8,128)(2,1)S(1)} collective-permute-done((bf16[4,112,128]{2,1,0:T(8,128)(2,1)S(1)}, bf16[4,112,128]{2,1,0:T(8,128)(2,1)S(1)}, u32[]{:S(2)}, u32[]{:S(2)}) %collective-permute-start.1) | collective-permute-done | bytes 114720 | tf_op jit(solution)/shard_map/ppermute | solution.py:775
  28.6 1.6 %collective-permute-start.5 = (bf16[2,4,160,128]{3,2,1,0:T(8,128)(2,1)S(1)}, bf16[2,4,160,128]{3,2,1,0:T(8,128)(2,1)S(1)}, u32[]{:S(2)}, u32[]{:S(2)}) collective-permute-start(bf16[2,4,160,128]{3,2,1,0:T(8,128)(2,1)S(1)} %pad_maximum_fusion.2), channel_id=1, source_target_pairs={{0,4},{4,0},{1,5},{5,1},{2,6},{6,2},{3,7},{7,3},{8,12},{12,8},{9,1... | collective-permute-start | bytes 983048 | tf_op jit(solution)/shard_map/ppermute | solution.py:775
  30.9 10.9 %all_to_all.21.recv_ref = f32[16,4,128]{2,1,0:T(4,128)S(1)} all-to-all(f32[16,4,128]{2,1,0:T(4,128)S(1)} %get-tuple-element.97), channel_id=1, replica_groups=mesh['fz'=4,'fx'=2,'ty'=2,'tc'=2] {'fz','fx','ty'}, dimensions={0} | all-to-all | bytes 65536 | tf_op jit(solution)/shard_map/all_to_all | solution.py:835
  43.5 1.5 %collective-permute-done.6.got_ref = f32[128,512]{1,0:T(8,128)S(1)} collective-permute-done((f32[128,512]{1,0:T(8,128)S(1)}, f32[128,512]{1,0:T(8,128)S(1)}, u32[]{:S(2)}, u32[]{:S(2)}) %collective-permute-start.6) | collective-permute-done | bytes 262176 | tf_op jit(solution)/shard_map/ppermute | solution.py:775
  45.9 0.8 sums.1
  46.6 0.7 collective-permute-done.8.got_ref
  47.4 0.8 back.1
  48.1 0.7 collective-permute-start.9
  48.8 10.2 %all_to_all.22.recv_ref = f32[16,4,128]{2,1,0:T(4,128)S(1)} all-to-all(f32[16,4,128]{2,1,0:T(4,128)S(1)} %get-tuple-element.119), channel_id=1, replica_groups=mesh['fz'=4,'fx'=2,'ty'=2,'tc'=2] {'fz','fx','ty'}, dimensions={0} | all-to-all | bytes 65536 | tf_op jit(solution)/shard_map/all_to_all | solution.py:872
  59.1 0.9 %collective-permute-start.10 = (bf16[4,160,128]{2,1,0:T(8,128)(2,1)S(1)}, bf16[4,160,128]{2,1,0:T(8,128)(2,1)S(1)}, u32[]{:S(2)}, u32[]{:S(2)}) collective-permute-start(bf16[4,160,128]{2,1,0:T(8,128)(2,1)S(1)} %get-tuple-element.125), channel_id=1, source_target_pairs={{0,2},{2,0},{1,3},{3,1},{4,6},{6,4},{5,7},{7,5},{8,10},{10,8},{9,1... | collective-permute-start | bytes 491528 | tf_op jit(solution)/shard_map/ppermute | solution.py:775
  59.9 1.1 %third.1 = (bf16[432,128]{1,0:T(8,128)(2,1)S(1)}, bf16[432,128]{1,0:T(8,128)(2,1)S(1)}, bf16[432,128]{1,0:T(8,128)(2,1)S(1)}, bf16[432,128]{1,0:T(8,128)(2,1)S(1...) custom-call(f32[16,4,128]{2,1,0:T(4,128)S(1)} %all_to_all.22.recv_ref, f32[4,128]{1,0:T(4,128)S(1)} %copy-done.2, ...), custom_call_target="tpu_custom_call" | custom-call | bytes 5400000 | tf_op jit(solution)/shard_map/third/pallas_call | solution.py:758
  61.0 1.3 %collective-permute-start.11 = (bf16[432,128]{1,0:T(8,128)(2,1)S(1)}, bf16[432,128]{1,0:T(8,128)(2,1)S(1)}, u32[]{:S(2)}, u32[]{:S(2)}) collective-permute-start(bf16[432,128]{1,0:T(8,128)(2,1)S(1)} %get-tuple-element.134), channel_id=1, source_target_pairs={{0,2},{2,0},{1,3},{3,1},{4,6},{6,4},{5,7},{7,5},{8,10},{10,8},{9,1... | collective-permute-start | bytes 331784 | tf_op jit(solution)/shard_map/ppermute | solution.py:775
  62.9 1.7 %collective-permute-start.13 = (bf16[432,128]{1,0:T(8,128)(2,1)S(1)}, bf16[432,128]{1,0:T(8,128)(2,1)S(1)}, u32[]{:S(2)}, u32[]{:S(2)}) collective-permute-start(bf16[432,128]{1,0:T(8,128)(2,1)S(1)} %get-tuple-element.136), channel_id=1, source_target_pairs={{0,6},{2,4},{4,2},{6,0},{1,7},{3,5},{5,3},{7,1},{8,14},{10,12},{12... | collective-permute-start | bytes 331784 | tf_op jit(solution)/shard_map/ppermute | solution.py:779
  64.6 4.6 %collective-permute-done.11.y_ref = bf16[432,128]{1,0:T(8,128)(2,1)S(1)} collective-permute-done((bf16[432,128]{1,0:T(8,128)(2,1)S(1)}, bf16[432,128]{1,0:T(8,128)(2,1)S(1)}, u32[]{:S(2)}, u32[]{:S(2)}) %collective-permute-start.11) | collective-permute-done | bytes 110624 | tf_op jit(solution)/shard_map/ppermute | solution.py:775
  69.3 10.2 %all_to_all.23.got_ref = bf16[4,304,128]{2,1,0:T(8,128)(2,1)S(1)} all-to-all(bf16[4,304,128]{2,1,0:T(8,128)(2,1)S(1)} %plane_add.1), channel_id=1, replica_groups=mesh['fz'=4,'fx'=2,'ty'=2,'tc'=2] {'fz'}, dimensions={0} | all-to-all | bytes 622592 | tf_op jit(solution)/shard_map/all_to_all | solution.py:900
  80.1 0.8 matrices.1
  81.1 0.9 %finish.1 = (f32[128,512]{1,0:T(8,128)}, f32[1,16]{1,0:T(1,128)}, f32[1,512]{1,0:T(1,128)}, f32[1,512]{1,0:T(1,128)}, f32[1,512]{1,0:T(1,128)}, /*index=5*/f32[3...) custom-call(f32[24,128]{1,0:T(8,128)S(1)} %vectors.1.own_ref, f32[24,128]{1,0:T(8,128)S(1)} %collective-permute-done.14.other_ref, ...), custom_call_target="tpu_custom_call" | custom-call | bytes 1440000 | tf_op jit(solution)/shard_map/finish/pallas_call | solution.py:758
  (38 shorter events, 6.1 us)
Async XLA Ops:
  18.0 1.6 %copy-start = (bf16[128,512]{1,0:T(8,128)(2,1)S(1)}, bf16[128,512]{1,0:T(8,128)(2,1)}, u32[]{:S(2)}) copy-start(bf16[128,512]{1,0:T(8,128)(2,1)} %x_ref.3) | copy-start | bytes 393220
  18.0 5.1 %copy-start.1 = (bf16[128,512]{1,0:T(8,128)(2,1)S(1)}, bf16[128,512]{1,0:T(8,128)(2,1)}, u32[]{:S(2)}) copy-start(bf16[128,512]{1,0:T(8,128)(2,1)} %up_ref.3) | copy-start | bytes 393220
  18.0 5.1 %copy-start.2 = (f32[4,128]{1,0:T(4,128)S(1)}, f32[4,128]{1,0:T(4,128)}, u32[]{:S(2)}) copy-start(f32[4,128]{1,0:T(4,128)} %get-tuple-element.88.start_ref) | copy-start | bytes 6148
  18.0 10.5 %collective-permute-start.3 = (bf16[4,160,128]{2,1,0:T(8,128)(2,1)S(1)}, bf16[4,160,128]{2,1,0:T(8,128)(2,1)S(1)}, u32[]{:S(2)}, u32[]{:S(2)}) collective-permute-start(bf16[4,160,128]{2,1,0:T(8,128)(2,1)S(1)} %slice.9), channel_id=1, source_target_pairs={{0,2},{2,0},{1,3},{3,1},{4,6},{6,4},{5,7},{7,5},{8,10},{10,8},{9,1... | collective-permute-start | bytes 491528 | tf_op jit(solution)/shard_map/ppermute | solution.py:775
  19.6 3.5 %collective-permute-start.4 = (bf16[128,512]{1,0:T(8,128)(2,1)S(1)}, bf16[128,512]{1,0:T(8,128)(2,1)S(1)}, u32[]{:S(2)}, u32[]{:S(2)}) collective-permute-start(bf16[128,512]{1,0:T(8,128)(2,1)S(1)} %copy-done), channel_id=1, source_target_pairs={{0,1},{1,0},{2,3},{3,2},{4,5},{5,4},{6,7},{7,6},{8,9},{9,8},{10,11... | collective-permute-start | bytes 393224 | tf_op jit(solution)/shard_map/ppermute | solution.py:775
  19.6 6.8 %collective-permute-start.2 = (bf16[4,112,128]{2,1,0:T(8,128)(2,1)S(1)}, bf16[4,112,128]{2,1,0:T(8,128)(2,1)S(1)}, u32[]{:S(2)}, u32[]{:S(2)}) collective-permute-start(bf16[4,112,128]{2,1,0:T(8,128)(2,1)S(1)} %slice.8), channel_id=1, source_target_pairs={{0,6},{2,4},{4,2},{6,0},{1,7},{3,5},{5,3},{7,1},{8,14},{10,12},{12... | collective-permute-start | bytes 344072 | tf_op jit(solution)/shard_map/ppermute | solution.py:779
  21.3 6.6 %collective-permute-start.1 = (bf16[4,112,128]{2,1,0:T(8,128)(2,1)S(1)}, bf16[4,112,128]{2,1,0:T(8,128)(2,1)S(1)}, u32[]{:S(2)}, u32[]{:S(2)}) collective-permute-start(bf16[4,112,128]{2,1,0:T(8,128)(2,1)S(1)} %slice.8), channel_id=1, source_target_pairs={{0,4},{4,0},{1,5},{5,1},{2,6},{6,2},{3,7},{7,3},{8,12},{12,8},{9,1... | collective-permute-start | bytes 344072 | tf_op jit(solution)/shard_map/ppermute | solution.py:775
  21.9 6.7 %collective-permute-start = (bf16[4,112,128]{2,1,0:T(8,128)(2,1)S(1)}, bf16[4,112,128]{2,1,0:T(8,128)(2,1)S(1)}, u32[]{:S(2)}, u32[]{:S(2)}) collective-permute-start(bf16[4,112,128]{2,1,0:T(8,128)(2,1)S(1)} %slice.8), channel_id=1, source_target_pairs={{0,2},{2,0},{1,3},{3,1},{4,6},{6,4},{5,7},{7,5},{8,10},{10,8},{9,1... | collective-permute-start | bytes 344072 | tf_op jit(solution)/shard_map/ppermute | solution.py:775
  28.6 13.2 %collective-permute-start.5 = (bf16[2,4,160,128]{3,2,1,0:T(8,128)(2,1)S(1)}, bf16[2,4,160,128]{3,2,1,0:T(8,128)(2,1)S(1)}, u32[]{:S(2)}, u32[]{:S(2)}) collective-permute-start(bf16[2,4,160,128]{3,2,1,0:T(8,128)(2,1)S(1)} %pad_maximum_fusion.2), channel_id=1, source_target_pairs={{0,4},{4,0},{1,5},{5,1},{2,6},{6,2},{3,7},{7,3},{8,12},{12,8},{9,1... | collective-permute-start | bytes 983048 | tf_op jit(solution)/shard_map/ppermute | solution.py:775
  42.5 2.5 %collective-permute-start.7 = (bf16[2,2,4,160,128]{4,3,2,1,0:T(8,128)(2,1)S(1)}, bf16[2,2,4,160,128]{4,3,2,1,0:T(8,128)(2,1)S(1)}, u32[]{:S(2)}, u32[]{:S(2)}) collective-permute-start(bf16[2,2,4,160,128]{4,3,2,1,0:T(8,128)(2,1)S(1)} %pad_maximum_fusion.cw_ref), channel_id=1, source_target_pairs={{0,1},{1,0},{2,3},{3,2},{4,5},{5,4},{6,7},{7,6},{8,9},{9,8},{10,11... | collective-permute-start | bytes 1966088 | tf_op jit(solution)/shard_map/ppermute | solution.py:775
  42.9 2.1 %collective-permute-start.6 = (f32[128,512]{1,0:T(8,128)S(1)}, f32[128,512]{1,0:T(8,128)S(1)}, u32[]{:S(2)}, u32[]{:S(2)}) collective-permute-start(f32[128,512]{1,0:T(8,128)S(1)} %get-tuple-element.107), channel_id=1, source_target_pairs={{0,1},{1,0},{2,3},{3,2},{4,5},{5,4},{6,7},{7,6},{8,9},{9,8},{10,11... | collective-permute-start | bytes 786440 | tf_op jit(solution)/shard_map/ppermute | solution.py:775
  45.7 1.7 %collective-permute-start.8 = (bf16[128,1280]{1,0:T(8,128)(2,1)S(1)}, bf16[128,1280]{1,0:T(8,128)(2,1)S(1)}, u32[]{:S(2)}, u32[]{:S(2)}) collective-permute-start(bf16[128,1280]{1,0:T(8,128)(2,1)S(1)} %get-tuple-element.116), channel_id=1, source_target_pairs={{0,1},{1,0},{2,3},{3,2},{4,5},{5,4},{6,7},{7,6},{8,9},{9,8},{10,11... | collective-permute-start | bytes 983048 | tf_op jit(solution)/shard_map/ppermute | solution.py:775
  48.1 10.8 %collective-permute-start.9 = (bf16[2,4,160,128]{3,2,1,0:T(8,128)(2,1)S(1)}, bf16[2,4,160,128]{3,2,1,0:T(8,128)(2,1)S(1)}, u32[]{:S(2)}, u32[]{:S(2)}) collective-permute-start(bf16[2,4,160,128]{3,2,1,0:T(8,128)(2,1)S(1)} %get-tuple-element.120), channel_id=1, source_target_pairs={{0,4},{4,0},{1,5},{5,1},{2,6},{6,2},{3,7},{7,3},{8,12},{12,8},{9,1... | collective-permute-start | bytes 983048 | tf_op jit(solution)/shard_map/ppermute | solution.py:775
  59.1 10.1 %collective-permute-start.10 = (bf16[4,160,128]{2,1,0:T(8,128)(2,1)S(1)}, bf16[4,160,128]{2,1,0:T(8,128)(2,1)S(1)}, u32[]{:S(2)}, u32[]{:S(2)}) collective-permute-start(bf16[4,160,128]{2,1,0:T(8,128)(2,1)S(1)} %get-tuple-element.125), channel_id=1, source_target_pairs={{0,2},{2,0},{1,3},{3,1},{4,6},{6,4},{5,7},{7,5},{8,10},{10,8},{9,1... | collective-permute-start | bytes 491528 | tf_op jit(solution)/shard_map/ppermute | solution.py:775
  61.0 8.1 %collective-permute-start.11 = (bf16[432,128]{1,0:T(8,128)(2,1)S(1)}, bf16[432,128]{1,0:T(8,128)(2,1)S(1)}, u32[]{:S(2)}, u32[]{:S(2)}) collective-permute-start(bf16[432,128]{1,0:T(8,128)(2,1)S(1)} %get-tuple-element.134), channel_id=1, source_target_pairs={{0,2},{2,0},{1,3},{3,1},{4,6},{6,4},{5,7},{7,5},{8,10},{10,8},{9,1... | collective-permute-start | bytes 331784 | tf_op jit(solution)/shard_map/ppermute | solution.py:775
  62.3 6.8 %collective-permute-start.12 = (bf16[432,128]{1,0:T(8,128)(2,1)S(1)}, bf16[432,128]{1,0:T(8,128)(2,1)S(1)}, u32[]{:S(2)}, u32[]{:S(2)}) collective-permute-start(bf16[432,128]{1,0:T(8,128)(2,1)S(1)} %get-tuple-element.135), channel_id=1, source_target_pairs={{0,4},{4,0},{1,5},{5,1},{2,6},{6,2},{3,7},{7,3},{8,12},{12,8},{9,1... | collective-permute-start | bytes 331784 | tf_op jit(solution)/shard_map/ppermute | solution.py:775
  62.9 6.2 %collective-permute-start.13 = (bf16[432,128]{1,0:T(8,128)(2,1)S(1)}, bf16[432,128]{1,0:T(8,128)(2,1)S(1)}, u32[]{:S(2)}, u32[]{:S(2)}) collective-permute-start(bf16[432,128]{1,0:T(8,128)(2,1)S(1)} %get-tuple-element.136), channel_id=1, source_target_pairs={{0,6},{2,4},{4,2},{6,0},{1,7},{3,5},{5,3},{7,1},{8,14},{10,12},{12... | collective-permute-start | bytes 331784 | tf_op jit(solution)/shard_map/ppermute | solution.py:779
  79.5 1.6 %collective-permute-start.15 = (f32[128,512]{1,0:T(8,128)S(1)}, f32[128,512]{1,0:T(8,128)S(1)}, u32[]{:S(2)}, u32[]{:S(2)}) collective-permute-start(f32[128,512]{1,0:T(8,128)S(1)} %get-tuple-element.139), channel_id=1, source_target_pairs={{0,1},{1,0},{2,3},{3,2},{4,5},{5,4},{6,7},{7,6},{8,9},{9,8},{10,11... | collective-permute-start | bytes 786440 | tf_op jit(solution)/shard_map/ppermute | solution.py:775
  79.5 1.5 %collective-permute-start.14 = (f32[24,128]{1,0:T(8,128)S(1)}, f32[24,128]{1,0:T(8,128)S(1)}, u32[]{:S(2)}, u32[]{:S(2)}) collective-permute-start(f32[24,128]{1,0:T(8,128)S(1)} %vectors.1.own_ref), channel_id=1, source_target_pairs={{0,1},{1,0},{2,3},{3,2},{4,5},{5,4},{6,7},{7,6},{8,9},{9,8},{10,11... | collective-permute-start | bytes 36872 | tf_op jit(solution)/shard_map/ppermute | solution.py:775

commit v8 on v7

--- a/solution.py
+++ b/solution.py
@@ -441,11 +441,9 @@
     natural(lambda m, z, x: cw_ref[lax.axis_index("fx") ^ x, m, z, 0:96, :], c_ref)
 
 
-def readout_kernel(twice_ref, c_ref, own_ref, away_ref, scratch):
-    rows = own_ref.shape[0]
-    scratch[...] = dot(twice_ref[...], c_ref[...], NN)
-    own_ref[...] = scratch[own_rows(rows), :]
-    away_ref[...] = scratch[other_rows(rows), :]
+def readout_kernel(core, twice_ref, c_ref, out_ref):
+    where = (own_rows, other_rows)[core](out_ref.shape[0])
+    out_ref[...] = dot(twice_ref[where, :], c_ref[...], NN)
 
 
 def second_kernel(
@@ -458,7 +456,7 @@
             lanes = pl.ds(pl.multiple_of(slot_pos(m, core) * 128, 128), 128)
             for f in range(GROUPS):
                 place = (f // 2) * 2 + (lax.axis_index("fx") ^ (f % 2))
-                gate_ref[pl.ds(pl.multiple_of(place * 64, 64), 64), lanes] = piece(ref, m, f, 96, 64)
+                gate_ref[pl.ds(pl.multiple_of(place * 64, 64), 64), lanes] = piece(ref, m, f, 96 * (1 - core), 64)
     skip, gate_bias = feat_ref[1:2], feat_ref[2:3]
     normed = normed_ref[own_rows(rows), :].astype(F32)
     mixed = (own_ref[...] + got_ref[...]) + skip * normed
@@ -842,10 +840,9 @@
         [pltpu.VMEM((8, 128), F32)],
     )
     if fast:
-        other_cw = swap(tied(cw, twice), "tc")
-    own, away = call(
-        readout_kernel, (sds((rows, width)), sds((rows, width))), (twice, c_all), [pltpu.VMEM((pair, width), F32)]
-    )
+        other_cw = swap(cw[:, :, :, 96:], "tc")
+    readout = lambda core: call(functools.partial(readout_kernel, core), sds((rows, width)), (twice, c_all))
+    away, own = readout(1), readout(0)
     branch, d_mixed, dlogit, kept, away = call(
         second_kernel,
         (sds((rows, width), BF16), sds((rows, width)), sds((rows, width), BF16), *[sds((rows, 2 * width + 256), BF16)] * 2),
@@ -947,7 +944,7 @@
         slots = jnp.stack(slots, axis=1)
         if i == 0:
             g, cw = slots[:, :, :, :112], slots[:, :, :, 112:]
-    return g, cw, slots[:, :, :, 112:]
+    return g, cw, slots[:, :, :, 208:]
 
 
 def reduced(layer_out, grad_in, stay_cw, leave_cw, plane_b, count_all, fsdp, width):

time: 82.4 us -> 82 us (level)
  waiting for transfers between devices: 11.8 us -> 10.7 us
    ppermute x14, waiting for transfers between devices: 9.14 us -> 8.07 us  [swap(): return lax.ppermute(value, axis, [(0, 1), (1, 0)])]
    pallas_call x15 -> x16, Pallas kernels: 9.28 us -> 9.4 us  [call(): pl.pallas_call(kernel, out_shape=outs, in_specs=specs or [VM] * len(args)...]
  transfers between devices with their start and end apart: 16 -> 16, of which waited for: 7 -> 7; matrix products, arithmetic and copies ran while one was open for 0% -> 0% of each run, Pallas kernels for 5% -> 6%
where the time goes in v8:
time: 82 us; the launch traced here: 81.6 us
  blocking collectives  46.9 us (57%)
  starting transfers between devices  13.6 us (17%)
  waiting for transfers between devices  10.7 us (13%)
  Pallas kernels  9.4 us (11%)
    all_to_all x2, blocking collectives, on_device(): came = lax.all_to_all(carry, same_core, 0, 0, tiled=True)  21 us
    all_to_all x1, blocking collectives, on_device(): mine = lax.all_to_all(sent, 'fz', 0, 0, tiled=True)  15.6 us
    all_to_all x1, blocking collectives, on_device(): got = lax.all_to_all(sent, 'fz', 0, 0, tiled=True)  10.3 us
    ppermute x14, starting transfers between devices, swap(): return lax.ppermute(value, axis, [(0, 1), (1, 0)])  10 us
    pallas_call x16, Pallas kernels, call(): pl.pallas_call(kernel, out_shape=outs, in_specs=specs or [VM] * len(args)...  9.4 us
    ppermute x14, waiting for transfers between devices, swap(): return lax.ppermute(value, axis, [(0, 1), (1, 0)])  8.07 us
    ppermute x2, starting transfers between devices, across(): return lax.ppermute(value, ('fx', 'ty'), [(n, 3 - n) for n in range(4)])  3.59 us
    ppermute x2, waiting for transfers between devices, across(): return lax.ppermute(value, ('fx', 'ty'), [(n, 3 - n) for n in range(4)])  2.66 us
  transfers between devices with their start and end apart: 16, of which 7 were waited for; matrix products, arithmetic and copies ran while one was open for 0% of the time, Pallas kernels for 6%

profile of v8, /device:TPU:0, one launch (start us, length us, event | category | flops | bytes accessed | tf_op | source)
XLA Modules:
  0.0 81.6 jit_solution(9939982273648445410)
XLA Ops:
  0.7 1.8 %pack.1 = (bf16[4,272,128]{2,1,0:T(8,128)(2,1)}, f32[4,128]{1,0:T(4,128)}) custom-call(s32[4]{0:T(128)} %refs_0_.1, bf16[64,96]{1,0:T(8,128)(2,1)} %bitcast.44, bf16[64,96]{1,0:T(8,128)(2,1)} %bitcast.45, bf16[64,96]{1,0:T(8,128)(2,1)} %bitcast.46, bf16[64,96]{1,0:T(8,128)(2,1)} %bitcast.47, bf16[64,512]{1,0:T(8,128)(2,1)} %bitcast.43, ...), custom_call_target="tpu_custom_call" | custom-call | bytes 5400000 | tf_op jit(solution)/shard_map/pack/pallas_call | solution.py:756
  2.4 15.6 %all_to_all.20 = bf16[4,272,128]{2,1,0:T(8,128)(2,1)S(1)} all-to-all(bf16[4,272,128]{2,1,0:T(8,128)(2,1)} %get-tuple-element.82), channel_id=1, replica_groups=mesh['fz'=4,'fx'=2,'ty'=2,'tc'=2] {'fz'}, dimensions={0} | all-to-all | bytes 557056 | tf_op jit(solution)/shard_map/all_to_all | solution.py:811
  18.0 1.6 %collective-permute-start.3 = (bf16[4,160,128]{2,1,0:T(8,128)(2,1)S(1)}, bf16[4,160,128]{2,1,0:T(8,128)(2,1)S(1)}, u32[]{:S(2)}, u32[]{:S(2)}) collective-permute-start(bf16[4,160,128]{2,1,0:T(8,128)(2,1)S(1)} %slice.13), channel_id=1, source_target_pairs={{0,2},{2,0},{1,3},{3,1},{4,6},{6,4},{5,7},{7,5},{8,10},{10,8},{9,1... | collective-permute-start | bytes 491528 | tf_op jit(solution)/shard_map/ppermute | solution.py:773
  19.6 1.7 %collective-permute-start.2 = (bf16[4,112,128]{2,1,0:T(8,128)(2,1)S(1)}, bf16[4,112,128]{2,1,0:T(8,128)(2,1)S(1)}, u32[]{:S(2)}, u32[]{:S(2)}) collective-permute-start(bf16[4,112,128]{2,1,0:T(8,128)(2,1)S(1)} %slice.12), channel_id=1, source_target_pairs={{0,6},{2,4},{4,2},{6,0},{1,7},{3,5},{5,3},{7,1},{8,14},{10,12},{12... | collective-permute-start | bytes 344072 | tf_op jit(solution)/shard_map/ppermute | solution.py:777
  21.9 1.2 %collective-permute-start = (bf16[4,112,128]{2,1,0:T(8,128)(2,1)S(1)}, bf16[4,112,128]{2,1,0:T(8,128)(2,1)S(1)}, u32[]{:S(2)}, u32[]{:S(2)}) collective-permute-start(bf16[4,112,128]{2,1,0:T(8,128)(2,1)S(1)} %slice.12), channel_id=1, source_target_pairs={{0,2},{2,0},{1,3},{3,1},{4,6},{6,4},{5,7},{7,5},{8,10},{10,8},{9,1... | collective-permute-start | bytes 344072 | tf_op jit(solution)/shard_map/ppermute | solution.py:773
  23.1 0.7 standardize.1
  23.8 2.7 %collective-permute-done.2 = bf16[4,112,128]{2,1,0:T(8,128)(2,1)S(1)} collective-permute-done((bf16[4,112,128]{2,1,0:T(8,128)(2,1)S(1)}, bf16[4,112,128]{2,1,0:T(8,128)(2,1)S(1)}, u32[]{:S(2)}, u32[]{:S(2)}) %collective-permute-start.2) | collective-permute-done | bytes 114720 | tf_op jit(solution)/shard_map/ppermute | solution.py:777
  26.5 1.4 %collective-permute-done.1 = bf16[4,112,128]{2,1,0:T(8,128)(2,1)S(1)} collective-permute-done((bf16[4,112,128]{2,1,0:T(8,128)(2,1)S(1)}, bf16[4,112,128]{2,1,0:T(8,128)(2,1)S(1)}, u32[]{:S(2)}, u32[]{:S(2)}) %collective-permute-start.1) | collective-permute-done | bytes 114720 | tf_op jit(solution)/shard_map/ppermute | solution.py:773
  28.6 1.6 %collective-permute-start.5 = (bf16[2,4,160,128]{3,2,1,0:T(8,128)(2,1)S(1)}, bf16[2,4,160,128]{3,2,1,0:T(8,128)(2,1)S(1)}, u32[]{:S(2)}, u32[]{:S(2)}) collective-permute-start(bf16[2,4,160,128]{3,2,1,0:T(8,128)(2,1)S(1)} %pad_maximum_fusion.2), channel_id=1, source_target_pairs={{0,4},{4,0},{1,5},{5,1},{2,6},{6,2},{3,7},{7,3},{8,12},{12,8},{9,1... | collective-permute-start | bytes 983048 | tf_op jit(solution)/shard_map/ppermute | solution.py:773
  30.9 10.9 %all_to_all.21.recv_ref = f32[16,4,128]{2,1,0:T(4,128)S(1)} all-to-all(f32[16,4,128]{2,1,0:T(4,128)S(1)} %get-tuple-element.94), channel_id=1, replica_groups=mesh['fz'=4,'fx'=2,'ty'=2,'tc'=2] {'fz','fx','ty'}, dimensions={0} | all-to-all | bytes 65536 | tf_op jit(solution)/shard_map/all_to_all | solution.py:833
  43.6 0.9 %collective-permute-done.6.got_ref = f32[128,512]{1,0:T(8,128)S(1)} collective-permute-done((f32[128,512]{1,0:T(8,128)S(1)}, f32[128,512]{1,0:T(8,128)S(1)}, u32[]{:S(2)}, u32[]{:S(2)}) %collective-permute-start.6) | collective-permute-done | bytes 262176 | tf_op jit(solution)/shard_map/ppermute | solution.py:773
  44.5 0.6 second.1
  45.6 0.8 sums.1
  46.9 0.8 back.1
  47.7 0.7 collective-permute-start.9
  48.4 10.2 %all_to_all.22.recv_ref = f32[16,4,128]{2,1,0:T(4,128)S(1)} all-to-all(f32[16,4,128]{2,1,0:T(4,128)S(1)} %get-tuple-element.113), channel_id=1, replica_groups=mesh['fz'=4,'fx'=2,'ty'=2,'tc'=2] {'fz','fx','ty'}, dimensions={0} | all-to-all | bytes 65536 | tf_op jit(solution)/shard_map/all_to_all | solution.py:869
  58.6 1.1 %collective-permute-start.10 = (bf16[4,160,128]{2,1,0:T(8,128)(2,1)S(1)}, bf16[4,160,128]{2,1,0:T(8,128)(2,1)S(1)}, u32[]{:S(2)}, u32[]{:S(2)}) collective-permute-start(bf16[4,160,128]{2,1,0:T(8,128)(2,1)S(1)} %get-tuple-element.119), channel_id=1, source_target_pairs={{0,2},{2,0},{1,3},{3,1},{4,6},{6,4},{5,7},{7,5},{8,10},{10,8},{9,1... | collective-permute-start | bytes 491528 | tf_op jit(solution)/shard_map/ppermute | solution.py:773
  59.7 1.1 %third.1 = (bf16[432,128]{1,0:T(8,128)(2,1)S(1)}, bf16[432,128]{1,0:T(8,128)(2,1)S(1)}, bf16[432,128]{1,0:T(8,128)(2,1)S(1)}, bf16[432,128]{1,0:T(8,128)(2,1)S(1...) custom-call(f32[16,4,128]{2,1,0:T(4,128)S(1)} %all_to_all.22.recv_ref, f32[4,128]{1,0:T(4,128)S(1)} %copy-done.2, ...), custom_call_target="tpu_custom_call" | custom-call | bytes 5400000 | tf_op jit(solution)/shard_map/third/pallas_call | solution.py:756
  60.8 1.1 %collective-permute-start.11 = (bf16[432,128]{1,0:T(8,128)(2,1)S(1)}, bf16[432,128]{1,0:T(8,128)(2,1)S(1)}, u32[]{:S(2)}, u32[]{:S(2)}) collective-permute-start(bf16[432,128]{1,0:T(8,128)(2,1)S(1)} %get-tuple-element.128), channel_id=1, source_target_pairs={{0,2},{2,0},{1,3},{3,1},{4,6},{6,4},{5,7},{7,5},{8,10},{10,8},{9,1... | collective-permute-start | bytes 331784 | tf_op jit(solution)/shard_map/ppermute | solution.py:773
  62.5 1.9 %collective-permute-start.13 = (bf16[432,128]{1,0:T(8,128)(2,1)S(1)}, bf16[432,128]{1,0:T(8,128)(2,1)S(1)}, u32[]{:S(2)}, u32[]{:S(2)}) collective-permute-start(bf16[432,128]{1,0:T(8,128)(2,1)S(1)} %get-tuple-element.130), channel_id=1, source_target_pairs={{0,6},{2,4},{4,2},{6,0},{1,7},{3,5},{5,3},{7,1},{8,14},{10,12},{12... | collective-permute-start | bytes 331784 | tf_op jit(solution)/shard_map/ppermute | solution.py:777
  64.4 4.4 %collective-permute-done.11.y_ref = bf16[432,128]{1,0:T(8,128)(2,1)S(1)} collective-permute-done((bf16[432,128]{1,0:T(8,128)(2,1)S(1)}, bf16[432,128]{1,0:T(8,128)(2,1)S(1)}, u32[]{:S(2)}, u32[]{:S(2)}) %collective-permute-start.11) | collective-permute-done | bytes 110624 | tf_op jit(solution)/shard_map/ppermute | solution.py:773
  68.8 10.3 %all_to_all.23.got_ref = bf16[4,304,128]{2,1,0:T(8,128)(2,1)S(1)} all-to-all(bf16[4,304,128]{2,1,0:T(8,128)(2,1)S(1)} %plane_add.1), channel_id=1, replica_groups=mesh['fz'=4,'fx'=2,'ty'=2,'tc'=2] {'fz'}, dimensions={0} | all-to-all | bytes 622592 | tf_op jit(solution)/shard_map/all_to_all | solution.py:897
  79.7 0.8 matrices.1
  80.7 0.9 %finish.1 = (f32[128,512]{1,0:T(8,128)}, f32[1,16]{1,0:T(1,128)}, f32[1,512]{1,0:T(1,128)}, f32[1,512]{1,0:T(1,128)}, f32[1,512]{1,0:T(1,128)}, /*index=5*/f32[3...) custom-call(f32[24,128]{1,0:T(8,128)S(1)} %vectors.1.own_ref, f32[24,128]{1,0:T(8,128)S(1)} %collective-permute-done.14.other_ref, ...), custom_call_target="tpu_custom_call" | custom-call | bytes 1440000 | tf_op jit(solution)/shard_map/finish/pallas_call | solution.py:756
  (40 shorter events, 6.3 us)
Async XLA Ops:
  18.0 1.6 %copy-start = (bf16[128,512]{1,0:T(8,128)(2,1)S(1)}, bf16[128,512]{1,0:T(8,128)(2,1)}, u32[]{:S(2)}) copy-start(bf16[128,512]{1,0:T(8,128)(2,1)} %x_ref.3) | copy-start | bytes 393220
  18.0 5.1 %copy-start.1 = (bf16[128,512]{1,0:T(8,128)(2,1)S(1)}, bf16[128,512]{1,0:T(8,128)(2,1)}, u32[]{:S(2)}) copy-start(bf16[128,512]{1,0:T(8,128)(2,1)} %up_ref.3) | copy-start | bytes 393220
  18.0 5.1 %copy-start.2 = (f32[4,128]{1,0:T(4,128)S(1)}, f32[4,128]{1,0:T(4,128)}, u32[]{:S(2)}) copy-start(f32[4,128]{1,0:T(4,128)} %get-tuple-element.85.start_ref) | copy-start | bytes 6148
  18.0 10.5 %collective-permute-start.3 = (bf16[4,160,128]{2,1,0:T(8,128)(2,1)S(1)}, bf16[4,160,128]{2,1,0:T(8,128)(2,1)S(1)}, u32[]{:S(2)}, u32[]{:S(2)}) collective-permute-start(bf16[4,160,128]{2,1,0:T(8,128)(2,1)S(1)} %slice.13), channel_id=1, source_target_pairs={{0,2},{2,0},{1,3},{3,1},{4,6},{6,4},{5,7},{7,5},{8,10},{10,8},{9,1... | collective-permute-start | bytes 491528 | tf_op jit(solution)/shard_map/ppermute | solution.py:773
  19.6 3.5 %collective-permute-start.4 = (bf16[128,512]{1,0:T(8,128)(2,1)S(1)}, bf16[128,512]{1,0:T(8,128)(2,1)S(1)}, u32[]{:S(2)}, u32[]{:S(2)}) collective-permute-start(bf16[128,512]{1,0:T(8,128)(2,1)S(1)} %copy-done), channel_id=1, source_target_pairs={{0,1},{1,0},{2,3},{3,2},{4,5},{5,4},{6,7},{7,6},{8,9},{9,8},{10,11... | collective-permute-start | bytes 393224 | tf_op jit(solution)/shard_map/ppermute | solution.py:773
  19.6 6.8 %collective-permute-start.2 = (bf16[4,112,128]{2,1,0:T(8,128)(2,1)S(1)}, bf16[4,112,128]{2,1,0:T(8,128)(2,1)S(1)}, u32[]{:S(2)}, u32[]{:S(2)}) collective-permute-start(bf16[4,112,128]{2,1,0:T(8,128)(2,1)S(1)} %slice.12), channel_id=1, source_target_pairs={{0,6},{2,4},{4,2},{6,0},{1,7},{3,5},{5,3},{7,1},{8,14},{10,12},{12... | collective-permute-start | bytes 344072 | tf_op jit(solution)/shard_map/ppermute | solution.py:777
  21.3 6.6 %collective-permute-start.1 = (bf16[4,112,128]{2,1,0:T(8,128)(2,1)S(1)}, bf16[4,112,128]{2,1,0:T(8,128)(2,1)S(1)}, u32[]{:S(2)}, u32[]{:S(2)}) collective-permute-start(bf16[4,112,128]{2,1,0:T(8,128)(2,1)S(1)} %slice.12), channel_id=1, source_target_pairs={{0,4},{4,0},{1,5},{5,1},{2,6},{6,2},{3,7},{7,3},{8,12},{12,8},{9,1... | collective-permute-start | bytes 344072 | tf_op jit(solution)/shard_map/ppermute | solution.py:773
  21.9 6.7 %collective-permute-start = (bf16[4,112,128]{2,1,0:T(8,128)(2,1)S(1)}, bf16[4,112,128]{2,1,0:T(8,128)(2,1)S(1)}, u32[]{:S(2)}, u32[]{:S(2)}) collective-permute-start(bf16[4,112,128]{2,1,0:T(8,128)(2,1)S(1)} %slice.12), channel_id=1, source_target_pairs={{0,2},{2,0},{1,3},{3,1},{4,6},{6,4},{5,7},{7,5},{8,10},{10,8},{9,1... | collective-permute-start | bytes 344072 | tf_op jit(solution)/shard_map/ppermute | solution.py:773
  28.6 13.2 %collective-permute-start.5 = (bf16[2,4,160,128]{3,2,1,0:T(8,128)(2,1)S(1)}, bf16[2,4,160,128]{3,2,1,0:T(8,128)(2,1)S(1)}, u32[]{:S(2)}, u32[]{:S(2)}) collective-permute-start(bf16[2,4,160,128]{3,2,1,0:T(8,128)(2,1)S(1)} %pad_maximum_fusion.2), channel_id=1, source_target_pairs={{0,4},{4,0},{1,5},{5,1},{2,6},{6,2},{3,7},{7,3},{8,12},{12,8},{9,1... | collective-permute-start | bytes 983048 | tf_op jit(solution)/shard_map/ppermute | solution.py:773
  41.9 1.7 %collective-permute-start.7 = (bf16[2,2,4,64,128]{4,3,2,1,0:T(8,128)(2,1)S(1)}, bf16[2,2,4,64,128]{4,3,2,1,0:T(8,128)(2,1)S(1)}, u32[]{:S(2)}, u32[]{:S(2)}) collective-permute-start(bf16[2,2,4,64,128]{4,3,2,1,0:T(8,128)(2,1)S(1)} %fusion), channel_id=1, source_target_pairs={{0,1},{1,0},{2,3},{3,2},{4,5},{5,4},{6,7},{7,6},{8,9},{9,8},{10,11... | collective-permute-start | bytes 786440 | tf_op jit(solution)/shard_map/ppermute | solution.py:773
  42.8 1.7 %collective-permute-start.6 = (f32[128,512]{1,0:T(8,128)S(1)}, f32[128,512]{1,0:T(8,128)S(1)}, u32[]{:S(2)}, u32[]{:S(2)}) collective-permute-start(f32[128,512]{1,0:T(8,128)S(1)} %readout.3), channel_id=1, source_target_pairs={{0,1},{1,0},{2,3},{3,2},{4,5},{5,4},{6,7},{7,6},{8,9},{9,8},{10,11... | collective-permute-start | bytes 786440 | tf_op jit(solution)/shard_map/ppermute | solution.py:773
  45.2 1.7 %collective-permute-start.8 = (bf16[128,1280]{1,0:T(8,128)(2,1)S(1)}, bf16[128,1280]{1,0:T(8,128)(2,1)S(1)}, u32[]{:S(2)}, u32[]{:S(2)}) collective-permute-start(bf16[128,1280]{1,0:T(8,128)(2,1)S(1)} %get-tuple-element.110), channel_id=1, source_target_pairs={{0,1},{1,0},{2,3},{3,2},{4,5},{5,4},{6,7},{7,6},{8,9},{9,8},{10,11... | collective-permute-start | bytes 983048 | tf_op jit(solution)/shard_map/ppermute | solution.py:773
  47.7 10.9 %collective-permute-start.9 = (bf16[2,4,160,128]{3,2,1,0:T(8,128)(2,1)S(1)}, bf16[2,4,160,128]{3,2,1,0:T(8,128)(2,1)S(1)}, u32[]{:S(2)}, u32[]{:S(2)}) collective-permute-start(bf16[2,4,160,128]{3,2,1,0:T(8,128)(2,1)S(1)} %get-tuple-element.114), channel_id=1, source_target_pairs={{0,4},{4,0},{1,5},{5,1},{2,6},{6,2},{3,7},{7,3},{8,12},{12,8},{9,1... | collective-permute-start | bytes 983048 | tf_op jit(solution)/shard_map/ppermute | solution.py:773
  58.6 10.1 %collective-permute-start.10 = (bf16[4,160,128]{2,1,0:T(8,128)(2,1)S(1)}, bf16[4,160,128]{2,1,0:T(8,128)(2,1)S(1)}, u32[]{:S(2)}, u32[]{:S(2)}) collective-permute-start(bf16[4,160,128]{2,1,0:T(8,128)(2,1)S(1)} %get-tuple-element.119), channel_id=1, source_target_pairs={{0,2},{2,0},{1,3},{3,1},{4,6},{6,4},{5,7},{7,5},{8,10},{10,8},{9,1... | collective-permute-start | bytes 491528 | tf_op jit(solution)/shard_map/ppermute | solution.py:773
  60.8 7.9 %collective-permute-start.11 = (bf16[432,128]{1,0:T(8,128)(2,1)S(1)}, bf16[432,128]{1,0:T(8,128)(2,1)S(1)}, u32[]{:S(2)}, u32[]{:S(2)}) collective-permute-start(bf16[432,128]{1,0:T(8,128)(2,1)S(1)} %get-tuple-element.128), channel_id=1, source_target_pairs={{0,2},{2,0},{1,3},{3,1},{4,6},{6,4},{5,7},{7,5},{8,10},{10,8},{9,1... | collective-permute-start | bytes 331784 | tf_op jit(solution)/shard_map/ppermute | solution.py:773
  61.9 6.9 %collective-permute-start.12 = (bf16[432,128]{1,0:T(8,128)(2,1)S(1)}, bf16[432,128]{1,0:T(8,128)(2,1)S(1)}, u32[]{:S(2)}, u32[]{:S(2)}) collective-permute-start(bf16[432,128]{1,0:T(8,128)(2,1)S(1)} %get-tuple-element.129), channel_id=1, source_target_pairs={{0,4},{4,0},{1,5},{5,1},{2,6},{6,2},{3,7},{7,3},{8,12},{12,8},{9,1... | collective-permute-start | bytes 331784 | tf_op jit(solution)/shard_map/ppermute | solution.py:773
  62.5 6.3 %collective-permute-start.13 = (bf16[432,128]{1,0:T(8,128)(2,1)S(1)}, bf16[432,128]{1,0:T(8,128)(2,1)S(1)}, u32[]{:S(2)}, u32[]{:S(2)}) collective-permute-start(bf16[432,128]{1,0:T(8,128)(2,1)S(1)} %get-tuple-element.130), channel_id=1, source_target_pairs={{0,6},{2,4},{4,2},{6,0},{1,7},{3,5},{5,3},{7,1},{8,14},{10,12},{12... | collective-permute-start | bytes 331784 | tf_op jit(solution)/shard_map/ppermute | solution.py:777
  79.1 1.6 %collective-permute-start.15 = (f32[128,512]{1,0:T(8,128)S(1)}, f32[128,512]{1,0:T(8,128)S(1)}, u32[]{:S(2)}, u32[]{:S(2)}) collective-permute-start(f32[128,512]{1,0:T(8,128)S(1)} %get-tuple-element.133), channel_id=1, source_target_pairs={{0,1},{1,0},{2,3},{3,2},{4,5},{5,4},{6,7},{7,6},{8,9},{9,8},{10,11... | collective-permute-start | bytes 786440 | tf_op jit(solution)/shard_map/ppermute | solution.py:773
  79.1 1.5 %collective-permute-start.14 = (f32[24,128]{1,0:T(8,128)S(1)}, f32[24,128]{1,0:T(8,128)S(1)}, u32[]{:S(2)}, u32[]{:S(2)}) collective-permute-start(f32[24,128]{1,0:T(8,128)S(1)} %vectors.1.own_ref), channel_id=1, source_target_pairs={{0,1},{1,0},{2,3},{3,2},{4,5},{5,4},{6,7},{7,6},{8,9},{9,8},{10,11... | collective-permute-start | bytes 36872 | tf_op jit(solution)/shard_map/ppermute | solution.py:773

commit v9 on v8

--- a/solution.py
+++ b/solution.py
@@ -615,7 +615,7 @@
             side[here, :] = jnp.where(flip, even, odd).astype(BF16)
     all_ref[...] = dot(dv, b_ref[...], NN)
     away = all_ref[other_rows(half), :]
-    dnaway_ref[...] = away
+    dnaway_ref[...] = away.astype(BF16)
     own = all_ref[own_rows(half), :] + dmixed_ref[...] * feat_ref[1:2]
     dn_ref[...] = own
     to_scale = column_sum(own * xhat_ref[own_rows(half), :]) + column_sum(away * xhat_ref[other_rows(half), :])
@@ -654,7 +654,7 @@
 def input_grad(dn_ref, got_ref, up_ref, xhat_ref, inv_ref, feat_ref, gin_ref, tiles):
     rows, width = up_ref.shape
     xhat = xhat_ref[own_rows(rows), :]
-    d_xhat = (dn_ref[...] + got_ref[...]) * feat_ref[0:1]
+    d_xhat = (dn_ref[...] + got_ref[...].astype(F32)) * feat_ref[0:1]
     mean = jnp.sum(d_xhat, axis=1, keepdims=True) / width
     mean_hat = jnp.sum(d_xhat * xhat, axis=1, keepdims=True) / width
     in_tiles(tiles, slice(None), inv_ref[:, 0:1] * (d_xhat - mean - xhat * mean_hat))
@@ -874,7 +874,7 @@
         came = tied(came, leave_cw)
     stay_b, y_b, x_b, xy_b, d_normed, away = call(
         third_kernel,
-        (*[sds((432, 128), BF16)] * 4, sds((rows, width)), sds((rows, width))),
+        (*[sds((432, 128), BF16)] * 4, sds((rows, width)), sds((rows, width), BF16)),
         (came, starts, count, normed, xhat, v, lane, row_prm, feat, state, d_state, enter, d_mixed, part, b_all),
         [pltpu.VMEM((8, 128), F32), pltpu.VMEM((pair, 512), BF16), pltpu.VMEM((pair, width), F32), pltpu.VMEM((24, 128), F32)],
     )

time: 82 us -> 81.8 us (level)
  no operation moved by 1% of the time
where the time goes in v9:
time: 81.8 us; the launch traced here: 81.5 us
  blocking collectives  46.8 us (57%)
  starting transfers between devices  13.6 us (17%)
  waiting for transfers between devices  10.7 us (13%)
  Pallas kernels  9.33 us (11%)
  between operations  0.82 us (1%)
    all_to_all x2, blocking collectives, on_device(): came = lax.all_to_all(carry, same_core, 0, 0, tiled=True)  21 us
    all_to_all x1, blocking collectives, on_device(): mine = lax.all_to_all(sent, 'fz', 0, 0, tiled=True)  15.6 us
    all_to_all x1, blocking collectives, on_device(): got = lax.all_to_all(sent, 'fz', 0, 0, tiled=True)  10.2 us
    ppermute x14, starting transfers between devices, swap(): return lax.ppermute(value, axis, [(0, 1), (1, 0)])  10 us
    pallas_call x16, Pallas kernels, call(): pl.pallas_call(kernel, out_shape=outs, in_specs=specs or [VM] * len(args)...  9.33 us
    ppermute x14, waiting for transfers between devices, swap(): return lax.ppermute(value, axis, [(0, 1), (1, 0)])  8.01 us
    ppermute x2, starting transfers between devices, across(): return lax.ppermute(value, ('fx', 'ty'), [(n, 3 - n) for n in range(4)])  3.58 us
    ppermute x2, waiting for transfers between devices, across(): return lax.ppermute(value, ('fx', 'ty'), [(n, 3 - n) for n in range(4)])  2.66 us
  transfers between devices with their start and end apart: 16, of which 7 were waited for; matrix products, arithmetic and copies ran while one was open for 0% of the time, Pallas kernels for 6%

profile of v9, /device:TPU:0, one launch (start us, length us, event | category | flops | bytes accessed | tf_op | source)
XLA Modules:
  0.0 81.5 jit_solution(17511554199728767866)
XLA Ops:
  0.7 1.8 %pack.1 = (bf16[4,272,128]{2,1,0:T(8,128)(2,1)}, f32[4,128]{1,0:T(4,128)}) custom-call(s32[4]{0:T(128)} %refs_0_.1, bf16[64,96]{1,0:T(8,128)(2,1)} %bitcast.44, bf16[64,96]{1,0:T(8,128)(2,1)} %bitcast.45, bf16[64,96]{1,0:T(8,128)(2,1)} %bitcast.46, bf16[64,96]{1,0:T(8,128)(2,1)} %bitcast.47, bf16[64,512]{1,0:T(8,128)(2,1)} %bitcast.43, ...), custom_call_target="tpu_custom_call" | custom-call | bytes 5400000 | tf_op jit(solution)/shard_map/pack/pallas_call | solution.py:756
  2.4 15.6 %all_to_all.20 = bf16[4,272,128]{2,1,0:T(8,128)(2,1)S(1)} all-to-all(bf16[4,272,128]{2,1,0:T(8,128)(2,1)} %get-tuple-element.82), channel_id=1, replica_groups=mesh['fz'=4,'fx'=2,'ty'=2,'tc'=2] {'fz'}, dimensions={0} | all-to-all | bytes 557056 | tf_op jit(solution)/shard_map/all_to_all | solution.py:811
  18.0 1.6 %collective-permute-start.3 = (bf16[4,160,128]{2,1,0:T(8,128)(2,1)S(1)}, bf16[4,160,128]{2,1,0:T(8,128)(2,1)S(1)}, u32[]{:S(2)}, u32[]{:S(2)}) collective-permute-start(bf16[4,160,128]{2,1,0:T(8,128)(2,1)S(1)} %slice.13), channel_id=1, source_target_pairs={{0,2},{2,0},{1,3},{3,1},{4,6},{6,4},{5,7},{7,5},{8,10},{10,8},{9,1... | collective-permute-start | bytes 491528 | tf_op jit(solution)/shard_map/ppermute | solution.py:773
  19.6 1.7 %collective-permute-start.2 = (bf16[4,112,128]{2,1,0:T(8,128)(2,1)S(1)}, bf16[4,112,128]{2,1,0:T(8,128)(2,1)S(1)}, u32[]{:S(2)}, u32[]{:S(2)}) collective-permute-start(bf16[4,112,128]{2,1,0:T(8,128)(2,1)S(1)} %slice.12), channel_id=1, source_target_pairs={{0,6},{2,4},{4,2},{6,0},{1,7},{3,5},{5,3},{7,1},{8,14},{10,12},{12... | collective-permute-start | bytes 344072 | tf_op jit(solution)/shard_map/ppermute | solution.py:777
  21.9 1.2 %collective-permute-start = (bf16[4,112,128]{2,1,0:T(8,128)(2,1)S(1)}, bf16[4,112,128]{2,1,0:T(8,128)(2,1)S(1)}, u32[]{:S(2)}, u32[]{:S(2)}) collective-permute-start(bf16[4,112,128]{2,1,0:T(8,128)(2,1)S(1)} %slice.12), channel_id=1, source_target_pairs={{0,2},{2,0},{1,3},{3,1},{4,6},{6,4},{5,7},{7,5},{8,10},{10,8},{9,1... | collective-permute-start | bytes 344072 | tf_op jit(solution)/shard_map/ppermute | solution.py:773
  23.1 0.7 standardize.1
  23.8 2.7 %collective-permute-done.2 = bf16[4,112,128]{2,1,0:T(8,128)(2,1)S(1)} collective-permute-done((bf16[4,112,128]{2,1,0:T(8,128)(2,1)S(1)}, bf16[4,112,128]{2,1,0:T(8,128)(2,1)S(1)}, u32[]{:S(2)}, u32[]{:S(2)}) %collective-permute-start.2) | collective-permute-done | bytes 114720 | tf_op jit(solution)/shard_map/ppermute | solution.py:777
  26.5 1.4 %collective-permute-done.1 = bf16[4,112,128]{2,1,0:T(8,128)(2,1)S(1)} collective-permute-done((bf16[4,112,128]{2,1,0:T(8,128)(2,1)S(1)}, bf16[4,112,128]{2,1,0:T(8,128)(2,1)S(1)}, u32[]{:S(2)}, u32[]{:S(2)}) %collective-permute-start.1) | collective-permute-done | bytes 114720 | tf_op jit(solution)/shard_map/ppermute | solution.py:773
  28.6 1.6 %collective-permute-start.5 = (bf16[2,4,160,128]{3,2,1,0:T(8,128)(2,1)S(1)}, bf16[2,4,160,128]{3,2,1,0:T(8,128)(2,1)S(1)}, u32[]{:S(2)}, u32[]{:S(2)}) collective-permute-start(bf16[2,4,160,128]{3,2,1,0:T(8,128)(2,1)S(1)} %pad_maximum_fusion.2), channel_id=1, source_target_pairs={{0,4},{4,0},{1,5},{5,1},{2,6},{6,2},{3,7},{7,3},{8,12},{12,8},{9,1... | collective-permute-start | bytes 983048 | tf_op jit(solution)/shard_map/ppermute | solution.py:773
  30.9 10.9 %all_to_all.21.recv_ref = f32[16,4,128]{2,1,0:T(4,128)S(1)} all-to-all(f32[16,4,128]{2,1,0:T(4,128)S(1)} %get-tuple-element.94), channel_id=1, replica_groups=mesh['fz'=4,'fx'=2,'ty'=2,'tc'=2] {'fz','fx','ty'}, dimensions={0} | all-to-all | bytes 65536 | tf_op jit(solution)/shard_map/all_to_all | solution.py:833
  43.6 0.9 %collective-permute-done.6.got_ref = f32[128,512]{1,0:T(8,128)S(1)} collective-permute-done((f32[128,512]{1,0:T(8,128)S(1)}, f32[128,512]{1,0:T(8,128)S(1)}, u32[]{:S(2)}, u32[]{:S(2)}) %collective-permute-start.6) | collective-permute-done | bytes 262176 | tf_op jit(solution)/shard_map/ppermute | solution.py:773
  44.5 0.6 second.1
  45.6 0.8 sums.1
  46.9 0.8 back.1
  47.6 0.7 collective-permute-start.9
  48.3 10.2 %all_to_all.22.recv_ref = f32[16,4,128]{2,1,0:T(4,128)S(1)} all-to-all(f32[16,4,128]{2,1,0:T(4,128)S(1)} %get-tuple-element.113), channel_id=1, replica_groups=mesh['fz'=4,'fx'=2,'ty'=2,'tc'=2] {'fz','fx','ty'}, dimensions={0} | all-to-all | bytes 65536 | tf_op jit(solution)/shard_map/all_to_all | solution.py:869
  58.6 1.1 %collective-permute-start.10 = (bf16[4,160,128]{2,1,0:T(8,128)(2,1)S(1)}, bf16[4,160,128]{2,1,0:T(8,128)(2,1)S(1)}, u32[]{:S(2)}, u32[]{:S(2)}) collective-permute-start(bf16[4,160,128]{2,1,0:T(8,128)(2,1)S(1)} %get-tuple-element.119), channel_id=1, source_target_pairs={{0,2},{2,0},{1,3},{3,1},{4,6},{6,4},{5,7},{7,5},{8,10},{10,8},{9,1... | collective-permute-start | bytes 491528 | tf_op jit(solution)/shard_map/ppermute | solution.py:773
  59.7 1.0 %third.1 = (bf16[432,128]{1,0:T(8,128)(2,1)S(1)}, bf16[432,128]{1,0:T(8,128)(2,1)S(1)}, bf16[432,128]{1,0:T(8,128)(2,1)S(1)}, bf16[432,128]{1,0:T(8,128)(2,1)S(1...) custom-call(f32[16,4,128]{2,1,0:T(4,128)S(1)} %all_to_all.22.recv_ref, f32[4,128]{1,0:T(4,128)S(1)} %copy-done.2, ...), custom_call_target="tpu_custom_call" | custom-call | bytes 5400000 | tf_op jit(solution)/shard_map/third/pallas_call | solution.py:756
  60.7 1.1 %collective-permute-start.11 = (bf16[432,128]{1,0:T(8,128)(2,1)S(1)}, bf16[432,128]{1,0:T(8,128)(2,1)S(1)}, u32[]{:S(2)}, u32[]{:S(2)}) collective-permute-start(bf16[432,128]{1,0:T(8,128)(2,1)S(1)} %get-tuple-element.128), channel_id=1, source_target_pairs={{0,2},{2,0},{1,3},{3,1},{4,6},{6,4},{5,7},{7,5},{8,10},{10,8},{9,1... | collective-permute-start | bytes 331784 | tf_op jit(solution)/shard_map/ppermute | solution.py:773
  62.4 1.9 %collective-permute-start.13 = (bf16[432,128]{1,0:T(8,128)(2,1)S(1)}, bf16[432,128]{1,0:T(8,128)(2,1)S(1)}, u32[]{:S(2)}, u32[]{:S(2)}) collective-permute-start(bf16[432,128]{1,0:T(8,128)(2,1)S(1)} %get-tuple-element.130), channel_id=1, source_target_pairs={{0,6},{2,4},{4,2},{6,0},{1,7},{3,5},{5,3},{7,1},{8,14},{10,12},{12... | collective-permute-start | bytes 331784 | tf_op jit(solution)/shard_map/ppermute | solution.py:777
  64.3 4.4 %collective-permute-done.11.y_ref = bf16[432,128]{1,0:T(8,128)(2,1)S(1)} collective-permute-done((bf16[432,128]{1,0:T(8,128)(2,1)S(1)}, bf16[432,128]{1,0:T(8,128)(2,1)S(1)}, u32[]{:S(2)}, u32[]{:S(2)}) %collective-permute-start.11) | collective-permute-done | bytes 110624 | tf_op jit(solution)/shard_map/ppermute | solution.py:773
  68.8 10.2 %all_to_all.23.got_ref = bf16[4,304,128]{2,1,0:T(8,128)(2,1)S(1)} all-to-all(bf16[4,304,128]{2,1,0:T(8,128)(2,1)S(1)} %plane_add.1), channel_id=1, replica_groups=mesh['fz'=4,'fx'=2,'ty'=2,'tc'=2] {'fz'}, dimensions={0} | all-to-all | bytes 622592 | tf_op jit(solution)/shard_map/all_to_all | solution.py:897
  79.7 0.8 matrices.1
  80.5 1.0 %finish.1 = (f32[128,512]{1,0:T(8,128)}, f32[1,16]{1,0:T(1,128)}, f32[1,512]{1,0:T(1,128)}, f32[1,512]{1,0:T(1,128)}, f32[1,512]{1,0:T(1,128)}, /*index=5*/f32[3...) custom-call(f32[24,128]{1,0:T(8,128)S(1)} %vectors.1.own_ref, f32[24,128]{1,0:T(8,128)S(1)} %collective-permute-done.14.other_ref, ...), custom_call_target="tpu_custom_call" | custom-call | bytes 1440000 | tf_op jit(solution)/shard_map/finish/pallas_call | solution.py:756
  (40 shorter events, 6.2 us)
Async XLA Ops:
  18.0 1.6 %copy-start = (bf16[128,512]{1,0:T(8,128)(2,1)S(1)}, bf16[128,512]{1,0:T(8,128)(2,1)}, u32[]{:S(2)}) copy-start(bf16[128,512]{1,0:T(8,128)(2,1)} %x_ref.3) | copy-start | bytes 393220
  18.0 5.1 %copy-start.1 = (bf16[128,512]{1,0:T(8,128)(2,1)S(1)}, bf16[128,512]{1,0:T(8,128)(2,1)}, u32[]{:S(2)}) copy-start(bf16[128,512]{1,0:T(8,128)(2,1)} %up_ref.3) | copy-start | bytes 393220
  18.0 5.1 %copy-start.2 = (f32[4,128]{1,0:T(4,128)S(1)}, f32[4,128]{1,0:T(4,128)}, u32[]{:S(2)}) copy-start(f32[4,128]{1,0:T(4,128)} %get-tuple-element.85.start_ref) | copy-start | bytes 6148
  18.0 10.5 %collective-permute-start.3 = (bf16[4,160,128]{2,1,0:T(8,128)(2,1)S(1)}, bf16[4,160,128]{2,1,0:T(8,128)(2,1)S(1)}, u32[]{:S(2)}, u32[]{:S(2)}) collective-permute-start(bf16[4,160,128]{2,1,0:T(8,128)(2,1)S(1)} %slice.13), channel_id=1, source_target_pairs={{0,2},{2,0},{1,3},{3,1},{4,6},{6,4},{5,7},{7,5},{8,10},{10,8},{9,1... | collective-permute-start | bytes 491528 | tf_op jit(solution)/shard_map/ppermute | solution.py:773
  19.6 3.5 %collective-permute-start.4 = (bf16[128,512]{1,0:T(8,128)(2,1)S(1)}, bf16[128,512]{1,0:T(8,128)(2,1)S(1)}, u32[]{:S(2)}, u32[]{:S(2)}) collective-permute-start(bf16[128,512]{1,0:T(8,128)(2,1)S(1)} %copy-done), channel_id=1, source_target_pairs={{0,1},{1,0},{2,3},{3,2},{4,5},{5,4},{6,7},{7,6},{8,9},{9,8},{10,11... | collective-permute-start | bytes 393224 | tf_op jit(solution)/shard_map/ppermute | solution.py:773
  19.6 6.8 %collective-permute-start.2 = (bf16[4,112,128]{2,1,0:T(8,128)(2,1)S(1)}, bf16[4,112,128]{2,1,0:T(8,128)(2,1)S(1)}, u32[]{:S(2)}, u32[]{:S(2)}) collective-permute-start(bf16[4,112,128]{2,1,0:T(8,128)(2,1)S(1)} %slice.12), channel_id=1, source_target_pairs={{0,6},{2,4},{4,2},{6,0},{1,7},{3,5},{5,3},{7,1},{8,14},{10,12},{12... | collective-permute-start | bytes 344072 | tf_op jit(solution)/shard_map/ppermute | solution.py:777
  21.3 6.6 %collective-permute-start.1 = (bf16[4,112,128]{2,1,0:T(8,128)(2,1)S(1)}, bf16[4,112,128]{2,1,0:T(8,128)(2,1)S(1)}, u32[]{:S(2)}, u32[]{:S(2)}) collective-permute-start(bf16[4,112,128]{2,1,0:T(8,128)(2,1)S(1)} %slice.12), channel_id=1, source_target_pairs={{0,4},{4,0},{1,5},{5,1},{2,6},{6,2},{3,7},{7,3},{8,12},{12,8},{9,1... | collective-permute-start | bytes 344072 | tf_op jit(solution)/shard_map/ppermute | solution.py:773
  21.9 6.7 %collective-permute-start = (bf16[4,112,128]{2,1,0:T(8,128)(2,1)S(1)}, bf16[4,112,128]{2,1,0:T(8,128)(2,1)S(1)}, u32[]{:S(2)}, u32[]{:S(2)}) collective-permute-start(bf16[4,112,128]{2,1,0:T(8,128)(2,1)S(1)} %slice.12), channel_id=1, source_target_pairs={{0,2},{2,0},{1,3},{3,1},{4,6},{6,4},{5,7},{7,5},{8,10},{10,8},{9,1... | collective-permute-start | bytes 344072 | tf_op jit(solution)/shard_map/ppermute | solution.py:773
  28.6 13.2 %collective-permute-start.5 = (bf16[2,4,160,128]{3,2,1,0:T(8,128)(2,1)S(1)}, bf16[2,4,160,128]{3,2,1,0:T(8,128)(2,1)S(1)}, u32[]{:S(2)}, u32[]{:S(2)}) collective-permute-start(bf16[2,4,160,128]{3,2,1,0:T(8,128)(2,1)S(1)} %pad_maximum_fusion.2), channel_id=1, source_target_pairs={{0,4},{4,0},{1,5},{5,1},{2,6},{6,2},{3,7},{7,3},{8,12},{12,8},{9,1... | collective-permute-start | bytes 983048 | tf_op jit(solution)/shard_map/ppermute | solution.py:773
  41.9 1.7 %collective-permute-start.7 = (bf16[2,2,4,64,128]{4,3,2,1,0:T(8,128)(2,1)S(1)}, bf16[2,2,4,64,128]{4,3,2,1,0:T(8,128)(2,1)S(1)}, u32[]{:S(2)}, u32[]{:S(2)}) collective-permute-start(bf16[2,2,4,64,128]{4,3,2,1,0:T(8,128)(2,1)S(1)} %fusion), channel_id=1, source_target_pairs={{0,1},{1,0},{2,3},{3,2},{4,5},{5,4},{6,7},{7,6},{8,9},{9,8},{10,11... | collective-permute-start | bytes 786440 | tf_op jit(solution)/shard_map/ppermute | solution.py:773
  42.8 1.7 %collective-permute-start.6 = (f32[128,512]{1,0:T(8,128)S(1)}, f32[128,512]{1,0:T(8,128)S(1)}, u32[]{:S(2)}, u32[]{:S(2)}) collective-permute-start(f32[128,512]{1,0:T(8,128)S(1)} %readout.3), channel_id=1, source_target_pairs={{0,1},{1,0},{2,3},{3,2},{4,5},{5,4},{6,7},{7,6},{8,9},{9,8},{10,11... | collective-permute-start | bytes 786440 | tf_op jit(solution)/shard_map/ppermute | solution.py:773
  45.2 1.7 %collective-permute-start.8 = (bf16[128,1280]{1,0:T(8,128)(2,1)S(1)}, bf16[128,1280]{1,0:T(8,128)(2,1)S(1)}, u32[]{:S(2)}, u32[]{:S(2)}) collective-permute-start(bf16[128,1280]{1,0:T(8,128)(2,1)S(1)} %get-tuple-element.110), channel_id=1, source_target_pairs={{0,1},{1,0},{2,3},{3,2},{4,5},{5,4},{6,7},{7,6},{8,9},{9,8},{10,11... | collective-permute-start | bytes 983048 | tf_op jit(solution)/shard_map/ppermute | solution.py:773
  47.6 10.9 %collective-permute-start.9 = (bf16[2,4,160,128]{3,2,1,0:T(8,128)(2,1)S(1)}, bf16[2,4,160,128]{3,2,1,0:T(8,128)(2,1)S(1)}, u32[]{:S(2)}, u32[]{:S(2)}) collective-permute-start(bf16[2,4,160,128]{3,2,1,0:T(8,128)(2,1)S(1)} %get-tuple-element.114), channel_id=1, source_target_pairs={{0,4},{4,0},{1,5},{5,1},{2,6},{6,2},{3,7},{7,3},{8,12},{12,8},{9,1... | collective-permute-start | bytes 983048 | tf_op jit(solution)/shard_map/ppermute | solution.py:773
  58.6 10.1 %collective-permute-start.10 = (bf16[4,160,128]{2,1,0:T(8,128)(2,1)S(1)}, bf16[4,160,128]{2,1,0:T(8,128)(2,1)S(1)}, u32[]{:S(2)}, u32[]{:S(2)}) collective-permute-start(bf16[4,160,128]{2,1,0:T(8,128)(2,1)S(1)} %get-tuple-element.119), channel_id=1, source_target_pairs={{0,2},{2,0},{1,3},{3,1},{4,6},{6,4},{5,7},{7,5},{8,10},{10,8},{9,1... | collective-permute-start | bytes 491528 | tf_op jit(solution)/shard_map/ppermute | solution.py:773
  60.7 8.0 %collective-permute-start.11 = (bf16[432,128]{1,0:T(8,128)(2,1)S(1)}, bf16[432,128]{1,0:T(8,128)(2,1)S(1)}, u32[]{:S(2)}, u32[]{:S(2)}) collective-permute-start(bf16[432,128]{1,0:T(8,128)(2,1)S(1)} %get-tuple-element.128), channel_id=1, source_target_pairs={{0,2},{2,0},{1,3},{3,1},{4,6},{6,4},{5,7},{7,5},{8,10},{10,8},{9,1... | collective-permute-start | bytes 331784 | tf_op jit(solution)/shard_map/ppermute | solution.py:773
  61.8 6.9 %collective-permute-start.12 = (bf16[432,128]{1,0:T(8,128)(2,1)S(1)}, bf16[432,128]{1,0:T(8,128)(2,1)S(1)}, u32[]{:S(2)}, u32[]{:S(2)}) collective-permute-start(bf16[432,128]{1,0:T(8,128)(2,1)S(1)} %get-tuple-element.129), channel_id=1, source_target_pairs={{0,4},{4,0},{1,5},{5,1},{2,6},{6,2},{3,7},{7,3},{8,12},{12,8},{9,1... | collective-permute-start | bytes 331784 | tf_op jit(solution)/shard_map/ppermute | solution.py:773
  62.4 6.3 %collective-permute-start.13 = (bf16[432,128]{1,0:T(8,128)(2,1)S(1)}, bf16[432,128]{1,0:T(8,128)(2,1)S(1)}, u32[]{:S(2)}, u32[]{:S(2)}) collective-permute-start(bf16[432,128]{1,0:T(8,128)(2,1)S(1)} %get-tuple-element.130), channel_id=1, source_target_pairs={{0,6},{2,4},{4,2},{6,0},{1,7},{3,5},{5,3},{7,1},{8,14},{10,12},{12... | collective-permute-start | bytes 331784 | tf_op jit(solution)/shard_map/ppermute | solution.py:777
  79.1 1.4 %collective-permute-start.15 = (bf16[128,512]{1,0:T(8,128)(2,1)S(1)}, bf16[128,512]{1,0:T(8,128)(2,1)S(1)}, u32[]{:S(2)}, u32[]{:S(2)}) collective-permute-start(bf16[128,512]{1,0:T(8,128)(2,1)S(1)} %get-tuple-element.133), channel_id=1, source_target_pairs={{0,1},{1,0},{2,3},{3,2},{4,5},{5,4},{6,7},{7,6},{8,9},{9,8},{10,11... | collective-permute-start | bytes 393224 | tf_op jit(solution)/shard_map/ppermute | solution.py:773
  79.1 1.4 %collective-permute-start.14 = (f32[24,128]{1,0:T(8,128)S(1)}, f32[24,128]{1,0:T(8,128)S(1)}, u32[]{:S(2)}, u32[]{:S(2)}) collective-permute-start(f32[24,128]{1,0:T(8,128)S(1)} %vectors.1.own_ref), channel_id=1, source_target_pairs={{0,1},{1,0},{2,3},{3,2},{4,5},{5,4},{6,7},{7,6},{8,9},{9,8},{10,11... | collective-permute-start | bytes 36872 | tf_op jit(solution)/shard_map/ppermute | solution.py:773

commit v10 on v9

--- a/solution.py
+++ b/solution.py
@@ -259,15 +259,14 @@
     count_ref[...] = starts_until(offsets_of(start_ref), pair_pos() * 2 * rows, 2 * rows)
 
 
-def norm_kernel(xhat_ref, g_ref, normed_ref, feat_ref):
+def first_kernel(
+    pairs, xhat_ref, count_ref, g_ref, normed_ref, feat_ref, b_ref, v_ref, lane_ref, row_ref, send_ref, scratch
+):
+    rows = normed_ref.shape[0]
     scale, bias = feature_rows(g_ref, VEC)
     feat_ref[0:1] = scale
     feat_ref[1:2], feat_ref[2:3] = feature_rows(g_ref, VEC + 1)
     normed_ref[...] = (xhat_ref[...] * scale + bias).astype(BF16)
-
-
-def first_kernel(pairs, normed_ref, count_ref, g_ref, b_ref, v_ref, lane_ref, row_ref, send_ref, scratch):
-    rows = normed_ref.shape[0]
     natural(lambda m, z, x: g_ref[lax.axis_index("fx") ^ x, m, z, 0:96, :], b_ref)
     v_ref[...] = dot(normed_ref[...], b_ref[...], NT)
 
@@ -823,11 +822,10 @@
             ln_scale, ln_bias, decay_rate, lam_im, log_dt, in_re, in_im, out_re, out_im, skip, glu_weight, glu_bias
         )
 
-    normed, feat = call(norm_kernel, (sds((pair, width), BF16), sds((8, width))), (xhat, g))
-    b_all, v, lane, row_prm, carry = call(
+    normed, feat, b_all, v, lane, row_prm, carry = call(
         functools.partial(first_kernel, pairs),
-        (sds((512, width), BF16), sds((pair, 512)), sds((8, 256)), sds((8, 8, 128)), sds((pairs, 4, 128))),
-        (normed, count, g),
+        (sds((pair, width), BF16), sds((8, width)), sds((512, width), BF16), sds((pair, 512)), sds((8, 256)), sds((8, 8, 128)), sds((pairs, 4, 128))),
+        (xhat, count, g),
         [pltpu.VMEM((8, 128), F32)],
     )
     came = lax.all_to_all(carry, same_core, 0, 0, tiled=True)

time: 81.8 us -> 81.7 us (level)
    pallas_call x16 -> x15, Pallas kernels: 9.33 us -> 9.24 us  [call(): pl.pallas_call(kernel, out_shape=outs, in_specs=specs or [VM] * len(args)...]
where the time goes in v10:
time: 81.7 us; the launch traced here: 81.3 us
  blocking collectives  46.8 us (57%)
  starting transfers between devices  13.6 us (17%)
  waiting for transfers between devices  10.7 us (13%)
  Pallas kernels  9.24 us (11%)
    all_to_all x2, blocking collectives, on_device(): came = lax.all_to_all(carry, same_core, 0, 0, tiled=True)  21 us
    all_to_all x1, blocking collectives, on_device(): mine = lax.all_to_all(sent, 'fz', 0, 0, tiled=True)  15.6 us
    all_to_all x1, blocking collectives, on_device(): got = lax.all_to_all(sent, 'fz', 0, 0, tiled=True)  10.2 us
    ppermute x14, starting transfers between devices, swap(): return lax.ppermute(value, axis, [(0, 1), (1, 0)])  10 us
    pallas_call x15, Pallas kernels, call(): pl.pallas_call(kernel, out_shape=outs, in_specs=specs or [VM] * len(args)...  9.24 us
    ppermute x14, waiting for transfers between devices, swap(): return lax.ppermute(value, axis, [(0, 1), (1, 0)])  7.99 us
    ppermute x2, starting transfers between devices, across(): return lax.ppermute(value, ('fx', 'ty'), [(n, 3 - n) for n in range(4)])  3.59 us
    ppermute x2, waiting for transfers between devices, across(): return lax.ppermute(value, ('fx', 'ty'), [(n, 3 - n) for n in range(4)])  2.67 us
  transfers between devices with their start and end apart: 16, of which 7 were waited for; matrix products, arithmetic and copies ran while one was open for 0% of the time, Pallas kernels for 6%

profile of v10, /device:TPU:0, one launch (start us, length us, event | category | flops | bytes accessed | tf_op | source)
XLA Modules:
  0.0 81.3 jit_solution(15334528779354603055)
XLA Ops:
  0.7 1.8 %pack.1 = (bf16[4,272,128]{2,1,0:T(8,128)(2,1)}, f32[4,128]{1,0:T(4,128)}) custom-call(s32[4]{0:T(128)} %refs_0_.1, bf16[64,96]{1,0:T(8,128)(2,1)} %bitcast.43, bf16[64,96]{1,0:T(8,128)(2,1)} %bitcast.44, bf16[64,96]{1,0:T(8,128)(2,1)} %bitcast.45, bf16[64,96]{1,0:T(8,128)(2,1)} %bitcast.46, bf16[64,512]{1,0:T(8,128)(2,1)} %bitcast.42, ...), custom_call_target="tpu_custom_call" | custom-call | bytes 5400000 | tf_op jit(solution)/shard_map/pack/pallas_call | solution.py:755
  2.4 15.6 %all_to_all.20 = bf16[4,272,128]{2,1,0:T(8,128)(2,1)S(1)} all-to-all(bf16[4,272,128]{2,1,0:T(8,128)(2,1)} %get-tuple-element.82), channel_id=1, replica_groups=mesh['fz'=4,'fx'=2,'ty'=2,'tc'=2] {'fz'}, dimensions={0} | all-to-all | bytes 557056 | tf_op jit(solution)/shard_map/all_to_all | solution.py:810
  18.1 1.6 %collective-permute-start.3 = (bf16[4,160,128]{2,1,0:T(8,128)(2,1)S(1)}, bf16[4,160,128]{2,1,0:T(8,128)(2,1)S(1)}, u32[]{:S(2)}, u32[]{:S(2)}) collective-permute-start(bf16[4,160,128]{2,1,0:T(8,128)(2,1)S(1)} %slice.13), channel_id=1, source_target_pairs={{0,2},{2,0},{1,3},{3,1},{4,6},{6,4},{5,7},{7,5},{8,10},{10,8},{9,1... | collective-permute-start | bytes 491528 | tf_op jit(solution)/shard_map/ppermute | solution.py:772
  19.6 1.7 %collective-permute-start.2 = (bf16[4,112,128]{2,1,0:T(8,128)(2,1)S(1)}, bf16[4,112,128]{2,1,0:T(8,128)(2,1)S(1)}, u32[]{:S(2)}, u32[]{:S(2)}) collective-permute-start(bf16[4,112,128]{2,1,0:T(8,128)(2,1)S(1)} %slice.12), channel_id=1, source_target_pairs={{0,6},{2,4},{4,2},{6,0},{1,7},{3,5},{5,3},{7,1},{8,14},{10,12},{12... | collective-permute-start | bytes 344072 | tf_op jit(solution)/shard_map/ppermute | solution.py:776
  21.9 1.2 %collective-permute-start = (bf16[4,112,128]{2,1,0:T(8,128)(2,1)S(1)}, bf16[4,112,128]{2,1,0:T(8,128)(2,1)S(1)}, u32[]{:S(2)}, u32[]{:S(2)}) collective-permute-start(bf16[4,112,128]{2,1,0:T(8,128)(2,1)S(1)} %slice.12), channel_id=1, source_target_pairs={{0,2},{2,0},{1,3},{3,1},{4,6},{6,4},{5,7},{7,5},{8,10},{10,8},{9,1... | collective-permute-start | bytes 344072 | tf_op jit(solution)/shard_map/ppermute | solution.py:772
  23.1 0.7 standardize.1
  23.8 2.7 %collective-permute-done.2 = bf16[4,112,128]{2,1,0:T(8,128)(2,1)S(1)} collective-permute-done((bf16[4,112,128]{2,1,0:T(8,128)(2,1)S(1)}, bf16[4,112,128]{2,1,0:T(8,128)(2,1)S(1)}, u32[]{:S(2)}, u32[]{:S(2)}) %collective-permute-start.2) | collective-permute-done | bytes 114720 | tf_op jit(solution)/shard_map/ppermute | solution.py:776
  26.5 1.4 %collective-permute-done.1 = bf16[4,112,128]{2,1,0:T(8,128)(2,1)S(1)} collective-permute-done((bf16[4,112,128]{2,1,0:T(8,128)(2,1)S(1)}, bf16[4,112,128]{2,1,0:T(8,128)(2,1)S(1)}, u32[]{:S(2)}, u32[]{:S(2)}) %collective-permute-start.1) | collective-permute-done | bytes 114720 | tf_op jit(solution)/shard_map/ppermute | solution.py:772
  28.6 1.6 %collective-permute-start.5 = (bf16[2,4,160,128]{3,2,1,0:T(8,128)(2,1)S(1)}, bf16[2,4,160,128]{3,2,1,0:T(8,128)(2,1)S(1)}, u32[]{:S(2)}, u32[]{:S(2)}) collective-permute-start(bf16[2,4,160,128]{3,2,1,0:T(8,128)(2,1)S(1)} %pad_maximum_fusion.2), channel_id=1, source_target_pairs={{0,4},{4,0},{1,5},{5,1},{2,6},{6,2},{3,7},{7,3},{8,12},{12,8},{9,1... | collective-permute-start | bytes 983048 | tf_op jit(solution)/shard_map/ppermute | solution.py:772
  30.8 10.9 %all_to_all.21.recv_ref = f32[16,4,128]{2,1,0:T(4,128)S(1)} all-to-all(f32[16,4,128]{2,1,0:T(4,128)S(1)} %get-tuple-element.93), channel_id=1, replica_groups=mesh['fz'=4,'fx'=2,'ty'=2,'tc'=2] {'fz','fx','ty'}, dimensions={0} | all-to-all | bytes 65536 | tf_op jit(solution)/shard_map/all_to_all | solution.py:831
  43.5 0.9 %collective-permute-done.6.got_ref = f32[128,512]{1,0:T(8,128)S(1)} collective-permute-done((f32[128,512]{1,0:T(8,128)S(1)}, f32[128,512]{1,0:T(8,128)S(1)}, u32[]{:S(2)}, u32[]{:S(2)}) %collective-permute-start.6) | collective-permute-done | bytes 262176 | tf_op jit(solution)/shard_map/ppermute | solution.py:772
  44.4 0.6 second.1
  45.5 0.8 sums.1
  46.8 0.8 back.1
  47.5 0.7 collective-permute-start.9
  48.2 10.2 %all_to_all.22.recv_ref = f32[16,4,128]{2,1,0:T(4,128)S(1)} all-to-all(f32[16,4,128]{2,1,0:T(4,128)S(1)} %get-tuple-element.113), channel_id=1, replica_groups=mesh['fz'=4,'fx'=2,'ty'=2,'tc'=2] {'fz','fx','ty'}, dimensions={0} | all-to-all | bytes 65536 | tf_op jit(solution)/shard_map/all_to_all | solution.py:867
  58.5 1.1 %collective-permute-start.10 = (bf16[4,160,128]{2,1,0:T(8,128)(2,1)S(1)}, bf16[4,160,128]{2,1,0:T(8,128)(2,1)S(1)}, u32[]{:S(2)}, u32[]{:S(2)}) collective-permute-start(bf16[4,160,128]{2,1,0:T(8,128)(2,1)S(1)} %get-tuple-element.119), channel_id=1, source_target_pairs={{0,2},{2,0},{1,3},{3,1},{4,6},{6,4},{5,7},{7,5},{8,10},{10,8},{9,1... | collective-permute-start | bytes 491528 | tf_op jit(solution)/shard_map/ppermute | solution.py:772
  59.6 1.1 %third.1 = (bf16[432,128]{1,0:T(8,128)(2,1)S(1)}, bf16[432,128]{1,0:T(8,128)(2,1)S(1)}, bf16[432,128]{1,0:T(8,128)(2,1)S(1)}, bf16[432,128]{1,0:T(8,128)(2,1)S(1...) custom-call(f32[16,4,128]{2,1,0:T(4,128)S(1)} %all_to_all.22.recv_ref, f32[4,128]{1,0:T(4,128)S(1)} %copy-done.2, ...), custom_call_target="tpu_custom_call" | custom-call | bytes 5400000 | tf_op jit(solution)/shard_map/third/pallas_call | solution.py:755
  60.6 1.1 %collective-permute-start.11 = (bf16[432,128]{1,0:T(8,128)(2,1)S(1)}, bf16[432,128]{1,0:T(8,128)(2,1)S(1)}, u32[]{:S(2)}, u32[]{:S(2)}) collective-permute-start(bf16[432,128]{1,0:T(8,128)(2,1)S(1)} %get-tuple-element.128), channel_id=1, source_target_pairs={{0,2},{2,0},{1,3},{3,1},{4,6},{6,4},{5,7},{7,5},{8,10},{10,8},{9,1... | collective-permute-start | bytes 331784 | tf_op jit(solution)/shard_map/ppermute | solution.py:772
  62.3 1.9 %collective-permute-start.13 = (bf16[432,128]{1,0:T(8,128)(2,1)S(1)}, bf16[432,128]{1,0:T(8,128)(2,1)S(1)}, u32[]{:S(2)}, u32[]{:S(2)}) collective-permute-start(bf16[432,128]{1,0:T(8,128)(2,1)S(1)} %get-tuple-element.130), channel_id=1, source_target_pairs={{0,6},{2,4},{4,2},{6,0},{1,7},{3,5},{5,3},{7,1},{8,14},{10,12},{12... | collective-permute-start | bytes 331784 | tf_op jit(solution)/shard_map/ppermute | solution.py:776
  64.2 4.4 %collective-permute-done.11.y_ref = bf16[432,128]{1,0:T(8,128)(2,1)S(1)} collective-permute-done((bf16[432,128]{1,0:T(8,128)(2,1)S(1)}, bf16[432,128]{1,0:T(8,128)(2,1)S(1)}, u32[]{:S(2)}, u32[]{:S(2)}) %collective-permute-start.11) | collective-permute-done | bytes 110624 | tf_op jit(solution)/shard_map/ppermute | solution.py:772
  68.7 10.2 %all_to_all.23.got_ref = bf16[4,304,128]{2,1,0:T(8,128)(2,1)S(1)} all-to-all(bf16[4,304,128]{2,1,0:T(8,128)(2,1)S(1)} %plane_add.1), channel_id=1, replica_groups=mesh['fz'=4,'fx'=2,'ty'=2,'tc'=2] {'fz'}, dimensions={0} | all-to-all | bytes 622592 | tf_op jit(solution)/shard_map/all_to_all | solution.py:895
  79.5 0.8 matrices.1
  80.4 1.0 %finish.1 = (f32[128,512]{1,0:T(8,128)}, f32[1,16]{1,0:T(1,128)}, f32[1,512]{1,0:T(1,128)}, f32[1,512]{1,0:T(1,128)}, f32[1,512]{1,0:T(1,128)}, /*index=5*/f32[3...) custom-call(f32[24,128]{1,0:T(8,128)S(1)} %vectors.1.own_ref, f32[24,128]{1,0:T(8,128)S(1)} %collective-permute-done.14.other_ref, ...), custom_call_target="tpu_custom_call" | custom-call | bytes 1440000 | tf_op jit(solution)/shard_map/finish/pallas_call | solution.py:755
  (39 shorter events, 6.0 us)
Async XLA Ops:
  18.0 1.6 %copy-start = (bf16[128,512]{1,0:T(8,128)(2,1)S(1)}, bf16[128,512]{1,0:T(8,128)(2,1)}, u32[]{:S(2)}) copy-start(bf16[128,512]{1,0:T(8,128)(2,1)} %x_ref.3) | copy-start | bytes 393220
  18.0 5.1 %copy-start.1 = (bf16[128,512]{1,0:T(8,128)(2,1)S(1)}, bf16[128,512]{1,0:T(8,128)(2,1)}, u32[]{:S(2)}) copy-start(bf16[128,512]{1,0:T(8,128)(2,1)} %up_ref.3) | copy-start | bytes 393220
  18.0 5.1 %copy-start.2 = (f32[4,128]{1,0:T(4,128)S(1)}, f32[4,128]{1,0:T(4,128)}, u32[]{:S(2)}) copy-start(f32[4,128]{1,0:T(4,128)} %get-tuple-element.85.start_ref) | copy-start | bytes 6148
  18.1 10.5 %collective-permute-start.3 = (bf16[4,160,128]{2,1,0:T(8,128)(2,1)S(1)}, bf16[4,160,128]{2,1,0:T(8,128)(2,1)S(1)}, u32[]{:S(2)}, u32[]{:S(2)}) collective-permute-start(bf16[4,160,128]{2,1,0:T(8,128)(2,1)S(1)} %slice.13), channel_id=1, source_target_pairs={{0,2},{2,0},{1,3},{3,1},{4,6},{6,4},{5,7},{7,5},{8,10},{10,8},{9,1... | collective-permute-start | bytes 491528 | tf_op jit(solution)/shard_map/ppermute | solution.py:772
  19.6 3.5 %collective-permute-start.4 = (bf16[128,512]{1,0:T(8,128)(2,1)S(1)}, bf16[128,512]{1,0:T(8,128)(2,1)S(1)}, u32[]{:S(2)}, u32[]{:S(2)}) collective-permute-start(bf16[128,512]{1,0:T(8,128)(2,1)S(1)} %copy-done), channel_id=1, source_target_pairs={{0,1},{1,0},{2,3},{3,2},{4,5},{5,4},{6,7},{7,6},{8,9},{9,8},{10,11... | collective-permute-start | bytes 393224 | tf_op jit(solution)/shard_map/ppermute | solution.py:772
  19.6 6.8 %collective-permute-start.2 = (bf16[4,112,128]{2,1,0:T(8,128)(2,1)S(1)}, bf16[4,112,128]{2,1,0:T(8,128)(2,1)S(1)}, u32[]{:S(2)}, u32[]{:S(2)}) collective-permute-start(bf16[4,112,128]{2,1,0:T(8,128)(2,1)S(1)} %slice.12), channel_id=1, source_target_pairs={{0,6},{2,4},{4,2},{6,0},{1,7},{3,5},{5,3},{7,1},{8,14},{10,12},{12... | collective-permute-start | bytes 344072 | tf_op jit(solution)/shard_map/ppermute | solution.py:776
  21.4 6.6 %collective-permute-start.1 = (bf16[4,112,128]{2,1,0:T(8,128)(2,1)S(1)}, bf16[4,112,128]{2,1,0:T(8,128)(2,1)S(1)}, u32[]{:S(2)}, u32[]{:S(2)}) collective-permute-start(bf16[4,112,128]{2,1,0:T(8,128)(2,1)S(1)} %slice.12), channel_id=1, source_target_pairs={{0,4},{4,0},{1,5},{5,1},{2,6},{6,2},{3,7},{7,3},{8,12},{12,8},{9,1... | collective-permute-start | bytes 344072 | tf_op jit(solution)/shard_map/ppermute | solution.py:772
  21.9 6.7 %collective-permute-start = (bf16[4,112,128]{2,1,0:T(8,128)(2,1)S(1)}, bf16[4,112,128]{2,1,0:T(8,128)(2,1)S(1)}, u32[]{:S(2)}, u32[]{:S(2)}) collective-permute-start(bf16[4,112,128]{2,1,0:T(8,128)(2,1)S(1)} %slice.12), channel_id=1, source_target_pairs={{0,2},{2,0},{1,3},{3,1},{4,6},{6,4},{5,7},{7,5},{8,10},{10,8},{9,1... | collective-permute-start | bytes 344072 | tf_op jit(solution)/shard_map/ppermute | solution.py:772
  28.6 13.1 %collective-permute-start.5 = (bf16[2,4,160,128]{3,2,1,0:T(8,128)(2,1)S(1)}, bf16[2,4,160,128]{3,2,1,0:T(8,128)(2,1)S(1)}, u32[]{:S(2)}, u32[]{:S(2)}) collective-permute-start(bf16[2,4,160,128]{3,2,1,0:T(8,128)(2,1)S(1)} %pad_maximum_fusion.2), channel_id=1, source_target_pairs={{0,4},{4,0},{1,5},{5,1},{2,6},{6,2},{3,7},{7,3},{8,12},{12,8},{9,1... | collective-permute-start | bytes 983048 | tf_op jit(solution)/shard_map/ppermute | solution.py:772
  41.8 1.7 %collective-permute-start.7 = (bf16[2,2,4,64,128]{4,3,2,1,0:T(8,128)(2,1)S(1)}, bf16[2,2,4,64,128]{4,3,2,1,0:T(8,128)(2,1)S(1)}, u32[]{:S(2)}, u32[]{:S(2)}) collective-permute-start(bf16[2,2,4,64,128]{4,3,2,1,0:T(8,128)(2,1)S(1)} %fusion), channel_id=1, source_target_pairs={{0,1},{1,0},{2,3},{3,2},{4,5},{5,4},{6,7},{7,6},{8,9},{9,8},{10,11... | collective-permute-start | bytes 786440 | tf_op jit(solution)/shard_map/ppermute | solution.py:772
  42.7 1.7 %collective-permute-start.6 = (f32[128,512]{1,0:T(8,128)S(1)}, f32[128,512]{1,0:T(8,128)S(1)}, u32[]{:S(2)}, u32[]{:S(2)}) collective-permute-start(f32[128,512]{1,0:T(8,128)S(1)} %readout.3), channel_id=1, source_target_pairs={{0,1},{1,0},{2,3},{3,2},{4,5},{5,4},{6,7},{7,6},{8,9},{9,8},{10,11... | collective-permute-start | bytes 786440 | tf_op jit(solution)/shard_map/ppermute | solution.py:772
  45.1 1.7 %collective-permute-start.8 = (bf16[128,1280]{1,0:T(8,128)(2,1)S(1)}, bf16[128,1280]{1,0:T(8,128)(2,1)S(1)}, u32[]{:S(2)}, u32[]{:S(2)}) collective-permute-start(bf16[128,1280]{1,0:T(8,128)(2,1)S(1)} %get-tuple-element.110), channel_id=1, source_target_pairs={{0,1},{1,0},{2,3},{3,2},{4,5},{5,4},{6,7},{7,6},{8,9},{9,8},{10,11... | collective-permute-start | bytes 983048 | tf_op jit(solution)/shard_map/ppermute | solution.py:772
  47.5 10.8 %collective-permute-start.9 = (bf16[2,4,160,128]{3,2,1,0:T(8,128)(2,1)S(1)}, bf16[2,4,160,128]{3,2,1,0:T(8,128)(2,1)S(1)}, u32[]{:S(2)}, u32[]{:S(2)}) collective-permute-start(bf16[2,4,160,128]{3,2,1,0:T(8,128)(2,1)S(1)} %get-tuple-element.114), channel_id=1, source_target_pairs={{0,4},{4,0},{1,5},{5,1},{2,6},{6,2},{3,7},{7,3},{8,12},{12,8},{9,1... | collective-permute-start | bytes 983048 | tf_op jit(solution)/shard_map/ppermute | solution.py:772
  58.5 10.1 %collective-permute-start.10 = (bf16[4,160,128]{2,1,0:T(8,128)(2,1)S(1)}, bf16[4,160,128]{2,1,0:T(8,128)(2,1)S(1)}, u32[]{:S(2)}, u32[]{:S(2)}) collective-permute-start(bf16[4,160,128]{2,1,0:T(8,128)(2,1)S(1)} %get-tuple-element.119), channel_id=1, source_target_pairs={{0,2},{2,0},{1,3},{3,1},{4,6},{6,4},{5,7},{7,5},{8,10},{10,8},{9,1... | collective-permute-start | bytes 491528 | tf_op jit(solution)/shard_map/ppermute | solution.py:772
  60.6 8.0 %collective-permute-start.11 = (bf16[432,128]{1,0:T(8,128)(2,1)S(1)}, bf16[432,128]{1,0:T(8,128)(2,1)S(1)}, u32[]{:S(2)}, u32[]{:S(2)}) collective-permute-start(bf16[432,128]{1,0:T(8,128)(2,1)S(1)} %get-tuple-element.128), channel_id=1, source_target_pairs={{0,2},{2,0},{1,3},{3,1},{4,6},{6,4},{5,7},{7,5},{8,10},{10,8},{9,1... | collective-permute-start | bytes 331784 | tf_op jit(solution)/shard_map/ppermute | solution.py:772
  61.7 6.9 %collective-permute-start.12 = (bf16[432,128]{1,0:T(8,128)(2,1)S(1)}, bf16[432,128]{1,0:T(8,128)(2,1)S(1)}, u32[]{:S(2)}, u32[]{:S(2)}) collective-permute-start(bf16[432,128]{1,0:T(8,128)(2,1)S(1)} %get-tuple-element.129), channel_id=1, source_target_pairs={{0,4},{4,0},{1,5},{5,1},{2,6},{6,2},{3,7},{7,3},{8,12},{12,8},{9,1... | collective-permute-start | bytes 331784 | tf_op jit(solution)/shard_map/ppermute | solution.py:772
  62.3 6.3 %collective-permute-start.13 = (bf16[432,128]{1,0:T(8,128)(2,1)S(1)}, bf16[432,128]{1,0:T(8,128)(2,1)S(1)}, u32[]{:S(2)}, u32[]{:S(2)}) collective-permute-start(bf16[432,128]{1,0:T(8,128)(2,1)S(1)} %get-tuple-element.130), channel_id=1, source_target_pairs={{0,6},{2,4},{4,2},{6,0},{1,7},{3,5},{5,3},{7,1},{8,14},{10,12},{12... | collective-permute-start | bytes 331784 | tf_op jit(solution)/shard_map/ppermute | solution.py:776
  79.0 1.4 %collective-permute-start.15 = (bf16[128,512]{1,0:T(8,128)(2,1)S(1)}, bf16[128,512]{1,0:T(8,128)(2,1)S(1)}, u32[]{:S(2)}, u32[]{:S(2)}) collective-permute-start(bf16[128,512]{1,0:T(8,128)(2,1)S(1)} %get-tuple-element.133), channel_id=1, source_target_pairs={{0,1},{1,0},{2,3},{3,2},{4,5},{5,4},{6,7},{7,6},{8,9},{9,8},{10,11... | collective-permute-start | bytes 393224 | tf_op jit(solution)/shard_map/ppermute | solution.py:772
  79.0 1.4 %collective-permute-start.14 = (f32[24,128]{1,0:T(8,128)S(1)}, f32[24,128]{1,0:T(8,128)S(1)}, u32[]{:S(2)}, u32[]{:S(2)}) collective-permute-start(f32[24,128]{1,0:T(8,128)S(1)} %vectors.1.own_ref), channel_id=1, source_target_pairs={{0,1},{1,0},{2,3},{3,2},{4,5},{5,4},{6,7},{7,6},{8,9},{9,8},{10,11... | collective-permute-start | bytes 36872 | tf_op jit(solution)/shard_map/ppermute | solution.py:772

commit v11 on v10

--- a/solution.py
+++ b/solution.py
@@ -416,7 +416,7 @@
 
 
 def states_kernel(
-    recv_ref, start_ref, count_ref, v_ref, lane_ref, row_ref, cw_ref, state_ref, twice_ref, enter_ref, c_ref, scratch
+    recv_ref, start_ref, count_ref, v_ref, lane_ref, row_ref, cw_ref, state_ref, twice_ref, enter_ref, c_ref, away_ref, scratch
 ):
     rows = v_ref.shape[0]
     count = count_ref[...]
@@ -438,11 +438,11 @@
     twice_ref[:, 0:256] = state_ref[:, 0:256].astype(BF16) * 2
     twice_ref[:, 256:512] = state_ref[:, 256:512].astype(BF16) * -2
     natural(lambda m, z, x: cw_ref[lax.axis_index("fx") ^ x, m, z, 0:96, :], c_ref)
-
-
-def readout_kernel(core, twice_ref, c_ref, out_ref):
-    where = (own_rows, other_rows)[core](out_ref.shape[0])
-    out_ref[...] = dot(twice_ref[where, :], c_ref[...], NN)
+    away_ref[...] = dot(twice_ref[other_rows(rows // 2), :], c_ref[...], NN)
+
+
+def readout_kernel(twice_ref, c_ref, out_ref):
+    out_ref[...] = dot(twice_ref[own_rows(out_ref.shape[0]), :], c_ref[...], NN)
 
 
 def second_kernel(
@@ -831,16 +831,15 @@
     came = lax.all_to_all(carry, same_core, 0, 0, tiled=True)
     if fast:
         cw = jnp.stack(tied((side_cw, far_cw), came))
-    state, twice, enter, c_all = call(
+    state, twice, enter, c_all, away = call(
         states_kernel,
-        (sds((pair, 512)), sds((pair, 512), BF16), sds((8, 512)), sds((512, width), BF16)),
+        (sds((pair, 512)), sds((pair, 512), BF16), sds((8, 512)), sds((512, width), BF16), sds((rows, width))),
         (came, starts, count, v, lane, row_prm, cw),
         [pltpu.VMEM((8, 128), F32)],
     )
     if fast:
         other_cw = swap(cw[:, :, :, 96:], "tc")
-    readout = lambda core: call(functools.partial(readout_kernel, core), sds((rows, width)), (twice, c_all))
-    away, own = readout(1), readout(0)
+    own = call(readout_kernel, sds((rows, width)), (twice, c_all))
     branch, d_mixed, dlogit, kept, away = call(
         second_kernel,
         (sds((rows, width), BF16), sds((rows, width)), sds((rows, width), BF16), *[sds((rows, 2 * width + 256), BF16)] * 2),

time: 81.7 us -> 81.6 us (level)
    pallas_call x15 -> x14, Pallas kernels: 9.24 us -> 9.24 us  [call(): pl.pallas_call(kernel, out_shape=outs, in_specs=specs or [VM] * len(args)...]
where the time goes in v11:
time: 81.6 us; the launch traced here: 81.3 us
  blocking collectives  46.8 us (57%)
  starting transfers between devices  13.6 us (17%)
  waiting for transfers between devices  10.6 us (13%)
  Pallas kernels  9.24 us (11%)
    all_to_all x2, blocking collectives, on_device(): came = lax.all_to_all(carry, same_core, 0, 0, tiled=True)  21 us
    all_to_all x1, blocking collectives, on_device(): mine = lax.all_to_all(sent, 'fz', 0, 0, tiled=True)  15.6 us
    all_to_all x1, blocking collectives, on_device(): got = lax.all_to_all(sent, 'fz', 0, 0, tiled=True)  10.3 us
    ppermute x14, starting transfers between devices, swap(): return lax.ppermute(value, axis, [(0, 1), (1, 0)])  9.99 us
    pallas_call x14, Pallas kernels, call(): pl.pallas_call(kernel, out_shape=outs, in_specs=specs or [VM] * len(args)...  9.24 us
    ppermute x14, waiting for transfers between devices, swap(): return lax.ppermute(value, axis, [(0, 1), (1, 0)])  7.95 us
    ppermute x2, starting transfers between devices, across(): return lax.ppermute(value, ('fx', 'ty'), [(n, 3 - n) for n in range(4)])  3.58 us
    ppermute x2, waiting for transfers between devices, across(): return lax.ppermute(value, ('fx', 'ty'), [(n, 3 - n) for n in range(4)])  2.66 us
  transfers between devices with their start and end apart: 16, of which 7 were waited for; matrix products, arithmetic and copies ran while one was open for 0% of the time, Pallas kernels for 6%

profile of v11, /device:TPU:0, one launch (start us, length us, event | category | flops | bytes accessed | tf_op | source)
XLA Modules:
  0.0 81.3 jit_solution(13028642275787871379)
XLA Ops:
  0.7 1.8 %pack.1 = (bf16[4,272,128]{2,1,0:T(8,128)(2,1)}, f32[4,128]{1,0:T(4,128)}) custom-call(s32[4]{0:T(128)} %refs_0_.1, bf16[64,96]{1,0:T(8,128)(2,1)} %bitcast.43, bf16[64,96]{1,0:T(8,128)(2,1)} %bitcast.44, bf16[64,96]{1,0:T(8,128)(2,1)} %bitcast.45, bf16[64,96]{1,0:T(8,128)(2,1)} %bitcast.46, bf16[64,512]{1,0:T(8,128)(2,1)} %bitcast.42, ...), custom_call_target="tpu_custom_call" | custom-call | bytes 5400000 | tf_op jit(solution)/shard_map/pack/pallas_call | solution.py:755
  2.4 15.6 %all_to_all.20 = bf16[4,272,128]{2,1,0:T(8,128)(2,1)S(1)} all-to-all(bf16[4,272,128]{2,1,0:T(8,128)(2,1)} %get-tuple-element.83), channel_id=1, replica_groups=mesh['fz'=4,'fx'=2,'ty'=2,'tc'=2] {'fz'}, dimensions={0} | all-to-all | bytes 557056 | tf_op jit(solution)/shard_map/all_to_all | solution.py:810
  18.1 1.6 %collective-permute-start.3 = (bf16[4,160,128]{2,1,0:T(8,128)(2,1)S(1)}, bf16[4,160,128]{2,1,0:T(8,128)(2,1)S(1)}, u32[]{:S(2)}, u32[]{:S(2)}) collective-permute-start(bf16[4,160,128]{2,1,0:T(8,128)(2,1)S(1)} %slice.13), channel_id=1, source_target_pairs={{0,2},{2,0},{1,3},{3,1},{4,6},{6,4},{5,7},{7,5},{8,10},{10,8},{9,1... | collective-permute-start | bytes 491528 | tf_op jit(solution)/shard_map/ppermute | solution.py:772
  19.6 1.7 %collective-permute-start.2 = (bf16[4,112,128]{2,1,0:T(8,128)(2,1)S(1)}, bf16[4,112,128]{2,1,0:T(8,128)(2,1)S(1)}, u32[]{:S(2)}, u32[]{:S(2)}) collective-permute-start(bf16[4,112,128]{2,1,0:T(8,128)(2,1)S(1)} %slice.12), channel_id=1, source_target_pairs={{0,6},{2,4},{4,2},{6,0},{1,7},{3,5},{5,3},{7,1},{8,14},{10,12},{12... | collective-permute-start | bytes 344072 | tf_op jit(solution)/shard_map/ppermute | solution.py:776
  21.9 1.2 %collective-permute-start = (bf16[4,112,128]{2,1,0:T(8,128)(2,1)S(1)}, bf16[4,112,128]{2,1,0:T(8,128)(2,1)S(1)}, u32[]{:S(2)}, u32[]{:S(2)}) collective-permute-start(bf16[4,112,128]{2,1,0:T(8,128)(2,1)S(1)} %slice.12), channel_id=1, source_target_pairs={{0,2},{2,0},{1,3},{3,1},{4,6},{6,4},{5,7},{7,5},{8,10},{10,8},{9,1... | collective-permute-start | bytes 344072 | tf_op jit(solution)/shard_map/ppermute | solution.py:772
  23.1 0.7 standardize.1
  23.8 2.7 %collective-permute-done.2 = bf16[4,112,128]{2,1,0:T(8,128)(2,1)S(1)} collective-permute-done((bf16[4,112,128]{2,1,0:T(8,128)(2,1)S(1)}, bf16[4,112,128]{2,1,0:T(8,128)(2,1)S(1)}, u32[]{:S(2)}, u32[]{:S(2)}) %collective-permute-start.2) | collective-permute-done | bytes 114720 | tf_op jit(solution)/shard_map/ppermute | solution.py:776
  26.5 1.4 %collective-permute-done.1 = bf16[4,112,128]{2,1,0:T(8,128)(2,1)S(1)} collective-permute-done((bf16[4,112,128]{2,1,0:T(8,128)(2,1)S(1)}, bf16[4,112,128]{2,1,0:T(8,128)(2,1)S(1)}, u32[]{:S(2)}, u32[]{:S(2)}) %collective-permute-start.1) | collective-permute-done | bytes 114720 | tf_op jit(solution)/shard_map/ppermute | solution.py:772
  28.6 1.6 %collective-permute-start.5 = (bf16[2,4,160,128]{3,2,1,0:T(8,128)(2,1)S(1)}, bf16[2,4,160,128]{3,2,1,0:T(8,128)(2,1)S(1)}, u32[]{:S(2)}, u32[]{:S(2)}) collective-permute-start(bf16[2,4,160,128]{3,2,1,0:T(8,128)(2,1)S(1)} %pad_maximum_fusion.2), channel_id=1, source_target_pairs={{0,4},{4,0},{1,5},{5,1},{2,6},{6,2},{3,7},{7,3},{8,12},{12,8},{9,1... | collective-permute-start | bytes 983048 | tf_op jit(solution)/shard_map/ppermute | solution.py:772
  30.8 10.9 %all_to_all.21.recv_ref = f32[16,4,128]{2,1,0:T(4,128)S(1)} all-to-all(f32[16,4,128]{2,1,0:T(4,128)S(1)} %get-tuple-element.94), channel_id=1, replica_groups=mesh['fz'=4,'fx'=2,'ty'=2,'tc'=2] {'fz','fx','ty'}, dimensions={0} | all-to-all | bytes 65536 | tf_op jit(solution)/shard_map/all_to_all | solution.py:831
  41.9 0.7 states.1
  43.4 0.9 %collective-permute-done.6.got_ref = f32[128,512]{1,0:T(8,128)S(1)} collective-permute-done((f32[128,512]{1,0:T(8,128)S(1)}, f32[128,512]{1,0:T(8,128)S(1)}, u32[]{:S(2)}, u32[]{:S(2)}) %collective-permute-start.6) | collective-permute-done | bytes 262176 | tf_op jit(solution)/shard_map/ppermute | solution.py:772
  45.4 0.8 sums.1
  46.7 0.8 back.1
  47.5 0.7 collective-permute-start.9
  48.1 10.2 %all_to_all.22.recv_ref = f32[16,4,128]{2,1,0:T(4,128)S(1)} all-to-all(f32[16,4,128]{2,1,0:T(4,128)S(1)} %get-tuple-element.115), channel_id=1, replica_groups=mesh['fz'=4,'fx'=2,'ty'=2,'tc'=2] {'fz','fx','ty'}, dimensions={0} | all-to-all | bytes 65536 | tf_op jit(solution)/shard_map/all_to_all | solution.py:866
  58.4 1.1 %collective-permute-start.10 = (bf16[4,160,128]{2,1,0:T(8,128)(2,1)S(1)}, bf16[4,160,128]{2,1,0:T(8,128)(2,1)S(1)}, u32[]{:S(2)}, u32[]{:S(2)}) collective-permute-start(bf16[4,160,128]{2,1,0:T(8,128)(2,1)S(1)} %get-tuple-element.121), channel_id=1, source_target_pairs={{0,2},{2,0},{1,3},{3,1},{4,6},{6,4},{5,7},{7,5},{8,10},{10,8},{9,1... | collective-permute-start | bytes 491528 | tf_op jit(solution)/shard_map/ppermute | solution.py:772
  59.5 1.1 %third.1 = (bf16[432,128]{1,0:T(8,128)(2,1)S(1)}, bf16[432,128]{1,0:T(8,128)(2,1)S(1)}, bf16[432,128]{1,0:T(8,128)(2,1)S(1)}, bf16[432,128]{1,0:T(8,128)(2,1)S(1...) custom-call(f32[16,4,128]{2,1,0:T(4,128)S(1)} %all_to_all.22.recv_ref, f32[4,128]{1,0:T(4,128)S(1)} %copy-done.2, ...), custom_call_target="tpu_custom_call" | custom-call | bytes 5400000 | tf_op jit(solution)/shard_map/third/pallas_call | solution.py:755
  60.6 1.1 %collective-permute-start.11 = (bf16[432,128]{1,0:T(8,128)(2,1)S(1)}, bf16[432,128]{1,0:T(8,128)(2,1)S(1)}, u32[]{:S(2)}, u32[]{:S(2)}) collective-permute-start(bf16[432,128]{1,0:T(8,128)(2,1)S(1)} %get-tuple-element.130), channel_id=1, source_target_pairs={{0,2},{2,0},{1,3},{3,1},{4,6},{6,4},{5,7},{7,5},{8,10},{10,8},{9,1... | collective-permute-start | bytes 331784 | tf_op jit(solution)/shard_map/ppermute | solution.py:772
  62.3 1.9 %collective-permute-start.13 = (bf16[432,128]{1,0:T(8,128)(2,1)S(1)}, bf16[432,128]{1,0:T(8,128)(2,1)S(1)}, u32[]{:S(2)}, u32[]{:S(2)}) collective-permute-start(bf16[432,128]{1,0:T(8,128)(2,1)S(1)} %get-tuple-element.132), channel_id=1, source_target_pairs={{0,6},{2,4},{4,2},{6,0},{1,7},{3,5},{5,3},{7,1},{8,14},{10,12},{12... | collective-permute-start | bytes 331784 | tf_op jit(solution)/shard_map/ppermute | solution.py:776
  64.1 4.4 %collective-permute-done.11.y_ref = bf16[432,128]{1,0:T(8,128)(2,1)S(1)} collective-permute-done((bf16[432,128]{1,0:T(8,128)(2,1)S(1)}, bf16[432,128]{1,0:T(8,128)(2,1)S(1)}, u32[]{:S(2)}, u32[]{:S(2)}) %collective-permute-start.11) | collective-permute-done | bytes 110624 | tf_op jit(solution)/shard_map/ppermute | solution.py:772
  68.6 10.3 %all_to_all.23.got_ref = bf16[4,304,128]{2,1,0:T(8,128)(2,1)S(1)} all-to-all(bf16[4,304,128]{2,1,0:T(8,128)(2,1)S(1)} %plane_add.1), channel_id=1, replica_groups=mesh['fz'=4,'fx'=2,'ty'=2,'tc'=2] {'fz'}, dimensions={0} | all-to-all | bytes 622592 | tf_op jit(solution)/shard_map/all_to_all | solution.py:894
  79.5 0.8 matrices.1
  80.3 1.0 %finish.1 = (f32[128,512]{1,0:T(8,128)}, f32[1,16]{1,0:T(1,128)}, f32[1,512]{1,0:T(1,128)}, f32[1,512]{1,0:T(1,128)}, f32[1,512]{1,0:T(1,128)}, /*index=5*/f32[3...) custom-call(f32[24,128]{1,0:T(8,128)S(1)} %vectors.1.own_ref, f32[24,128]{1,0:T(8,128)S(1)} %collective-permute-done.14.other_ref, ...), custom_call_target="tpu_custom_call" | custom-call | bytes 1440000 | tf_op jit(solution)/shard_map/finish/pallas_call | solution.py:755
  (38 shorter events, 5.9 us)
Async XLA Ops:
  18.0 1.6 %copy-start = (bf16[128,512]{1,0:T(8,128)(2,1)S(1)}, bf16[128,512]{1,0:T(8,128)(2,1)}, u32[]{:S(2)}) copy-start(bf16[128,512]{1,0:T(8,128)(2,1)} %x_ref.3) | copy-start | bytes 393220
  18.0 5.1 %copy-start.1 = (bf16[128,512]{1,0:T(8,128)(2,1)S(1)}, bf16[128,512]{1,0:T(8,128)(2,1)}, u32[]{:S(2)}) copy-start(bf16[128,512]{1,0:T(8,128)(2,1)} %up_ref.3) | copy-start | bytes 393220
  18.0 5.1 %copy-start.2 = (f32[4,128]{1,0:T(4,128)S(1)}, f32[4,128]{1,0:T(4,128)}, u32[]{:S(2)}) copy-start(f32[4,128]{1,0:T(4,128)} %get-tuple-element.86.start_ref) | copy-start | bytes 6148
  18.1 10.5 %collective-permute-start.3 = (bf16[4,160,128]{2,1,0:T(8,128)(2,1)S(1)}, bf16[4,160,128]{2,1,0:T(8,128)(2,1)S(1)}, u32[]{:S(2)}, u32[]{:S(2)}) collective-permute-start(bf16[4,160,128]{2,1,0:T(8,128)(2,1)S(1)} %slice.13), channel_id=1, source_target_pairs={{0,2},{2,0},{1,3},{3,1},{4,6},{6,4},{5,7},{7,5},{8,10},{10,8},{9,1... | collective-permute-start | bytes 491528 | tf_op jit(solution)/shard_map/ppermute | solution.py:772
  19.6 3.5 %collective-permute-start.4 = (bf16[128,512]{1,0:T(8,128)(2,1)S(1)}, bf16[128,512]{1,0:T(8,128)(2,1)S(1)}, u32[]{:S(2)}, u32[]{:S(2)}) collective-permute-start(bf16[128,512]{1,0:T(8,128)(2,1)S(1)} %copy-done), channel_id=1, source_target_pairs={{0,1},{1,0},{2,3},{3,2},{4,5},{5,4},{6,7},{7,6},{8,9},{9,8},{10,11... | collective-permute-start | bytes 393224 | tf_op jit(solution)/shard_map/ppermute | solution.py:772
  19.6 6.8 %collective-permute-start.2 = (bf16[4,112,128]{2,1,0:T(8,128)(2,1)S(1)}, bf16[4,112,128]{2,1,0:T(8,128)(2,1)S(1)}, u32[]{:S(2)}, u32[]{:S(2)}) collective-permute-start(bf16[4,112,128]{2,1,0:T(8,128)(2,1)S(1)} %slice.12), channel_id=1, source_target_pairs={{0,6},{2,4},{4,2},{6,0},{1,7},{3,5},{5,3},{7,1},{8,14},{10,12},{12... | collective-permute-start | bytes 344072 | tf_op jit(solution)/shard_map/ppermute | solution.py:776
  21.4 6.6 %collective-permute-start.1 = (bf16[4,112,128]{2,1,0:T(8,128)(2,1)S(1)}, bf16[4,112,128]{2,1,0:T(8,128)(2,1)S(1)}, u32[]{:S(2)}, u32[]{:S(2)}) collective-permute-start(bf16[4,112,128]{2,1,0:T(8,128)(2,1)S(1)} %slice.12), channel_id=1, source_target_pairs={{0,4},{4,0},{1,5},{5,1},{2,6},{6,2},{3,7},{7,3},{8,12},{12,8},{9,1... | collective-permute-start | bytes 344072 | tf_op jit(solution)/shard_map/ppermute | solution.py:772
  21.9 6.7 %collective-permute-start = (bf16[4,112,128]{2,1,0:T(8,128)(2,1)S(1)}, bf16[4,112,128]{2,1,0:T(8,128)(2,1)S(1)}, u32[]{:S(2)}, u32[]{:S(2)}) collective-permute-start(bf16[4,112,128]{2,1,0:T(8,128)(2,1)S(1)} %slice.12), channel_id=1, source_target_pairs={{0,2},{2,0},{1,3},{3,1},{4,6},{6,4},{5,7},{7,5},{8,10},{10,8},{9,1... | collective-permute-start | bytes 344072 | tf_op jit(solution)/shard_map/ppermute | solution.py:772
  28.6 13.1 %collective-permute-start.5 = (bf16[2,4,160,128]{3,2,1,0:T(8,128)(2,1)S(1)}, bf16[2,4,160,128]{3,2,1,0:T(8,128)(2,1)S(1)}, u32[]{:S(2)}, u32[]{:S(2)}) collective-permute-start(bf16[2,4,160,128]{3,2,1,0:T(8,128)(2,1)S(1)} %pad_maximum_fusion.2), channel_id=1, source_target_pairs={{0,4},{4,0},{1,5},{5,1},{2,6},{6,2},{3,7},{7,3},{8,12},{12,8},{9,1... | collective-permute-start | bytes 983048 | tf_op jit(solution)/shard_map/ppermute | solution.py:772
  41.8 1.6 %collective-permute-start.7 = (bf16[2,2,4,64,128]{4,3,2,1,0:T(8,128)(2,1)S(1)}, bf16[2,2,4,64,128]{4,3,2,1,0:T(8,128)(2,1)S(1)}, u32[]{:S(2)}, u32[]{:S(2)}) collective-permute-start(bf16[2,2,4,64,128]{4,3,2,1,0:T(8,128)(2,1)S(1)} %fusion), channel_id=1, source_target_pairs={{0,1},{1,0},{2,3},{3,2},{4,5},{5,4},{6,7},{7,6},{8,9},{9,8},{10,11... | collective-permute-start | bytes 786440 | tf_op jit(solution)/shard_map/ppermute | solution.py:772
  42.6 1.7 %collective-permute-start.6 = (f32[128,512]{1,0:T(8,128)S(1)}, f32[128,512]{1,0:T(8,128)S(1)}, u32[]{:S(2)}, u32[]{:S(2)}) collective-permute-start(f32[128,512]{1,0:T(8,128)S(1)} %get-tuple-element.103), channel_id=1, source_target_pairs={{0,1},{1,0},{2,3},{3,2},{4,5},{5,4},{6,7},{7,6},{8,9},{9,8},{10,11... | collective-permute-start | bytes 786440 | tf_op jit(solution)/shard_map/ppermute | solution.py:772
  45.0 1.7 %collective-permute-start.8 = (bf16[128,1280]{1,0:T(8,128)(2,1)S(1)}, bf16[128,1280]{1,0:T(8,128)(2,1)S(1)}, u32[]{:S(2)}, u32[]{:S(2)}) collective-permute-start(bf16[128,1280]{1,0:T(8,128)(2,1)S(1)} %get-tuple-element.112), channel_id=1, source_target_pairs={{0,1},{1,0},{2,3},{3,2},{4,5},{5,4},{6,7},{7,6},{8,9},{9,8},{10,11... | collective-permute-start | bytes 983048 | tf_op jit(solution)/shard_map/ppermute | solution.py:772
  47.5 10.8 %collective-permute-start.9 = (bf16[2,4,160,128]{3,2,1,0:T(8,128)(2,1)S(1)}, bf16[2,4,160,128]{3,2,1,0:T(8,128)(2,1)S(1)}, u32[]{:S(2)}, u32[]{:S(2)}) collective-permute-start(bf16[2,4,160,128]{3,2,1,0:T(8,128)(2,1)S(1)} %get-tuple-element.116), channel_id=1, source_target_pairs={{0,4},{4,0},{1,5},{5,1},{2,6},{6,2},{3,7},{7,3},{8,12},{12,8},{9,1... | collective-permute-start | bytes 983048 | tf_op jit(solution)/shard_map/ppermute | solution.py:772
  58.4 10.1 %collective-permute-start.10 = (bf16[4,160,128]{2,1,0:T(8,128)(2,1)S(1)}, bf16[4,160,128]{2,1,0:T(8,128)(2,1)S(1)}, u32[]{:S(2)}, u32[]{:S(2)}) collective-permute-start(bf16[4,160,128]{2,1,0:T(8,128)(2,1)S(1)} %get-tuple-element.121), channel_id=1, source_target_pairs={{0,2},{2,0},{1,3},{3,1},{4,6},{6,4},{5,7},{7,5},{8,10},{10,8},{9,1... | collective-permute-start | bytes 491528 | tf_op jit(solution)/shard_map/ppermute | solution.py:772
  60.6 7.9 %collective-permute-start.11 = (bf16[432,128]{1,0:T(8,128)(2,1)S(1)}, bf16[432,128]{1,0:T(8,128)(2,1)S(1)}, u32[]{:S(2)}, u32[]{:S(2)}) collective-permute-start(bf16[432,128]{1,0:T(8,128)(2,1)S(1)} %get-tuple-element.130), channel_id=1, source_target_pairs={{0,2},{2,0},{1,3},{3,1},{4,6},{6,4},{5,7},{7,5},{8,10},{10,8},{9,1... | collective-permute-start | bytes 331784 | tf_op jit(solution)/shard_map/ppermute | solution.py:772
  61.7 6.9 %collective-permute-start.12 = (bf16[432,128]{1,0:T(8,128)(2,1)S(1)}, bf16[432,128]{1,0:T(8,128)(2,1)S(1)}, u32[]{:S(2)}, u32[]{:S(2)}) collective-permute-start(bf16[432,128]{1,0:T(8,128)(2,1)S(1)} %get-tuple-element.131), channel_id=1, source_target_pairs={{0,4},{4,0},{1,5},{5,1},{2,6},{6,2},{3,7},{7,3},{8,12},{12,8},{9,1... | collective-permute-start | bytes 331784 | tf_op jit(solution)/shard_map/ppermute | solution.py:772
  62.3 6.3 %collective-permute-start.13 = (bf16[432,128]{1,0:T(8,128)(2,1)S(1)}, bf16[432,128]{1,0:T(8,128)(2,1)S(1)}, u32[]{:S(2)}, u32[]{:S(2)}) collective-permute-start(bf16[432,128]{1,0:T(8,128)(2,1)S(1)} %get-tuple-element.132), channel_id=1, source_target_pairs={{0,6},{2,4},{4,2},{6,0},{1,7},{3,5},{5,3},{7,1},{8,14},{10,12},{12... | collective-permute-start | bytes 331784 | tf_op jit(solution)/shard_map/ppermute | solution.py:776
  78.9 1.4 %collective-permute-start.15 = (bf16[128,512]{1,0:T(8,128)(2,1)S(1)}, bf16[128,512]{1,0:T(8,128)(2,1)S(1)}, u32[]{:S(2)}, u32[]{:S(2)}) collective-permute-start(bf16[128,512]{1,0:T(8,128)(2,1)S(1)} %get-tuple-element.135), channel_id=1, source_target_pairs={{0,1},{1,0},{2,3},{3,2},{4,5},{5,4},{6,7},{7,6},{8,9},{9,8},{10,11... | collective-permute-start | bytes 393224 | tf_op jit(solution)/shard_map/ppermute | solution.py:772
  78.9 1.4 %collective-permute-start.14 = (f32[24,128]{1,0:T(8,128)S(1)}, f32[24,128]{1,0:T(8,128)S(1)}, u32[]{:S(2)}, u32[]{:S(2)}) collective-permute-start(f32[24,128]{1,0:T(8,128)S(1)} %vectors.1.own_ref), channel_id=1, source_target_pairs={{0,1},{1,0},{2,3},{3,2},{4,5},{5,4},{6,7},{7,6},{8,9},{9,8},{10,11... | collective-permute-start | bytes 36872 | tf_op jit(solution)/shard_map/ppermute | solution.py:772
